TPU v7x, 256 devices: a whole 4x4x8 slice. The times are simulated.
256 devices in a mesh: gx: 32 (over z, y), gy: 8 (over x, core).
Axes of the slice: x: 4, y: 4, z: 8, core: 2. Of those that a mesh axis runs over, the one named last changes fastest.
Arguments:
- right_side: float32 [2, 128, 64, 384], P(None, 'gx', 'gy'), may hold values from -6 to 6
- velocity_table: float32 [16], replicated, may hold values from 2500 to 5000
- layer_index: int32 [128, 64, 384], P('gx', 'gy'), may hold values from 0 to 15
- absorb_level: int32 [128, 64, 384], P('gx', 'gy'), may hold values from 0 to 3
Outputs:
- solution_field: float32 [2, 128, 64, 384], P(None, 'gx', 'gy')
All inputs are finite; a program needn't handle non-finite values.
Results may differ from a plain program's by a relative error of at most 0.0001.
Values sent between devices are 32-bit elements; how exact they have to be, the bound alone decides.
No kernel may reach another device: no remote copies, remote signals or barrier semaphores. Data moves between devices by JAX's collectives and lax.ppermute only.
A program may use at most 64 MiB of HBM per device.

v0:
```python
import math

import jax
import jax.numpy as jnp
from jax import lax
from jax.sharding import PartitionSpec as P

NU = 2
NC = 8


OMEGA = 0.6
BETA = 0.5
ABSORB = 0.25
KH_FACTOR = 2.0 * math.pi * 6.0 * 20.0


def extended_2(block, sides, width):
    for axis, dim in sides:
        count = lax.axis_size(axis)
        forward = [(i, i + 1) for i in range(count - 1)]
        backward = [(target, source) for source, target in forward]
        low = lax.ppermute(
            lax.slice_in_dim(block, block.shape[dim] - width, None, axis=dim), axis, forward
        )
        high = lax.ppermute(lax.slice_in_dim(block, 0, width, axis=dim), axis, backward)
        block = jnp.concatenate([low, block, high], axis=dim)
    return block


def complex_product(first, second):
    return jnp.stack(
        [first[0] * second[0] - first[1] * second[1], first[0] * second[1] + first[1] * second[0]]
    )


def neighbour_sum(padded):
    total = padded[:, 2:, 1:-1, 1:-1] + padded[:, :-2, 1:-1, 1:-1]
    total = total + padded[:, 1:-1, 2:, 1:-1] + padded[:, 1:-1, :-2, 1:-1]
    total = total + padded[:, 1:-1, 1:-1, 2:] + padded[:, 1:-1, 1:-1, :-2]
    return total


def pad_faces(field):
    extended = extended_2(field, (("gx", 1), ("gy", 2)), 1)
    return jnp.pad(extended, ((0, 0), (0, 0), (0, 0), (1, 1)))


def apply_operator(field, padded, shift_term, grid_level):
    return (6.0 * field - neighbour_sum(padded)) * 0.25**grid_level - complex_product(
        shift_term, field
    )


def restrict(field):
    size_x, size_y, size_z = (field.shape[1], field.shape[2], field.shape[3])
    return field.reshape(2, size_x // 2, 2, size_y // 2, 2, size_z // 2, 2).mean(axis=(2, 4, 6))


def prolong(field):
    return jnp.repeat(jnp.repeat(jnp.repeat(field, 2, 1), 2, 2), 2, 3)


def inverse_of(shift_term, grid_level):
    diag_real = 6.0 * 0.25**grid_level - shift_term[0]
    diag_imag = -shift_term[1]
    denom = diag_real * diag_real + diag_imag * diag_imag
    return jnp.stack([diag_real / denom, -diag_imag / denom])


def smooth(update, source, shift_term, inverse_diag, grid_level, sweeps, padder):
    for sweep in range(sweeps):
        image = apply_operator(update, padder(update), shift_term, grid_level)
        update = update + OMEGA * complex_product(inverse_diag, source - image)
    return update


def coarse_solve(source, shift_term, inverse_diag):
    return smooth(jnp.zeros_like(source), source, shift_term, inverse_diag, 2, NC, pad_faces)


def vcycle(source, shifts, inverses, grid_level):
    if grid_level == 2:
        return coarse_solve(source, shifts[2], inverses[2])
    update = smooth(
        jnp.zeros_like(source),
        source,
        shifts[grid_level],
        inverses[grid_level],
        grid_level,
        NU,
        pad_faces,
    )
    residual = source - apply_operator(update, pad_faces(update), shifts[grid_level], grid_level)
    correction = vcycle(restrict(residual), shifts, inverses, grid_level + 1)
    update = update + prolong(correction)
    return smooth(
        update, source, shifts[grid_level], inverses[grid_level], grid_level, NU, pad_faces
    )


def local(right_side, velocity_table, layer_index, absorb_level):
    velocity = jnp.zeros(layer_index.shape, jnp.float32)
    for layer_number in range(velocity_table.shape[0]):
        velocity = jnp.where(layer_index == layer_number, velocity_table[layer_number], velocity)
    kh_square = (KH_FACTOR / velocity) ** 2
    damping = BETA + ABSORB * absorb_level.astype(jnp.float32)
    shift_zero = jnp.stack([kh_square, -kh_square * damping])
    shift_one = restrict(shift_zero)
    shift_two = restrict(shift_one)
    shifts = (shift_zero, shift_one, shift_two)
    inverses = (inverse_of(shift_zero, 0), inverse_of(shift_one, 1), inverse_of(shift_two, 2))
    first = vcycle(right_side, shifts, inverses, 0)
    residual = right_side - apply_operator(first, pad_faces(first), shift_zero, 0)
    first = first + vcycle(residual, shifts, inverses, 0)
    return first


def solution(mesh):
    placed = (P(None, "gx", "gy", None), P(), P("gx", "gy", None), P("gx", "gy", None))
    return jax.shard_map(
        local, mesh=mesh, in_specs=placed, out_specs=P(None, "gx", "gy", None), check_vma=False
    )
```

profile of v0, /device:TPU:126, one launch (start us, length us, event | category | flops | bytes accessed | tf_op | source)
XLA Modules:
  0.0 662.0 jit_solution(8435892169947883428)
XLA Ops:
  0.0 4.7 collective-permute-start.25
  6.6 7.2 %collective-permute-start.1 = (f32[2,1,8,384]{3,2,1,0:T(8,128)S(1)}, f32[2,1,8,384]{3,2,1,0:T(8,128)S(1)}, u32[]{:S(2)}, u32[]{:S(2)}) collective-permute-start(f32[2,1,8,384]{3,2,1,0:T(8,128)S(1)} %broadcast.929), channel_id=1, source_target_pairs={{0,8},{8,16},{16,24},{24,32},{32,40},{40,48},{48,56},{56,64},{64,7... | collective-permute-start | bytes 73736 | tf_op jit(solution)/shard_map/ppermute | solution.py:23
  15.8 7.2 %collective-permute-start.13 = (f32[2,1,4,192]{3,2,1,0:T(4,128)S(1)}, f32[2,1,4,192]{3,2,1,0:T(4,128)S(1)}, u32[]{:S(2)}, u32[]{:S(2)}) collective-permute-start(f32[2,1,4,192]{3,2,1,0:T(4,128)S(1)} %broadcast.934), channel_id=1, source_target_pairs={{0,8},{8,16},{16,24},{24,32},{32,40},{40,48},{48,56},{56,64},{64,7... | collective-permute-start | bytes 18440 | tf_op jit(solution)/shard_map/ppermute | solution.py:23
  25.0 10.9 %add_multiply_fusion = (f32[4,8,384]{2,1,0:T(8,128)S(1)}, f32[4,8,384]{2,1,0:T(8,128)S(1)}) fusion(s32[4,8,384]{2,1,0:T(8,128)} %param.7, f32[]{:T(128)} %bitcast.15, s32[4,8,384]{2,1,0:T(8,128)} %param.6, f32[]{:T(128)} %bitcast.14, f32[]{:T(128)} %bitcast.13, f32[]{:T(128)} %bitcast.12, f32[]{:T(128)} %bitcast.11, f32[]{:T(128)} %bitcast.10, f32[]{:T(128)} %bitcast.9, ...), kind=kLoop, calls=%fused_computation.330 | loop fusion | flops 479232 | bytes 196672 | tf_op jit(solution)/shard_map/mul | solution.py:108
  39.9 4.9 stack.525
  58.2 7.2 %collective-permute-start.5 = (f32[2,1,8,384]{3,2,1,0:T(8,128)S(1)}, f32[2,1,8,384]{3,2,1,0:T(8,128)S(1)}, u32[]{:S(2)}, u32[]{:S(2)}) collective-permute-start(f32[2,1,8,384]{3,2,1,0:T(8,128)S(1)} %get-tuple-element.92), channel_id=1, source_target_pairs={{0,8},{8,16},{16,24},{24,32},{32,40},{40,48},{48,56},{56,64},{64,7... | collective-permute-start | bytes 73736 | tf_op jit(solution)/shard_map/ppermute | solution.py:23
  82.1 5.8 collective-permute-start.9
  90.0 7.0 %collective-permute-done.8 = f32[2,1,8,384]{3,2,1,0:T(8,128)S(1)} collective-permute-done((f32[2,1,8,384]{3,2,1,0:T(8,128)S(1)}, f32[2,1,8,384]{3,2,1,0:T(8,128)S(1)}, u32[]{:S(2)}, u32[]{:S(2)}) %collective-permute-start.8) | collective-permute-done | bytes 24608 | tf_op jit(solution)/shard_map/ppermute | solution.py:26
  104.4 8.1 %reshape.2946 = f32[2,2,2,4,2,192,2]{6,5,4,3,2,1,0:T(8,128)} reshape(f32[2,4,8,384]{3,2,1,0:T(8,128)S(1)} %fusion.52) | data formatting | bytes 196608 | tf_op jit(solution)/shard_map/reshape | solution.py:57
  118.5 3.9 collective-permute-start.16
  135.3 5.2 collective-permute-start.21
  142.6 6.8 %collective-permute-done.20 = f32[2,1,4,192]{3,2,1,0:T(4,128)S(1)} collective-permute-done((f32[2,1,4,192]{3,2,1,0:T(4,128)S(1)}, f32[2,1,4,192]{3,2,1,0:T(4,128)S(1)}, u32[]{:S(2)}, u32[]{:S(2)}) %collective-permute-start.20) | collective-permute-done | bytes 6176 | tf_op jit(solution)/shard_map/ppermute | solution.py:26
  159.1 4.1 collective-permute-start.28
  163.3 4.9 collective-permute-done.28
  177.1 3.9 collective-permute-start.32
  181.1 4.9 collective-permute-done.32
  198.9 4.9 collective-permute-done.36
  216.7 4.9 collective-permute-done.40
  230.6 3.9 collective-permute-start.44
  234.5 4.9 collective-permute-done.44
  252.3 4.9 collective-permute-done.48
  270.2 4.9 collective-permute-done.52
  284.4 3.9 collective-permute-start.56
  288.4 4.9 collective-permute-done.56
  306.4 4.9 collective-permute-done.60
  325.8 5.1 collective-permute-done.64
  341.0 3.9 collective-permute-start.68
  344.9 5.1 collective-permute-done.68
  363.5 5.1 collective-permute-done.72
  382.0 5.1 collective-permute-done.76
  400.5 5.1 collective-permute-done.80
  413.1 8.1 %reshape.2950 = f32[2,2,2,4,2,192,2]{6,5,4,3,2,1,0:T(8,128)} reshape(f32[2,4,8,384]{3,2,1,0:T(8,128)S(1)} %fusion.22) | data formatting | bytes 196608 | tf_op jit(solution)/shard_map/reshape | solution.py:57
  430.5 4.9 collective-permute-done.84
  448.6 4.9 collective-permute-done.88
  467.0 4.9 collective-permute-done.92
  484.9 4.9 collective-permute-done.96
  502.7 4.9 collective-permute-done.100
  520.5 4.9 collective-permute-done.104
  534.4 3.9 collective-permute-start.108
  538.3 4.9 collective-permute-done.108
  556.1 4.9 collective-permute-done.112
  574.0 4.9 collective-permute-done.116
  588.2 3.9 collective-permute-start.120
  592.1 4.9 collective-permute-done.120
  610.2 4.9 collective-permute-done.124
  625.6 3.9 collective-permute-start.128
  629.6 5.1 collective-permute-done.128
  648.6 5.1 collective-permute-done.132
  (557 shorter events, 406.7 us)
Async XLA Ops:
  0.0 52.0 %collective-permute-start.25 = (f32[2,1,2,96]{3,2,1,0:T(2,128)S(1)}, f32[2,1,2,96]{3,2,1,0:T(2,128)S(1)}, u32[]{:S(2)}, u32[]{:S(2)}) collective-permute-start(f32[2,1,2,96]{3,2,1,0:T(2,128)S(1)} %broadcast.940), channel_id=1, source_target_pairs={{0,8},{8,16},{16,24},{24,32},{32,40},{40,48},{48,56},{56,64},{64,7... | collective-permute-start | bytes 4616 | tf_op jit(solution)/shard_map/ppermute | solution.py:23
  4.7 49.7 %collective-permute-start.24 = (f32[2,1,2,96]{3,2,1,0:T(2,128)S(1)}, f32[2,1,2,96]{3,2,1,0:T(2,128)S(1)}, u32[]{:S(2)}, u32[]{:S(2)}) collective-permute-start(f32[2,1,2,96]{3,2,1,0:T(2,128)S(1)} %broadcast.940), channel_id=1, source_target_pairs={{8,0},{16,8},{24,16},{32,24},{40,32},{48,40},{56,48},{64,56},{72,6... | collective-permute-start | bytes 4616 | tf_op jit(solution)/shard_map/ppermute | solution.py:26
  6.6 41.4 %collective-permute-start.1 = (f32[2,1,8,384]{3,2,1,0:T(8,128)S(1)}, f32[2,1,8,384]{3,2,1,0:T(8,128)S(1)}, u32[]{:S(2)}, u32[]{:S(2)}) collective-permute-start(f32[2,1,8,384]{3,2,1,0:T(8,128)S(1)} %broadcast.929), channel_id=1, source_target_pairs={{0,8},{8,16},{16,24},{24,32},{32,40},{40,48},{48,56},{56,64},{64,7... | collective-permute-start | bytes 73736 | tf_op jit(solution)/shard_map/ppermute | solution.py:23
  13.9 36.1 %collective-permute-start = (f32[2,1,8,384]{3,2,1,0:T(8,128)S(1)}, f32[2,1,8,384]{3,2,1,0:T(8,128)S(1)}, u32[]{:S(2)}, u32[]{:S(2)}) collective-permute-start(f32[2,1,8,384]{3,2,1,0:T(8,128)S(1)} %broadcast.929), channel_id=1, source_target_pairs={{8,0},{16,8},{24,16},{32,24},{40,32},{48,40},{56,48},{64,56},{72,6... | collective-permute-start | bytes 73736 | tf_op jit(solution)/shard_map/ppermute | solution.py:26
  15.8 51.6 %collective-permute-start.13 = (f32[2,1,4,192]{3,2,1,0:T(4,128)S(1)}, f32[2,1,4,192]{3,2,1,0:T(4,128)S(1)}, u32[]{:S(2)}, u32[]{:S(2)}) collective-permute-start(f32[2,1,4,192]{3,2,1,0:T(4,128)S(1)} %broadcast.934), channel_id=1, source_target_pairs={{0,8},{8,16},{16,24},{24,32},{32,40},{40,48},{48,56},{56,64},{64,7... | collective-permute-start | bytes 18440 | tf_op jit(solution)/shard_map/ppermute | solution.py:23
  48.0 19.4 %collective-permute-start.12 = (f32[2,1,4,192]{3,2,1,0:T(4,128)S(1)}, f32[2,1,4,192]{3,2,1,0:T(4,128)S(1)}, u32[]{:S(2)}, u32[]{:S(2)}) collective-permute-start(f32[2,1,4,192]{3,2,1,0:T(4,128)S(1)} %broadcast.934), channel_id=1, source_target_pairs={{8,0},{16,8},{24,16},{32,24},{40,32},{48,40},{56,48},{64,56},{72,6... | collective-permute-start | bytes 18440 | tf_op jit(solution)/shard_map/ppermute | solution.py:26
  58.2 14.8 %collective-permute-start.5 = (f32[2,1,8,384]{3,2,1,0:T(8,128)S(1)}, f32[2,1,8,384]{3,2,1,0:T(8,128)S(1)}, u32[]{:S(2)}, u32[]{:S(2)}) collective-permute-start(f32[2,1,8,384]{3,2,1,0:T(8,128)S(1)} %get-tuple-element.92), channel_id=1, source_target_pairs={{0,8},{8,16},{16,24},{24,32},{32,40},{40,48},{48,56},{56,64},{64,7... | collective-permute-start | bytes 73736 | tf_op jit(solution)/shard_map/ppermute | solution.py:23
  65.5 9.0 %collective-permute-start.4 = (f32[2,1,8,384]{3,2,1,0:T(8,128)S(1)}, f32[2,1,8,384]{3,2,1,0:T(8,128)S(1)}, u32[]{:S(2)}, u32[]{:S(2)}) collective-permute-start(f32[2,1,8,384]{3,2,1,0:T(8,128)S(1)} %get-tuple-element.93), channel_id=1, source_target_pairs={{8,0},{16,8},{24,16},{32,24},{40,32},{48,40},{56,48},{64,56},{72,6... | collective-permute-start | bytes 73736 | tf_op jit(solution)/shard_map/ppermute | solution.py:26
  67.5 22.3 %collective-permute-start.15 = (f32[2,4,1,192]{3,2,1,0:T(1,128)S(1)}, f32[2,4,1,192]{3,2,1,0:T(1,128)S(1)}, u32[]{:S(2)}, u32[]{:S(2)}) collective-permute-start(f32[2,4,1,192]{3,2,1,0:T(1,128)S(1)} %get-tuple-element.142), channel_id=1, source_target_pairs={{0,1},{1,2},{2,3},{3,4},{4,5},{5,6},{6,7},{8,9},{9,10},{10,11},{11... | collective-permute-start | bytes 18440 | tf_op jit(solution)/shard_map/ppermute | solution.py:23
  69.4 20.4 %collective-permute-start.14 = (f32[2,4,1,192]{3,2,1,0:T(1,128)S(1)}, f32[2,4,1,192]{3,2,1,0:T(1,128)S(1)}, u32[]{:S(2)}, u32[]{:S(2)}) collective-permute-start(f32[2,4,1,192]{3,2,1,0:T(1,128)S(1)} %get-tuple-element.143), channel_id=1, source_target_pairs={{1,0},{2,1},{3,2},{4,3},{5,4},{6,5},{7,6},{9,8},{10,9},{11,10},{12... | collective-permute-start | bytes 18440 | tf_op jit(solution)/shard_map/ppermute | solution.py:26
  82.1 7.9 %collective-permute-start.9 = (f32[2,1,8,384]{3,2,1,0:T(8,128)S(1)}, f32[2,1,8,384]{3,2,1,0:T(8,128)S(1)}, u32[]{:S(2)}, u32[]{:S(2)}) collective-permute-start(f32[2,1,8,384]{3,2,1,0:T(8,128)S(1)} %get-tuple-element.90), channel_id=1, source_target_pairs={{0,8},{8,16},{16,24},{24,32},{32,40},{40,48},{48,56},{56,64},{64,7... | collective-permute-start | bytes 73736 | tf_op jit(solution)/shard_map/ppermute | solution.py:23
  87.9 9.0 %collective-permute-start.8 = (f32[2,1,8,384]{3,2,1,0:T(8,128)S(1)}, f32[2,1,8,384]{3,2,1,0:T(8,128)S(1)}, u32[]{:S(2)}, u32[]{:S(2)}) collective-permute-start(f32[2,1,8,384]{3,2,1,0:T(8,128)S(1)} %get-tuple-element.91), channel_id=1, source_target_pairs={{8,0},{16,8},{24,16},{32,24},{40,32},{48,40},{56,48},{64,56},{72,6... | collective-permute-start | bytes 73736 | tf_op jit(solution)/shard_map/ppermute | solution.py:26
  116.6 11.5 %collective-permute-start.17 = (f32[2,1,4,192]{3,2,1,0:T(4,128)S(1)}, f32[2,1,4,192]{3,2,1,0:T(4,128)S(1)}, u32[]{:S(2)}, u32[]{:S(2)}) collective-permute-start(f32[2,1,4,192]{3,2,1,0:T(4,128)S(1)} %get-tuple-element.160), channel_id=1, source_target_pairs={{0,8},{8,16},{16,24},{24,32},{32,40},{40,48},{48,56},{56,64},{64,7... | collective-permute-start | bytes 18440 | tf_op jit(solution)/shard_map/ppermute | solution.py:23
  118.5 9.5 %collective-permute-start.16 = (f32[2,1,4,192]{3,2,1,0:T(4,128)S(1)}, f32[2,1,4,192]{3,2,1,0:T(4,128)S(1)}, u32[]{:S(2)}, u32[]{:S(2)}) collective-permute-start(f32[2,1,4,192]{3,2,1,0:T(4,128)S(1)} %get-tuple-element.161), channel_id=1, source_target_pairs={{8,0},{16,8},{24,16},{32,24},{40,32},{48,40},{56,48},{64,56},{72,6... | collective-permute-start | bytes 18440 | tf_op jit(solution)/shard_map/ppermute | solution.py:26
  122.5 20.0 %collective-permute-start.27 = (f32[2,3,1,96]{3,2,1,0:T(1,128)S(1)}, f32[2,3,1,96]{3,2,1,0:T(1,128)S(1)}, u32[]{:S(2)}, u32[]{:S(2)}) collective-permute-start(f32[2,3,1,96]{3,2,1,0:T(1,128)S(1)} %get-tuple-element.192), channel_id=1, source_target_pairs={{0,1},{1,2},{2,3},{3,4},{4,5},{5,6},{6,7},{8,9},{9,10},{10,11},{11... | collective-permute-start | bytes 6920 | tf_op jit(solution)/shard_map/ppermute | solution.py:23
  124.4 18.1 %collective-permute-start.26 = (f32[2,3,1,96]{3,2,1,0:T(1,128)S(1)}, f32[2,3,1,96]{3,2,1,0:T(1,128)S(1)}, u32[]{:S(2)}, u32[]{:S(2)}) collective-permute-start(f32[2,3,1,96]{3,2,1,0:T(1,128)S(1)} %get-tuple-element.193), channel_id=1, source_target_pairs={{1,0},{2,1},{3,2},{4,3},{5,4},{6,5},{7,6},{9,8},{10,9},{11,10},{12... | collective-permute-start | bytes 6920 | tf_op jit(solution)/shard_map/ppermute | solution.py:26
  135.3 7.3 %collective-permute-start.21 = (f32[2,1,4,192]{3,2,1,0:T(4,128)S(1)}, f32[2,1,4,192]{3,2,1,0:T(4,128)S(1)}, u32[]{:S(2)}, u32[]{:S(2)}) collective-permute-start(f32[2,1,4,192]{3,2,1,0:T(4,128)S(1)} %get-tuple-element.158), channel_id=1, source_target_pairs={{0,8},{8,16},{16,24},{24,32},{32,40},{40,48},{48,56},{56,64},{64,7... | collective-permute-start | bytes 18440 | tf_op jit(solution)/shard_map/ppermute | solution.py:23
  140.6 8.9 %collective-permute-start.20 = (f32[2,1,4,192]{3,2,1,0:T(4,128)S(1)}, f32[2,1,4,192]{3,2,1,0:T(4,128)S(1)}, u32[]{:S(2)}, u32[]{:S(2)}) collective-permute-start(f32[2,1,4,192]{3,2,1,0:T(4,128)S(1)} %get-tuple-element.159), channel_id=1, source_target_pairs={{8,0},{16,8},{24,16},{32,24},{40,32},{48,40},{56,48},{64,56},{72,6... | collective-permute-start | bytes 18440 | tf_op jit(solution)/shard_map/ppermute | solution.py:26
  157.2 6.0 collective-permute-start.29
  159.1 9.0 %collective-permute-start.28 = (f32[2,1,2,96]{3,2,1,0:T(2,128)S(1)}, f32[2,1,2,96]{3,2,1,0:T(2,128)S(1)}, u32[]{:S(2)}, u32[]{:S(2)}) collective-permute-start(f32[2,1,2,96]{3,2,1,0:T(2,128)S(1)} %broadcast_multiply_fusion.2), channel_id=1, source_target_pairs={{8,0},{16,8},{24,16},{32,24},{40,32},{48,40},{56,48},{64,56},{72,6... | collective-permute-start | bytes 4616 | tf_op jit(solution)/shard_map/ppermute | solution.py:26
  177.1 8.8 %collective-permute-start.32 = (f32[2,1,2,96]{3,2,1,0:T(2,128)S(1)}, f32[2,1,2,96]{3,2,1,0:T(2,128)S(1)}, u32[]{:S(2)}, u32[]{:S(2)}) collective-permute-start(f32[2,1,2,96]{3,2,1,0:T(2,128)S(1)} %fusion.245), channel_id=1, source_target_pairs={{8,0},{16,8},{24,16},{32,24},{40,32},{48,40},{56,48},{64,56},{72,6... | collective-permute-start | bytes 4616 | tf_op jit(solution)/shard_map/ppermute | solution.py:26
  194.9 8.8 %collective-permute-start.36 = (f32[2,1,2,96]{3,2,1,0:T(2,128)S(1)}, f32[2,1,2,96]{3,2,1,0:T(2,128)S(1)}, u32[]{:S(2)}, u32[]{:S(2)}) collective-permute-start(f32[2,1,2,96]{3,2,1,0:T(2,128)S(1)} %fusion.246), channel_id=1, source_target_pairs={{8,0},{16,8},{24,16},{32,24},{40,32},{48,40},{56,48},{64,56},{72,6... | collective-permute-start | bytes 4616 | tf_op jit(solution)/shard_map/ppermute | solution.py:26
  212.8 8.8 %collective-permute-start.40 = (f32[2,1,2,96]{3,2,1,0:T(2,128)S(1)}, f32[2,1,2,96]{3,2,1,0:T(2,128)S(1)}, u32[]{:S(2)}, u32[]{:S(2)}) collective-permute-start(f32[2,1,2,96]{3,2,1,0:T(2,128)S(1)} %fusion.247), channel_id=1, source_target_pairs={{8,0},{16,8},{24,16},{32,24},{40,32},{48,40},{56,48},{64,56},{72,6... | collective-permute-start | bytes 4616 | tf_op jit(solution)/shard_map/ppermute | solution.py:26
  228.7 5.9 collective-permute-start.45
  230.6 8.8 %collective-permute-start.44 = (f32[2,1,2,96]{3,2,1,0:T(2,128)S(1)}, f32[2,1,2,96]{3,2,1,0:T(2,128)S(1)}, u32[]{:S(2)}, u32[]{:S(2)}) collective-permute-start(f32[2,1,2,96]{3,2,1,0:T(2,128)S(1)} %fusion.248), channel_id=1, source_target_pairs={{8,0},{16,8},{24,16},{32,24},{40,32},{48,40},{56,48},{64,56},{72,6... | collective-permute-start | bytes 4616 | tf_op jit(solution)/shard_map/ppermute | solution.py:26
  248.4 8.8 %collective-permute-start.48 = (f32[2,1,2,96]{3,2,1,0:T(2,128)S(1)}, f32[2,1,2,96]{3,2,1,0:T(2,128)S(1)}, u32[]{:S(2)}, u32[]{:S(2)}) collective-permute-start(f32[2,1,2,96]{3,2,1,0:T(2,128)S(1)} %fusion.249), channel_id=1, source_target_pairs={{8,0},{16,8},{24,16},{32,24},{40,32},{48,40},{56,48},{64,56},{72,6... | collective-permute-start | bytes 4616 | tf_op jit(solution)/shard_map/ppermute | solution.py:26
  266.2 8.8 %collective-permute-start.52 = (f32[2,1,2,96]{3,2,1,0:T(2,128)S(1)}, f32[2,1,2,96]{3,2,1,0:T(2,128)S(1)}, u32[]{:S(2)}, u32[]{:S(2)}) collective-permute-start(f32[2,1,2,96]{3,2,1,0:T(2,128)S(1)} %fusion.250), channel_id=1, source_target_pairs={{8,0},{16,8},{24,16},{32,24},{40,32},{48,40},{56,48},{64,56},{72,6... | collective-permute-start | bytes 4616 | tf_op jit(solution)/shard_map/ppermute | solution.py:26
  282.5 5.9 collective-permute-start.57
  284.4 8.9 %collective-permute-start.56 = (f32[2,1,4,192]{3,2,1,0:T(4,128)S(1)}, f32[2,1,4,192]{3,2,1,0:T(4,128)S(1)}, u32[]{:S(2)}, u32[]{:S(2)}) collective-permute-start(f32[2,1,4,192]{3,2,1,0:T(4,128)S(1)} %get-tuple-element.155), channel_id=1, source_target_pairs={{8,0},{16,8},{24,16},{32,24},{40,32},{48,40},{56,48},{64,56},{72,6... | collective-permute-start | bytes 18440 | tf_op jit(solution)/shard_map/ppermute | solution.py:26
  302.4 8.9 %collective-permute-start.60 = (f32[2,1,4,192]{3,2,1,0:T(4,128)S(1)}, f32[2,1,4,192]{3,2,1,0:T(4,128)S(1)}, u32[]{:S(2)}, u32[]{:S(2)}) collective-permute-start(f32[2,1,4,192]{3,2,1,0:T(4,128)S(1)} %get-tuple-element.153), channel_id=1, source_target_pairs={{8,0},{16,8},{24,16},{32,24},{40,32},{48,40},{56,48},{64,56},{72,6... | collective-permute-start | bytes 18440 | tf_op jit(solution)/shard_map/ppermute | solution.py:26
  321.8 9.0 %collective-permute-start.64 = (f32[2,1,8,384]{3,2,1,0:T(8,128)S(1)}, f32[2,1,8,384]{3,2,1,0:T(8,128)S(1)}, u32[]{:S(2)}, u32[]{:S(2)}) collective-permute-start(f32[2,1,8,384]{3,2,1,0:T(8,128)S(1)} %get-tuple-element.89), channel_id=1, source_target_pairs={{8,0},{16,8},{24,16},{32,24},{40,32},{48,40},{56,48},{64,56},{72,6... | collective-permute-start | bytes 73736 | tf_op jit(solution)/shard_map/ppermute | solution.py:26
  341.0 9.0 %collective-permute-start.68 = (f32[2,1,8,384]{3,2,1,0:T(8,128)S(1)}, f32[2,1,8,384]{3,2,1,0:T(8,128)S(1)}, u32[]{:S(2)}, u32[]{:S(2)}) collective-permute-start(f32[2,1,8,384]{3,2,1,0:T(8,128)S(1)} %get-tuple-element.87), channel_id=1, source_target_pairs={{8,0},{16,8},{24,16},{32,24},{40,32},{48,40},{56,48},{64,56},{72,6... | collective-permute-start | bytes 73736 | tf_op jit(solution)/shard_map/ppermute | solution.py:26
  359.5 9.0 %collective-permute-start.72 = (f32[2,1,8,384]{3,2,1,0:T(8,128)S(1)}, f32[2,1,8,384]{3,2,1,0:T(8,128)S(1)}, u32[]{:S(2)}, u32[]{:S(2)}) collective-permute-start(f32[2,1,8,384]{3,2,1,0:T(8,128)S(1)} %get-tuple-element.85), channel_id=1, source_target_pairs={{8,0},{16,8},{24,16},{32,24},{40,32},{48,40},{56,48},{64,56},{72,6... | collective-permute-start | bytes 73736 | tf_op jit(solution)/shard_map/ppermute | solution.py:26
  378.1 9.0 %collective-permute-start.76 = (f32[2,1,8,384]{3,2,1,0:T(8,128)S(1)}, f32[2,1,8,384]{3,2,1,0:T(8,128)S(1)}, u32[]{:S(2)}, u32[]{:S(2)}) collective-permute-start(f32[2,1,8,384]{3,2,1,0:T(8,128)S(1)} %get-tuple-element.83), channel_id=1, source_target_pairs={{8,0},{16,8},{24,16},{32,24},{40,32},{48,40},{56,48},{64,56},{72,6... | collective-permute-start | bytes 73736 | tf_op jit(solution)/shard_map/ppermute | solution.py:26
  396.6 9.0 %collective-permute-start.80 = (f32[2,1,8,384]{3,2,1,0:T(8,128)S(1)}, f32[2,1,8,384]{3,2,1,0:T(8,128)S(1)}, u32[]{:S(2)}, u32[]{:S(2)}) collective-permute-start(f32[2,1,8,384]{3,2,1,0:T(8,128)S(1)} %get-tuple-element.81), channel_id=1, source_target_pairs={{8,0},{16,8},{24,16},{32,24},{40,32},{48,40},{56,48},{64,56},{72,6... | collective-permute-start | bytes 73736 | tf_op jit(solution)/shard_map/ppermute | solution.py:26
  426.6 8.9 %collective-permute-start.84 = (f32[2,1,4,192]{3,2,1,0:T(4,128)S(1)}, f32[2,1,4,192]{3,2,1,0:T(4,128)S(1)}, u32[]{:S(2)}, u32[]{:S(2)}) collective-permute-start(f32[2,1,4,192]{3,2,1,0:T(4,128)S(1)} %get-tuple-element.151), channel_id=1, source_target_pairs={{8,0},{16,8},{24,16},{32,24},{40,32},{48,40},{56,48},{64,56},{72,6... | collective-permute-start | bytes 18440 | tf_op jit(solution)/shard_map/ppermute | solution.py:26
  444.6 8.9 %collective-permute-start.88 = (f32[2,1,4,192]{3,2,1,0:T(4,128)S(1)}, f32[2,1,4,192]{3,2,1,0:T(4,128)S(1)}, u32[]{:S(2)}, u32[]{:S(2)}) collective-permute-start(f32[2,1,4,192]{3,2,1,0:T(4,128)S(1)} %get-tuple-element.149), channel_id=1, source_target_pairs={{8,0},{16,8},{24,16},{32,24},{40,32},{48,40},{56,48},{64,56},{72,6... | collective-permute-start | bytes 18440 | tf_op jit(solution)/shard_map/ppermute | solution.py:26
  463.1 8.8 %collective-permute-start.92 = (f32[2,1,2,96]{3,2,1,0:T(2,128)S(1)}, f32[2,1,2,96]{3,2,1,0:T(2,128)S(1)}, u32[]{:S(2)}, u32[]{:S(2)}) collective-permute-start(f32[2,1,2,96]{3,2,1,0:T(2,128)S(1)} %broadcast_multiply_fusion.1), channel_id=1, source_target_pairs={{8,0},{16,8},{24,16},{32,24},{40,32},{48,40},{56,48},{64,56},{72,6... | collective-permute-start | bytes 4616 | tf_op jit(solution)/shard_map/ppermute | solution.py:26
  480.9 8.8 %collective-permute-start.96 = (f32[2,1,2,96]{3,2,1,0:T(2,128)S(1)}, f32[2,1,2,96]{3,2,1,0:T(2,128)S(1)}, u32[]{:S(2)}, u32[]{:S(2)}) collective-permute-start(f32[2,1,2,96]{3,2,1,0:T(2,128)S(1)} %fusion.257), channel_id=1, source_target_pairs={{8,0},{16,8},{24,16},{32,24},{40,32},{48,40},{56,48},{64,56},{72,6... | collective-permute-start | bytes 4616 | tf_op jit(solution)/shard_map/ppermute | solution.py:26
  498.7 8.8 %collective-permute-start.100 = (f32[2,1,2,96]{3,2,1,0:T(2,128)S(1)}, f32[2,1,2,96]{3,2,1,0:T(2,128)S(1)}, u32[]{:S(2)}, u32[]{:S(2)}) collective-permute-start(f32[2,1,2,96]{3,2,1,0:T(2,128)S(1)} %fusion.258), channel_id=1, source_target_pairs={{8,0},{16,8},{24,16},{32,24},{40,32},{48,40},{56,48},{64,56},{72,6... | collective-permute-start | bytes 4616 | tf_op jit(solution)/shard_map/ppermute | solution.py:26
  516.6 8.8 %collective-permute-start.104 = (f32[2,1,2,96]{3,2,1,0:T(2,128)S(1)}, f32[2,1,2,96]{3,2,1,0:T(2,128)S(1)}, u32[]{:S(2)}, u32[]{:S(2)}) collective-permute-start(f32[2,1,2,96]{3,2,1,0:T(2,128)S(1)} %fusion.259), channel_id=1, source_target_pairs={{8,0},{16,8},{24,16},{32,24},{40,32},{48,40},{56,48},{64,56},{72,6... | collective-permute-start | bytes 4616 | tf_op jit(solution)/shard_map/ppermute | solution.py:26
  534.4 8.8 %collective-permute-start.108 = (f32[2,1,2,96]{3,2,1,0:T(2,128)S(1)}, f32[2,1,2,96]{3,2,1,0:T(2,128)S(1)}, u32[]{:S(2)}, u32[]{:S(2)}) collective-permute-start(f32[2,1,2,96]{3,2,1,0:T(2,128)S(1)} %fusion.260), channel_id=1, source_target_pairs={{8,0},{16,8},{24,16},{32,24},{40,32},{48,40},{56,48},{64,56},{72,6... | collective-permute-start | bytes 4616 | tf_op jit(solution)/shard_map/ppermute | solution.py:26
  552.2 8.8 %collective-permute-start.112 = (f32[2,1,2,96]{3,2,1,0:T(2,128)S(1)}, f32[2,1,2,96]{3,2,1,0:T(2,128)S(1)}, u32[]{:S(2)}, u32[]{:S(2)}) collective-permute-start(f32[2,1,2,96]{3,2,1,0:T(2,128)S(1)} %fusion.261), channel_id=1, source_target_pairs={{8,0},{16,8},{24,16},{32,24},{40,32},{48,40},{56,48},{64,56},{72,6... | collective-permute-start | bytes 4616 | tf_op jit(solution)/shard_map/ppermute | solution.py:26
  570.0 8.8 %collective-permute-start.116 = (f32[2,1,2,96]{3,2,1,0:T(2,128)S(1)}, f32[2,1,2,96]{3,2,1,0:T(2,128)S(1)}, u32[]{:S(2)}, u32[]{:S(2)}) collective-permute-start(f32[2,1,2,96]{3,2,1,0:T(2,128)S(1)} %fusion.262), channel_id=1, source_target_pairs={{8,0},{16,8},{24,16},{32,24},{40,32},{48,40},{56,48},{64,56},{72,6... | collective-permute-start | bytes 4616 | tf_op jit(solution)/shard_map/ppermute | solution.py:26
  588.2 8.9 %collective-permute-start.120 = (f32[2,1,4,192]{3,2,1,0:T(4,128)S(1)}, f32[2,1,4,192]{3,2,1,0:T(4,128)S(1)}, u32[]{:S(2)}, u32[]{:S(2)}) collective-permute-start(f32[2,1,4,192]{3,2,1,0:T(4,128)S(1)} %get-tuple-element.147), channel_id=1, source_target_pairs={{8,0},{16,8},{24,16},{32,24},{40,32},{48,40},{56,48},{64,56},{72,6... | collective-permute-start | bytes 18440 | tf_op jit(solution)/shard_map/ppermute | solution.py:26
  606.2 8.9 %collective-permute-start.124 = (f32[2,1,4,192]{3,2,1,0:T(4,128)S(1)}, f32[2,1,4,192]{3,2,1,0:T(4,128)S(1)}, u32[]{:S(2)}, u32[]{:S(2)}) collective-permute-start(f32[2,1,4,192]{3,2,1,0:T(4,128)S(1)} %get-tuple-element.145), channel_id=1, source_target_pairs={{8,0},{16,8},{24,16},{32,24},{40,32},{48,40},{56,48},{64,56},{72,6... | collective-permute-start | bytes 18440 | tf_op jit(solution)/shard_map/ppermute | solution.py:26
  625.6 9.0 %collective-permute-start.128 = (f32[2,1,8,384]{3,2,1,0:T(8,128)S(1)}, f32[2,1,8,384]{3,2,1,0:T(8,128)S(1)}, u32[]{:S(2)}, u32[]{:S(2)}) collective-permute-start(f32[2,1,8,384]{3,2,1,0:T(8,128)S(1)} %get-tuple-element.79), channel_id=1, source_target_pairs={{8,0},{16,8},{24,16},{32,24},{40,32},{48,40},{56,48},{64,56},{72,6... | collective-permute-start | bytes 73736 | tf_op jit(solution)/shard_map/ppermute | solution.py:26
  644.7 9.0 %collective-permute-start.132 = (f32[2,1,8,384]{3,2,1,0:T(8,128)S(1)}, f32[2,1,8,384]{3,2,1,0:T(8,128)S(1)}, u32[]{:S(2)}, u32[]{:S(2)}) collective-permute-start(f32[2,1,8,384]{3,2,1,0:T(8,128)S(1)} %get-tuple-element.77), channel_id=1, source_target_pairs={{8,0},{16,8},{24,16},{32,24},{40,32},{48,40},{56,48},{64,56},{72,6... | collective-permute-start | bytes 73736 | tf_op jit(solution)/shard_map/ppermute | solution.py:26
  (92 other events, 542.3 us)
where the time goes:
time: 666 us; the launch traced here: 662 us
  starting transfers between devices  390 us (59%)
  waiting for transfers between devices  204 us (31%)
  other arithmetic  33.7 us (5%)
  local copies, waits for them, and re-layouts  31.2 us (5%)
    ppermute x68, starting transfers between devices, extended_2(): lax.ppermute(lax.slice_in_dim(block, 0, width, axis=dim), axis, backward)  230 us
    ppermute x68, waiting for transfers between devices, extended_2(): lax.ppermute(lax.slice_in_dim(block, 0, width, axis=dim), axis, backward)  177 us
    ppermute x68, starting transfers between devices, extended_2(): lax.ppermute(lax.slice_in_dim(block, block.shape[dim] - width, None, axis...  160 us
    ppermute x68, waiting for transfers between devices, extended_2(): lax.ppermute(lax.slice_in_dim(block, block.shape[dim] - width, None, axis...  27.1 us
    reshape x2, local copies, waits for them, and re-layouts, restrict(): field.reshape(2, size_x // 2, 2, size_y // 2, 2, size_z // 2, 2)  16.1 us
  transfers between devices with their start and end apart: 136, of which 62 were waited for; matrix products, arithmetic and copies ran while one was open for 4% of the time, Pallas kernels for 0%

commit v1 on v0

v1 whole, which is shorter than its diff:
```python
import math

import jax
import jax.numpy as jnp
from jax import lax
from jax.experimental import pallas as pl
from jax.experimental.pallas import tpu as pltpu
from jax.sharding import PartitionSpec as P


NC = 8
OMEGA = 0.6
BETA = 0.5
ABSORB = 0.25
KH_FACTOR = 2.0 * math.pi * 6.0 * 20.0

F32 = jnp.float32
BF16 = jnp.bfloat16
VM = pl.BlockSpec(memory_space=pltpu.VMEM)
SM = pl.BlockSpec(memory_space=pltpu.SMEM)
PARAMS = pltpu.CompilerParams(vmem_limit_bytes=60 * 1024 * 1024)


def shape(*dims):
    return jax.ShapeDtypeStruct(dims, F32)


def scratch(*dims):
    return pltpu.VMEM(dims, F32)


def sort_matrix(rows, columns, flip):
    first = lax.broadcasted_iota(jnp.int32, (rows, columns), 0)
    second = lax.broadcasted_iota(jnp.int32, (rows, columns), 1)
    if flip:
        first, second = second, first
    lane = second % 128
    hit = (first == 4 * lane + second // 128) & (lane < 96)
    return jnp.where(hit, 1.0, 0.0).astype(BF16)


def exact_dot(values, matrix):
    high = values.astype(BF16)
    rest = values - high.astype(F32)
    middle = rest.astype(BF16)
    low = (rest - middle.astype(F32)).astype(BF16)
    dot = lambda part: jnp.dot(part, matrix, preferred_element_type=F32)
    return (dot(low) + dot(middle)) + dot(high)


def scaled_inverse(real, imag, scale):
    diag_real = 6.0 * scale - real
    diag_imag = -imag
    factor = OMEGA / (diag_real * diag_real + diag_imag * diag_imag)
    factor = jnp.where(real > 0.0, factor, 0.0)
    return diag_real * factor, -diag_imag * factor


def product(a, b):
    return a[0] * b[0] - a[1] * b[1], a[0] * b[1] + a[1] * b[0]


def pair_rows(value, temp):
    temp[8:32, :] = value
    row = lax.broadcasted_iota(jnp.int32, (24, 128), 0)
    return value + jnp.where(row % 2 == 0, temp[9:33, :], temp[7:31, :])


def neighbour(ref, x, c, r, count, step):
    center = lambda s: ref[x, c, s, 8:32, :]
    up = center(r + 1) if r < count - 1 else pltpu.roll(center(0), 127, 1)
    down = center(r - 1) if r > 0 else pltpu.roll(center(count - 1), 1, 1)
    total = ref[x - 1, c, r, 8:32, :] + ref[x + 1, c, r, 8:32, :]
    total = total + ref[x, c, r, 8 - step : 32 - step, :] + ref[x, c, r, 8 + step : 32 + step, :]
    return total + (up + down)


def sweep(old, new, weight, weight_at, source, source_at, low, high, count, step, scale):
    def body(x, _):
        for r in range(count):
            parts = []
            for c in range(2):
                total = neighbour(old, x, c, r, count, step)
                if scale != 1.0:
                    total = total * scale
                parts.append(source[x + source_at, c, r, 8:32, :] + total)
            w = [weight[x + weight_at, c, r, 8:32, :] for c in range(2)]
            moved = product(w, parts)
            for c in range(2):
                new[x, c, r, 8:32, :] = (1.0 - OMEGA) * old[x, c, r, 8:32, :] + moved[c]
        return 0

    lax.fori_loop(low, high, body, 0)


def clear(ref, count):
    def body(x, _):
        ref[x] = jnp.zeros(ref.shape[1:], F32)
        return 0

    lax.fori_loop(0, count, body, 0)


def pack_kernel(table, right_side, layer_index, absorb_level, packed, inverse_two, temp):
    matrix = sort_matrix(384, 512, False)
    field = exact_dot(right_side[...].reshape(64, 384), matrix)
    both = jnp.concatenate(
        [layer_index[...].reshape(32, 384), absorb_level[...].reshape(32, 384)], axis=0
    )
    codes = jnp.dot(both.astype(F32).astype(BF16), matrix, preferred_element_type=F32)
    inside = lax.broadcasted_iota(jnp.int32, (32, 128), 1) < 96
    total = [jnp.zeros((32, 128), F32), jnp.zeros((32, 128), F32)]
    for r in range(4):
        lanes = slice(r * 128, r * 128 + 128)
        layer = codes[0:32, lanes]
        velocity = jnp.full((32, 128), table[0], F32)
        for n in range(1, 16):
            velocity = jnp.where(layer == float(n), table[n], velocity)
        ratio = KH_FACTOR / velocity
        real = jnp.where(inside, ratio * ratio, 0.0)
        imag = -real * (BETA + ABSORB * codes[32:64, lanes])
        total = [total[0] + real, total[1] + imag]
        for x in range(4):
            rows = slice(x * 8, x * 8 + 8)
            packed[x, 0, r] = field[x * 8 : x * 8 + 8, lanes]
            packed[x, 1, r] = field[32 + x * 8 : 40 + x * 8, lanes]
            packed[x, 2, r] = real[rows]
            packed[x, 3, r] = imag[rows]
    means = []
    for c in range(2):
        t = total[c]
        t = (t[0:8] + t[8:16]) + (t[16:24] + t[24:32])
        temp[c] = t
        means.append(
            [
                ((temp[c, 4 * k : 4 * k + 1] + temp[c, 4 * k + 1 : 4 * k + 2])
                 + (temp[c, 4 * k + 2 : 4 * k + 3] + temp[c, 4 * k + 3 : 4 * k + 4])) * (1.0 / 64.0)
                for k in range(2)
            ]
        )
    for k in range(2):
        w = scaled_inverse(means[0][k], means[1][k], 0.0625)
        for c in range(2):
            inverse_two[0:1, (c * 2 + k) * 128 : (c * 2 + k) * 128 + 128] = w[c]


def pack(table, right_side, layer_index, absorb_level):
    return pl.pallas_call(
        pack_kernel,
        name="pack",
        out_shape=(shape(4, 4, 4, 8, 128), shape(1, 512)),
        in_specs=[SM, VM, VM, VM],
        out_specs=(VM, VM),
        scratch_shapes=[scratch(2, 8, 128)],
        compiler_params=PARAMS,
    )(table, right_side, layer_index, absorb_level)


def set_rows(target, x, c, r, low, mid, high):
    target[x, c, r, 8:16, :] = low
    target[x, c, r, 16:24, :] = mid
    target[x, c, r, 24:32, :] = high


def down_body(source, weight, diag, weight_one, diag_one, guess, out_guess, out_one, out_two, one, s1, t1, temp):
    def first(x, _):
        for r in range(4):
            f = [source[x, c, r, 8:32, :] for c in range(2)]
            w = [weight[x, c, r, 8:32, :] for c in range(2)]
            e = product(w, f)
            for c in range(2):
                guess[x, c, r, 8:32, :] = e[c]
        return 0

    lax.fori_loop(0, 16, first, 0)
    sweep(guess, out_guess, weight, 0, source, 0, 1, 15, 4, 1, 1.0)

    def residual(k, _):
        for s in range(2):
            sums = [None, None]
            for half in range(2):
                x = 2 + 2 * k + half
                for r in (2 * s, 2 * s + 1):
                    e = [out_guess[x, c, r, 8:32, :] for c in range(2)]
                    d = [diag[x, c, r, 8:32, :] for c in range(2)]
                    moved = product(d, e)
                    for c in range(2):
                        value = source[x, c, r, 8:32, :] + neighbour(out_guess, x, c, r, 4, 1) - moved[c]
                        sums[c] = value if sums[c] is None else sums[c] + value
            g = [pair_rows(sums[c], temp.at[c]) * 0.125 for c in range(2)]
            w = [weight_one[k, c, s, 8:32, :] for c in range(2)]
            e = product(w, g)
            for c in range(2):
                s1[k, c, s, 8:32, :] = g[c]
                one[k, c, s, 8:32, :] = e[c]
        return 0

    lax.fori_loop(0, 6, residual, 0)
    sweep(one, t1, weight_one, 0, s1, 0, 1, 5, 2, 2, 0.25)

    total = [None, None]
    for k in (2, 3):
        for s in range(2):
            e = [t1[k, c, s, 8:32, :] for c in range(2)]
            d = [diag_one[k, c, s, 8:32, :] for c in range(2)]
            moved = product(d, e)
            for c in range(2):
                value = s1[k, c, s, 8:32, :] + 0.25 * neighbour(t1, k, c, s, 2, 2) - moved[c]
                total[c] = value if total[c] is None else total[c] + value
    for c in range(2):
        temp[c, 8:32, :] = total[c]
        for k in range(2):
            row = 16 + 4 * k
            value = (temp[c, row : row + 1, :] + temp[c, row + 2 : row + 3, :]) * 0.125
            out_two[0:1, (c * 2 + k) * 128 : (c * 2 + k) * 128 + 128] = value

    def send(k, _):
        for s in range(2):
            for c in range(2):
                out_one[k, c, s * 4 : s * 4 + 4, :] = t1[k + 1, c, s, pl.ds(16, 4, 2), :]
                out_one[k, c + 2, s * 4 : s * 4 + 4, :] = s1[k + 1, c, s, pl.ds(16, 4, 2), :]
                if out_one.shape[1] > 4:
                    out_one[k, c + 4, s * 4 : s * 4 + 4, :] = weight_one[k + 1, c, s, pl.ds(16, 4, 2), :]
        return 0

    lax.fori_loop(0, 4, send, 0)


def down_first_kernel(mid, low, high, source, weight, diag, weight_one, diag_one, out_guess, out_one, out_two,
                      guess, one, s1, t1, temp):
    clear(guess, 16)
    clear(out_guess, 16)
    for ref in (one, s1, t1, weight_one, diag_one):
        clear(ref, 6)
    temp[...] = jnp.zeros(temp.shape, F32)
    zero = jnp.zeros((8, 128), F32)

    def fill(x, edge):
        for r in range(4):
            for c in range(4):
                parts = (zero, mid[x, c, r], zero) if edge else (low[x - 1, c, r], mid[x, c, r], high[x - 1, c, r])
                set_rows(source if c < 2 else diag, x, c % 2, r, *parts)
            real, imag = diag[x, 0, r, 8:32, :], diag[x, 1, r, 8:32, :]
            w = scaled_inverse(real, imag, 1.0)
            for c in range(2):
                weight[x, c, r, 8:32, :] = w[c]

    def filled(x, _):
        fill(x, False)
        return 0

    fill(0, True)
    lax.fori_loop(1, 15, filled, 0)
    fill(15, True)

    def coarse(k, _):
        for s in range(2):
            shift = []
            for c in range(2):
                total = None
                for half in range(2):
                    for r in (2 * s, 2 * s + 1):
                        value = diag[2 + 2 * k + half, c, r, 8:32, :]
                        total = value if total is None else total + value
                shift.append(pair_rows(total, temp.at[c]) * 0.125)
            w = scaled_inverse(shift[0], shift[1], 0.25)
            d = (1.5 - shift[0], -shift[1])
            for c in range(2):
                weight_one[k, c, s, 8:32, :] = w[c]
                diag_one[k, c, s, 8:32, :] = d[c]
        return 0

    lax.fori_loop(0, 6, coarse, 0)

    def turn(x, _):
        for r in range(4):
            diag[x, 0, r, 8:32, :] = 6.0 - diag[x, 0, r, 8:32, :]
            diag[x, 1, r, 8:32, :] = -diag[x, 1, r, 8:32, :]
        return 0

    lax.fori_loop(0, 16, turn, 0)
    down_body(source, weight, diag, weight_one, diag_one, guess, out_guess, out_one, out_two, one, s1, t1, temp)


FINE = (16, 2, 4, 40, 128)
COARSE = (6, 2, 2, 40, 128)
DOWN_SCRATCH = [scratch(*FINE), scratch(*COARSE), scratch(*COARSE), scratch(*COARSE), scratch(2, 40, 128)]


def down_first(mid, low, high):
    return pl.pallas_call(
        down_first_kernel,
        name="down_first",
        out_shape=(shape(*FINE), shape(*FINE), shape(*FINE), shape(*COARSE), shape(*COARSE), shape(*FINE),
                   shape(4, 6, 8, 128), shape(1, 512)),
        in_specs=[VM] * 3,
        out_specs=(VM,) * 8,
        scratch_shapes=DOWN_SCRATCH,
        compiler_params=PARAMS,
    )(mid, low, high)


def down_second_kernel(mid, low, high, weight, diag, weight_one, diag_one, out_source, out_guess, out_one, out_two,
                       guess, one, s1, t1, temp):
    clear(guess, 16)
    clear(out_guess, 16)
    for ref in (one, s1, t1):
        clear(ref, 6)
    temp[...] = jnp.zeros(temp.shape, F32)
    zero = jnp.zeros((8, 128), F32)

    def fill(x, edge):
        for r in range(4):
            for c in range(2):
                parts = (zero, mid[x, c, r], zero) if edge else (low[x - 1, c, r], mid[x, c, r], high[x - 1, c, r])
                set_rows(out_source, x, c, r, *parts)

    def filled(x, _):
        fill(x, False)
        return 0

    fill(0, True)
    lax.fori_loop(1, 15, filled, 0)
    fill(15, True)
    down_body(out_source, weight, diag, weight_one, diag_one, guess, out_guess, out_one, out_two, one, s1, t1, temp)


def down_second(mid, low, high, weight, diag, weight_one, diag_one):
    return pl.pallas_call(
        down_second_kernel,
        name="down_second",
        out_shape=(shape(*FINE), shape(*FINE), shape(4, 4, 8, 128), shape(1, 512)),
        in_specs=[VM] * 7,
        out_specs=(VM,) * 4,
        scratch_shapes=DOWN_SCRATCH,
        compiler_params=PARAMS,
    )(mid, low, high, weight, diag, weight_one, diag_one)


def solve_two(source, weight, ping, pong, planes, groups):
    clear(ping, planes + 8)
    clear(pong, planes + 8)
    rows = slice(8, 8 + groups)

    def start(x, _):
        for k in range(2):
            lanes = [slice((c * 2 + k) * 128, (c * 2 + k) * 128 + 128) for c in range(2)]
            e = product([weight[x, :, l] for l in lanes], [source[x, :, l] for l in lanes])
            for c in range(2):
                ping[x + 4, c * 2 + k, rows, :] = e[c]
        return 0

    lax.fori_loop(0, planes, start, 0)

    def step(old, new):
        def body(x, _):
            for k in range(2):
                parts, center = [], []
                for c in range(2):
                    here = old[x + 4, c * 2 + k, rows, :]
                    other = c * 2 + 1 - k
                    total = old[x + 3, c * 2 + k, rows, :] + old[x + 5, c * 2 + k, rows, :]
                    if k == 0:
                        total = total + old[x + 4, other, rows, :] + old[x + 4, other, 7 : 7 + groups, :]
                    else:
                        total = total + old[x + 4, other, rows, :] + old[x + 4, other, 9 : 9 + groups, :]
                    total = total + (pltpu.roll(here, 1, 1) + pltpu.roll(here, 127, 1))
                    lanes = slice((c * 2 + k) * 128, (c * 2 + k) * 128 + 128)
                    parts.append(source[x, :, lanes] + 0.0625 * total)
                    center.append(here)
                w = [weight[x, :, (c * 2 + k) * 128 : (c * 2 + k) * 128 + 128] for c in range(2)]
                moved = product(w, parts)
                for c in range(2):
                    new[x + 4, c * 2 + k, rows, :] = (1.0 - OMEGA) * center[c] + moved[c]
            return 0

        lax.fori_loop(0, planes, body, 0)

    pairs = (ping, pong)
    for number in range(NC - 1):
        step(pairs[number % 2], pairs[(number + 1) % 2])
    return pairs[(NC - 1) % 2]


def spread_rows(target, x, c, tile, block):
    for s in range(2):
        for twice in range(2):
            target[x, c, s, pl.ds(8 + 8 * tile + twice, 4, 2), :] = block[s * 4 : s * 4 + 4, :]


def add_two(answer, one, where, first, count):
    gx, gy = where[0], where[1]
    row = lax.broadcasted_iota(jnp.int32, (8, 128), 0)
    for j in range(count):
        x = gx + 4 + (first + j) // 2
        for c in range(2):
            for tile in range(3):
                spot = gy + 7 + tile
                low = jnp.broadcast_to(answer[x, c * 2, pl.ds(spot, 1), :], (8, 128))
                high = jnp.broadcast_to(answer[x, c * 2 + 1, pl.ds(spot, 1), :], (8, 128))
                value = jnp.where(row < 4, low, high)
                at = slice(8 + 8 * tile, 16 + 8 * tile)
                for s in range(2):
                    one[j, c, s, at, :] = one[j, c, s, at, :] + value


def up_first_kernel(planes, groups, where, source_two, weight_two, near_low, near_high, far_low, far_high, own,
                    source, weight, diag, guess, out_source, out_first, out_weight,
                    ping, pong, one, s1, t1, ea, eb):
    answer = solve_two(source_two, weight_two, ping, pong, planes, groups)
    for ref in (one, t1, s1):
        clear(ref, 12)
    clear(out_weight, 12)
    j = 0
    for ref, low, high in ((far_low, 0, 3), (near_low, 0, 2), (own, 0, 2), (near_high, 0, 2), (far_high, 0, 3)):
        for k in range(low, high):
            for c in range(2):
                for tile in range(3):
                    spread_rows(one, j, c, tile, ref[k, tile, c])
                    spread_rows(s1, j, c, tile, ref[k, tile, c + 2])
                    spread_rows(out_weight, j, c, tile, ref[k, tile, c + 4])
            j += 1
    add_two(answer, one, where, -5, 12)
    sweep(one, t1, out_weight, 0, s1, 0, 1, 11, 2, 2, 0.25)
    sweep(t1, one, out_weight, 0, s1, 0, 2, 10, 2, 2, 0.25)
    clear(ea, 16)
    clear(eb, 16)

    def correct(x1, _):
        for half in range(2):
            x = 2 * x1 - 4 + half
            for r in range(4):
                for c in range(2):
                    ea[x, c, r, 8:32, :] = guess[x, c, r, 8:32, :] + one[x1, c, r // 2, 8:32, :]
        return 0

    lax.fori_loop(2, 10, correct, 0)
    sweep(ea, eb, weight, 0, source, 0, 2, 14, 4, 1, 1.0)
    sweep(eb, ea, weight, 0, source, 0, 3, 13, 4, 1, 1.0)

    def rest(x, _):
        for r in range(4):
            e = [ea[x, c, r, 8:32, :] for c in range(2)]
            moved = product([diag[x, c, r, 8:32, :] for c in range(2)], e)
            for c in range(2):
                value = source[x, c, r, 8:32, :] + neighbour(ea, x, c, r, 4, 1) - moved[c]
                out_source[x - 4, c, r] = value[8:16]
        return 0

    lax.fori_loop(4, 12, rest, 0)
    for x in range(4):
        for c in range(2):
            for r in range(4):
                out_first[x, c, r] = ea[x + 6, c, r, 16:24, :]


def up_first(where, source_two, weight_two, near_low, near_high, far_low, far_high, own, source, weight, diag, guess):
    planes, groups = source_two.shape[0], source_two.shape[1]
    two = scratch(planes + 8, 4, 16 + groups, 128)
    level = scratch(12, 2, 2, 40, 128)
    return pl.pallas_call(
        lambda *refs: up_first_kernel(planes, groups, *refs),
        name="up_first",
        out_shape=(shape(8, 2, 4, 8, 128), shape(4, 2, 4, 8, 128), shape(12, 2, 2, 40, 128)),
        in_specs=[SM] + [VM] * 11,
        out_specs=(VM,) * 3,
        scratch_shapes=[two, two, level, level, level, scratch(*FINE), scratch(*FINE)],
        compiler_params=PARAMS,
    )(where, source_two, weight_two, near_low, near_high, far_low, far_high, own, source, weight, diag, guess)


def up_second_kernel(planes, groups, where, source_two, weight_two, near_low, near_high, own,
                     source, weight, guess, weight_one, first, result,
                     ping, pong, one, s1, t1, ea, eb):
    answer = solve_two(source_two, weight_two, ping, pong, planes, groups)
    for ref in (one, t1, s1):
        clear(ref, 8)
    j = 0
    for ref, low, high in ((near_low, 0, 3), (own, 0, 2), (near_high, 0, 3)):
        for k in range(low, high):
            for c in range(2):
                for tile in range(3):
                    spread_rows(one, j, c, tile, ref[k, tile, c])
                    spread_rows(s1, j, c, tile, ref[k, tile, c + 2])
            j += 1
    add_two(answer, one, where, -3, 8)
    sweep(one, t1, weight_one, 2, s1, 0, 1, 7, 2, 2, 0.25)
    sweep(t1, one, weight_one, 2, s1, 0, 2, 6, 2, 2, 0.25)
    clear(ea, 16)
    clear(eb, 16)

    def correct(x1, _):
        for half in range(2):
            x = 2 * x1 + half
            for r in range(4):
                for c in range(2):
                    ea[x, c, r, 8:32, :] = guess[x, c, r, 8:32, :] + one[x1, c, r // 2, 8:32, :]
        return 0

    lax.fori_loop(2, 6, correct, 0)
    sweep(ea, eb, weight, 0, source, 0, 5, 11, 4, 1, 1.0)
    sweep(eb, ea, weight, 0, source, 0, 6, 10, 4, 1, 1.0)
    blocks = []
    for c in range(2):
        for x in range(4):
            blocks.append(
                jnp.concatenate([first[x, c, r] + ea[x + 6, c, r, 16:24, :] for r in range(4)], axis=1)
            )
    values = jnp.concatenate(blocks, axis=0)
    result[...] = exact_dot(values, sort_matrix(512, 384, True)).reshape(2, 4, 8, 384)


def up_second(where, source_two, weight_two, near_low, near_high, own, source, weight, guess, weight_one, first):
    planes, groups = source_two.shape[0], source_two.shape[1]
    two = scratch(planes + 8, 4, 16 + groups, 128)
    level = scratch(8, 2, 2, 40, 128)
    return pl.pallas_call(
        lambda *refs: up_second_kernel(planes, groups, *refs),
        name="up_second",
        out_shape=shape(2, 4, 8, 384),
        in_specs=[SM] + [VM] * 10,
        out_specs=VM,
        scratch_shapes=[two, two, level, level, level, scratch(*FINE), scratch(*FINE)],
        compiler_params=PARAMS,
    )(where, source_two, weight_two, near_low, near_high, own, source, weight, guess, weight_one, first)


def shifted(block, axis, by):
    count = lax.axis_size(axis)
    pairs = [(i, i + by) for i in range(count) if 0 <= i + by < count]
    return lax.ppermute(block, axis, pairs)


def gather_two(row):
    count_y, count_x = lax.axis_size("gy"), lax.axis_size("gx")
    column = lax.all_to_all(jnp.broadcast_to(row[None], (count_y, 1, 512)), "gy", 0, 0)
    column = column.reshape(1, count_y, 512)
    return lax.all_to_all(jnp.broadcast_to(column, (count_x, count_y, 512)), "gx", 0, 0)


def y_sides(block):
    return shifted(block, "gy", 1), shifted(block, "gy", -1)


def y_tiles(block):
    low, high = y_sides(block)
    return jnp.stack([low, block, high], axis=1)


def local(right_side, velocity_table, layer_index, absorb_level):
    where = jnp.stack([lax.axis_index("gx"), lax.axis_index("gy")]).astype(jnp.int32)
    packed, inverse_two = pack(velocity_table, right_side, layer_index, absorb_level)
    weight_two = gather_two(inverse_two)
    mid = jnp.concatenate(
        [
            shifted(packed[2:], "gx", 2),
            shifted(packed, "gx", 1),
            packed,
            shifted(packed, "gx", -1),
            shifted(packed[:2], "gx", -2),
        ]
    )
    low, high = y_sides(mid[1:15])
    source, weight, diag, weight_one, diag_one, guess, one, two = down_first(mid, low, high)
    source_two = gather_two(two)
    tiles = y_tiles(one)
    near_low, near_high = shifted(tiles[1:3], "gx", 1), shifted(tiles[1:3], "gx", -1)
    far_low, far_high = shifted(tiles[0:3], "gx", 2), shifted(tiles[1:4], "gx", -2)
    rest, first, weight_one_wide = up_first(
        where, source_two, weight_two, near_low, near_high, far_low, far_high, tiles[1:3], source, weight, diag, guess
    )
    mid = jnp.concatenate([shifted(rest[0:6], "gx", 1), rest[2:6], shifted(rest[2:8], "gx", -1)])
    low, high = y_sides(mid[1:15])
    source, guess, one, two = down_second(mid, low, high, weight, diag, weight_one, diag_one)
    source_two = gather_two(two)
    tiles = y_tiles(one)
    near_low, near_high = shifted(tiles[0:3], "gx", 1), shifted(tiles[1:4], "gx", -1)
    return up_second(
        where, source_two, weight_two, near_low, near_high, tiles[1:3], source, weight, guess, weight_one_wide, first
    )


def solution(mesh):
    placed = (P(None, "gx", "gy", None), P(), P("gx", "gy", None), P("gx", "gy", None))
    return jax.shard_map(
        local, mesh=mesh, in_specs=placed, out_specs=P(None, "gx", "gy", None), check_vma=False
    )
```

time: 666 us -> 270 us (0.41)
  the two profiles are of different devices: /device:TPU:126 before, /device:TPU:1 now
where the time goes in v1:
time: 270 us; the launch traced here: 266 us
  starting transfers between devices  101 us (37%)
  Pallas kernels  79 us (29%)
  waiting for transfers between devices  65.2 us (24%)
  local copies, waits for them, and re-layouts  12.7 us (5%)
  blocking collectives  6.47 us (2%)
    ppermute x20, starting transfers between devices, shifted(): return lax.ppermute(block, axis, pairs)  57.9 us
    ppermute x20, waiting for transfers between devices, shifted(): return lax.ppermute(block, axis, pairs)  44.3 us
    all_to_all x3, starting transfers between devices, gather_two(): lax.all_to_all(jnp.broadcast_to(column, (count_x, count_y, 512)), 'gx', 0...  34.1 us
    pallas_call x1, Pallas kernels, up_first(): pl.pallas_call(lambda *refs: up_first_kernel(planes, groups, *refs), name...  30.6 us
    pallas_call x1, Pallas kernels, up_second(): pl.pallas_call(lambda *refs: up_second_kernel(planes, groups, *refs), nam...  27 us
    all_to_all x3, waiting for transfers between devices, gather_two(): lax.all_to_all(jnp.broadcast_to(column, (count_x, count_y, 512)), 'gx', 0...  16.3 us
    pallas_call x1, Pallas kernels, down_first(): pl.pallas_call(down_first_kernel, name='down_first', out_shape=(shape(*FI...  10.3 us
    all_to_all x2, starting transfers between devices, gather_two(): lax.all_to_all(jnp.broadcast_to(row[None], (count_y, 1, 512)), 'gy', 0, 0)  9.06 us
  transfers between devices with their start and end apart: 25, of which 16 were waited for; matrix products, arithmetic and copies ran while one was open for 2% of the time, Pallas kernels for 4%

profile of v1, /device:TPU:1, one launch (start us, length us, event | category | flops | bytes accessed | tf_op | source)
XLA Modules:
  0.0 266.5 jit_solution(6821427121177058904)
XLA Ops:
  0.0 2.1 pack.1
  2.2 4.2 %collective-permute-start.1 = (f32[4,4,4,8,128]{4,3,2,1,0:T(8,128)}, f32[4,4,4,8,128]{4,3,2,1,0:T(8,128)S(1)}, u32[]{:S(2)}, u32[]{:S(2)}) collective-permute-start(f32[4,4,4,8,128]{4,3,2,1,0:T(8,128)} %get-tuple-element.22), channel_id=1, source_target_pairs={{0,8},{8,16},{16,24},{24,32},{32,40},{40,48},{48,56},{56,64},{64,7... | collective-permute-start | bytes 786440 | tf_op jit(solution)/shard_map/ppermute | solution.py:531
  6.3 1.0 fusion.2
  7.3 4.5 %collective-permute-start = (f32[2,4,4,8,128]{4,3,2,1,0:T(8,128)S(1)}, f32[2,4,4,8,128]{4,3,2,1,0:T(8,128)S(1)}, u32[]{:S(2)}, u32[]{:S(2)}) collective-permute-start(f32[2,4,4,8,128]{4,3,2,1,0:T(8,128)S(1)} %get-tuple-element.44), channel_id=1, source_target_pairs={{0,16},{8,24},{16,32},{24,40},{32,48},{40,56},{48,64},{56,72},{64,... | collective-permute-start | bytes 393224 | tf_op jit(solution)/shard_map/ppermute | solution.py:531
  11.8 1.3 collective-permute-start.2
  13.1 1.3 collective-permute-start.3
  15.5 5.1 %collective-permute-done.2 = f32[4,4,4,8,128]{4,3,2,1,0:T(8,128)S(1)} collective-permute-done((f32[4,4,4,8,128]{4,3,2,1,0:T(8,128)}, f32[4,4,4,8,128]{4,3,2,1,0:T(8,128)S(1)}, u32[]{:S(2)}, u32[]{:S(2)}) %collective-permute-start.2) | collective-permute-done | bytes 262176 | tf_op jit(solution)/shard_map/ppermute | solution.py:531
  20.7 7.6 %collective-permute-start.4 = (f32[14,4,4,8,128]{4,3,2,1,0:T(8,128)S(1)}, f32[14,4,4,8,128]{4,3,2,1,0:T(8,128)S(1)}, u32[]{:S(2)}, u32[]{:S(2)}) collective-permute-start(f32[14,4,4,8,128]{4,3,2,1,0:T(8,128)S(1)} %slice.54), channel_id=1, source_target_pairs={{0,1},{1,2},{2,3},{3,4},{4,5},{5,6},{6,7},{8,9},{9,10},{10,11},{11... | collective-permute-start | bytes 2752520 | tf_op jit(solution)/shard_map/ppermute | solution.py:531
  28.3 1.9 collective-permute-start.5
  30.8 5.0 %all-to-all-start.2 = ((f32[8,1,512]{2,1,0:T(1,128)}), f32[8,1,512]{2,1,0:T(1,128)S(1)}, u32[]{:S(2)}, u32[]{:S(2)}) async-start(f32[8,1,512]{2,1,0:T(1,128)} %broadcast_in_dim.50), calls=%async_computation.2 | async-start | bytes 32768 | tf_op jit(solution)/shard_map/all_to_all | solution.py:536
  35.8 2.9 %collective-permute-done.4.low = f32[14,4,4,8,128]{4,3,2,1,0:T(8,128)S(1)} collective-permute-done((f32[14,4,4,8,128]{4,3,2,1,0:T(8,128)S(1)}, f32[14,4,4,8,128]{4,3,2,1,0:T(8,128)S(1)}, u32[]{:S(2)}, u32[]{:S(2)}) %collective-permute-start.4) | collective-permute-done | bytes 917536 | tf_op jit(solution)/shard_map/ppermute | solution.py:531
  38.7 4.5 %collective-permute-done.5.high = f32[14,4,4,8,128]{4,3,2,1,0:T(8,128)} collective-permute-done((f32[14,4,4,8,128]{4,3,2,1,0:T(8,128)S(1)}, f32[14,4,4,8,128]{4,3,2,1,0:T(8,128)}, u32[]{:S(2)}, u32[]{:S(2)}) %collective-permute-start.5) | collective-permute-done | bytes 917536 | tf_op jit(solution)/shard_map/ppermute | solution.py:531
  43.2 10.3 %down_first.1 = (f32[16,2,4,40,128]{4,3,2,1,0:T(8,128)}, f32[16,2,4,40,128]{4,3,2,1,0:T(8,128)}, f32[16,2,4,40,128]{4,3,2,1,0:T(8,128)}, f32[6,2,2,40,128]{4,3,2...) custom-call(f32[16,4,4,8,128]{4,3,2,1,0:T(8,128)} %copy-done.2, ...), custom_call_target="tpu_custom_call" | custom-call | tf_op jit(solution)/shard_map/down_first/pallas_call | solution.py:291
  53.5 1.3 broadcast_in_dim.46
  54.8 4.1 %all-to-all-start = ((f32[8,1,512]{2,1,0:T(1,128)}), f32[8,1,512]{2,1,0:T(1,128)S(1)}, u32[]{:S(2)}, u32[]{:S(2)}) async-start(f32[8,1,512]{2,1,0:T(1,128)} %broadcast_in_dim.46), calls=%async_computation | async-start | bytes 32768 | tf_op jit(solution)/shard_map/all_to_all | solution.py:536
  58.9 4.6 %all-to-all-done = f32[8,1,512]{2,1,0:T(1,128)S(1)} async-done(((f32[8,1,512]{2,1,0:T(1,128)}), f32[8,1,512]{2,1,0:T(1,128)S(1)}, u32[]{:S(2)}, u32[]{:S(2)}) %all-to-all-start) | async-done | bytes 16416 | tf_op jit(solution)/shard_map/all_to_all | solution.py:536
  64.4 13.8 %all-to-all-start.3 = ((f32[32,8,512]{2,1,0:T(8,128)}), f32[32,8,512]{2,1,0:T(8,128)S(1)}, u32[]{:S(2)}, u32[]{:S(2)}) async-start(f32[32,8,512]{2,1,0:T(8,128)} %broadcast_in_dim.52), calls=%async_computation.3 | async-start | bytes 1048576 | tf_op jit(solution)/shard_map/all_to_all | solution.py:538
  78.3 16.3 %all-to-all-done.3.refs_2_ = f32[32,8,512]{2,1,0:T(8,128)S(1)} async-done(((f32[32,8,512]{2,1,0:T(8,128)}), f32[32,8,512]{2,1,0:T(8,128)S(1)}, u32[]{:S(2)}, u32[]{:S(2)}) %all-to-all-start.3) | async-done | bytes 524320 | tf_op jit(solution)/shard_map/all_to_all | solution.py:538
  95.5 5.2 %all-to-all-start.1 = ((f32[32,8,512]{2,1,0:T(8,128)}), f32[32,8,512]{2,1,0:T(8,128)S(1)}, u32[]{:S(2)}, u32[]{:S(2)}) async-start(f32[32,8,512]{2,1,0:T(8,128)} %broadcast_in_dim.48), calls=%async_computation.1 | async-start | bytes 1048576 | tf_op jit(solution)/shard_map/all_to_all | solution.py:538
  100.8 3.9 %collective-permute-start.6 = (f32[4,6,8,128]{3,2,1,0:T(8,128)S(1)}, f32[4,6,8,128]{3,2,1,0:T(8,128)S(1)}, u32[]{:S(2)}, u32[]{:S(2)}) collective-permute-start(f32[4,6,8,128]{3,2,1,0:T(8,128)S(1)} %copy-done.15), channel_id=1, source_target_pairs={{0,1},{1,2},{2,3},{3,4},{4,5},{5,6},{6,7},{8,9},{9,10},{10,11},{11... | collective-permute-start | bytes 294920 | tf_op jit(solution)/shard_map/ppermute | solution.py:531
  104.7 1.9 collective-permute-start.7
  106.6 4.3 %collective-permute-done.7 = f32[4,6,8,128]{3,2,1,0:T(8,128)S(1)} collective-permute-done((f32[4,6,8,128]{3,2,1,0:T(8,128)S(1)}, f32[4,6,8,128]{3,2,1,0:T(8,128)S(1)}, u32[]{:S(2)}, u32[]{:S(2)}) %collective-permute-start.7) | collective-permute-done | bytes 98336 | tf_op jit(solution)/shard_map/ppermute | solution.py:531
  111.0 4.9 %collective-permute-start.10 = (f32[3,3,6,8,128]{4,3,2,1,0:T(8,128)S(1)}, f32[3,3,6,8,128]{4,3,2,1,0:T(8,128)S(1)}, u32[]{:S(2)}, u32[]{:S(2)}) collective-permute-start(f32[3,3,6,8,128]{4,3,2,1,0:T(8,128)S(1)} %get-tuple-element.40), channel_id=1, source_target_pairs={{0,16},{8,24},{16,32},{24,40},{32,48},{40,56},{48,64},{56,72},{64,... | collective-permute-start | bytes 663560 | tf_op jit(solution)/shard_map/ppermute | solution.py:531
  115.9 1.3 collective-permute-start.11
  117.2 2.2 collective-permute-start.8
  119.4 1.3 collective-permute-start.9
  121.4 5.5 %collective-permute-done.8.refs_3_ = f32[2,3,6,8,128]{4,3,2,1,0:T(8,128)S(1)} collective-permute-done((f32[2,3,6,8,128]{4,3,2,1,0:T(8,128)S(1)}, f32[2,3,6,8,128]{4,3,2,1,0:T(8,128)S(1)}, u32[]{:S(2)}, u32[]{:S(2)}) %collective-permute-start.8) | collective-permute-done | bytes 147488 | tf_op jit(solution)/shard_map/ppermute | solution.py:531
  128.8 30.6 %up_first.1 = (f32[8,2,4,8,128]{4,3,2,1,0:T(8,128)}, f32[4,2,4,8,128]{4,3,2,1,0:T(8,128)}, f32[12,2,2,40,128]{4,3,2,1,0:T(8,128)}) custom-call(s32[2]{0:T(128)} %pad_add_fusion.refs_0_, f32[32,8,512]{2,1,0:T(8,128)} %copy-done.3, f32[32,8,512]{2,1,0:T(8,128)} %copy-done, f32[2,3,6,8,128]{4,3,2,1,0:T(8,128)} %copy-done.11, f32[2,3,6,8,128]{4,3,2,1,0:T(8,128)} %copy-done.12, ...), custom_call_target="tpu_custom_call" | custom-call | tf_op jit(solution)/shard_map/up_first/pallas_call | solution.py:461
  159.4 1.0 fusion.1
  160.4 3.0 %collective-permute-start.12 = (f32[6,2,4,8,128]{4,3,2,1,0:T(8,128)S(1)}, f32[6,2,4,8,128]{4,3,2,1,0:T(8,128)S(1)}, u32[]{:S(2)}, u32[]{:S(2)}) collective-permute-start(f32[6,2,4,8,128]{4,3,2,1,0:T(8,128)S(1)} %get-tuple-element.41), channel_id=1, source_target_pairs={{0,8},{8,16},{16,24},{24,32},{32,40},{40,48},{48,56},{56,64},{64,7... | collective-permute-start | bytes 589832 | tf_op jit(solution)/shard_map/ppermute | solution.py:531
  163.4 1.3 collective-permute-start.13
  165.6 2.2 collective-permute-done.12
  167.8 3.7 %collective-permute-done.13 = f32[6,2,4,8,128]{4,3,2,1,0:T(8,128)S(1)} collective-permute-done((f32[6,2,4,8,128]{4,3,2,1,0:T(8,128)S(1)}, f32[6,2,4,8,128]{4,3,2,1,0:T(8,128)S(1)}, u32[]{:S(2)}, u32[]{:S(2)}) %collective-permute-start.13) | collective-permute-done | bytes 196640 | tf_op jit(solution)/shard_map/ppermute | solution.py:531
  171.6 5.4 %collective-permute-start.14 = (f32[14,2,4,8,128]{4,3,2,1,0:T(8,128)S(1)}, f32[14,2,4,8,128]{4,3,2,1,0:T(8,128)S(1)}, u32[]{:S(2)}, u32[]{:S(2)}) collective-permute-start(f32[14,2,4,8,128]{4,3,2,1,0:T(8,128)S(1)} %slice.58), channel_id=1, source_target_pairs={{0,1},{1,2},{2,3},{3,4},{4,5},{5,6},{6,7},{8,9},{9,10},{10,11},{11... | collective-permute-start | bytes 1376264 | tf_op jit(solution)/shard_map/ppermute | solution.py:531
  177.0 1.9 collective-permute-start.15
  178.9 3.5 %collective-permute-done.14.low = f32[14,2,4,8,128]{4,3,2,1,0:T(8,128)S(1)} collective-permute-done((f32[14,2,4,8,128]{4,3,2,1,0:T(8,128)S(1)}, f32[14,2,4,8,128]{4,3,2,1,0:T(8,128)S(1)}, u32[]{:S(2)}, u32[]{:S(2)}) %collective-permute-start.14) | collective-permute-done | bytes 458784 | tf_op jit(solution)/shard_map/ppermute | solution.py:531
  182.4 4.4 %collective-permute-done.15.high = f32[14,2,4,8,128]{4,3,2,1,0:T(8,128)S(1)} collective-permute-done((f32[14,2,4,8,128]{4,3,2,1,0:T(8,128)S(1)}, f32[14,2,4,8,128]{4,3,2,1,0:T(8,128)S(1)}, u32[]{:S(2)}, u32[]{:S(2)}) %collective-permute-start.15) | collective-permute-done | bytes 458784 | tf_op jit(solution)/shard_map/ppermute | solution.py:531
  187.6 9.0 %down_second.1 = (f32[16,2,4,40,128]{4,3,2,1,0:T(8,128)}, f32[16,2,4,40,128]{4,3,2,1,0:T(8,128)}, f32[4,4,8,128]{3,2,1,0:T(8,128)}, f32[1,512]{1,0:T(1,128)}) custom-call(f32[16,2,4,8,128]{4,3,2,1,0:T(8,128)} %copy-done.1, f32[14,2,4,8,128]{4,3,2,1,0:T(8,128)} %copy-done.7, f32[14,2,4,8,128]{4,3,2,1,0:T(8,128)} %copy-done.8, ...), custom_call_target="tpu_custom_call" | custom-call | tf_op jit(solution)/shard_map/down_second/pallas_call | solution.py:329
  197.3 6.5 %all_to_all.30 = f32[8,1,512]{2,1,0:T(1,128)S(1)} all-to-all(f32[8,1,512]{2,1,0:T(1,128)S(1)} %broadcast_in_dim.54), channel_id=1, replica_groups=mesh['gx'=32,'gy'=8] {'gy'}, dimensions={0} | all-to-all | bytes 32768 | tf_op jit(solution)/shard_map/all_to_all | solution.py:536
  204.6 15.1 %all-to-all-start.5 = ((f32[32,8,512]{2,1,0:T(8,128)}), f32[32,8,512]{2,1,0:T(8,128)S(1)}, u32[]{:S(2)}, u32[]{:S(2)}) async-start(f32[32,8,512]{2,1,0:T(8,128)} %broadcast_in_dim.56), calls=%async_computation.5 | async-start | bytes 1048576 | tf_op jit(solution)/shard_map/all_to_all | solution.py:538
  219.6 2.9 %collective-permute-start.17 = (f32[4,4,8,128]{3,2,1,0:T(8,128)}, f32[4,4,8,128]{3,2,1,0:T(8,128)S(1)}, u32[]{:S(2)}, u32[]{:S(2)}) collective-permute-start(f32[4,4,8,128]{3,2,1,0:T(8,128)} %get-tuple-element.34), channel_id=1, source_target_pairs={{1,0},{2,1},{3,2},{4,3},{5,4},{6,5},{7,6},{9,8},{10,9},{11,10},{12... | collective-permute-start | bytes 196616 | tf_op jit(solution)/shard_map/ppermute | solution.py:531
  222.5 2.7 collective-permute-start.16
  225.5 1.3 collective-permute-done.16
  227.7 3.1 %collective-permute-start.18 = (f32[3,3,4,8,128]{4,3,2,1,0:T(8,128)S(1)}, f32[3,3,4,8,128]{4,3,2,1,0:T(8,128)S(1)}, u32[]{:S(2)}, u32[]{:S(2)}) collective-permute-start(f32[3,3,4,8,128]{4,3,2,1,0:T(8,128)S(1)} %get-tuple-element.46), channel_id=1, source_target_pairs={{0,8},{8,16},{16,24},{24,32},{32,40},{40,48},{48,56},{56,64},{64,7... | collective-permute-start | bytes 442376 | tf_op jit(solution)/shard_map/ppermute | solution.py:531
  230.9 1.3 collective-permute-start.19
  232.8 2.6 collective-permute-done.18.refs_3_
  235.5 3.1 %collective-permute-done.19.refs_4_ = f32[3,3,4,8,128]{4,3,2,1,0:T(8,128)S(1)} collective-permute-done((f32[3,3,4,8,128]{4,3,2,1,0:T(8,128)S(1)}, f32[3,3,4,8,128]{4,3,2,1,0:T(8,128)S(1)}, u32[]{:S(2)}, u32[]{:S(2)}) %collective-permute-start.19) | collective-permute-done | bytes 147488 | tf_op jit(solution)/shard_map/ppermute | solution.py:531
  239.4 27.0 %up_second.1 = f32[2,4,8,384]{3,2,1,0:T(8,128)} custom-call(s32[2]{0:T(128)} %pad_add_fusion.refs_0_, f32[32,8,512]{2,1,0:T(8,128)} %copy-done.4, f32[32,8,512]{2,1,0:T(8,128)} %copy-done, f32[3,3,4,8,128]{4,3,2,1,0:T(8,128)} %copy-done.13, f32[3,3,4,8,128]{4,3,2,1,0:T(8,128)} %copy-done.14, f32[2,3,4,8,128]{4,3,2,1,0:T(8,128)} %slice.61.refs_5_, ...), custom_call_target="tpu_custom_call" | custom-call | tf_op jit(solution)/shard_map/up_second/pallas_call | solution.py:517
  (69 shorter events, 12.1 us)
Async XLA Ops:
  2.1 28.1 %copy-start.16 = (f32[1,512]{1,0:T(1,128)S(1)}, f32[1,512]{1,0:T(1,128)}, u32[]{:S(2)}) copy-start(f32[1,512]{1,0:T(1,128)} %get-tuple-element.24) | copy-start | bytes 6148
  2.2 12.3 %collective-permute-start.1 = (f32[4,4,4,8,128]{4,3,2,1,0:T(8,128)}, f32[4,4,4,8,128]{4,3,2,1,0:T(8,128)S(1)}, u32[]{:S(2)}, u32[]{:S(2)}) collective-permute-start(f32[4,4,4,8,128]{4,3,2,1,0:T(8,128)} %get-tuple-element.22), channel_id=1, source_target_pairs={{0,8},{8,16},{16,24},{24,32},{32,40},{40,48},{48,56},{56,64},{64,7... | collective-permute-start | bytes 786440 | tf_op jit(solution)/shard_map/ppermute | solution.py:531
  7.3 7.1 %collective-permute-start = (f32[2,4,4,8,128]{4,3,2,1,0:T(8,128)S(1)}, f32[2,4,4,8,128]{4,3,2,1,0:T(8,128)S(1)}, u32[]{:S(2)}, u32[]{:S(2)}) collective-permute-start(f32[2,4,4,8,128]{4,3,2,1,0:T(8,128)S(1)} %get-tuple-element.44), channel_id=1, source_target_pairs={{0,16},{8,24},{16,32},{24,40},{32,48},{40,56},{48,64},{56,72},{64,... | collective-permute-start | bytes 393224 | tf_op jit(solution)/shard_map/ppermute | solution.py:531
  11.8 8.7 %collective-permute-start.2 = (f32[4,4,4,8,128]{4,3,2,1,0:T(8,128)}, f32[4,4,4,8,128]{4,3,2,1,0:T(8,128)S(1)}, u32[]{:S(2)}, u32[]{:S(2)}) collective-permute-start(f32[4,4,4,8,128]{4,3,2,1,0:T(8,128)} %get-tuple-element.22), channel_id=1, source_target_pairs={{8,0},{16,8},{24,16},{32,24},{40,32},{48,40},{56,48},{64,56},{72,6... | collective-permute-start | bytes 786440 | tf_op jit(solution)/shard_map/ppermute | solution.py:531
  13.1 7.5 %collective-permute-start.3 = (f32[2,4,4,8,128]{4,3,2,1,0:T(8,128)S(1)}, f32[2,4,4,8,128]{4,3,2,1,0:T(8,128)S(1)}, u32[]{:S(2)}, u32[]{:S(2)}) collective-permute-start(f32[2,4,4,8,128]{4,3,2,1,0:T(8,128)S(1)} %get-tuple-element.43), channel_id=1, source_target_pairs={{16,0},{24,8},{32,16},{40,24},{48,32},{56,40},{64,48},{72,56},{80,... | collective-permute-start | bytes 393224 | tf_op jit(solution)/shard_map/ppermute | solution.py:531
  20.6 22.6 %copy-start.2 = (f32[16,4,4,8,128]{4,3,2,1,0:T(8,128)}, f32[16,4,4,8,128]{4,3,2,1,0:T(8,128)S(1)}, u32[]{:S(2)}) copy-start(f32[16,4,4,8,128]{4,3,2,1,0:T(8,128)S(1)} %constant_dynamic-update-slice_fusion.mid) | copy-start | bytes 3145732
  20.7 18.0 %collective-permute-start.4 = (f32[14,4,4,8,128]{4,3,2,1,0:T(8,128)S(1)}, f32[14,4,4,8,128]{4,3,2,1,0:T(8,128)S(1)}, u32[]{:S(2)}, u32[]{:S(2)}) collective-permute-start(f32[14,4,4,8,128]{4,3,2,1,0:T(8,128)S(1)} %slice.54), channel_id=1, source_target_pairs={{0,1},{1,2},{2,3},{3,4},{4,5},{5,6},{6,7},{8,9},{9,10},{10,11},{11... | collective-permute-start | bytes 2752520 | tf_op jit(solution)/shard_map/ppermute | solution.py:531
  28.3 14.9 %collective-permute-start.5 = (f32[14,4,4,8,128]{4,3,2,1,0:T(8,128)S(1)}, f32[14,4,4,8,128]{4,3,2,1,0:T(8,128)}, u32[]{:S(2)}, u32[]{:S(2)}) collective-permute-start(f32[14,4,4,8,128]{4,3,2,1,0:T(8,128)S(1)} %slice.54), channel_id=1, source_target_pairs={{1,0},{2,1},{3,2},{4,3},{5,4},{6,5},{7,6},{9,8},{10,9},{11,10},{12... | collective-permute-start | bytes 2752520 | tf_op jit(solution)/shard_map/ppermute | solution.py:531
  30.8 22.7 %all-to-all-start.2 = ((f32[8,1,512]{2,1,0:T(1,128)}), f32[8,1,512]{2,1,0:T(1,128)S(1)}, u32[]{:S(2)}, u32[]{:S(2)}) async-start(f32[8,1,512]{2,1,0:T(1,128)} %broadcast_in_dim.50), calls=%async_computation.2 | async-start | bytes 32768 | tf_op jit(solution)/shard_map/all_to_all | solution.py:536
  38.7 4.5 %copy-start.5 = (f32[14,4,4,8,128]{4,3,2,1,0:T(8,128)}, f32[14,4,4,8,128]{4,3,2,1,0:T(8,128)S(1)}, u32[]{:S(2)}) copy-start(f32[14,4,4,8,128]{4,3,2,1,0:T(8,128)S(1)} %collective-permute-done.4.low) | copy-start | bytes 2752516
  53.5 47.3 %copy-start.15 = (f32[4,6,8,128]{3,2,1,0:T(8,128)S(1)}, f32[4,6,8,128]{3,2,1,0:T(8,128)}, u32[]{:S(2)}) copy-start(f32[4,6,8,128]{3,2,1,0:T(8,128)} %get-tuple-element.25) | copy-start | bytes 294916
  54.8 8.7 %all-to-all-start = ((f32[8,1,512]{2,1,0:T(1,128)}), f32[8,1,512]{2,1,0:T(1,128)S(1)}, u32[]{:S(2)}, u32[]{:S(2)}) async-start(f32[8,1,512]{2,1,0:T(1,128)} %broadcast_in_dim.46), calls=%async_computation | async-start | bytes 32768 | tf_op jit(solution)/shard_map/all_to_all | solution.py:536
  64.4 30.2 %all-to-all-start.3 = ((f32[32,8,512]{2,1,0:T(8,128)}), f32[32,8,512]{2,1,0:T(8,128)S(1)}, u32[]{:S(2)}, u32[]{:S(2)}) async-start(f32[32,8,512]{2,1,0:T(8,128)} %broadcast_in_dim.52), calls=%async_computation.3 | async-start | bytes 1048576 | tf_op jit(solution)/shard_map/all_to_all | solution.py:538
  94.6 33.2 %copy-start = (f32[32,8,512]{2,1,0:T(8,128)}, f32[32,8,512]{2,1,0:T(8,128)S(1)}, u32[]{:S(2)}) copy-start(f32[32,8,512]{2,1,0:T(8,128)S(1)} %all-to-all-done.3.refs_2_) | copy-start | bytes 1572868
  95.5 32.3 %all-to-all-start.1 = ((f32[32,8,512]{2,1,0:T(8,128)}), f32[32,8,512]{2,1,0:T(8,128)S(1)}, u32[]{:S(2)}, u32[]{:S(2)}) async-start(f32[32,8,512]{2,1,0:T(8,128)} %broadcast_in_dim.48), calls=%async_computation.1 | async-start | bytes 1048576 | tf_op jit(solution)/shard_map/all_to_all | solution.py:538
  100.8 5.8 %collective-permute-start.6 = (f32[4,6,8,128]{3,2,1,0:T(8,128)S(1)}, f32[4,6,8,128]{3,2,1,0:T(8,128)S(1)}, u32[]{:S(2)}, u32[]{:S(2)}) collective-permute-start(f32[4,6,8,128]{3,2,1,0:T(8,128)S(1)} %copy-done.15), channel_id=1, source_target_pairs={{0,1},{1,2},{2,3},{3,4},{4,5},{5,6},{6,7},{8,9},{9,10},{10,11},{11... | collective-permute-start | bytes 294920 | tf_op jit(solution)/shard_map/ppermute | solution.py:531
  104.7 6.2 %collective-permute-start.7 = (f32[4,6,8,128]{3,2,1,0:T(8,128)S(1)}, f32[4,6,8,128]{3,2,1,0:T(8,128)S(1)}, u32[]{:S(2)}, u32[]{:S(2)}) collective-permute-start(f32[4,6,8,128]{3,2,1,0:T(8,128)S(1)} %copy-done.15), channel_id=1, source_target_pairs={{1,0},{2,1},{3,2},{4,3},{5,4},{6,5},{7,6},{9,8},{10,9},{11,10},{12... | collective-permute-start | bytes 294920 | tf_op jit(solution)/shard_map/ppermute | solution.py:531
  111.0 16.8 %collective-permute-start.10 = (f32[3,3,6,8,128]{4,3,2,1,0:T(8,128)S(1)}, f32[3,3,6,8,128]{4,3,2,1,0:T(8,128)S(1)}, u32[]{:S(2)}, u32[]{:S(2)}) collective-permute-start(f32[3,3,6,8,128]{4,3,2,1,0:T(8,128)S(1)} %get-tuple-element.40), channel_id=1, source_target_pairs={{0,16},{8,24},{16,32},{24,40},{32,48},{40,56},{48,64},{56,72},{64,... | collective-permute-start | bytes 663560 | tf_op jit(solution)/shard_map/ppermute | solution.py:531
  115.9 11.9 %collective-permute-start.11 = (f32[3,3,6,8,128]{4,3,2,1,0:T(8,128)S(1)}, f32[3,3,6,8,128]{4,3,2,1,0:T(8,128)S(1)}, u32[]{:S(2)}, u32[]{:S(2)}) collective-permute-start(f32[3,3,6,8,128]{4,3,2,1,0:T(8,128)S(1)} %get-tuple-element.39), channel_id=1, source_target_pairs={{16,0},{24,8},{32,16},{40,24},{48,32},{56,40},{64,48},{72,56},{80,... | collective-permute-start | bytes 663560 | tf_op jit(solution)/shard_map/ppermute | solution.py:531
  117.2 10.6 %copy-start.6 = (f32[2,3,6,8,128]{4,3,2,1,0:T(8,128)}, f32[2,3,6,8,128]{4,3,2,1,0:T(8,128)S(1)}, u32[]{:S(2)}) copy-start(f32[2,3,6,8,128]{4,3,2,1,0:T(8,128)S(1)} %slice.55.refs_7_) | copy-start | bytes 442372
  117.2 9.6 %collective-permute-start.8 = (f32[2,3,6,8,128]{4,3,2,1,0:T(8,128)S(1)}, f32[2,3,6,8,128]{4,3,2,1,0:T(8,128)S(1)}, u32[]{:S(2)}, u32[]{:S(2)}) collective-permute-start(f32[2,3,6,8,128]{4,3,2,1,0:T(8,128)S(1)} %slice.55.refs_7_), channel_id=1, source_target_pairs={{0,8},{8,16},{16,24},{24,32},{32,40},{40,48},{48,56},{56,64},{64,7... | collective-permute-start | bytes 442376 | tf_op jit(solution)/shard_map/ppermute | solution.py:531
  119.4 8.3 %collective-permute-start.9 = (f32[2,3,6,8,128]{4,3,2,1,0:T(8,128)S(1)}, f32[2,3,6,8,128]{4,3,2,1,0:T(8,128)S(1)}, u32[]{:S(2)}, u32[]{:S(2)}) collective-permute-start(f32[2,3,6,8,128]{4,3,2,1,0:T(8,128)S(1)} %slice.55.refs_7_), channel_id=1, source_target_pairs={{8,0},{16,8},{24,16},{32,24},{40,32},{48,40},{56,48},{64,56},{72,6... | collective-permute-start | bytes 442376 | tf_op jit(solution)/shard_map/ppermute | solution.py:531
  126.8 1.0 copy-start.11
  127.8 0.7 copy-start.12
  127.8 0.8 copy-start.9
  127.8 0.8 copy-start.10
  127.8 1.0 copy-start.3
  160.4 7.4 %collective-permute-start.12 = (f32[6,2,4,8,128]{4,3,2,1,0:T(8,128)S(1)}, f32[6,2,4,8,128]{4,3,2,1,0:T(8,128)S(1)}, u32[]{:S(2)}, u32[]{:S(2)}) collective-permute-start(f32[6,2,4,8,128]{4,3,2,1,0:T(8,128)S(1)} %get-tuple-element.41), channel_id=1, source_target_pairs={{0,8},{8,16},{16,24},{24,32},{32,40},{40,48},{48,56},{56,64},{64,7... | collective-permute-start | bytes 589832 | tf_op jit(solution)/shard_map/ppermute | solution.py:531
  163.4 8.1 %collective-permute-start.13 = (f32[6,2,4,8,128]{4,3,2,1,0:T(8,128)S(1)}, f32[6,2,4,8,128]{4,3,2,1,0:T(8,128)S(1)}, u32[]{:S(2)}, u32[]{:S(2)}) collective-permute-start(f32[6,2,4,8,128]{4,3,2,1,0:T(8,128)S(1)} %get-tuple-element.42), channel_id=1, source_target_pairs={{8,0},{16,8},{24,16},{32,24},{40,32},{48,40},{56,48},{64,56},{72,6... | collective-permute-start | bytes 589832 | tf_op jit(solution)/shard_map/ppermute | solution.py:531
  171.5 15.3 %copy-start.1 = (f32[16,2,4,8,128]{4,3,2,1,0:T(8,128)}, f32[16,2,4,8,128]{4,3,2,1,0:T(8,128)S(1)}, u32[]{:S(2)}) copy-start(f32[16,2,4,8,128]{4,3,2,1,0:T(8,128)S(1)} %pad_maximum_fusion.mid) | copy-start | bytes 1572868
  171.6 10.8 %collective-permute-start.14 = (f32[14,2,4,8,128]{4,3,2,1,0:T(8,128)S(1)}, f32[14,2,4,8,128]{4,3,2,1,0:T(8,128)S(1)}, u32[]{:S(2)}, u32[]{:S(2)}) collective-permute-start(f32[14,2,4,8,128]{4,3,2,1,0:T(8,128)S(1)} %slice.58), channel_id=1, source_target_pairs={{0,1},{1,2},{2,3},{3,4},{4,5},{5,6},{6,7},{8,9},{9,10},{10,11},{11... | collective-permute-start | bytes 1376264 | tf_op jit(solution)/shard_map/ppermute | solution.py:531
  177.0 9.8 %collective-permute-start.15 = (f32[14,2,4,8,128]{4,3,2,1,0:T(8,128)S(1)}, f32[14,2,4,8,128]{4,3,2,1,0:T(8,128)S(1)}, u32[]{:S(2)}, u32[]{:S(2)}) collective-permute-start(f32[14,2,4,8,128]{4,3,2,1,0:T(8,128)S(1)} %slice.58), channel_id=1, source_target_pairs={{1,0},{2,1},{3,2},{4,3},{5,4},{6,5},{7,6},{9,8},{10,9},{11,10},{12... | collective-permute-start | bytes 1376264 | tf_op jit(solution)/shard_map/ppermute | solution.py:531
  182.4 4.4 %copy-start.7 = (f32[14,2,4,8,128]{4,3,2,1,0:T(8,128)}, f32[14,2,4,8,128]{4,3,2,1,0:T(8,128)S(1)}, u32[]{:S(2)}) copy-start(f32[14,2,4,8,128]{4,3,2,1,0:T(8,128)S(1)} %collective-permute-done.14.low) | copy-start | bytes 1376260
  186.8 0.8 copy-start.8
  204.6 34.0 %all-to-all-start.5 = ((f32[32,8,512]{2,1,0:T(8,128)}), f32[32,8,512]{2,1,0:T(8,128)S(1)}, u32[]{:S(2)}, u32[]{:S(2)}) async-start(f32[32,8,512]{2,1,0:T(8,128)} %broadcast_in_dim.56), calls=%async_computation.5 | async-start | bytes 1048576 | tf_op jit(solution)/shard_map/all_to_all | solution.py:538
  219.6 5.9 %collective-permute-start.17 = (f32[4,4,8,128]{3,2,1,0:T(8,128)}, f32[4,4,8,128]{3,2,1,0:T(8,128)S(1)}, u32[]{:S(2)}, u32[]{:S(2)}) collective-permute-start(f32[4,4,8,128]{3,2,1,0:T(8,128)} %get-tuple-element.34), channel_id=1, source_target_pairs={{1,0},{2,1},{3,2},{4,3},{5,4},{6,5},{7,6},{9,8},{10,9},{11,10},{12... | collective-permute-start | bytes 196616 | tf_op jit(solution)/shard_map/ppermute | solution.py:531
  222.5 4.3 %collective-permute-start.16 = (f32[4,4,8,128]{3,2,1,0:T(8,128)}, f32[4,4,8,128]{3,2,1,0:T(8,128)S(1)}, u32[]{:S(2)}, u32[]{:S(2)}) collective-permute-start(f32[4,4,8,128]{3,2,1,0:T(8,128)} %get-tuple-element.34), channel_id=1, source_target_pairs={{0,1},{1,2},{2,3},{3,4},{4,5},{5,6},{6,7},{8,9},{9,10},{10,11},{11... | collective-permute-start | bytes 196616 | tf_op jit(solution)/shard_map/ppermute | solution.py:531
  227.7 7.8 %collective-permute-start.18 = (f32[3,3,4,8,128]{4,3,2,1,0:T(8,128)S(1)}, f32[3,3,4,8,128]{4,3,2,1,0:T(8,128)S(1)}, u32[]{:S(2)}, u32[]{:S(2)}) collective-permute-start(f32[3,3,4,8,128]{4,3,2,1,0:T(8,128)S(1)} %get-tuple-element.46), channel_id=1, source_target_pairs={{0,8},{8,16},{16,24},{24,32},{32,40},{40,48},{48,56},{56,64},{64,7... | collective-permute-start | bytes 442376 | tf_op jit(solution)/shard_map/ppermute | solution.py:531
  230.9 7.7 %collective-permute-start.19 = (f32[3,3,4,8,128]{4,3,2,1,0:T(8,128)S(1)}, f32[3,3,4,8,128]{4,3,2,1,0:T(8,128)S(1)}, u32[]{:S(2)}, u32[]{:S(2)}) collective-permute-start(f32[3,3,4,8,128]{4,3,2,1,0:T(8,128)S(1)} %get-tuple-element.45), channel_id=1, source_target_pairs={{8,0},{16,8},{24,16},{32,24},{40,32},{48,40},{56,48},{64,56},{72,6... | collective-permute-start | bytes 442376 | tf_op jit(solution)/shard_map/ppermute | solution.py:531
  235.5 3.1 %copy-start.13 = (f32[3,3,4,8,128]{4,3,2,1,0:T(8,128)}, f32[3,3,4,8,128]{4,3,2,1,0:T(8,128)S(1)}, u32[]{:S(2)}) copy-start(f32[3,3,4,8,128]{4,3,2,1,0:T(8,128)S(1)} %collective-permute-done.18.refs_3_) | copy-start | bytes 442372
  238.6 0.7 copy-start.14
  238.6 0.8 copy-start.4

commit v2 on v1

v2 whole, which is shorter than its diff:
```python
import math

import jax
import jax.numpy as jnp
from jax import lax
from jax.experimental import pallas as pl
from jax.experimental.pallas import tpu as pltpu
from jax.sharding import PartitionSpec as P


NC = 8
WINDOW = 21
OMEGA = 0.6
BETA = 0.5
ABSORB = 0.25
KH_FACTOR = 2.0 * math.pi * 6.0 * 20.0

F32 = jnp.float32
BF16 = jnp.bfloat16
VM = pl.BlockSpec(memory_space=pltpu.VMEM)
SM = pl.BlockSpec(memory_space=pltpu.SMEM)
PARAMS = pltpu.CompilerParams(vmem_limit_bytes=24 * 1024 * 1024)


def shape(*dims):
    return jax.ShapeDtypeStruct(dims, F32)


def scratch(*dims):
    return pltpu.VMEM(dims, F32)


def sort_matrix(rows, columns, flip):
    first = lax.broadcasted_iota(jnp.int32, (rows, columns), 0)
    second = lax.broadcasted_iota(jnp.int32, (rows, columns), 1)
    if flip:
        first, second = second, first
    lane = second % 128
    hit = (first == 4 * lane + second // 128) & (lane < 96)
    return jnp.where(hit, 1.0, 0.0).astype(BF16)


def exact_dot(values, matrix):
    high = values.astype(BF16)
    rest = values - high.astype(F32)
    middle = rest.astype(BF16)
    low = (rest - middle.astype(F32)).astype(BF16)
    dot = lambda part: jnp.dot(part, matrix, preferred_element_type=F32)
    return (dot(low) + dot(middle)) + dot(high)


def scaled_inverse(real, imag, scale):
    diag_real = 6.0 * scale - real
    diag_imag = -imag
    factor = OMEGA / (diag_real * diag_real + diag_imag * diag_imag)
    factor = jnp.where(real > 0.0, factor, 0.0)
    return diag_real * factor, -diag_imag * factor


def product(a, b):
    return a[0] * b[0] - a[1] * b[1], a[0] * b[1] + a[1] * b[0]


def pair_rows(value, temp):
    temp[8:32, :] = value
    row = lax.broadcasted_iota(jnp.int32, (24, 128), 0)
    return value + jnp.where(row % 2 == 0, temp[9:33, :], temp[7:31, :])


def neighbour(ref, x, c, r, count, step):
    center = lambda s: ref[x, c, s, 8:32, :]
    up = center(r + 1) if r < count - 1 else pltpu.roll(center(0), 127, 1)
    down = center(r - 1) if r > 0 else pltpu.roll(center(count - 1), 1, 1)
    total = ref[x - 1, c, r, 8:32, :] + ref[x + 1, c, r, 8:32, :]
    total = total + ref[x, c, r, 8 - step : 32 - step, :] + ref[x, c, r, 8 + step : 32 + step, :]
    return total + (up + down)


def sweep(old, new, weight, weight_at, source, source_at, low, high, count, step, scale):
    def body(x, _):
        for r in range(count):
            parts = []
            for c in range(2):
                total = neighbour(old, x, c, r, count, step)
                if scale != 1.0:
                    total = total * scale
                parts.append(source[x + source_at, c, r] + total)
            w = [weight[x + weight_at, c, r] for c in range(2)]
            moved = product(w, parts)
            for c in range(2):
                new[x, c, r, 8:32, :] = (1.0 - OMEGA) * old[x, c, r, 8:32, :] + moved[c]
        return 0

    lax.fori_loop(low, high, body, 0)


def clear(ref, count):
    def body(x, _):
        ref[x] = jnp.zeros(ref.shape[1:], F32)
        return 0

    lax.fori_loop(0, count, body, 0)


def clear_edges(ref, count):
    zero = jnp.zeros((8, 128), F32)

    def body(x, _):
        for c in range(2):
            for r in range(ref.shape[2]):
                ref[x, c, r, 0:8, :] = zero
                ref[x, c, r, 32:40, :] = zero
        return 0

    lax.fori_loop(0, count, body, 0)


def dense(target, pieces):
    lane = lax.broadcasted_iota(jnp.int32, (1, 128), 1)
    for n in range(3):
        tail = pltpu.roll(pieces[n + 1], 128 - 32 * (n + 1), 1)
        head = pieces[n] if n == 0 else pltpu.roll(pieces[n], 128 - 32 * n, 1)
        target[0:1, n * 128 : n * 128 + 128] = jnp.where(lane < 96 - 32 * n, head, tail)


def loose(block):
    lane = lax.broadcasted_iota(jnp.int32, (block.shape[0], 128), 1)
    parts = [block[:, n * 128 : n * 128 + 128] for n in range(3)]
    result = []
    for k in range(4):
        if k == 0:
            value = parts[0]
        elif k == 3:
            value = pltpu.roll(parts[2], 96, 1)
        else:
            value = jnp.where(lane < 32 * k, pltpu.roll(parts[k - 1], 32 * k, 1), pltpu.roll(parts[k], 32 * k, 1))
        result.append(jnp.where(lane < 96, value, 0.0))
    return result


def pack_kernel(table, right_side, layer_index, absorb_level, packed, inverse_two, temp):
    matrix = sort_matrix(384, 512, False)
    field = exact_dot(right_side[...].reshape(64, 384), matrix)
    both = jnp.concatenate(
        [layer_index[...].reshape(32, 384), absorb_level[...].reshape(32, 384)], axis=0
    )
    codes = jnp.dot(both.astype(F32).astype(BF16), matrix, preferred_element_type=F32)
    inside = lax.broadcasted_iota(jnp.int32, (32, 128), 1) < 96
    total = [jnp.zeros((32, 128), F32), jnp.zeros((32, 128), F32)]
    for r in range(4):
        lanes = slice(r * 128, r * 128 + 128)
        layer = codes[0:32, lanes]
        velocity = jnp.full((32, 128), table[0], F32)
        for n in range(1, 16):
            velocity = jnp.where(layer == float(n), table[n], velocity)
        ratio = KH_FACTOR / velocity
        real = jnp.where(inside, ratio * ratio, 0.0)
        imag = -real * (BETA + ABSORB * codes[32:64, lanes])
        total = [total[0] + real, total[1] + imag]
        for x in range(4):
            rows = slice(x * 8, x * 8 + 8)
            packed[x, 0, r] = field[x * 8 : x * 8 + 8, lanes]
            packed[x, 1, r] = field[32 + x * 8 : 40 + x * 8, lanes]
            packed[x, 2, r] = real[rows]
            packed[x, 3, r] = imag[rows]
    means = []
    for c in range(2):
        t = total[c]
        t = (t[0:8] + t[8:16]) + (t[16:24] + t[24:32])
        temp[c] = t
        means.append(
            [
                ((temp[c, 4 * k : 4 * k + 1] + temp[c, 4 * k + 1 : 4 * k + 2])
                 + (temp[c, 4 * k + 2 : 4 * k + 3] + temp[c, 4 * k + 3 : 4 * k + 4])) * (1.0 / 64.0)
                for k in range(2)
            ]
        )
    w = [scaled_inverse(means[0][k], means[1][k], 0.0625) for k in range(2)]
    dense(inverse_two, [w[k][c] for c in range(2) for k in range(2)])


def pack(table, right_side, layer_index, absorb_level):
    return pl.pallas_call(
        pack_kernel,
        name="pack",
        out_shape=(shape(4, 4, 4, 8, 128), shape(1, 384)),
        in_specs=[SM, VM, VM, VM],
        out_specs=(VM, VM),
        scratch_shapes=[scratch(2, 8, 128)],
        compiler_params=PARAMS,
    )(table, right_side, layer_index, absorb_level)


def set_rows(target, x, c, r, low, mid, high):
    target[x, c, r, 0:8, :] = low
    target[x, c, r, 8:16, :] = mid
    target[x, c, r, 16:24, :] = high


def down_body(source, weight, diag, weight_one, diag_one, guess, out_guess, out_one, out_two, one, s1, t1, temp):
    def first(x, _):
        for r in range(4):
            f = [source[x, c, r] for c in range(2)]
            w = [weight[x, c, r] for c in range(2)]
            e = product(w, f)
            for c in range(2):
                guess[x, c, r, 8:32, :] = e[c]
        return 0

    lax.fori_loop(0, 16, first, 0)
    sweep(guess, out_guess, weight, 0, source, 0, 1, 15, 4, 1, 1.0)

    def residual(k, _):
        for s in range(2):
            sums = [None, None]
            for half in range(2):
                x = 2 + 2 * k + half
                for r in (2 * s, 2 * s + 1):
                    e = [out_guess[x, c, r, 8:32, :] for c in range(2)]
                    d = [diag[x, c, r] for c in range(2)]
                    moved = product(d, e)
                    for c in range(2):
                        value = source[x, c, r] + neighbour(out_guess, x, c, r, 4, 1) - moved[c]
                        sums[c] = value if sums[c] is None else sums[c] + value
            g = [pair_rows(sums[c], temp.at[c]) * 0.125 for c in range(2)]
            w = [weight_one[k, c, s] for c in range(2)]
            e = product(w, g)
            for c in range(2):
                s1[k, c, s] = g[c]
                one[k, c, s, 8:32, :] = e[c]
        return 0

    lax.fori_loop(0, 6, residual, 0)
    sweep(one, t1, weight_one, 0, s1, 0, 1, 5, 2, 2, 0.25)

    total = [None, None]
    for k in (2, 3):
        for s in range(2):
            e = [t1[k, c, s, 8:32, :] for c in range(2)]
            d = [diag_one[k, c, s] for c in range(2)]
            moved = product(d, e)
            for c in range(2):
                value = s1[k, c, s] + 0.25 * neighbour(t1, k, c, s, 2, 2) - moved[c]
                total[c] = value if total[c] is None else total[c] + value
    pieces = []
    for c in range(2):
        temp[c, 8:32, :] = total[c]
        for k in range(2):
            row = 16 + 4 * k
            pieces.append((temp[c, row : row + 1, :] + temp[c, row + 2 : row + 3, :]) * 0.125)
    dense(out_two, pieces)

    def send(k, _):
        for s in range(2):
            for c in range(2):
                out_one[k, c, s * 4 : s * 4 + 4, :] = t1[k + 1, c, s, pl.ds(16, 4, 2), :]
                out_one[k, c + 2, s * 4 : s * 4 + 4, :] = s1[k + 1, c, s, pl.ds(8, 4, 2), :]
                if out_one.shape[1] > 4:
                    out_one[k, c + 4, s * 4 : s * 4 + 4, :] = weight_one[k + 1, c, s, pl.ds(8, 4, 2), :]
        return 0

    lax.fori_loop(0, 4, send, 0)


def down_first_kernel(before, mid, after, low, high, source, weight, diag, weight_one, diag_one, out_guess, out_one, out_two,
                      guess, one, s1, t1, temp):
    clear_edges(guess, 16)
    clear_edges(out_guess, 16)
    clear_edges(one, 6)
    clear_edges(t1, 6)
    zero = jnp.zeros((8, 128), F32)

    def fill(x, edge):
        for r in range(4):
            for c in range(4):
                if edge is None:
                    parts = (low[x - 1, c, r], mid[x - 1, c, r], high[x - 1, c, r])
                else:
                    parts = (zero, edge[c, r], zero)
                set_rows(source if c < 2 else diag, x, c % 2, r, *parts)
            real, imag = diag[x, 0, r], diag[x, 1, r]
            w = scaled_inverse(real, imag, 1.0)
            for c in range(2):
                weight[x, c, r] = w[c]

    def filled(x, _):
        fill(x, None)
        return 0

    fill(0, before.at[0])
    lax.fori_loop(1, 15, filled, 0)
    fill(15, after.at[after.shape[0] - 1])

    def coarse(k, _):
        for s in range(2):
            shift = []
            for c in range(2):
                total = None
                for half in range(2):
                    for r in (2 * s, 2 * s + 1):
                        value = diag[2 + 2 * k + half, c, r]
                        total = value if total is None else total + value
                shift.append(pair_rows(total, temp.at[c]) * 0.125)
            w = scaled_inverse(shift[0], shift[1], 0.25)
            d = (1.5 - shift[0], -shift[1])
            for c in range(2):
                weight_one[k, c, s] = w[c]
                diag_one[k, c, s] = d[c]
        return 0

    lax.fori_loop(0, 6, coarse, 0)

    def turn(x, _):
        for r in range(4):
            diag[x, 0, r] = 6.0 - diag[x, 0, r]
            diag[x, 1, r] = -diag[x, 1, r]
        return 0

    lax.fori_loop(0, 16, turn, 0)
    down_body(source, weight, diag, weight_one, diag_one, guess, out_guess, out_one, out_two, one, s1, t1, temp)


FINE = (16, 2, 4, 24, 128)
WIDE = (16, 2, 4, 40, 128)
COARSE = (6, 2, 2, 24, 128)
COARSE_WIDE = (6, 2, 2, 40, 128)
DOWN_SCRATCH = [scratch(*WIDE), scratch(*COARSE_WIDE), scratch(*COARSE), scratch(*COARSE_WIDE), scratch(2, 40, 128)]


def down_first(before, mid, after, low, high):
    return pl.pallas_call(
        down_first_kernel,
        name="down_first",
        out_shape=(shape(*FINE), shape(*FINE), shape(*FINE), shape(*COARSE), shape(*COARSE), shape(*WIDE),
                   shape(4, 6, 8, 128), shape(1, 384)),
        in_specs=[VM] * 5,
        out_specs=(VM,) * 8,
        scratch_shapes=DOWN_SCRATCH,
        compiler_params=PARAMS,
    )(before, mid, after, low, high)


def down_second_kernel(before, mid, after, low, high, weight, diag, weight_one, diag_one, out_source, out_guess, out_one, out_two,
                       guess, one, s1, t1, temp):
    clear_edges(guess, 16)
    clear_edges(out_guess, 16)
    clear_edges(one, 6)
    clear_edges(t1, 6)
    zero = jnp.zeros((8, 128), F32)

    def fill(x, edge):
        for r in range(4):
            for c in range(2):
                if edge is None:
                    parts = (low[x - 1, c, r], mid[x - 1, c, r], high[x - 1, c, r])
                else:
                    parts = (zero, edge[c, r], zero)
                set_rows(out_source, x, c, r, *parts)

    def filled(x, _):
        fill(x, None)
        return 0

    fill(0, before.at[0])
    lax.fori_loop(1, 15, filled, 0)
    fill(15, after.at[after.shape[0] - 1])
    down_body(out_source, weight, diag, weight_one, diag_one, guess, out_guess, out_one, out_two, one, s1, t1, temp)


def down_second(before, mid, after, low, high, weight, diag, weight_one, diag_one):
    return pl.pallas_call(
        down_second_kernel,
        name="down_second",
        out_shape=(shape(*FINE), shape(*WIDE), shape(4, 4, 8, 128), shape(1, 384)),
        in_specs=[VM] * 9,
        out_specs=(VM,) * 4,
        scratch_shapes=DOWN_SCRATCH,
        compiler_params=PARAMS,
    )(before, mid, after, low, high, weight, diag, weight_one, diag_one)


def unpack_two(packed, target, planes):
    def body(x, _):
        for k, part in enumerate(loose(packed[x])):
            target[x, k] = part
        return 0

    lax.fori_loop(0, planes, body, 0)


def solve_two(begin, source, weight, ping, pong, window, groups):
    clear(ping, window + 8)
    clear(pong, window + 8)
    rows = slice(8, 8 + groups)
    block = next(b for b in (7, 4, 1) if window % b == 0)

    def over(body):
        def several(number, _):
            for n in range(block):
                body(number * block + n)
            return 0

        lax.fori_loop(0, window // block, several, 0)

    def start(x):
        for k in range(2):
            e = product([weight[begin + x, k], weight[begin + x, 2 + k]], [source[begin + x, k], source[begin + x, 2 + k]])
            for c in range(2):
                ping[x + 4, c * 2 + k, rows, :] = e[c]

    over(start)

    def step(old, new):
        def body(x):
            here = [old[x + 4, n, rows, :] for n in range(4)]
            for k in range(2):
                parts = []
                for c in range(2):
                    n, other = c * 2 + k, c * 2 + 1 - k
                    side = old[x + 4, other, 7 : 7 + groups, :] if k == 0 else old[x + 4, other, 9 : 9 + groups, :]
                    total = (old[x + 3, n, rows, :] + old[x + 5, n, rows, :]) + (here[other] + side)
                    total = total + (pltpu.roll(here[n], 1, 1) + pltpu.roll(here[n], 127, 1))
                    parts.append(source[begin + x, n] + 0.0625 * total)
                moved = product([weight[begin + x, k], weight[begin + x, 2 + k]], parts)
                for c in range(2):
                    new[x + 4, c * 2 + k, rows, :] = (1.0 - OMEGA) * here[c * 2 + k] + moved[c]

        over(body)

    pairs = (ping, pong)
    for number in range(NC - 1):
        step(pairs[number % 2], pairs[(number + 1) % 2])
    return pairs[(NC - 1) % 2]


def spread_rows(target, at, x, c, tile, block):
    for s in range(2):
        for twice in range(2):
            target[x, c, s, pl.ds(at + 8 * tile + twice, 4, 2), :] = block[s * 4 : s * 4 + 4, :]


def add_two(answer, begin, one, where, first, count):
    gx, gy = where[0] - begin, where[1]
    row = lax.broadcasted_iota(jnp.int32, (8, 128), 0)
    for j in range(count):
        x = gx + 4 + (first + j) // 2
        for c in range(2):
            for tile in range(3):
                spot = gy + 7 + tile
                low = jnp.broadcast_to(answer[x, c * 2, pl.ds(spot, 1), :], (8, 128))
                high = jnp.broadcast_to(answer[x, c * 2 + 1, pl.ds(spot, 1), :], (8, 128))
                value = jnp.where(row < 4, low, high)
                at = slice(8 + 8 * tile, 16 + 8 * tile)
                for s in range(2):
                    one[j, c, s, at, :] = one[j, c, s, at, :] + value


def up_first_kernel(planes, groups, where, source_two, weight_two, near_low, near_high, far_low, far_high, own,
                    source, weight, diag, guess, out_source, out_first, out_weight,
                    out_low, out_high, out_two, packed_two, ping, pong, one, s1, t1, ea, eb):
    window = min(planes, WINDOW)
    begin = jnp.clip(where[0] - 10, 0, planes - window)
    unpack_two(weight_two, out_two, planes)
    unpack_two(source_two, packed_two, planes)
    answer = solve_two(begin, packed_two, out_two, ping, pong, window, groups)
    clear_edges(one, 12)
    clear_edges(t1, 12)
    j = 0
    for ref, low, high in ((far_low, 0, 3), (near_low, 0, 2), (own, 0, 2), (near_high, 0, 2), (far_high, 0, 3)):
        for k in range(low, high):
            for c in range(2):
                for tile in range(3):
                    spread_rows(one, 8, j, c, tile, ref[k, tile, c])
                    spread_rows(s1, 0, j, c, tile, ref[k, tile, c + 2])
                    spread_rows(out_weight, 0, j, c, tile, ref[k, tile, c + 4])
            j += 1
    add_two(answer, begin, one, where, -5, 12)
    sweep(one, t1, out_weight, 0, s1, 0, 1, 11, 2, 2, 0.25)
    sweep(t1, one, out_weight, 0, s1, 0, 2, 10, 2, 2, 0.25)
    clear_edges(ea, 16)
    clear_edges(eb, 16)

    def correct(x1, _):
        for half in range(2):
            x = 2 * x1 - 4 + half
            for r in range(4):
                for c in range(2):
                    ea[x, c, r, 8:32, :] = guess[x, c, r, 8:32, :] + one[x1, c, r // 2, 8:32, :]
        return 0

    lax.fori_loop(2, 10, correct, 0)
    sweep(ea, eb, weight, 0, source, 0, 2, 14, 4, 1, 1.0)
    sweep(eb, ea, weight, 0, source, 0, 3, 13, 4, 1, 1.0)

    def rest(targets):
        def body(x, _):
            for r in range(4):
                e = [ea[x, c, r, 8:32, :] for c in range(2)]
                moved = product([diag[x, c, r] for c in range(2)], e)
                for c in range(2):
                    value = source[x, c, r] + neighbour(ea, x, c, r, 4, 1) - moved[c]
                    for target, first in targets:
                        target[x - first, c, r] = value[8:16]
            return 0

        return body

    lax.fori_loop(4, 6, rest([(out_low, 4)]), 0)
    lax.fori_loop(6, 10, rest([(out_low, 4), (out_source, 6), (out_high, 6)]), 0)
    lax.fori_loop(10, 12, rest([(out_high, 6)]), 0)
    for x in range(4):
        for c in range(2):
            for r in range(4):
                out_first[x, c, r] = ea[x + 6, c, r, 16:24, :]


def up_first(where, source_two, weight_two, near_low, near_high, far_low, far_high, own, source, weight, diag, guess):
    planes, groups = source_two.shape[0], source_two.shape[1]
    two = scratch(min(planes, WINDOW) + 8, 4, 16 + groups, 128)
    level, wide = scratch(12, 2, 2, 24, 128), scratch(12, 2, 2, 40, 128)
    return pl.pallas_call(
        lambda *refs: up_first_kernel(planes, groups, *refs),
        name="up_first",
        out_shape=(shape(4, 2, 4, 8, 128), shape(4, 2, 4, 8, 128), shape(12, 2, 2, 24, 128),
                   shape(6, 2, 4, 8, 128), shape(6, 2, 4, 8, 128), shape(planes, 4, groups, 128)),
        in_specs=[SM] + [VM] * 11,
        out_specs=(VM,) * 6,
        scratch_shapes=[scratch(planes, 4, groups, 128), two, two, wide, level, wide, scratch(*WIDE), scratch(*WIDE)],
        compiler_params=PARAMS,
    )(where, source_two, weight_two, near_low, near_high, far_low, far_high, own, source, weight, diag, guess)


def up_second_kernel(planes, groups, where, source_two, weight_two, near_low, near_high, own,
                     source, weight, guess, weight_one, first, result,
                     packed_two, ping, pong, one, s1, t1, ea, eb):
    window = min(planes, WINDOW)
    begin = jnp.clip(where[0] - 10, 0, planes - window)
    unpack_two(source_two, packed_two, planes)
    answer = solve_two(begin, packed_two, weight_two, ping, pong, window, groups)
    clear_edges(one, 8)
    clear_edges(t1, 8)
    j = 0
    for ref, low, high in ((near_low, 0, 3), (own, 0, 2), (near_high, 0, 3)):
        for k in range(low, high):
            for c in range(2):
                for tile in range(3):
                    spread_rows(one, 8, j, c, tile, ref[k, tile, c])
                    spread_rows(s1, 0, j, c, tile, ref[k, tile, c + 2])
            j += 1
    add_two(answer, begin, one, where, -3, 8)
    sweep(one, t1, weight_one, 2, s1, 0, 1, 7, 2, 2, 0.25)
    sweep(t1, one, weight_one, 2, s1, 0, 2, 6, 2, 2, 0.25)
    clear_edges(ea, 16)
    clear_edges(eb, 16)

    def correct(x1, _):
        for half in range(2):
            x = 2 * x1 + half
            for r in range(4):
                for c in range(2):
                    ea[x, c, r, 8:32, :] = guess[x, c, r, 8:32, :] + one[x1, c, r // 2, 8:32, :]
        return 0

    lax.fori_loop(2, 6, correct, 0)
    sweep(ea, eb, weight, 0, source, 0, 5, 11, 4, 1, 1.0)
    sweep(eb, ea, weight, 0, source, 0, 6, 10, 4, 1, 1.0)
    blocks = []
    for c in range(2):
        for x in range(4):
            blocks.append(
                jnp.concatenate([first[x, c, r] + ea[x + 6, c, r, 16:24, :] for r in range(4)], axis=1)
            )
    values = jnp.concatenate(blocks, axis=0)
    result[...] = exact_dot(values, sort_matrix(512, 384, True)).reshape(2, 4, 8, 384)


def up_second(where, source_two, weight_two, near_low, near_high, own, source, weight, guess, weight_one, first):
    planes, groups = source_two.shape[0], source_two.shape[1]
    two = scratch(min(planes, WINDOW) + 8, 4, 16 + groups, 128)
    level, wide = scratch(8, 2, 2, 24, 128), scratch(8, 2, 2, 40, 128)
    return pl.pallas_call(
        lambda *refs: up_second_kernel(planes, groups, *refs),
        name="up_second",
        out_shape=shape(2, 4, 8, 384),
        in_specs=[SM] + [VM] * 10,
        out_specs=VM,
        scratch_shapes=[scratch(planes, 4, groups, 128), two, two, wide, level, wide, scratch(*WIDE), scratch(*WIDE)],
        compiler_params=PARAMS,
    )(where, source_two, weight_two, near_low, near_high, own, source, weight, guess, weight_one, first)


def shifted(block, axis, by):
    count = lax.axis_size(axis)
    pairs = [(i, i + by) for i in range(count) if 0 <= i + by < count]
    return lax.ppermute(block, axis, pairs)


def gather_two(row):
    count_y, count_x = lax.axis_size("gy"), lax.axis_size("gx")
    width = row.shape[0]
    sent = jnp.broadcast_to(row[None], (count_x * count_y, width, 384))
    got = lax.all_to_all(sent, ("gx", "gy"), 0, 0)
    return [got[:, n].reshape(count_x, count_y, 384) for n in range(width)]


def y_sides(block):
    return shifted(block, "gy", 1), shifted(block, "gy", -1)


def y_tiles(block):
    low, high = y_sides(block)
    return jnp.stack([low, block, high], axis=1)


def local(right_side, velocity_table, layer_index, absorb_level):
    where = jnp.stack([lax.axis_index("gx"), lax.axis_index("gy")]).astype(jnp.int32)
    packed, inverse_two = pack(velocity_table, right_side, layer_index, absorb_level)
    before, after = shifted(packed[2:], "gx", 2), shifted(packed[:2], "gx", -2)
    mid = jnp.concatenate(
        [before[1:], shifted(packed, "gx", 1), packed, shifted(packed, "gx", -1), after[:1]]
    )
    low, high = y_sides(mid)
    source, weight, diag, weight_one, diag_one, guess, one, two = down_first(before, mid, after, low, high)
    source_two, weight_two = gather_two(jnp.concatenate([two, inverse_two]))
    tiles = y_tiles(one)
    near_low, near_high = shifted(tiles[1:3], "gx", 1), shifted(tiles[1:3], "gx", -1)
    far_low, far_high = shifted(tiles[0:3], "gx", 2), shifted(tiles[1:4], "gx", -2)
    rest, first, weight_one_wide, rest_low, rest_high, weight_two = up_first(
        where, source_two, weight_two, near_low, near_high, far_low, far_high, tiles[1:3], source, weight, diag, guess
    )
    before, after = shifted(rest_low, "gx", 1), shifted(rest_high, "gx", -1)
    mid = jnp.concatenate([before[1:], rest, after[:5]])
    low, high = y_sides(mid)
    source, guess, one, two = down_second(before, mid, after, low, high, weight, diag, weight_one, diag_one)
    (source_two,) = gather_two(two)
    tiles = y_tiles(one)
    near_low, near_high = shifted(tiles[0:3], "gx", 1), shifted(tiles[1:4], "gx", -1)
    return up_second(
        where, source_two, weight_two, near_low, near_high, tiles[1:3], source, weight, guess, weight_one_wide, first
    )


def solution(mesh):
    placed = (P(None, "gx", "gy", None), P(), P("gx", "gy", None), P("gx", "gy", None))
    return jax.shard_map(
        local, mesh=mesh, in_specs=placed, out_specs=P(None, "gx", "gy", None), check_vma=False
    )
```

time: 270 us -> 203 us (0.75)
  the two profiles are of different devices: /device:TPU:1 before, /device:TPU:134 now
where the time goes in v2:
time: 203 us; the launch traced here: 202 us
  starting transfers between devices  94.1 us (46%)
  waiting for transfers between devices  52.5 us (26%)
  Pallas kernels  31.7 us (16%)
  local copies, waits for them, and re-layouts  23.1 us (11%)
    ppermute x20, starting transfers between devices, shifted(): return lax.ppermute(block, axis, pairs)  63.7 us
    ppermute x20, waiting for transfers between devices, shifted(): return lax.ppermute(block, axis, pairs)  52.4 us
    all_to_all x2, starting transfers between devices, gather_two(): got = lax.all_to_all(sent, ('gx', 'gy'), 0, 0)  30.4 us
    unnamed x50, local copies, waits for them, and re-layouts  17.3 us
    pallas_call x1, Pallas kernels, up_first(): pl.pallas_call(lambda *refs: up_first_kernel(planes, groups, *refs), name...  14 us
    pallas_call x1, Pallas kernels, up_second(): pl.pallas_call(lambda *refs: up_second_kernel(planes, groups, *refs), nam...  9.4 us
  transfers between devices with their start and end apart: 22, of which 16 were waited for; matrix products, arithmetic and copies ran while one was open for 2% of the time, Pallas kernels for 0%

profile of v2, /device:TPU:134, one launch (start us, length us, event | category | flops | bytes accessed | tf_op | source)
XLA Modules:
  0.0 202.0 jit_solution(1136147587709984672)
XLA Ops:
  3.1 1.1 pack.1
  4.3 5.1 %collective-permute-start = (f32[2,4,4,8,128]{4,3,2,1,0:T(8,128)S(1)}, f32[2,4,4,8,128]{4,3,2,1,0:T(8,128)S(1)}, u32[]{:S(2)}, u32[]{:S(2)}) collective-permute-start(f32[2,4,4,8,128]{4,3,2,1,0:T(8,128)S(1)} %get-tuple-element.50), channel_id=1, source_target_pairs={{0,16},{8,24},{16,32},{24,40},{32,48},{40,56},{48,64},{56,72},{64,... | collective-permute-start | bytes 393224 | tf_op jit(solution)/shard_map/ppermute | solution.py:595
  9.4 2.6 %collective-permute-start.1 = (f32[4,4,4,8,128]{4,3,2,1,0:T(8,128)S(1)}, f32[4,4,4,8,128]{4,3,2,1,0:T(8,128)S(1)}, u32[]{:S(2)}, u32[]{:S(2)}) collective-permute-start(f32[4,4,4,8,128]{4,3,2,1,0:T(8,128)S(1)} %get-tuple-element.25), channel_id=1, source_target_pairs={{0,8},{8,16},{16,24},{24,32},{32,40},{40,48},{48,56},{56,64},{64,7... | collective-permute-start | bytes 786440 | tf_op jit(solution)/shard_map/ppermute | solution.py:595
  12.0 6.6 %collective-permute-start.2 = (f32[4,4,4,8,128]{4,3,2,1,0:T(8,128)S(1)}, f32[4,4,4,8,128]{4,3,2,1,0:T(8,128)S(1)}, u32[]{:S(2)}, u32[]{:S(2)}) collective-permute-start(f32[4,4,4,8,128]{4,3,2,1,0:T(8,128)S(1)} %get-tuple-element.25), channel_id=1, source_target_pairs={{8,0},{16,8},{24,16},{32,24},{40,32},{48,40},{56,48},{64,56},{72,6... | collective-permute-start | bytes 786440 | tf_op jit(solution)/shard_map/ppermute | solution.py:595
  18.6 1.9 collective-permute-start.3
  20.6 1.8 collective-permute-done.1
  22.5 2.5 %collective-permute-done.2 = f32[4,4,4,8,128]{4,3,2,1,0:T(8,128)S(1)} collective-permute-done((f32[4,4,4,8,128]{4,3,2,1,0:T(8,128)S(1)}, f32[4,4,4,8,128]{4,3,2,1,0:T(8,128)S(1)}, u32[]{:S(2)}, u32[]{:S(2)}) %collective-permute-start.2) | collective-permute-done | bytes 262176 | tf_op jit(solution)/shard_map/ppermute | solution.py:595
  25.0 2.0 collective-permute-done.3.after
  27.0 1.9 collective-permute-start.5
  28.9 2.5 %collective-permute-start.4 = (f32[14,4,4,8,128]{4,3,2,1,0:T(8,128)S(1)}, f32[14,4,4,8,128]{4,3,2,1,0:T(8,128)S(1)}, u32[]{:S(2)}, u32[]{:S(2)}) collective-permute-start(f32[14,4,4,8,128]{4,3,2,1,0:T(8,128)S(1)} %slice_dynamic-update-slice_fusion.mid), channel_id=1, source_target_pairs={{0,1},{1,2},{2,3},{3,4},{4,5},{5,6},{6,7},{8,9},{9,10},{10,11},{11... | collective-permute-start | bytes 2752520 | tf_op jit(solution)/shard_map/ppermute | solution.py:595
  31.4 8.4 %collective-permute-done.5.high = f32[14,4,4,8,128]{4,3,2,1,0:T(8,128)S(1)} collective-permute-done((f32[14,4,4,8,128]{4,3,2,1,0:T(8,128)S(1)}, f32[14,4,4,8,128]{4,3,2,1,0:T(8,128)S(1)}, u32[]{:S(2)}, u32[]{:S(2)}) %collective-permute-start.5) | collective-permute-done | bytes 917536 | tf_op jit(solution)/shard_map/ppermute | solution.py:595
  39.8 3.8 %collective-permute-done.4.low = f32[14,4,4,8,128]{4,3,2,1,0:T(8,128)S(1)} collective-permute-done((f32[14,4,4,8,128]{4,3,2,1,0:T(8,128)S(1)}, f32[14,4,4,8,128]{4,3,2,1,0:T(8,128)S(1)}, u32[]{:S(2)}, u32[]{:S(2)}) %collective-permute-start.4) | collective-permute-done | bytes 917536 | tf_op jit(solution)/shard_map/ppermute | solution.py:595
  43.6 4.0 %down_first.1 = (f32[16,2,4,24,128]{4,3,2,1,0:T(8,128)S(1)}, f32[16,2,4,24,128]{4,3,2,1,0:T(8,128)S(1)}, f32[16,2,4,24,128]{4,3,2,1,0:T(8,128)S(1)}, f32[6,2,2,2...) custom-call(f32[2,4,4,8,128]{4,3,2,1,0:T(8,128)S(1)} %collective-per, ...), custom_call_target="tpu_custom_call" | custom-call | tf_op jit(solution)/shard_map/down_first/pallas_call | solution.py:331
  47.6 1.5 copy-done.2
  49.1 1.2 copy-done.4
  52.8 15.4 %all-to-all-start = ((f32[256,2,384]{2,1,0:T(2,128)}), f32[256,2,384]{2,1,0:T(2,128)}, u32[]{:S(2)}, u32[]{:S(2)}) async-start(f32[256,2,384]{2,1,0:T(2,128)} %broadcast_in_dim.6), calls=%async_computation | async-start | bytes 1572864 | tf_op jit(solution)/shard_map/all_to_all | solution.py:602
  68.2 2.5 %collective-permute-start.7 = (f32[4,6,8,128]{3,2,1,0:T(8,128)S(1)}, f32[4,6,8,128]{3,2,1,0:T(8,128)S(1)}, u32[]{:S(2)}, u32[]{:S(2)}) collective-permute-start(f32[4,6,8,128]{3,2,1,0:T(8,128)S(1)} %get-tuple-element.28), channel_id=1, source_target_pairs={{1,0},{2,1},{3,2},{4,3},{5,4},{6,5},{7,6},{9,8},{10,9},{11,10},{12... | collective-permute-start | bytes 294920 | tf_op jit(solution)/shard_map/ppermute | solution.py:595
  70.7 1.9 collective-permute-start.6
  73.6 3.8 %collective-permute-done.6 = f32[4,6,8,128]{3,2,1,0:T(8,128)S(1)} collective-permute-done((f32[4,6,8,128]{3,2,1,0:T(8,128)S(1)}, f32[4,6,8,128]{3,2,1,0:T(8,128)S(1)}, u32[]{:S(2)}, u32[]{:S(2)}) %collective-permute-start.6) | collective-permute-done | bytes 98336 | tf_op jit(solution)/shard_map/ppermute | solution.py:595
  77.4 4.9 %collective-permute-start.9 = (f32[2,3,6,8,128]{4,3,2,1,0:T(8,128)S(1)}, f32[2,3,6,8,128]{4,3,2,1,0:T(8,128)}, u32[]{:S(2)}, u32[]{:S(2)}) collective-permute-start(f32[2,3,6,8,128]{4,3,2,1,0:T(8,128)S(1)} %slice.62.refs_7_), channel_id=1, source_target_pairs={{8,0},{16,8},{24,16},{32,24},{40,32},{48,40},{56,48},{64,56},{72,6... | collective-permute-start | bytes 442376 | tf_op jit(solution)/shard_map/ppermute | solution.py:595
  82.3 1.9 collective-permute-start.8
  85.0 4.0 %collective-permute-start.11 = (f32[3,3,6,8,128]{4,3,2,1,0:T(8,128)}, f32[3,3,6,8,128]{4,3,2,1,0:T(8,128)S(1)}, u32[]{:S(2)}, u32[]{:S(2)}) collective-permute-start(f32[3,3,6,8,128]{4,3,2,1,0:T(8,128)} %get-tuple-element.47), channel_id=1, source_target_pairs={{16,0},{24,8},{32,16},{40,24},{48,32},{56,40},{64,48},{72,56},{80,... | collective-permute-start | bytes 663560 | tf_op jit(solution)/shard_map/ppermute | solution.py:595
  89.0 3.3 %collective-permute-start.10 = (f32[3,3,6,8,128]{4,3,2,1,0:T(8,128)}, f32[3,3,6,8,128]{4,3,2,1,0:T(8,128)}, u32[]{:S(2)}, u32[]{:S(2)}) collective-permute-start(f32[3,3,6,8,128]{4,3,2,1,0:T(8,128)} %get-tuple-element.48), channel_id=1, source_target_pairs={{0,16},{8,24},{16,32},{24,40},{32,48},{40,56},{48,64},{56,72},{64,... | collective-permute-start | bytes 663560 | tf_op jit(solution)/shard_map/ppermute | solution.py:595
  92.4 2.2 %fusion = (f32[256,1,384]{2,1,0:T(1,128)S(1)}, f32[256,1,384]{2,1,0:T(1,128)S(1)}) fusion(f32[256,2,384]{2,1,0:T(2,128)} %all-to-all-done), kind=kLoop, calls=%fused_computation.13 | loop fusion | bytes 1572864 | tf_op jit(solution)/shard_map/slice | solution.py:603
  94.6 2.8 %collective-permute-done.11.refs_6_ = f32[3,3,6,8,128]{4,3,2,1,0:T(8,128)S(1)} collective-permute-done((f32[3,3,6,8,128]{4,3,2,1,0:T(8,128)}, f32[3,3,6,8,128]{4,3,2,1,0:T(8,128)S(1)}, u32[]{:S(2)}, u32[]{:S(2)}) %collective-permute-start.11) | collective-permute-done | bytes 221216 | tf_op jit(solution)/shard_map/ppermute | solution.py:595
  97.4 3.4 %collective-permute-done.10.refs_5_ = f32[3,3,6,8,128]{4,3,2,1,0:T(8,128)} collective-permute-done((f32[3,3,6,8,128]{4,3,2,1,0:T(8,128)}, f32[3,3,6,8,128]{4,3,2,1,0:T(8,128)}, u32[]{:S(2)}, u32[]{:S(2)}) %collective-permute-start.10) | collective-permute-done | bytes 221216 | tf_op jit(solution)/shard_map/ppermute | solution.py:595
  100.8 1.4 copy-done.5
  102.2 14.0 %up_first.1 = (f32[4,2,4,8,128]{4,3,2,1,0:T(8,128)S(1)}, f32[4,2,4,8,128]{4,3,2,1,0:T(8,128)S(1)}, f32[12,2,2,24,128]{4,3,2,1,0:T(8,128)S(1)}, f32[6,2,4,8,128]{...) custom-call(s32[2]{0:T(128)S(1)} %pad_add_fusion.refs_0_, ...), custom_call_target="tpu_custom_call" | custom-call | tf_op jit(solution)/shard_map/up_first/pallas_call | solution.py:521
  116.2 6.1 %collective-permute-start.12 = (f32[6,2,4,8,128]{4,3,2,1,0:T(8,128)S(1)}, f32[6,2,4,8,128]{4,3,2,1,0:T(8,128)S(1)}, u32[]{:S(2)}, u32[]{:S(2)}) collective-permute-start(f32[6,2,4,8,128]{4,3,2,1,0:T(8,128)S(1)} %get-tuple-element.33), channel_id=1, source_target_pairs={{0,8},{8,16},{16,24},{24,32},{32,40},{40,48},{48,56},{56,64},{64,7... | collective-permute-start | bytes 589832 | tf_op jit(solution)/shard_map/ppermute | solution.py:595
  122.3 3.2 %collective-permute-start.13 = (f32[6,2,4,8,128]{4,3,2,1,0:T(8,128)S(1)}, f32[6,2,4,8,128]{4,3,2,1,0:T(8,128)S(1)}, u32[]{:S(2)}, u32[]{:S(2)}) collective-permute-start(f32[6,2,4,8,128]{4,3,2,1,0:T(8,128)S(1)} %get-tuple-element.35), channel_id=1, source_target_pairs={{8,0},{16,8},{24,16},{32,24},{40,32},{48,40},{56,48},{64,56},{72,6... | collective-permute-start | bytes 589832 | tf_op jit(solution)/shard_map/ppermute | solution.py:595
  125.5 1.7 collective-permute-done.12.before
  127.2 2.6 %collective-permute-done.13.after = f32[6,2,4,8,128]{4,3,2,1,0:T(8,128)S(1)} collective-permute-done((f32[6,2,4,8,128]{4,3,2,1,0:T(8,128)S(1)}, f32[6,2,4,8,128]{4,3,2,1,0:T(8,128)S(1)}, u32[]{:S(2)}, u32[]{:S(2)}) %collective-permute-start.13) | collective-permute-done | bytes 196640 | tf_op jit(solution)/shard_map/ppermute | solution.py:595
  129.9 1.9 collective-permute-start.15
  131.9 2.4 %collective-permute-start.14 = (f32[14,2,4,8,128]{4,3,2,1,0:T(8,128)S(1)}, f32[14,2,4,8,128]{4,3,2,1,0:T(8,128)S(1)}, u32[]{:S(2)}, u32[]{:S(2)}) collective-permute-start(f32[14,2,4,8,128]{4,3,2,1,0:T(8,128)S(1)} %pad_maximum_fusion.mid), channel_id=1, source_target_pairs={{0,1},{1,2},{2,3},{3,4},{4,5},{5,6},{6,7},{8,9},{9,10},{10,11},{11... | collective-permute-start | bytes 1376264 | tf_op jit(solution)/shard_map/ppermute | solution.py:595
  134.3 3.5 %collective-permute-done.15.high = f32[14,2,4,8,128]{4,3,2,1,0:T(8,128)S(1)} collective-permute-done((f32[14,2,4,8,128]{4,3,2,1,0:T(8,128)S(1)}, f32[14,2,4,8,128]{4,3,2,1,0:T(8,128)S(1)}, u32[]{:S(2)}, u32[]{:S(2)}) %collective-permute-start.15) | collective-permute-done | bytes 458784 | tf_op jit(solution)/shard_map/ppermute | solution.py:595
  137.8 3.8 %collective-permute-done.14.low = f32[14,2,4,8,128]{4,3,2,1,0:T(8,128)S(1)} collective-permute-done((f32[14,2,4,8,128]{4,3,2,1,0:T(8,128)S(1)}, f32[14,2,4,8,128]{4,3,2,1,0:T(8,128)S(1)}, u32[]{:S(2)}, u32[]{:S(2)}) %collective-permute-start.14) | collective-permute-done | bytes 458784 | tf_op jit(solution)/shard_map/ppermute | solution.py:595
  141.7 3.2 %down_second.1 = (f32[16,2,4,24,128]{4,3,2,1,0:T(8,128)S(1)}, f32[16,2,4,40,128]{4,3,2,1,0:T(8,128)S(1)}, f32[4,4,8,128]{3,2,1,0:T(8,128)S(1)}, f32[1,384]{1,0:T(1,128)S(1)}) custom-call(f32[6,2,4,8,128]{4,3,2,1,0:T(8,128)S(1)} %collective-permute-done.12.before, f32[14,2,4,8,128]{4,3,2,1,0:T(8,128)S(1)} %pad_maximum_fusion.mid, ...), custom_call_target="tpu_custom_call" | custom-call | tf_op jit(solution)/shard_map/down_second/pallas_call | solution.py:371
  144.9 1.5 copy-done
  146.4 1.2 copy-done.6
  148.6 15.0 %all-to-all-start.1 = ((f32[256,1,384]{2,1,0:T(1,128)}), f32[256,1,384]{2,1,0:T(1,128)}, u32[]{:S(2)}, u32[]{:S(2)}) async-start(f32[256,1,384]{2,1,0:T(1,128)} %broadcast_in_dim.16), calls=%async_computation.1 | async-start | bytes 786432 | tf_op jit(solution)/shard_map/all_to_all | solution.py:602
  163.6 2.5 %collective-permute-start.17 = (f32[4,4,8,128]{3,2,1,0:T(8,128)S(1)}, f32[4,4,8,128]{3,2,1,0:T(8,128)S(1)}, u32[]{:S(2)}, u32[]{:S(2)}) collective-permute-start(f32[4,4,8,128]{3,2,1,0:T(8,128)S(1)} %get-tuple-element.40), channel_id=1, source_target_pairs={{1,0},{2,1},{3,2},{4,3},{5,4},{6,5},{7,6},{9,8},{10,9},{11,10},{12... | collective-permute-start | bytes 196616 | tf_op jit(solution)/shard_map/ppermute | solution.py:595
  166.1 1.9 collective-permute-start.16
  168.4 3.5 %collective-permute-done.16 = f32[4,4,8,128]{3,2,1,0:T(8,128)S(1)} collective-permute-done((f32[4,4,8,128]{3,2,1,0:T(8,128)S(1)}, f32[4,4,8,128]{3,2,1,0:T(8,128)S(1)}, u32[]{:S(2)}, u32[]{:S(2)}) %collective-permute-start.16) | collective-permute-done | bytes 65568 | tf_op jit(solution)/shard_map/ppermute | solution.py:595
  172.6 4.7 %collective-permute-start.19 = (f32[3,3,4,8,128]{4,3,2,1,0:T(8,128)}, f32[3,3,4,8,128]{4,3,2,1,0:T(8,128)S(1)}, u32[]{:S(2)}, u32[]{:S(2)}) collective-permute-start(f32[3,3,4,8,128]{4,3,2,1,0:T(8,128)} %get-tuple-element.51), channel_id=1, source_target_pairs={{8,0},{16,8},{24,16},{32,24},{40,32},{48,40},{56,48},{64,56},{72,6... | collective-permute-start | bytes 442376 | tf_op jit(solution)/shard_map/ppermute | solution.py:595
  177.3 1.9 collective-permute-start.18
  180.3 7.6 %collective-permute-done.18.refs_3_ = f32[3,3,4,8,128]{4,3,2,1,0:T(8,128)S(1)} collective-permute-done((f32[3,3,4,8,128]{4,3,2,1,0:T(8,128)}, f32[3,3,4,8,128]{4,3,2,1,0:T(8,128)S(1)}, u32[]{:S(2)}, u32[]{:S(2)}) %collective-permute-start.18) | collective-permute-done | bytes 147488 | tf_op jit(solution)/shard_map/ppermute | solution.py:595
  187.8 1.7 copy-done.1
  192.6 9.4 %up_second.1 = f32[2,4,8,384]{3,2,1,0:T(8,128)} custom-call(s32[2]{0:T(128)S(1)} %pad_add_fusion.refs_0_, f32[32,8,384]{2,1,0:T(8,128)S(1)} %bitcast.15, f32[32,4,8,128]{3,2,1,0:T(8,128)S(1)} %copy-done.11, f32[3,3,4,8,128]{4,3,2,1,0:T(8,128)S(1)} %collective-permute-done.18.refs_3_, f32[3,3,4,8,128]{4,3,2,1,0:T(8,128)S(1)} %collective-permute-done.19.refs_4_, ...), custom_call_target="tpu_custom_call" | custom-call | tf_op jit(solution)/shard_map/up_second/pallas_call | solution.py:581
  (68 shorter events, 13.8 us)
Async XLA Ops:
  0.0 0.9 copy-start.18
  0.9 0.8 copy-start.19
  1.7 0.8 copy-start.20
  2.5 0.7 copy-start.21
  4.3 16.2 %collective-permute-start = (f32[2,4,4,8,128]{4,3,2,1,0:T(8,128)S(1)}, f32[2,4,4,8,128]{4,3,2,1,0:T(8,128)S(1)}, u32[]{:S(2)}, u32[]{:S(2)}) collective-permute-start(f32[2,4,4,8,128]{4,3,2,1,0:T(8,128)S(1)} %get-tuple-element.50), channel_id=1, source_target_pairs={{0,16},{8,24},{16,32},{24,40},{32,48},{40,56},{48,64},{56,72},{64,... | collective-permute-start | bytes 393224 | tf_op jit(solution)/shard_map/ppermute | solution.py:595
  9.4 13.0 %collective-permute-start.1 = (f32[4,4,4,8,128]{4,3,2,1,0:T(8,128)S(1)}, f32[4,4,4,8,128]{4,3,2,1,0:T(8,128)S(1)}, u32[]{:S(2)}, u32[]{:S(2)}) collective-permute-start(f32[4,4,4,8,128]{4,3,2,1,0:T(8,128)S(1)} %get-tuple-element.25), channel_id=1, source_target_pairs={{0,8},{8,16},{16,24},{24,32},{32,40},{40,48},{48,56},{56,64},{64,7... | collective-permute-start | bytes 786440 | tf_op jit(solution)/shard_map/ppermute | solution.py:595
  12.0 13.0 %collective-permute-start.2 = (f32[4,4,4,8,128]{4,3,2,1,0:T(8,128)S(1)}, f32[4,4,4,8,128]{4,3,2,1,0:T(8,128)S(1)}, u32[]{:S(2)}, u32[]{:S(2)}) collective-permute-start(f32[4,4,4,8,128]{4,3,2,1,0:T(8,128)S(1)} %get-tuple-element.25), channel_id=1, source_target_pairs={{8,0},{16,8},{24,16},{32,24},{40,32},{48,40},{56,48},{64,56},{72,6... | collective-permute-start | bytes 786440 | tf_op jit(solution)/shard_map/ppermute | solution.py:595
  18.6 8.4 %collective-permute-start.3 = (f32[2,4,4,8,128]{4,3,2,1,0:T(8,128)S(1)}, f32[2,4,4,8,128]{4,3,2,1,0:T(8,128)S(1)}, u32[]{:S(2)}, u32[]{:S(2)}) collective-permute-start(f32[2,4,4,8,128]{4,3,2,1,0:T(8,128)S(1)} %get-tuple-element.49), channel_id=1, source_target_pairs={{16,0},{24,8},{32,16},{40,24},{48,32},{56,40},{64,48},{72,56},{80,... | collective-permute-start | bytes 393224 | tf_op jit(solution)/shard_map/ppermute | solution.py:595
  27.0 12.8 %collective-permute-start.5 = (f32[14,4,4,8,128]{4,3,2,1,0:T(8,128)S(1)}, f32[14,4,4,8,128]{4,3,2,1,0:T(8,128)S(1)}, u32[]{:S(2)}, u32[]{:S(2)}) collective-permute-start(f32[14,4,4,8,128]{4,3,2,1,0:T(8,128)S(1)} %slice_dynamic-update-slice_fusion.mid), channel_id=1, source_target_pairs={{1,0},{2,1},{3,2},{4,3},{5,4},{6,5},{7,6},{9,8},{10,9},{11,10},{12... | collective-permute-start | bytes 2752520 | tf_op jit(solution)/shard_map/ppermute | solution.py:595
  28.9 14.7 %collective-permute-start.4 = (f32[14,4,4,8,128]{4,3,2,1,0:T(8,128)S(1)}, f32[14,4,4,8,128]{4,3,2,1,0:T(8,128)S(1)}, u32[]{:S(2)}, u32[]{:S(2)}) collective-permute-start(f32[14,4,4,8,128]{4,3,2,1,0:T(8,128)S(1)} %slice_dynamic-update-slice_fusion.mid), channel_id=1, source_target_pairs={{0,1},{1,2},{2,3},{3,4},{4,5},{5,6},{6,7},{8,9},{9,10},{10,11},{11... | collective-permute-start | bytes 2752520 | tf_op jit(solution)/shard_map/ppermute | solution.py:595
  47.6 1.5 copy-start.2
  49.1 1.2 copy-start.4
  50.3 0.7 copy-start.12
  51.0 0.7 copy-start.14
  52.8 39.5 %all-to-all-start = ((f32[256,2,384]{2,1,0:T(2,128)}), f32[256,2,384]{2,1,0:T(2,128)}, u32[]{:S(2)}, u32[]{:S(2)}) async-start(f32[256,2,384]{2,1,0:T(2,128)} %broadcast_in_dim.6), calls=%async_computation | async-start | bytes 1572864 | tf_op jit(solution)/shard_map/all_to_all | solution.py:602
  68.2 5.4 %collective-permute-start.7 = (f32[4,6,8,128]{3,2,1,0:T(8,128)S(1)}, f32[4,6,8,128]{3,2,1,0:T(8,128)S(1)}, u32[]{:S(2)}, u32[]{:S(2)}) collective-permute-start(f32[4,6,8,128]{3,2,1,0:T(8,128)S(1)} %get-tuple-element.28), channel_id=1, source_target_pairs={{1,0},{2,1},{3,2},{4,3},{5,4},{6,5},{7,6},{9,8},{10,9},{11,10},{12... | collective-permute-start | bytes 294920 | tf_op jit(solution)/shard_map/ppermute | solution.py:595
  70.7 6.7 %collective-permute-start.6 = (f32[4,6,8,128]{3,2,1,0:T(8,128)S(1)}, f32[4,6,8,128]{3,2,1,0:T(8,128)S(1)}, u32[]{:S(2)}, u32[]{:S(2)}) collective-permute-start(f32[4,6,8,128]{3,2,1,0:T(8,128)S(1)} %get-tuple-element.28), channel_id=1, source_target_pairs={{0,1},{1,2},{2,3},{3,4},{4,5},{5,6},{6,7},{8,9},{9,10},{10,11},{11... | collective-permute-start | bytes 294920 | tf_op jit(solution)/shard_map/ppermute | solution.py:595
  77.4 17.2 %collective-permute-start.9 = (f32[2,3,6,8,128]{4,3,2,1,0:T(8,128)S(1)}, f32[2,3,6,8,128]{4,3,2,1,0:T(8,128)}, u32[]{:S(2)}, u32[]{:S(2)}) collective-permute-start(f32[2,3,6,8,128]{4,3,2,1,0:T(8,128)S(1)} %slice.62.refs_7_), channel_id=1, source_target_pairs={{8,0},{16,8},{24,16},{32,24},{40,32},{48,40},{56,48},{64,56},{72,6... | collective-permute-start | bytes 442376 | tf_op jit(solution)/shard_map/ppermute | solution.py:595
  82.3 12.4 %collective-permute-start.8 = (f32[2,3,6,8,128]{4,3,2,1,0:T(8,128)S(1)}, f32[2,3,6,8,128]{4,3,2,1,0:T(8,128)}, u32[]{:S(2)}, u32[]{:S(2)}) collective-permute-start(f32[2,3,6,8,128]{4,3,2,1,0:T(8,128)S(1)} %slice.62.refs_7_), channel_id=1, source_target_pairs={{0,8},{8,16},{16,24},{24,32},{32,40},{40,48},{48,56},{56,64},{64,7... | collective-permute-start | bytes 442376 | tf_op jit(solution)/shard_map/ppermute | solution.py:595
  85.0 12.4 %collective-permute-start.11 = (f32[3,3,6,8,128]{4,3,2,1,0:T(8,128)}, f32[3,3,6,8,128]{4,3,2,1,0:T(8,128)S(1)}, u32[]{:S(2)}, u32[]{:S(2)}) collective-permute-start(f32[3,3,6,8,128]{4,3,2,1,0:T(8,128)} %get-tuple-element.47), channel_id=1, source_target_pairs={{16,0},{24,8},{32,16},{40,24},{48,32},{56,40},{64,48},{72,56},{80,... | collective-permute-start | bytes 663560 | tf_op jit(solution)/shard_map/ppermute | solution.py:595
  89.0 11.8 %collective-permute-start.10 = (f32[3,3,6,8,128]{4,3,2,1,0:T(8,128)}, f32[3,3,6,8,128]{4,3,2,1,0:T(8,128)}, u32[]{:S(2)}, u32[]{:S(2)}) collective-permute-start(f32[3,3,6,8,128]{4,3,2,1,0:T(8,128)} %get-tuple-element.48), channel_id=1, source_target_pairs={{0,16},{8,24},{16,32},{24,40},{32,48},{40,56},{48,64},{56,72},{64,... | collective-permute-start | bytes 663560 | tf_op jit(solution)/shard_map/ppermute | solution.py:595
  92.4 8.4 %copy-start.3 = (f32[16,2,4,40,128]{4,3,2,1,0:T(8,128)S(1)}, f32[16,2,4,40,128]{4,3,2,1,0:T(8,128)}, u32[]{:S(2)}) copy-start(f32[16,2,4,40,128]{4,3,2,1,0:T(8,128)} %copy-done.2) | copy-start | bytes 7864324
  100.8 1.4 copy-start.5
  116.2 25.5 %copy-start.8 = (f32[12,2,2,24,128]{4,3,2,1,0:T(8,128)}, f32[12,2,2,24,128]{4,3,2,1,0:T(8,128)S(1)}, u32[]{:S(2)}) copy-start(f32[12,2,2,24,128]{4,3,2,1,0:T(8,128)S(1)} %get-tuple-element.43.refs_9_) | copy-start | bytes 1769476
  116.2 25.5 %copy-start.10 = (f32[32,4,8,128]{3,2,1,0:T(8,128)}, f32[32,4,8,128]{3,2,1,0:T(8,128)S(1)}, u32[]{:S(2)}) copy-start(f32[32,4,8,128]{3,2,1,0:T(8,128)S(1)} %get-tuple-element.39.refs_2_) | copy-start | bytes 1572868
  116.2 25.5 %copy-start.16 = (f32[4,2,4,8,128]{4,3,2,1,0:T(8,128)}, f32[4,2,4,8,128]{4,3,2,1,0:T(8,128)S(1)}, u32[]{:S(2)}) copy-start(f32[4,2,4,8,128]{4,3,2,1,0:T(8,128)S(1)} %get-tuple-element.44.refs_10_) | copy-start | bytes 393220
  116.2 25.5 %copy-start.13 = (f32[6,2,2,24,128]{4,3,2,1,0:T(8,128)S(1)}, f32[6,2,2,24,128]{4,3,2,1,0:T(8,128)}, u32[]{:S(2)}) copy-start(f32[6,2,2,24,128]{4,3,2,1,0:T(8,128)} %copy-done.12) | copy-start | bytes 884740
  116.2 25.5 %copy-start.15 = (f32[6,2,2,24,128]{4,3,2,1,0:T(8,128)S(1)}, f32[6,2,2,24,128]{4,3,2,1,0:T(8,128)}, u32[]{:S(2)}) copy-start(f32[6,2,2,24,128]{4,3,2,1,0:T(8,128)} %copy-done.14) | copy-start | bytes 884740
  116.2 11.0 %collective-permute-start.12 = (f32[6,2,4,8,128]{4,3,2,1,0:T(8,128)S(1)}, f32[6,2,4,8,128]{4,3,2,1,0:T(8,128)S(1)}, u32[]{:S(2)}, u32[]{:S(2)}) collective-permute-start(f32[6,2,4,8,128]{4,3,2,1,0:T(8,128)S(1)} %get-tuple-element.33), channel_id=1, source_target_pairs={{0,8},{8,16},{16,24},{24,32},{32,40},{40,48},{48,56},{56,64},{64,7... | collective-permute-start | bytes 589832 | tf_op jit(solution)/shard_map/ppermute | solution.py:595
  122.3 7.6 %collective-permute-start.13 = (f32[6,2,4,8,128]{4,3,2,1,0:T(8,128)S(1)}, f32[6,2,4,8,128]{4,3,2,1,0:T(8,128)S(1)}, u32[]{:S(2)}, u32[]{:S(2)}) collective-permute-start(f32[6,2,4,8,128]{4,3,2,1,0:T(8,128)S(1)} %get-tuple-element.35), channel_id=1, source_target_pairs={{8,0},{16,8},{24,16},{32,24},{40,32},{48,40},{56,48},{64,56},{72,6... | collective-permute-start | bytes 589832 | tf_op jit(solution)/shard_map/ppermute | solution.py:595
  129.9 7.9 %collective-permute-start.15 = (f32[14,2,4,8,128]{4,3,2,1,0:T(8,128)S(1)}, f32[14,2,4,8,128]{4,3,2,1,0:T(8,128)S(1)}, u32[]{:S(2)}, u32[]{:S(2)}) collective-permute-start(f32[14,2,4,8,128]{4,3,2,1,0:T(8,128)S(1)} %pad_maximum_fusion.mid), channel_id=1, source_target_pairs={{1,0},{2,1},{3,2},{4,3},{5,4},{6,5},{7,6},{9,8},{10,9},{11,10},{12... | collective-permute-start | bytes 1376264 | tf_op jit(solution)/shard_map/ppermute | solution.py:595
  131.9 9.8 %collective-permute-start.14 = (f32[14,2,4,8,128]{4,3,2,1,0:T(8,128)S(1)}, f32[14,2,4,8,128]{4,3,2,1,0:T(8,128)S(1)}, u32[]{:S(2)}, u32[]{:S(2)}) collective-permute-start(f32[14,2,4,8,128]{4,3,2,1,0:T(8,128)S(1)} %pad_maximum_fusion.mid), channel_id=1, source_target_pairs={{0,1},{1,2},{2,3},{3,4},{4,5},{5,6},{6,7},{8,9},{9,10},{10,11},{11... | collective-permute-start | bytes 1376264 | tf_op jit(solution)/shard_map/ppermute | solution.py:595
  144.9 1.5 copy-start
  146.4 1.2 copy-start.6
  147.7 40.2 %copy-start.7 = (f32[16,2,4,24,128]{4,3,2,1,0:T(8,128)S(1)}, f32[16,2,4,24,128]{4,3,2,1,0:T(8,128)}, u32[]{:S(2)}) copy-start(f32[16,2,4,24,128]{4,3,2,1,0:T(8,128)} %copy-done.6) | copy-start | bytes 4718596
  148.6 30.6 %all-to-all-start.1 = ((f32[256,1,384]{2,1,0:T(1,128)}), f32[256,1,384]{2,1,0:T(1,128)}, u32[]{:S(2)}, u32[]{:S(2)}) async-start(f32[256,1,384]{2,1,0:T(1,128)} %broadcast_in_dim.16), calls=%async_computation.1 | async-start | bytes 786432 | tf_op jit(solution)/shard_map/all_to_all | solution.py:602
  163.6 4.7 %collective-permute-start.17 = (f32[4,4,8,128]{3,2,1,0:T(8,128)S(1)}, f32[4,4,8,128]{3,2,1,0:T(8,128)S(1)}, u32[]{:S(2)}, u32[]{:S(2)}) collective-permute-start(f32[4,4,8,128]{3,2,1,0:T(8,128)S(1)} %get-tuple-element.40), channel_id=1, source_target_pairs={{1,0},{2,1},{3,2},{4,3},{5,4},{6,5},{7,6},{9,8},{10,9},{11,10},{12... | collective-permute-start | bytes 196616 | tf_op jit(solution)/shard_map/ppermute | solution.py:595
  166.1 5.7 %collective-permute-start.16 = (f32[4,4,8,128]{3,2,1,0:T(8,128)S(1)}, f32[4,4,8,128]{3,2,1,0:T(8,128)S(1)}, u32[]{:S(2)}, u32[]{:S(2)}) collective-permute-start(f32[4,4,8,128]{3,2,1,0:T(8,128)S(1)} %get-tuple-element.40), channel_id=1, source_target_pairs={{0,1},{1,2},{2,3},{3,4},{4,5},{5,6},{6,7},{8,9},{9,10},{10,11},{11... | collective-permute-start | bytes 196616 | tf_op jit(solution)/shard_map/ppermute | solution.py:595
  172.6 7.7 %collective-permute-start.19 = (f32[3,3,4,8,128]{4,3,2,1,0:T(8,128)}, f32[3,3,4,8,128]{4,3,2,1,0:T(8,128)S(1)}, u32[]{:S(2)}, u32[]{:S(2)}) collective-permute-start(f32[3,3,4,8,128]{4,3,2,1,0:T(8,128)} %get-tuple-element.51), channel_id=1, source_target_pairs={{8,0},{16,8},{24,16},{32,24},{40,32},{48,40},{56,48},{64,56},{72,6... | collective-permute-start | bytes 442376 | tf_op jit(solution)/shard_map/ppermute | solution.py:595
  177.3 10.6 %collective-permute-start.18 = (f32[3,3,4,8,128]{4,3,2,1,0:T(8,128)}, f32[3,3,4,8,128]{4,3,2,1,0:T(8,128)S(1)}, u32[]{:S(2)}, u32[]{:S(2)}) collective-permute-start(f32[3,3,4,8,128]{4,3,2,1,0:T(8,128)} %get-tuple-element.52), channel_id=1, source_target_pairs={{0,8},{8,16},{16,24},{24,32},{32,40},{40,48},{48,56},{56,64},{64,7... | collective-permute-start | bytes 442376 | tf_op jit(solution)/shard_map/ppermute | solution.py:595
  187.8 1.7 copy-start.1
  189.6 1.1 copy-start.9
  190.6 1.0 copy-start.11
  191.7 0.9 copy-start.17

commit v3 on v0

v3 whole, which is shorter than its diff:
```python
import math
from types import SimpleNamespace

import jax
import jax.numpy as jnp
from jax import lax
from jax.experimental import pallas as pl
from jax.experimental.pallas import tpu as pltpu
from jax.sharding import PartitionSpec as P


NC = 8
WINDOW = 21
OMEGA = 0.6
BETA = 0.5
ABSORB = 0.25
KH_FACTOR = 2.0 * math.pi * 6.0 * 20.0

F32 = jnp.float32
BF16 = jnp.bfloat16
VM = pltpu.VMEM
SM = pltpu.SMEM
HB = pltpu.HBM
PARAMS = pltpu.CompilerParams(vmem_limit_bytes=32 * 1024 * 1024)


def run(name, kernel, inputs, outputs, scratch, copies):
    names = list(inputs) + list(outputs) + list(scratch) + ["sem"]
    result = pl.pallas_call(
        lambda *refs: kernel(SimpleNamespace(**dict(zip(names, refs)))),
        name=name,
        out_shape=tuple(jax.ShapeDtypeStruct(dims, F32) for dims, _ in outputs.values()),
        in_specs=[pl.BlockSpec(memory_space=space) for _, space in inputs.values()],
        out_specs=tuple(pl.BlockSpec(memory_space=space) for _, space in outputs.values()),
        scratch_shapes=[pltpu.VMEM(dims, F32) if isinstance(dims, tuple) else dims for dims in scratch.values()]
        + [pltpu.SemaphoreType.DMA((copies,))],
        compiler_params=PARAMS,
    )(*[array for array, _ in inputs.values()])
    return SimpleNamespace(**dict(zip(outputs, result)))


def sort_matrix(rows, columns, flip):
    first = lax.broadcasted_iota(jnp.int32, (rows, columns), 0)
    second = lax.broadcasted_iota(jnp.int32, (rows, columns), 1)
    if flip:
        first, second = second, first
    lane = second % 128
    hit = (first == 4 * lane + second // 128) & (lane < 96)
    return jnp.where(hit, 1.0, 0.0).astype(BF16)


def exact_dot(values, matrix):
    high = values.astype(BF16)
    rest = values - high.astype(F32)
    middle = rest.astype(BF16)
    low = (rest - middle.astype(F32)).astype(BF16)
    dot = lambda part: jnp.dot(part, matrix, preferred_element_type=F32)
    return (dot(low) + dot(middle)) + dot(high)


def scaled_inverse(real, imag, scale):
    diag_real = 6.0 * scale - real
    diag_imag = -imag
    factor = OMEGA / (diag_real * diag_real + diag_imag * diag_imag)
    factor = jnp.where(real > 0.0, factor, 0.0)
    return diag_real * factor, -diag_imag * factor


def product(a, b):
    return a[0] * b[0] - a[1] * b[1], a[0] * b[1] + a[1] * b[0]


def pair_rows(value, temp):
    temp[8:32, :] = value
    row = lax.broadcasted_iota(jnp.int32, (24, 128), 0)
    return value + jnp.where(row % 2 == 0, temp[9:33, :], temp[7:31, :])


def neighbour(ref, x, c, r, count, step):
    center = lambda s: ref[x, c, s, 8:32, :]
    up = center(r + 1) if r < count - 1 else pltpu.roll(center(0), 127, 1)
    down = center(r - 1) if r > 0 else pltpu.roll(center(count - 1), 1, 1)
    total = ref[x - 1, c, r, 8:32, :] + ref[x + 1, c, r, 8:32, :]
    total = total + ref[x, c, r, 8 - step : 32 - step, :] + ref[x, c, r, 8 + step : 32 + step, :]
    return total + (up + down)


def sweep(old, new, weight, weight_at, source, source_at, low, high, count, step, scale):
    def body(x, _):
        for r in range(count):
            parts = []
            for c in range(2):
                total = neighbour(old, x, c, r, count, step)
                if scale != 1.0:
                    total = total * scale
                parts.append(source[x + source_at, c, r] + total)
            w = [weight[x + weight_at, c, r] for c in range(2)]
            moved = product(w, parts)
            for c in range(2):
                new[x, c, r, 8:32, :] = (1.0 - OMEGA) * old[x, c, r, 8:32, :] + moved[c]
        return 0

    lax.fori_loop(low, high, body, 0)


def clear(ref, count):
    def body(x, _):
        ref[x] = jnp.zeros(ref.shape[1:], F32)
        return 0

    lax.fori_loop(0, count, body, 0)


def clear_edges(ref, count):
    zero = jnp.zeros((8, 128), F32)

    def body(x, _):
        for c in range(2):
            for r in range(ref.shape[2]):
                ref[x, c, r, 0:8, :] = zero
                ref[x, c, r, 32:40, :] = zero
        return 0

    lax.fori_loop(0, count, body, 0)


def dense(target, at, pieces):
    lane = lax.broadcasted_iota(jnp.int32, (1, 128), 1)
    for n in range(3):
        tail = pltpu.roll(pieces[n + 1], 128 - 32 * (n + 1), 1)
        head = pieces[n] if n == 0 else pltpu.roll(pieces[n], 128 - 32 * n, 1)
        target[0:1, at + n * 128 : at + n * 128 + 128] = jnp.where(lane < 96 - 32 * n, head, tail)


def loose(block):
    lane = lax.broadcasted_iota(jnp.int32, (block.shape[0], 128), 1)
    parts = [block[:, n * 128 : n * 128 + 128] for n in range(3)]
    result = []
    for k in range(4):
        if k == 0:
            value = parts[0]
        elif k == 3:
            value = pltpu.roll(parts[2], 96, 1)
        else:
            value = jnp.where(lane < 32 * k, pltpu.roll(parts[k - 1], 32 * k, 1), pltpu.roll(parts[k], 32 * k, 1))
        result.append(jnp.where(lane < 96, value, 0.0))
    return result


def pack_kernel(v):
    loads = [
        pltpu.make_async_copy(v.right_side, v.field, v.sem.at[0]),
        pltpu.make_async_copy(v.layer_index, v.layers, v.sem.at[1]),
        pltpu.make_async_copy(v.absorb_level, v.levels, v.sem.at[2]),
    ]
    for load in loads:
        load.start()
    matrix = sort_matrix(384, 512, False)
    for load in loads:
        load.wait()
    field = exact_dot(v.field[...].reshape(64, 384), matrix)
    both = jnp.concatenate([v.layers[...].reshape(32, 384), v.levels[...].reshape(32, 384)], axis=0)
    codes = jnp.dot(both.astype(F32).astype(BF16), matrix, preferred_element_type=F32)
    inside = lax.broadcasted_iota(jnp.int32, (32, 128), 1) < 96
    total = [jnp.zeros((32, 128), F32), jnp.zeros((32, 128), F32)]
    for r in range(4):
        lanes = slice(r * 128, r * 128 + 128)
        layer = codes[0:32, lanes]
        velocity = jnp.full((32, 128), v.table[0], F32)
        for n in range(1, v.table.shape[0]):
            velocity = jnp.where(layer == float(n), v.table[n], velocity)
        ratio = KH_FACTOR / velocity
        real = jnp.where(inside, ratio * ratio, 0.0)
        imag = -real * (BETA + ABSORB * codes[32:64, lanes])
        total = [total[0] + real, total[1] + imag]
        for x in range(4):
            rows = slice(x * 8, x * 8 + 8)
            values = (field[x * 8 : x * 8 + 8, lanes], field[32 + x * 8 : 40 + x * 8, lanes], real[rows], imag[rows])
            for c in range(4):
                v.packed[x, c, r] = values[c]
                if x < 2:
                    v.front[x, c, r] = values[c]
                else:
                    v.back[x - 2, c, r] = values[c]
    means = []
    for c in range(2):
        t = total[c]
        v.temp[c] = (t[0:8] + t[8:16]) + (t[16:24] + t[24:32])
        row = [v.temp[c, n : n + 1] for n in range(8)]
        means.append([((row[4 * k] + row[4 * k + 1]) + (row[4 * k + 2] + row[4 * k + 3])) * (1.0 / 64.0) for k in range(2)])
    w = [scaled_inverse(means[0][k], means[1][k], 0.0625) for k in range(2)]
    dense(v.inverse_two, 0, [w[k][c] for c in range(2) for k in range(2)])


def pack(table, right_side, layer_index, absorb_level):
    return run(
        "pack",
        pack_kernel,
        dict(table=(table, SM), right_side=(right_side, HB), layer_index=(layer_index, HB), absorb_level=(absorb_level, HB)),
        dict(packed=((4, 4, 4, 8, 128), VM), front=((2, 4, 4, 8, 128), VM), back=((2, 4, 4, 8, 128), VM),
             inverse_two=((1, 384), VM)),
        dict(field=right_side.shape, layers=pltpu.VMEM(layer_index.shape, jnp.int32),
             levels=pltpu.VMEM(absorb_level.shape, jnp.int32), temp=(2, 8, 128)),
        3,
    )


FINE = (16, 2, 4, 24, 128)
WIDE = (16, 2, 4, 40, 128)
COARSE = (6, 2, 2, 24, 128)
COARSE_WIDE = (6, 2, 2, 40, 128)


def keep(v, number, source, target):
    copy = pltpu.make_async_copy(source, target, v.sem.at[number])
    copy.start()
    return copy


def squeeze_rows(target, n, source, k, c, tile, top):
    for s in range(2):
        target[n, s * 4 : s * 4 + 4, :] = source[k, c, s, pl.ds(top + 8 * tile, 4, 2), :]


def down_body(v, source, weight, diag, weight_one, diag_one, first_copy, sends_weight):
    def first(x, _):
        for r in range(4):
            e = product([weight[x, c, r] for c in range(2)], [source[x, c, r] for c in range(2)])
            for c in range(2):
                v.start[x, c, r, 8:32, :] = e[c]
        return 0

    lax.fori_loop(0, 16, first, 0)
    sweep(v.start, v.guess, weight, 0, source, 0, 1, 15, 4, 1, 1.0)
    copies = [keep(v, first_copy, v.guess, v.out_guess)]

    def residual(k, _):
        for s in range(2):
            sums = [None, None]
            for half in range(2):
                x = 2 + 2 * k + half
                for r in (2 * s, 2 * s + 1):
                    e = [v.guess[x, c, r, 8:32, :] for c in range(2)]
                    moved = product([diag[x, c, r] for c in range(2)], e)
                    for c in range(2):
                        value = source[x, c, r] + neighbour(v.guess, x, c, r, 4, 1) - moved[c]
                        sums[c] = value if sums[c] is None else sums[c] + value
            g = [pair_rows(sums[c], v.temp.at[c]) * 0.125 for c in range(2)]
            e = product([weight_one[k, c, s] for c in range(2)], g)
            for c in range(2):
                v.source_one[k, c, s] = g[c]
                v.start_one[k, c, s, 8:32, :] = e[c]
        return 0

    lax.fori_loop(0, 6, residual, 0)
    copies.append(keep(v, first_copy + 1, v.source_one, v.out_source_one))
    sweep(v.start_one, v.guess_one, weight_one, 0, v.source_one, 0, 1, 5, 2, 2, 0.25)
    copies.append(keep(v, first_copy + 2, v.guess_one, v.out_guess_one))

    total = [None, None]
    for k in (2, 3):
        for s in range(2):
            e = [v.guess_one[k, c, s, 8:32, :] for c in range(2)]
            moved = product([diag_one[k, c, s] for c in range(2)], e)
            for c in range(2):
                value = v.source_one[k, c, s] + 0.25 * neighbour(v.guess_one, k, c, s, 2, 2) - moved[c]
                total[c] = value if total[c] is None else total[c] + value
    pieces = []
    for c in range(2):
        v.temp[c, 8:32, :] = total[c]
        for k in range(2):
            row = 16 + 4 * k
            pieces.append((v.temp[c, row : row + 1, :] + v.temp[c, row + 2 : row + 3, :]) * 0.125)
    dense(v.two, 0, pieces)

    for c in range(2):
        for k in range(4):
            squeeze_rows(v.send_y, k * 2 + c, v.guess_one, k + 1, c, 1, 8)
        for tile in range(3):
            for k in range(2):
                n = (k * 3 + tile) * 2 + c
                squeeze_rows(v.send_up, n, v.guess_one, k + 1, c, tile, 8)
                squeeze_rows(v.send_down, n, v.guess_one, k + 3, c, tile, 8)
        if sends_weight:
            for target, k in ((v.send_up, 1), (v.send_down, 4)):
                squeeze_rows(target, 12 + c, v.source_one, k, c, 1, 0)
                squeeze_rows(target, 14 + c, weight_one, k, c, 1, 0)
            squeeze_rows(v.send_far_up, c, v.guess_one, 2, c, 1, 8)
            squeeze_rows(v.send_far_down, c, v.guess_one, 3, c, 1, 8)
    return copies


def fill(v, target, at, count, x):
    for r in range(4):
        for c in range(count):
            target[x, c, r, 0:8, :] = v.low[x, at + c, r]
            target[x, c, r, 8:16, :] = v.mid[x, at + c, r]
            target[x, c, r, 16:24, :] = v.high[x, at + c, r]


def clear_down(v):
    clear_edges(v.start, 16)
    clear_edges(v.guess, 16)
    clear_edges(v.start_one, 6)
    clear_edges(v.guess_one, 6)


def down_first_kernel(v):
    clear_down(v)

    def filled(x, _):
        fill(v, v.source, 0, 2, x)
        fill(v, v.diag, 2, 2, x)
        for r in range(4):
            w = scaled_inverse(v.diag[x, 0, r], v.diag[x, 1, r], 1.0)
            for c in range(2):
                v.weight[x, c, r] = w[c]
        return 0

    lax.fori_loop(0, 16, filled, 0)
    copies = [keep(v, 0, v.source, v.out_source), keep(v, 1, v.weight, v.out_weight)]

    def coarse(k, _):
        for s in range(2):
            shift = []
            for c in range(2):
                total = None
                for half in range(2):
                    for r in (2 * s, 2 * s + 1):
                        value = v.diag[2 + 2 * k + half, c, r]
                        total = value if total is None else total + value
                shift.append(pair_rows(total, v.temp.at[c]) * 0.125)
            w = scaled_inverse(shift[0], shift[1], 0.25)
            d = (1.5 - shift[0], -shift[1])
            for c in range(2):
                v.weight_one[k, c, s] = w[c]
                v.diag_one[k, c, s] = d[c]
        return 0

    lax.fori_loop(0, 6, coarse, 0)

    def turn(x, _):
        for r in range(4):
            v.diag[x, 0, r] = 6.0 - v.diag[x, 0, r]
            v.diag[x, 1, r] = -v.diag[x, 1, r]
        return 0

    lax.fori_loop(0, 16, turn, 0)
    copies += [keep(v, 2, v.diag, v.out_diag), keep(v, 3, v.weight_one, v.out_weight_one),
               keep(v, 4, v.diag_one, v.out_diag_one)]
    copies += down_body(v, v.source, v.weight, v.diag, v.weight_one, v.diag_one, 5, True)
    v.two[0:1, 384:768] = v.inverse_two[...]
    for copy in copies:
        copy.wait()


def down_first(mid, low, high, inverse_two):
    return run(
        "down_first",
        down_first_kernel,
        dict(mid=(mid, VM), low=(low, VM), high=(high, VM), inverse_two=(inverse_two, VM)),
        dict(out_source=(FINE, HB), out_weight=(FINE, HB), out_diag=(FINE, HB), out_weight_one=(COARSE, HB),
             out_diag_one=(COARSE, HB), out_guess=(WIDE, HB), out_source_one=(COARSE, HB), out_guess_one=(COARSE_WIDE, HB),
             two=((1, 768), VM), send_y=((8, 8, 128), VM), send_up=((16, 8, 128), VM), send_down=((16, 8, 128), VM),
             send_far_up=((2, 8, 128), VM), send_far_down=((2, 8, 128), VM)),
        dict(source=FINE, weight=FINE, diag=FINE, weight_one=COARSE, diag_one=COARSE, start=WIDE, guess=WIDE,
             start_one=COARSE_WIDE, source_one=COARSE, guess_one=COARSE_WIDE, temp=(2, 40, 128)),
        8,
    )


def down_second_kernel(v):
    loads = [keep(v, 0, v.in_weight, v.weight), keep(v, 1, v.in_diag, v.diag),
             keep(v, 2, v.in_weight_one, v.weight_one), keep(v, 3, v.in_diag_one, v.diag_one)]
    clear_down(v)

    def filled(x, _):
        fill(v, v.source, 0, 2, x)
        return 0

    lax.fori_loop(0, 16, filled, 0)
    copies = [keep(v, 4, v.source, v.out_source)]
    for load in loads:
        load.wait()
    copies += down_body(v, v.source, v.weight, v.diag, v.weight_one, v.diag_one, 5, False)
    for copy in copies:
        copy.wait()


def down_second(mid, low, high, old):
    return run(
        "down_second",
        down_second_kernel,
        dict(mid=(mid, VM), low=(low, VM), high=(high, VM), in_weight=(old.out_weight, HB), in_diag=(old.out_diag, HB),
             in_weight_one=(old.out_weight_one, HB), in_diag_one=(old.out_diag_one, HB)),
        dict(out_source=(FINE, HB), out_guess=(WIDE, HB), out_source_one=(COARSE, HB), out_guess_one=(COARSE_WIDE, HB),
             two=((1, 384), VM), send_y=((8, 8, 128), VM), send_up=((12, 8, 128), VM), send_down=((12, 8, 128), VM)),
        dict(source=FINE, weight=FINE, diag=FINE, weight_one=COARSE, diag_one=COARSE, start=WIDE, guess=WIDE,
             start_one=COARSE_WIDE, source_one=COARSE, guess_one=COARSE_WIDE, temp=(2, 40, 128)),
        8,
    )


def unpack_two(packed, first, target, planes):
    def body(x, _):
        for k, part in enumerate(loose(packed[x, :, first : first + 384])):
            target[x, k] = part
        return 0

    lax.fori_loop(0, planes, body, 0)


def solve_two(begin, source, weight, ping, pong, window, groups):
    clear(ping, window + 8)
    clear(pong, window + 8)
    rows = slice(8, 8 + groups)
    block = next(b for b in (7, 4, 1) if window % b == 0)

    def over(body):
        def several(number, _):
            for n in range(block):
                body(number * block + n)
            return 0

        lax.fori_loop(0, window // block, several, 0)

    def start(x):
        for k in range(2):
            e = product([weight[begin + x, k], weight[begin + x, 2 + k]], [source[begin + x, k], source[begin + x, 2 + k]])
            for c in range(2):
                ping[x + 4, c * 2 + k, rows, :] = e[c]

    over(start)

    def step(old, new):
        def body(x):
            here = [old[x + 4, n, rows, :] for n in range(4)]
            for k in range(2):
                parts = []
                for c in range(2):
                    n, other = c * 2 + k, c * 2 + 1 - k
                    side = old[x + 4, other, 7 : 7 + groups, :] if k == 0 else old[x + 4, other, 9 : 9 + groups, :]
                    total = (old[x + 3, n, rows, :] + old[x + 5, n, rows, :]) + (here[other] + side)
                    total = total + (pltpu.roll(here[n], 1, 1) + pltpu.roll(here[n], 127, 1))
                    parts.append(source[begin + x, n] + 0.0625 * total)
                moved = product([weight[begin + x, k], weight[begin + x, 2 + k]], parts)
                for c in range(2):
                    new[x + 4, c * 2 + k, rows, :] = (1.0 - OMEGA) * here[c * 2 + k] + moved[c]

        over(body)

    pairs = (ping, pong)
    for number in range(NC - 1):
        step(pairs[number % 2], pairs[(number + 1) % 2])
    return pairs[(NC - 1) % 2]


def spread_rows(target, top, x, c, tile, block):
    for s in range(2):
        for twice in range(2):
            target[x, c, s, pl.ds(top + 8 * tile + twice, 4, 2), :] = block[s * 4 : s * 4 + 4, :]


def add_two(answer, gx, gy, one, first, count):
    row = lax.broadcasted_iota(jnp.int32, (8, 128), 0)
    for j in range(count):
        x = gx + 4 + (first + j) // 2
        for c in range(2):
            for tile in range(3):
                spot = gy + 7 + tile
                low = jnp.broadcast_to(answer[x, c * 2, pl.ds(spot, 1), :], (8, 128))
                high = jnp.broadcast_to(answer[x, c * 2 + 1, pl.ds(spot, 1), :], (8, 128))
                value = jnp.where(row < 4, low, high)
                at = slice(8 + 8 * tile, 16 + 8 * tile)
                for s in range(2):
                    one[j, c, s, at, :] = one[j, c, s, at, :] + value


def up_kernel(v, planes, groups, far):
    count = 8 + 2 * far
    loads = [keep(v, 0, v.in_source, v.source), keep(v, 1, v.in_weight, v.weight), keep(v, 2, v.in_guess, v.guess),
             keep(v, 3, v.in_guess_one, v.guess_one),
             keep(v, 4, v.in_source_one, v.source_one.at[2 * far : 6 + 2 * far]),
             keep(v, 5, v.in_weight_one, v.weight_one.at[2 * far : 6 + 2 * far])]
    if far:
        loads.append(keep(v, 6, v.in_diag, v.diag))
    else:
        loads.append(keep(v, 6, v.in_weight_two, v.weight_two))
        loads.append(keep(v, 7, v.in_first, v.first))
    window = min(planes, WINDOW)
    begin = jnp.clip(v.where[0] - 10, 0, planes - window)
    unpack_two(v.gathered, 0, v.source_two, planes)
    copies = []
    if far:
        unpack_two(v.gathered, 384, v.weight_two, planes)
        copies.append(keep(v, 7, v.weight_two, v.out_weight_two))
    else:
        loads[6].wait()
    answer = solve_two(begin, v.source_two, v.weight_two, v.ping, v.pong, window, groups)
    clear_edges(v.one, count)
    clear_edges(v.one_next, count)
    clear_edges(v.ea, 16)
    clear_edges(v.eb, 16)
    for load in loads[0:6]:
        load.wait()

    for k in range(4):
        for c in range(2):
            for s in range(2):
                v.one[k + 2 + far, c, s, 16:24, :] = v.guess_one[k + 1, c, s, 16:24, :]
            spread_rows(v.one, 8, k + 2 + far, c, 0, v.from_y_low[k * 2 + c])
            spread_rows(v.one, 8, k + 2 + far, c, 2, v.from_y_high[k * 2 + c])
    for c in range(2):
        for tile in range(3):
            for k in range(2):
                n = (k * 3 + tile) * 2 + c
                spread_rows(v.one, 8, far + k, c, tile, v.from_low[n])
                spread_rows(v.one, 8, 6 + far + k, c, tile, v.from_high[n])
    if far:
        zero = jnp.zeros((24, 128), F32)
        for c in range(2):
            for ref, edge, plane in ((v.from_low, v.from_far_low, 0), (v.from_high, v.from_far_high, 9)):
                inner = 1 if plane == 0 else 8
                for s in range(2):
                    v.one[plane, c, s, 8:32, :] = zero
                    v.source_one[inner, c, s] = zero
                    v.weight_one[inner, c, s] = zero
                spread_rows(v.one, 8, plane, c, 1, edge[c])
                spread_rows(v.source_one, 0, inner, c, 1, ref[12 + c])
                spread_rows(v.weight_one, 0, inner, c, 1, ref[14 + c])
    add_two(answer, v.where[0] - begin, v.where[1], v.one, -3 - far, count)
    shift = 0 if far else -1
    sweep(v.one, v.one_next, v.weight_one, shift, v.source_one, shift, 1, count - 1, 2, 2, 0.25)
    sweep(v.one_next, v.one, v.weight_one, shift, v.source_one, shift, 2, count - 2, 2, 2, 0.25)

    def correct(j, _):
        for half in range(2):
            x = 2 * (j - far) + half
            for r in range(4):
                for c in range(2):
                    v.ea[x, c, r, 8:32, :] = v.guess[x, c, r, 8:32, :] + v.one[j, c, r // 2, 8:32, :]
        return 0

    lax.fori_loop(2, count - 2, correct, 0)
    sweep(v.ea, v.eb, v.weight, 0, v.source, 0, 5 - far, 11 + far, 4, 1, 1.0)
    sweep(v.eb, v.ea, v.weight, 0, v.source, 0, 6 - far, 10 + far, 4, 1, 1.0)
    loads[6].wait() if far else loads[7].wait()
    return copies


def up_first_kernel(v, planes, groups):
    copies = up_kernel(v, planes, groups, 1)
    for x in range(4):
        for r in range(4):
            e = [v.ea[x + 6, c, r, 8:32, :] for c in range(2)]
            moved = product([v.diag[x + 6, c, r] for c in range(2)], e)
            for c in range(2):
                value = v.source[x + 6, c, r] + neighbour(v.ea, x + 6, c, r, 4, 1) - moved[c]
                v.packed[x, c, r] = value[8:16]
                if x < 2:
                    v.front[x, c, r] = value[8:16]
                else:
                    v.back[x - 2, c, r] = value[8:16]
                v.first[x, c, r] = e[c][8:16]
    copies.append(keep(v, 8, v.first, v.out_first))
    for copy in copies:
        copy.wait()


def up_second_kernel(v, planes, groups):
    up_kernel(v, planes, groups, 0)
    blocks = []
    for c in range(2):
        for x in range(4):
            blocks.append(
                jnp.concatenate([v.first[x, c, r] + v.ea[x + 6, c, r, 16:24, :] for r in range(4)], axis=1)
            )
    values = jnp.concatenate(blocks, axis=0)
    v.result[...] = exact_dot(values, sort_matrix(512, 384, True)).reshape(2, 4, 8, 384)


def up_scratch(planes, groups, far):
    level = (8 + 2 * far, 2, 2, 40, 128)
    source = (6 + 4 * far, 2, 2, 24, 128)
    two = (min(planes, WINDOW) + 8, 4, 16 + groups, 128)
    return dict(source=FINE, weight=FINE, guess=WIDE, guess_one=COARSE_WIDE, source_one=source, weight_one=source,
                source_two=(planes, 4, groups, 128), weight_two=(planes, 4, groups, 128), ping=two, pong=two,
                one=level, one_next=level, ea=WIDE, eb=WIDE, first=(4, 2, 4, 8, 128))


def up_inputs(where, gathered, messages, down, first_down):
    return dict(where=(where, SM), gathered=(gathered, VM), **{name: (array, VM) for name, array in messages.items()},
                in_source=(down.out_source, HB), in_weight=(first_down.out_weight, HB), in_guess=(down.out_guess, HB),
                in_guess_one=(down.out_guess_one, HB), in_source_one=(down.out_source_one, HB),
                in_weight_one=(first_down.out_weight_one, HB))


def up_first(where, gathered, messages, down):
    planes, groups = gathered.shape[0], gathered.shape[1]
    return run(
        "up_first",
        lambda v: up_first_kernel(v, planes, groups),
        dict(**up_inputs(where, gathered, messages, down, down), in_diag=(down.out_diag, HB)),
        dict(packed=((4, 2, 4, 8, 128), VM), front=((2, 2, 4, 8, 128), VM), back=((2, 2, 4, 8, 128), VM),
             out_first=((4, 2, 4, 8, 128), HB), out_weight_two=((planes, 4, groups, 128), HB)),
        dict(**up_scratch(planes, groups, 1), diag=FINE),
        9,
    )


def up_second(where, gathered, messages, down, first_down, first_up):
    planes, groups = gathered.shape[0], gathered.shape[1]
    return run(
        "up_second",
        lambda v: up_second_kernel(v, planes, groups),
        dict(**up_inputs(where, gathered, messages, down, first_down), in_weight_two=(first_up.out_weight_two, HB),
             in_first=(first_up.out_first, HB)),
        dict(result=((2, 4, 8, 384), VM)),
        up_scratch(planes, groups, 0),
        8,
    ).result


def shifted(block, axis, by):
    count = lax.axis_size(axis)
    pairs = [(i, i + by) for i in range(count) if 0 <= i + by < count]
    return lax.ppermute(block, axis, pairs)


def gather_two(row):
    count_y, count_x = lax.axis_size("gy"), lax.axis_size("gx")
    width = row.shape[1]
    sent = jnp.broadcast_to(row[None], (count_x * count_y, 1, width))
    return lax.all_to_all(sent, ("gx", "gy"), 0, 0).reshape(count_x, count_y, width)


def surround(own):
    mid = jnp.concatenate(
        [
            shifted(own.back, "gx", 2),
            shifted(own.packed, "gx", 1),
            own.packed,
            shifted(own.packed, "gx", -1),
            shifted(own.front, "gx", -2),
        ]
    )
    return mid, shifted(mid, "gy", 1), shifted(mid, "gy", -1)


def exchange_one(down):
    messages = dict(
        from_y_low=shifted(down.send_y, "gy", 1),
        from_y_high=shifted(down.send_y, "gy", -1),
        from_low=shifted(down.send_up, "gx", 1),
        from_high=shifted(down.send_down, "gx", -1),
    )
    if hasattr(down, "send_far_up"):
        messages["from_far_low"] = shifted(down.send_far_up, "gx", 2)
        messages["from_far_high"] = shifted(down.send_far_down, "gx", -2)
    return messages


def local(right_side, velocity_table, layer_index, absorb_level):
    where = jnp.stack([lax.axis_index("gx"), lax.axis_index("gy")]).astype(jnp.int32)
    packed = pack(velocity_table, right_side, layer_index, absorb_level)
    down = down_first(*surround(packed), packed.inverse_two)
    middle = up_first(where, gather_two(down.two), exchange_one(down), down)
    again = down_second(*surround(middle), down)
    return up_second(where, gather_two(again.two), exchange_one(again), again, down, middle)


def solution(mesh):
    placed = (P(None, "gx", "gy", None), P(), P("gx", "gy", None), P("gx", "gy", None))
    return jax.shard_map(
        local, mesh=mesh, in_specs=placed, out_specs=P(None, "gx", "gy", None), check_vma=False
    )
```

time: 666 us -> 213 us (0.32)
  the two profiles are of different devices: /device:TPU:126 before, /device:TPU:1 now
where the time goes in v3:
time: 213 us; the launch traced here: 212 us
  starting transfers between devices  95.5 us (45%)
  waiting for transfers between devices  49.4 us (23%)
  Pallas kernels  35.9 us (17%)
  local copies, waits for them, and re-layouts  29.6 us (14%)
    ppermute x22, starting transfers between devices, shifted(): return lax.ppermute(block, axis, pairs)  61.6 us
    pallas_call x5, Pallas kernels, run(): pl.pallas_call(lambda *refs: kernel(SimpleNamespace(**dict(zip(names, ref...  35.9 us
    ppermute x22, waiting for transfers between devices, shifted(): return lax.ppermute(block, axis, pairs)  34.8 us
    all_to_all x2, starting transfers between devices, gather_two(): lax.all_to_all(sent, ('gx', 'gy'), 0, 0).reshape(count_x, count_y, width)  33.9 us
    unnamed x76, local copies, waits for them, and re-layouts  27.3 us
    all_to_all x2, waiting for transfers between devices, gather_two(): lax.all_to_all(sent, ('gx', 'gy'), 0, 0).reshape(count_x, count_y, width)  14.5 us
  transfers between devices with their start and end apart: 24, of which 11 were waited for; matrix products, arithmetic and copies ran while one was open for 1% of the time, Pallas kernels for 0%

profile of v3, /device:TPU:1, one launch (start us, length us, event | category | flops | bytes accessed | tf_op | source)
XLA Modules:
  0.0 211.6 jit_solution(16352171365314109952)
XLA Ops:
  3.1 1.5 pack.1
  4.7 4.0 %collective-permute-start.1 = (f32[4,4,4,8,128]{4,3,2,1,0:T(8,128)S(1)}, f32[4,4,4,8,128]{4,3,2,1,0:T(8,128)S(1)}, u32[]{:S(2)}, u32[]{:S(2)}) collective-permute-start(f32[4,4,4,8,128]{4,3,2,1,0:T(8,128)S(1)} %get-tuple-element.37), channel_id=1, source_target_pairs={{0,8},{8,16},{16,24},{24,32},{32,40},{40,48},{48,56},{56,64},{64,7... | collective-permute-start | bytes 786440 | tf_op jit(solution)/shard_map/ppermute | solution.py:627
  8.7 4.5 %collective-permute-start = (f32[2,4,4,8,128]{4,3,2,1,0:T(8,128)S(1)}, f32[2,4,4,8,128]{4,3,2,1,0:T(8,128)S(1)}, u32[]{:S(2)}, u32[]{:S(2)}) collective-permute-start(f32[2,4,4,8,128]{4,3,2,1,0:T(8,128)S(1)} %get-tuple-element.36), channel_id=1, source_target_pairs={{0,16},{8,24},{16,32},{24,40},{32,48},{40,56},{48,64},{56,72},{64,... | collective-permute-start | bytes 393224 | tf_op jit(solution)/shard_map/ppermute | solution.py:627
  13.2 1.3 collective-permute-start.2
  14.5 1.3 collective-permute-start.3
  16.6 5.4 %collective-permute-done.2 = f32[4,4,4,8,128]{4,3,2,1,0:T(8,128)S(1)} collective-permute-done((f32[4,4,4,8,128]{4,3,2,1,0:T(8,128)S(1)}, f32[4,4,4,8,128]{4,3,2,1,0:T(8,128)S(1)}, u32[]{:S(2)}, u32[]{:S(2)}) %collective-permute-start.2) | collective-permute-done | bytes 262176 | tf_op jit(solution)/shard_map/ppermute | solution.py:627
  22.1 7.4 %collective-permute-start.4 = (f32[16,4,4,8,128]{4,3,2,1,0:T(8,128)S(1)}, f32[16,4,4,8,128]{4,3,2,1,0:T(8,128)S(1)}, u32[]{:S(2)}, u32[]{:S(2)}) collective-permute-start(f32[16,4,4,8,128]{4,3,2,1,0:T(8,128)S(1)} %constant_dynamic-update-slice_fusion.refs_0_), channel_id=1, source_target_pairs={{0,1},{1,2},{2,3},{3,4},{4,5},{5,6},{6,7},{8,9},{9,10},{10,11},{11... | collective-permute-start | bytes 3145736 | tf_op jit(solution)/shard_map/ppermute | solution.py:627
  29.4 1.9 collective-permute-start.5
  31.3 9.8 %collective-permute-done.4.refs_1_ = f32[16,4,4,8,128]{4,3,2,1,0:T(8,128)S(1)} collective-permute-done((f32[16,4,4,8,128]{4,3,2,1,0:T(8,128)S(1)}, f32[16,4,4,8,128]{4,3,2,1,0:T(8,128)S(1)}, u32[]{:S(2)}, u32[]{:S(2)}) %collective-permute-start.4) | collective-permute-done | bytes 1048608 | tf_op jit(solution)/shard_map/ppermute | solution.py:627
  41.1 4.4 %collective-permute-done.5.refs_2_ = f32[16,4,4,8,128]{4,3,2,1,0:T(8,128)S(1)} collective-permute-done((f32[16,4,4,8,128]{4,3,2,1,0:T(8,128)S(1)}, f32[16,4,4,8,128]{4,3,2,1,0:T(8,128)S(1)}, u32[]{:S(2)}, u32[]{:S(2)}) %collective-permute-start.5) | collective-permute-done | bytes 1048608 | tf_op jit(solution)/shard_map/ppermute | solution.py:627
  45.5 5.7 %down_first.1 = (f32[16,2,4,24,128]{4,3,2,1,0:T(8,128)S(1)}, f32[16,2,4,24,128]{4,3,2,1,0:T(8,128)S(1)}, f32[16,2,4,24,128]{4,3,2,1,0:T(8,128)S(1)}, f32[6,2,2,2...) custom-call(f32[16,4,4,8,128]{4,3,2,1,0:T(8,128)S(1)} %constant_dyna, ...), custom_call_target="tpu_custom_call" | custom-call | tf_op jit(solution)/shard_map/down_first/pallas_call | solution.py:29
  51.2 1.5 copy-done
  52.7 1.2 copy-done.4
  57.9 1.3 broadcast_in_dim.17
  59.2 17.4 %all-to-all-start = ((f32[256,1,768]{2,1,0:T(1,128)}), f32[256,1,768]{2,1,0:T(1,128)}, u32[]{:S(2)}, u32[]{:S(2)}) async-start(f32[256,1,768]{2,1,0:T(1,128)} %broadcast_in_dim.17), calls=%async_computation | async-start | bytes 1572864 | tf_op jit(solution)/shard_map/all_to_all | solution.py:634
  76.6 4.8 %collective-permute-start.10 = (f32[2,8,128]{2,1,0:T(8,128)S(1)}, f32[2,8,128]{2,1,0:T(8,128)S(1)}, u32[]{:S(2)}, u32[]{:S(2)}) collective-permute-start(f32[2,8,128]{2,1,0:T(8,128)S(1)} %get-tuple-element.44), channel_id=1, source_target_pairs={{0,16},{8,24},{16,32},{24,40},{32,48},{40,56},{48,64},{56,72},{64,... | collective-permute-start | bytes 24584 | tf_op jit(solution)/shard_map/ppermute | solution.py:627
  81.4 3.7 %collective-permute-start.6 = (f32[8,8,128]{2,1,0:T(8,128)}, f32[8,8,128]{2,1,0:T(8,128)S(1)}, u32[]{:S(2)}, u32[]{:S(2)}) collective-permute-start(f32[8,8,128]{2,1,0:T(8,128)} %get-tuple-element.41), channel_id=1, source_target_pairs={{0,1},{1,2},{2,3},{3,4},{4,5},{5,6},{6,7},{8,9},{9,10},{10,11},{11... | collective-permute-start | bytes 98312 | tf_op jit(solution)/shard_map/ppermute | solution.py:627
  85.0 1.9 collective-permute-start.7
  87.0 2.3 %collective-permute-start.8 = (f32[16,8,128]{2,1,0:T(8,128)}, f32[16,8,128]{2,1,0:T(8,128)S(1)}, u32[]{:S(2)}, u32[]{:S(2)}) collective-permute-start(f32[16,8,128]{2,1,0:T(8,128)} %copy-done.29), channel_id=1, source_target_pairs={{0,8},{8,16},{16,24},{24,32},{32,40},{40,48},{48,56},{56,64},{64,7... | collective-permute-start | bytes 196616 | tf_op jit(solution)/shard_map/ppermute | solution.py:627
  89.2 1.3 collective-permute-start.9
  90.5 1.3 collective-permute-start.11
  92.5 8.4 %all-to-all-done = f32[256,1,768]{2,1,0:T(1,128)} async-done(((f32[256,1,768]{2,1,0:T(1,128)}), f32[256,1,768]{2,1,0:T(1,128)}, u32[]{:S(2)}, u32[]{:S(2)}) %all-to-all-start) | async-done | bytes 786464 | tf_op jit(solution)/shard_map/all_to_all | solution.py:634
  100.9 1.3 copy.9
  102.5 1.7 copy-done.1
  104.3 1.0 copy-done.11
  106.2 13.2 %up_first.1 = (f32[4,2,4,8,128]{4,3,2,1,0:T(8,128)S(1)}, f32[2,2,4,8,128]{4,3,2,1,0:T(8,128)S(1)}, f32[2,2,4,8,128]{4,3,2,1,0:T(8,128)S(1)}, f32[4,2,4,8,128]{4,3,2,1,0:T(8,128)S(1)}, f32[32,4,8,128]{3,2,1,0:T(8,128)S(1)}) custom-call(s32[2]{0:T(128)S(1)} %copy-done.25, f32[32,8,768]{2,1,0:T(8,128)S(1)} %bitcast.8, ...), custom_call_target="tpu_custom_call" | custom-call | tf_op jit(solution)/shard_map/up_first/pallas_call | solution.py:29
  119.5 4.3 %collective-permute-start.12 = (f32[2,2,4,8,128]{4,3,2,1,0:T(8,128)S(1)}, f32[2,2,4,8,128]{4,3,2,1,0:T(8,128)S(1)}, u32[]{:S(2)}, u32[]{:S(2)}) collective-permute-start(f32[2,2,4,8,128]{4,3,2,1,0:T(8,128)S(1)} %get-tuple-element.53), channel_id=1, source_target_pairs={{0,16},{8,24},{16,32},{24,40},{32,48},{40,56},{48,64},{56,72},{64,... | collective-permute-start | bytes 196616 | tf_op jit(solution)/shard_map/ppermute | solution.py:627
  123.8 1.6 collective-permute-start.13
  125.4 1.3 collective-permute-start.14
  126.7 1.3 collective-permute-start.15
  128.5 2.7 %collective-permute-done.14 = f32[4,2,4,8,128]{4,3,2,1,0:T(8,128)S(1)} collective-permute-done((f32[4,2,4,8,128]{4,3,2,1,0:T(8,128)S(1)}, f32[4,2,4,8,128]{4,3,2,1,0:T(8,128)S(1)}, u32[]{:S(2)}, u32[]{:S(2)}) %collective-permute-start.14) | collective-permute-done | bytes 131104 | tf_op jit(solution)/shard_map/ppermute | solution.py:627
  131.1 2.9 %collective-permute-done.15 = f32[2,2,4,8,128]{4,3,2,1,0:T(8,128)S(1)} collective-permute-done((f32[2,2,4,8,128]{4,3,2,1,0:T(8,128)S(1)}, f32[2,2,4,8,128]{4,3,2,1,0:T(8,128)S(1)}, u32[]{:S(2)}, u32[]{:S(2)}) %collective-permute-start.15) | collective-permute-done | bytes 65568 | tf_op jit(solution)/shard_map/ppermute | solution.py:627
  134.1 5.4 %collective-permute-start.16 = (f32[16,2,4,8,128]{4,3,2,1,0:T(8,128)S(1)}, f32[16,2,4,8,128]{4,3,2,1,0:T(8,128)S(1)}, u32[]{:S(2)}, u32[]{:S(2)}) collective-permute-start(f32[16,2,4,8,128]{4,3,2,1,0:T(8,128)S(1)} %constant_dynamic-update-slice_fusion.5.refs_0_), channel_id=1, source_target_pairs={{0,1},{1,2},{2,3},{3,4},{4,5},{5,6},{6,7},{8,9},{9,10},{10,11},{11... | collective-permute-start | bytes 1572872 | tf_op jit(solution)/shard_map/ppermute | solution.py:627
  139.5 1.9 collective-permute-start.17
  141.4 4.2 %collective-permute-done.16.refs_1_ = f32[16,2,4,8,128]{4,3,2,1,0:T(8,128)S(1)} collective-permute-done((f32[16,2,4,8,128]{4,3,2,1,0:T(8,128)S(1)}, f32[16,2,4,8,128]{4,3,2,1,0:T(8,128)S(1)}, u32[]{:S(2)}, u32[]{:S(2)}) %collective-permute-start.16) | collective-permute-done | bytes 524320 | tf_op jit(solution)/shard_map/ppermute | solution.py:627
  145.6 4.4 %collective-permute-done.17.refs_2_ = f32[16,2,4,8,128]{4,3,2,1,0:T(8,128)S(1)} collective-permute-done((f32[16,2,4,8,128]{4,3,2,1,0:T(8,128)S(1)}, f32[16,2,4,8,128]{4,3,2,1,0:T(8,128)S(1)}, u32[]{:S(2)}, u32[]{:S(2)}) %collective-permute-start.17) | collective-permute-done | bytes 524320 | tf_op jit(solution)/shard_map/ppermute | solution.py:627
  150.0 4.9 %down_second.1 = (f32[16,2,4,24,128]{4,3,2,1,0:T(8,128)S(1)}, f32[16,2,4,40,128]{4,3,2,1,0:T(8,128)S(1)}, f32[6,2,2,24,128]{4,3,2,1,0:T(8,128)S(1)}, f32[6,2,2,4...) custom-call(f32[16,2,4,8,128]{4,3,2,1,0:T(8,128)S(1)} %constant_dyna, ...), custom_call_target="tpu_custom_call" | custom-call | tf_op jit(solution)/shard_map/down_second/pallas_call | solution.py:29
  154.9 1.5 copy-done.2
  156.3 1.2 copy-done.6
  161.2 16.6 %all-to-all-start.1 = ((f32[256,1,384]{2,1,0:T(1,128)}), f32[256,1,384]{2,1,0:T(1,128)}, u32[]{:S(2)}, u32[]{:S(2)}) async-start(f32[256,1,384]{2,1,0:T(1,128)} %broadcast_in_dim.19), calls=%async_computation.1 | async-start | bytes 786432 | tf_op jit(solution)/shard_map/all_to_all | solution.py:634
  177.8 3.3 %collective-permute-start.20 = (f32[12,8,128]{2,1,0:T(8,128)}, f32[12,8,128]{2,1,0:T(8,128)S(1)}, u32[]{:S(2)}, u32[]{:S(2)}) collective-permute-start(f32[12,8,128]{2,1,0:T(8,128)} %get-tuple-element.59), channel_id=1, source_target_pairs={{0,8},{8,16},{16,24},{24,32},{32,40},{40,48},{48,56},{56,64},{64,7... | collective-permute-start | bytes 147464 | tf_op jit(solution)/shard_map/ppermute | solution.py:627
  181.1 1.3 collective-permute-start.21
  182.4 3.7 %collective-permute-start.18 = (f32[8,8,128]{2,1,0:T(8,128)}, f32[8,8,128]{2,1,0:T(8,128)}, u32[]{:S(2)}, u32[]{:S(2)}) collective-permute-start(f32[8,8,128]{2,1,0:T(8,128)} %copy-done.31), channel_id=1, source_target_pairs={{0,1},{1,2},{2,3},{3,4},{4,5},{5,6},{6,7},{8,9},{9,10},{10,11},{11... | collective-permute-start | bytes 98312 | tf_op jit(solution)/shard_map/ppermute | solution.py:627
  186.0 1.9 collective-permute-start.19
  188.0 6.2 %all-to-all-done.1 = f32[256,1,384]{2,1,0:T(1,128)} async-done(((f32[256,1,384]{2,1,0:T(1,128)}), f32[256,1,384]{2,1,0:T(1,128)}, u32[]{:S(2)}, u32[]{:S(2)}) %all-to-all-start.1) | async-done | bytes 393248 | tf_op jit(solution)/shard_map/all_to_all | solution.py:634
  195.2 1.7 copy-done.3
  197.0 1.0 copy-done.9
  200.9 10.7 %up_second.1 = f32[2,4,8,384]{3,2,1,0:T(8,128)} custom-call(s32[2]{0:T(128)S(1)} %copy-done.26, f32[32,8,384]{2,1,0:T(8,128)S(1)} %bitcast.9, f32[8,8,128]{2,1,0:T(8,128)} %collective-permute-done.18.refs_2_, f32[8,8,128]{2,1,0:T(8,128)} %collective-permute-done.19.refs_3_, f32[12,8,128]{2,1,0:T(8,128)S(1)} %collective-permute-done.20.refs_4_, ...), custom_call_target="tpu_custom_call" | custom-call | tf_op jit(solution)/shard_map/up_second/pallas_call | solution.py:29
  (88 shorter events, 18.0 us)
Async XLA Ops:
  0.0 0.9 copy-start.22
  0.9 0.8 copy-start.23
  1.7 0.8 copy-start.24
  4.7 11.9 %collective-permute-start.1 = (f32[4,4,4,8,128]{4,3,2,1,0:T(8,128)S(1)}, f32[4,4,4,8,128]{4,3,2,1,0:T(8,128)S(1)}, u32[]{:S(2)}, u32[]{:S(2)}) collective-permute-start(f32[4,4,4,8,128]{4,3,2,1,0:T(8,128)S(1)} %get-tuple-element.37), channel_id=1, source_target_pairs={{0,8},{8,16},{16,24},{24,32},{32,40},{40,48},{48,56},{56,64},{64,7... | collective-permute-start | bytes 786440 | tf_op jit(solution)/shard_map/ppermute | solution.py:627
  8.7 7.8 %collective-permute-start = (f32[2,4,4,8,128]{4,3,2,1,0:T(8,128)S(1)}, f32[2,4,4,8,128]{4,3,2,1,0:T(8,128)S(1)}, u32[]{:S(2)}, u32[]{:S(2)}) collective-permute-start(f32[2,4,4,8,128]{4,3,2,1,0:T(8,128)S(1)} %get-tuple-element.36), channel_id=1, source_target_pairs={{0,16},{8,24},{16,32},{24,40},{32,48},{40,56},{48,64},{56,72},{64,... | collective-permute-start | bytes 393224 | tf_op jit(solution)/shard_map/ppermute | solution.py:627
  13.2 8.8 %collective-permute-start.2 = (f32[4,4,4,8,128]{4,3,2,1,0:T(8,128)S(1)}, f32[4,4,4,8,128]{4,3,2,1,0:T(8,128)S(1)}, u32[]{:S(2)}, u32[]{:S(2)}) collective-permute-start(f32[4,4,4,8,128]{4,3,2,1,0:T(8,128)S(1)} %get-tuple-element.37), channel_id=1, source_target_pairs={{8,0},{16,8},{24,16},{32,24},{40,32},{48,40},{56,48},{64,56},{72,6... | collective-permute-start | bytes 786440 | tf_op jit(solution)/shard_map/ppermute | solution.py:627
  14.5 7.5 %collective-permute-start.3 = (f32[2,4,4,8,128]{4,3,2,1,0:T(8,128)S(1)}, f32[2,4,4,8,128]{4,3,2,1,0:T(8,128)S(1)}, u32[]{:S(2)}, u32[]{:S(2)}) collective-permute-start(f32[2,4,4,8,128]{4,3,2,1,0:T(8,128)S(1)} %get-tuple-element.38), channel_id=1, source_target_pairs={{16,0},{24,8},{32,16},{40,24},{48,32},{56,40},{64,48},{72,56},{80,... | collective-permute-start | bytes 393224 | tf_op jit(solution)/shard_map/ppermute | solution.py:627
  22.1 19.1 %collective-permute-start.4 = (f32[16,4,4,8,128]{4,3,2,1,0:T(8,128)S(1)}, f32[16,4,4,8,128]{4,3,2,1,0:T(8,128)S(1)}, u32[]{:S(2)}, u32[]{:S(2)}) collective-permute-start(f32[16,4,4,8,128]{4,3,2,1,0:T(8,128)S(1)} %constant_dynamic-update-slice_fusion.refs_0_), channel_id=1, source_target_pairs={{0,1},{1,2},{2,3},{3,4},{4,5},{5,6},{6,7},{8,9},{9,10},{10,11},{11... | collective-permute-start | bytes 3145736 | tf_op jit(solution)/shard_map/ppermute | solution.py:627
  29.4 16.1 %collective-permute-start.5 = (f32[16,4,4,8,128]{4,3,2,1,0:T(8,128)S(1)}, f32[16,4,4,8,128]{4,3,2,1,0:T(8,128)S(1)}, u32[]{:S(2)}, u32[]{:S(2)}) collective-permute-start(f32[16,4,4,8,128]{4,3,2,1,0:T(8,128)S(1)} %constant_dynamic-update-slice_fusion.refs_0_), channel_id=1, source_target_pairs={{1,0},{2,1},{3,2},{4,3},{5,4},{6,5},{7,6},{9,8},{10,9},{11,10},{12... | collective-permute-start | bytes 3145736 | tf_op jit(solution)/shard_map/ppermute | solution.py:627
  51.2 1.5 copy-start
  52.7 1.2 copy-start.4
  53.8 0.8 copy-start.10
  59.2 41.7 %all-to-all-start = ((f32[256,1,768]{2,1,0:T(1,128)}), f32[256,1,768]{2,1,0:T(1,128)}, u32[]{:S(2)}, u32[]{:S(2)}) async-start(f32[256,1,768]{2,1,0:T(1,128)} %broadcast_in_dim.17), calls=%async_computation | async-start | bytes 1572864 | tf_op jit(solution)/shard_map/all_to_all | solution.py:634
  76.6 13.9 %collective-permute-start.10 = (f32[2,8,128]{2,1,0:T(8,128)S(1)}, f32[2,8,128]{2,1,0:T(8,128)S(1)}, u32[]{:S(2)}, u32[]{:S(2)}) collective-permute-start(f32[2,8,128]{2,1,0:T(8,128)S(1)} %get-tuple-element.44), channel_id=1, source_target_pairs={{0,16},{8,24},{16,32},{24,40},{32,48},{40,56},{48,64},{56,72},{64,... | collective-permute-start | bytes 24584 | tf_op jit(solution)/shard_map/ppermute | solution.py:627
  81.4 20.8 %collective-permute-start.6 = (f32[8,8,128]{2,1,0:T(8,128)}, f32[8,8,128]{2,1,0:T(8,128)S(1)}, u32[]{:S(2)}, u32[]{:S(2)}) collective-permute-start(f32[8,8,128]{2,1,0:T(8,128)} %get-tuple-element.41), channel_id=1, source_target_pairs={{0,1},{1,2},{2,3},{3,4},{4,5},{5,6},{6,7},{8,9},{9,10},{10,11},{11... | collective-permute-start | bytes 98312 | tf_op jit(solution)/shard_map/ppermute | solution.py:627
  85.0 17.2 %collective-permute-start.7 = (f32[8,8,128]{2,1,0:T(8,128)}, f32[8,8,128]{2,1,0:T(8,128)}, u32[]{:S(2)}, u32[]{:S(2)}) collective-permute-start(f32[8,8,128]{2,1,0:T(8,128)} %get-tuple-element.41), channel_id=1, source_target_pairs={{1,0},{2,1},{3,2},{4,3},{5,4},{6,5},{7,6},{9,8},{10,9},{11,10},{12... | collective-permute-start | bytes 98312 | tf_op jit(solution)/shard_map/ppermute | solution.py:627
  87.0 15.2 %collective-permute-start.8 = (f32[16,8,128]{2,1,0:T(8,128)}, f32[16,8,128]{2,1,0:T(8,128)S(1)}, u32[]{:S(2)}, u32[]{:S(2)}) collective-permute-start(f32[16,8,128]{2,1,0:T(8,128)} %copy-done.29), channel_id=1, source_target_pairs={{0,8},{8,16},{16,24},{24,32},{32,40},{40,48},{48,56},{56,64},{64,7... | collective-permute-start | bytes 196616 | tf_op jit(solution)/shard_map/ppermute | solution.py:627
  89.2 13.0 %collective-permute-start.9 = (f32[16,8,128]{2,1,0:T(8,128)}, f32[16,8,128]{2,1,0:T(8,128)}, u32[]{:S(2)}, u32[]{:S(2)}) collective-permute-start(f32[16,8,128]{2,1,0:T(8,128)} %copy-done.28), channel_id=1, source_target_pairs={{8,0},{16,8},{24,16},{32,24},{40,32},{48,40},{56,48},{64,56},{72,6... | collective-permute-start | bytes 196616 | tf_op jit(solution)/shard_map/ppermute | solution.py:627
  90.5 11.6 %collective-permute-start.11 = (f32[2,8,128]{2,1,0:T(8,128)}, f32[2,8,128]{2,1,0:T(8,128)S(1)}, u32[]{:S(2)}, u32[]{:S(2)}) collective-permute-start(f32[2,8,128]{2,1,0:T(8,128)} %copy-done.32), channel_id=1, source_target_pairs={{16,0},{24,8},{32,16},{40,24},{48,32},{56,40},{64,48},{72,56},{80,... | collective-permute-start | bytes 24584 | tf_op jit(solution)/shard_map/ppermute | solution.py:627
  100.9 1.6 copy-start.5
  100.9 1.6 copy-start.25
  102.5 1.7 copy-start.1
  104.3 1.0 copy-start.11
  105.3 1.0 copy-start.15
  106.2 43.7 %copy-start.19 = (f32[6,2,2,24,128]{4,3,2,1,0:T(8,128)S(1)}, f32[6,2,2,24,128]{4,3,2,1,0:T(8,128)}, u32[]{:S(2)}) copy-start(f32[6,2,2,24,128]{4,3,2,1,0:T(8,128)} %copy-done.18) | copy-start | bytes 884740
  119.4 30.5 %copy-start.8 = (f32[32,4,8,128]{3,2,1,0:T(8,128)}, f32[32,4,8,128]{3,2,1,0:T(8,128)S(1)}, u32[]{:S(2)}) copy-start(f32[32,4,8,128]{3,2,1,0:T(8,128)S(1)} %get-tuple-element.65.refs_12_) | copy-start | bytes 1572868
  119.4 30.5 %copy-start.20 = (f32[4,2,4,8,128]{4,3,2,1,0:T(8,128)}, f32[4,2,4,8,128]{4,3,2,1,0:T(8,128)S(1)}, u32[]{:S(2)}) copy-start(f32[4,2,4,8,128]{4,3,2,1,0:T(8,128)S(1)} %get-tuple-element.66.refs_13_) | copy-start | bytes 393220
  119.5 8.6 %collective-permute-start.12 = (f32[2,2,4,8,128]{4,3,2,1,0:T(8,128)S(1)}, f32[2,2,4,8,128]{4,3,2,1,0:T(8,128)S(1)}, u32[]{:S(2)}, u32[]{:S(2)}) collective-permute-start(f32[2,2,4,8,128]{4,3,2,1,0:T(8,128)S(1)} %get-tuple-element.53), channel_id=1, source_target_pairs={{0,16},{8,24},{16,32},{24,40},{32,48},{40,56},{48,64},{56,72},{64,... | collective-permute-start | bytes 196616 | tf_op jit(solution)/shard_map/ppermute | solution.py:627
  123.8 4.6 %collective-permute-start.13 = (f32[4,2,4,8,128]{4,3,2,1,0:T(8,128)S(1)}, f32[4,2,4,8,128]{4,3,2,1,0:T(8,128)S(1)}, u32[]{:S(2)}, u32[]{:S(2)}) collective-permute-start(f32[4,2,4,8,128]{4,3,2,1,0:T(8,128)S(1)} %get-tuple-element.54), channel_id=1, source_target_pairs={{0,8},{8,16},{16,24},{24,32},{32,40},{40,48},{48,56},{56,64},{64,7... | collective-permute-start | bytes 393224 | tf_op jit(solution)/shard_map/ppermute | solution.py:627
  125.4 5.7 %collective-permute-start.14 = (f32[4,2,4,8,128]{4,3,2,1,0:T(8,128)S(1)}, f32[4,2,4,8,128]{4,3,2,1,0:T(8,128)S(1)}, u32[]{:S(2)}, u32[]{:S(2)}) collective-permute-start(f32[4,2,4,8,128]{4,3,2,1,0:T(8,128)S(1)} %get-tuple-element.54), channel_id=1, source_target_pairs={{8,0},{16,8},{24,16},{32,24},{40,32},{48,40},{56,48},{64,56},{72,6... | collective-permute-start | bytes 393224 | tf_op jit(solution)/shard_map/ppermute | solution.py:627
  126.7 7.3 %collective-permute-start.15 = (f32[2,2,4,8,128]{4,3,2,1,0:T(8,128)S(1)}, f32[2,2,4,8,128]{4,3,2,1,0:T(8,128)S(1)}, u32[]{:S(2)}, u32[]{:S(2)}) collective-permute-start(f32[2,2,4,8,128]{4,3,2,1,0:T(8,128)S(1)} %get-tuple-element.55), channel_id=1, source_target_pairs={{16,0},{24,8},{32,16},{40,24},{48,32},{56,40},{64,48},{72,56},{80,... | collective-permute-start | bytes 196616 | tf_op jit(solution)/shard_map/ppermute | solution.py:627
  134.1 11.5 %collective-permute-start.16 = (f32[16,2,4,8,128]{4,3,2,1,0:T(8,128)S(1)}, f32[16,2,4,8,128]{4,3,2,1,0:T(8,128)S(1)}, u32[]{:S(2)}, u32[]{:S(2)}) collective-permute-start(f32[16,2,4,8,128]{4,3,2,1,0:T(8,128)S(1)} %constant_dynamic-update-slice_fusion.5.refs_0_), channel_id=1, source_target_pairs={{0,1},{1,2},{2,3},{3,4},{4,5},{5,6},{6,7},{8,9},{9,10},{10,11},{11... | collective-permute-start | bytes 1572872 | tf_op jit(solution)/shard_map/ppermute | solution.py:627
  139.5 10.5 %collective-permute-start.17 = (f32[16,2,4,8,128]{4,3,2,1,0:T(8,128)S(1)}, f32[16,2,4,8,128]{4,3,2,1,0:T(8,128)S(1)}, u32[]{:S(2)}, u32[]{:S(2)}) collective-permute-start(f32[16,2,4,8,128]{4,3,2,1,0:T(8,128)S(1)} %constant_dynamic-update-slice_fusion.5.refs_0_), channel_id=1, source_target_pairs={{1,0},{2,1},{3,2},{4,3},{5,4},{6,5},{7,6},{9,8},{10,9},{11,10},{12... | collective-permute-start | bytes 1572872 | tf_op jit(solution)/shard_map/ppermute | solution.py:627
  154.9 1.5 copy-start.2
  156.3 1.2 copy-start.6
  157.5 0.8 copy-start.12
  160.2 35.0 %copy-start.26 = (s32[2]{0:T(128)S(1)}, s32[2]{0:T(128)}, u32[]{:S(2)}) copy-start(s32[2]{0:T(128)} %pad_add_fusion.refs_0_) | copy-start | bytes 28
  160.2 35.0 %copy-start.7 = (f32[16,2,4,24,128]{4,3,2,1,0:T(8,128)S(1)}, f32[16,2,4,24,128]{4,3,2,1,0:T(8,128)}, u32[]{:S(2)}) copy-start(f32[16,2,4,24,128]{4,3,2,1,0:T(8,128)} %copy-done.6) | copy-start | bytes 4718596
  161.2 32.9 %all-to-all-start.1 = ((f32[256,1,384]{2,1,0:T(1,128)}), f32[256,1,384]{2,1,0:T(1,128)}, u32[]{:S(2)}, u32[]{:S(2)}) async-start(f32[256,1,384]{2,1,0:T(1,128)} %broadcast_in_dim.19), calls=%async_computation.1 | async-start | bytes 786432 | tf_op jit(solution)/shard_map/all_to_all | solution.py:634
  177.8 17.4 %collective-permute-start.20 = (f32[12,8,128]{2,1,0:T(8,128)}, f32[12,8,128]{2,1,0:T(8,128)S(1)}, u32[]{:S(2)}, u32[]{:S(2)}) collective-permute-start(f32[12,8,128]{2,1,0:T(8,128)} %get-tuple-element.59), channel_id=1, source_target_pairs={{0,8},{8,16},{16,24},{24,32},{32,40},{40,48},{48,56},{56,64},{64,7... | collective-permute-start | bytes 147464 | tf_op jit(solution)/shard_map/ppermute | solution.py:627
  181.1 14.1 %collective-permute-start.21 = (f32[12,8,128]{2,1,0:T(8,128)}, f32[12,8,128]{2,1,0:T(8,128)S(1)}, u32[]{:S(2)}, u32[]{:S(2)}) collective-permute-start(f32[12,8,128]{2,1,0:T(8,128)} %copy-done.30), channel_id=1, source_target_pairs={{8,0},{16,8},{24,16},{32,24},{40,32},{48,40},{56,48},{64,56},{72,6... | collective-permute-start | bytes 147464 | tf_op jit(solution)/shard_map/ppermute | solution.py:627
  182.4 12.8 %collective-permute-start.18 = (f32[8,8,128]{2,1,0:T(8,128)}, f32[8,8,128]{2,1,0:T(8,128)}, u32[]{:S(2)}, u32[]{:S(2)}) collective-permute-start(f32[8,8,128]{2,1,0:T(8,128)} %copy-done.31), channel_id=1, source_target_pairs={{0,1},{1,2},{2,3},{3,4},{4,5},{5,6},{6,7},{8,9},{9,10},{10,11},{11... | collective-permute-start | bytes 98312 | tf_op jit(solution)/shard_map/ppermute | solution.py:627
  186.0 9.1 %collective-permute-start.19 = (f32[8,8,128]{2,1,0:T(8,128)}, f32[8,8,128]{2,1,0:T(8,128)}, u32[]{:S(2)}, u32[]{:S(2)}) collective-permute-start(f32[8,8,128]{2,1,0:T(8,128)} %copy-done.31), channel_id=1, source_target_pairs={{1,0},{2,1},{3,2},{4,3},{5,4},{6,5},{7,6},{9,8},{10,9},{11,10},{12... | collective-permute-start | bytes 98312 | tf_op jit(solution)/shard_map/ppermute | solution.py:627
  195.2 1.7 copy-start.3
  196.9 1.0 copy-start.9
  198.0 1.0 copy-start.13
  199.0 1.0 copy-start.17
  200.0 0.9 copy-start.21
  (9 other events, 5.9 us)

commit v4 on v3

--- a/solution.py
+++ b/solution.py
@@ -29,13 +29,13 @@
     result = pl.pallas_call(
         lambda *refs: kernel(SimpleNamespace(**dict(zip(names, refs)))),
         name=name,
-        out_shape=tuple(jax.ShapeDtypeStruct(dims, F32) for dims, _ in outputs.values()),
+        out_shape=tuple(HB(dims, F32) if space is HB else jax.ShapeDtypeStruct(dims, F32) for dims, space in outputs.values()),
         in_specs=[pl.BlockSpec(memory_space=space) for _, space in inputs.values()],
         out_specs=tuple(pl.BlockSpec(memory_space=space) for _, space in outputs.values()),
         scratch_shapes=[pltpu.VMEM(dims, F32) if isinstance(dims, tuple) else dims for dims in scratch.values()]
         + [pltpu.SemaphoreType.DMA((copies,))],
         compiler_params=PARAMS,
-    )(*[array for array, _ in inputs.values()])
+    )(*[pltpu.with_memory_space_constraint(array, HB) if space is HB else array for array, space in inputs.values()])
     return SimpleNamespace(**dict(zip(outputs, result)))
 
 
@@ -76,12 +76,12 @@
     return value + jnp.where(row % 2 == 0, temp[9:33, :], temp[7:31, :])
 
 
-def neighbour(ref, x, c, r, count, step):
-    center = lambda s: ref[x, c, s, 8:32, :]
+def neighbour(ref, x, c, r, count, step, low=8, high=32):
+    center = lambda s: ref[x, c, s, low:high, :]
     up = center(r + 1) if r < count - 1 else pltpu.roll(center(0), 127, 1)
     down = center(r - 1) if r > 0 else pltpu.roll(center(count - 1), 1, 1)
-    total = ref[x - 1, c, r, 8:32, :] + ref[x + 1, c, r, 8:32, :]
-    total = total + ref[x, c, r, 8 - step : 32 - step, :] + ref[x, c, r, 8 + step : 32 + step, :]
+    total = ref[x - 1, c, r, low:high, :] + ref[x + 1, c, r, low:high, :]
+    total = total + ref[x, c, r, low - step : high - step, :] + ref[x, c, r, low + step : high + step, :]
     return total + (up + down)
 
 
@@ -124,27 +124,31 @@
     lax.fori_loop(0, count, body, 0)
 
 
-def dense(target, at, pieces):
-    lane = lax.broadcasted_iota(jnp.int32, (1, 128), 1)
+def dense(parts):
+    lane = lax.broadcasted_iota(jnp.int32, parts[0].shape, 1)
+    result = []
     for n in range(3):
-        tail = pltpu.roll(pieces[n + 1], 128 - 32 * (n + 1), 1)
-        head = pieces[n] if n == 0 else pltpu.roll(pieces[n], 128 - 32 * n, 1)
-        target[0:1, at + n * 128 : at + n * 128 + 128] = jnp.where(lane < 96 - 32 * n, head, tail)
-
-
-def loose(block):
-    lane = lax.broadcasted_iota(jnp.int32, (block.shape[0], 128), 1)
-    parts = [block[:, n * 128 : n * 128 + 128] for n in range(3)]
-    result = []
-    for k in range(4):
-        if k == 0:
-            value = parts[0]
-        elif k == 3:
-            value = pltpu.roll(parts[2], 96, 1)
+        head = parts[0] if n == 0 else pltpu.roll(parts[n], 128 - 32 * n, 1)
+        result.append(jnp.where(lane < 96 - 32 * n, head, pltpu.roll(parts[n + 1], 96 - 32 * n, 1)))
+    return result
+
+
+def loose(parts, clean):
+    lane = lax.broadcasted_iota(jnp.int32, parts[0].shape, 1)
+    result = [parts[0]]
+    for k in (1, 2):
+        result.append(jnp.where(lane < 32 * k, pltpu.roll(parts[k - 1], 32 * k, 1), pltpu.roll(parts[k], 32 * k, 1)))
+    result.append(pltpu.roll(parts[2], 96, 1))
+    return [jnp.where(lane < 96, value, 0.0) for value in result] if clean else result
+
+
+def put_dense(v, x, c, parts):
+    for n, tile in enumerate(dense(parts)):
+        v.packed[x, c, n] = tile
+        if x < 2:
+            v.front[x, c, n] = tile
         else:
-            value = jnp.where(lane < 32 * k, pltpu.roll(parts[k - 1], 32 * k, 1), pltpu.roll(parts[k], 32 * k, 1))
-        result.append(jnp.where(lane < 96, value, 0.0))
-    return result
+            v.back[x - 2, c, n] = tile
 
 
 def pack_kernel(v):
@@ -152,6 +156,7 @@
         pltpu.make_async_copy(v.right_side, v.field, v.sem.at[0]),
         pltpu.make_async_copy(v.layer_index, v.layers, v.sem.at[1]),
         pltpu.make_async_copy(v.absorb_level, v.levels, v.sem.at[2]),
+        pltpu.make_async_copy(v.speeds, v.table, v.sem.at[3]),
     ]
     for load in loads:
         load.start()
@@ -163,6 +168,7 @@
     codes = jnp.dot(both.astype(F32).astype(BF16), matrix, preferred_element_type=F32)
     inside = lax.broadcasted_iota(jnp.int32, (32, 128), 1) < 96
     total = [jnp.zeros((32, 128), F32), jnp.zeros((32, 128), F32)]
+    reals, imags = [], []
     for r in range(4):
         lanes = slice(r * 128, r * 128 + 128)
         layer = codes[0:32, lanes]
@@ -173,15 +179,15 @@
         real = jnp.where(inside, ratio * ratio, 0.0)
         imag = -real * (BETA + ABSORB * codes[32:64, lanes])
         total = [total[0] + real, total[1] + imag]
-        for x in range(4):
-            rows = slice(x * 8, x * 8 + 8)
-            values = (field[x * 8 : x * 8 + 8, lanes], field[32 + x * 8 : 40 + x * 8, lanes], real[rows], imag[rows])
-            for c in range(4):
-                v.packed[x, c, r] = values[c]
-                if x < 2:
-                    v.front[x, c, r] = values[c]
-                else:
-                    v.back[x - 2, c, r] = values[c]
+        reals.append(real)
+        imags.append(imag)
+    for x in range(4):
+        rows = slice(x * 8, x * 8 + 8)
+        for c in range(2):
+            at = 32 * c + x * 8
+            put_dense(v, x, c, [field[at : at + 8, r * 128 : r * 128 + 128] for r in range(4)])
+        put_dense(v, x, 2, [reals[r][rows] for r in range(4)])
+        put_dense(v, x, 3, [imags[r][rows] for r in range(4)])
     means = []
     for c in range(2):
         t = total[c]
@@ -189,24 +195,26 @@
         row = [v.temp[c, n : n + 1] for n in range(8)]
         means.append([((row[4 * k] + row[4 * k + 1]) + (row[4 * k + 2] + row[4 * k + 3])) * (1.0 / 64.0) for k in range(2)])
     w = [scaled_inverse(means[0][k], means[1][k], 0.0625) for k in range(2)]
-    dense(v.inverse_two, 0, [w[k][c] for c in range(2) for k in range(2)])
+    v.inverse_two[...] = jnp.concatenate(dense([w[k][c] for c in range(2) for k in range(2)]), axis=1)
 
 
 def pack(table, right_side, layer_index, absorb_level):
     return run(
         "pack",
         pack_kernel,
-        dict(table=(table, SM), right_side=(right_side, HB), layer_index=(layer_index, HB), absorb_level=(absorb_level, HB)),
-        dict(packed=((4, 4, 4, 8, 128), VM), front=((2, 4, 4, 8, 128), VM), back=((2, 4, 4, 8, 128), VM),
+        dict(speeds=(table, HB), right_side=(right_side, HB), layer_index=(layer_index, HB), absorb_level=(absorb_level, HB)),
+        dict(packed=((4, 4, 3, 8, 128), VM), front=((2, 4, 3, 8, 128), VM), back=((2, 4, 3, 8, 128), VM),
              inverse_two=((1, 384), VM)),
         dict(field=right_side.shape, layers=pltpu.VMEM(layer_index.shape, jnp.int32),
-             levels=pltpu.VMEM(absorb_level.shape, jnp.int32), temp=(2, 8, 128)),
-        3,
+             levels=pltpu.VMEM(absorb_level.shape, jnp.int32), table=pltpu.SMEM(table.shape, F32), temp=(2, 8, 128)),
+        4,
     )
 
 
 FINE = (16, 2, 4, 24, 128)
 WIDE = (16, 2, 4, 40, 128)
+PART = (8, 2, 4, 24, 128)
+INNER = (12, 2, 4, 24, 128)
 COARSE = (6, 2, 2, 24, 128)
 COARSE_WIDE = (6, 2, 2, 40, 128)
 
@@ -232,7 +240,7 @@
 
     lax.fori_loop(0, 16, first, 0)
     sweep(v.start, v.guess, weight, 0, source, 0, 1, 15, 4, 1, 1.0)
-    copies = [keep(v, first_copy, v.guess, v.out_guess)]
+    copies = [keep(v, first_copy, v.guess.at[2:14, :, :, 8:32, :], v.out_guess)]
 
     def residual(k, _):
         for s in range(2):
@@ -271,7 +279,8 @@
         for k in range(2):
             row = 16 + 4 * k
             pieces.append((v.temp[c, row : row + 1, :] + v.temp[c, row + 2 : row + 3, :]) * 0.125)
-    dense(v.two, 0, pieces)
+    for n, tile in enumerate(dense(pieces)):
+        v.two[0:1, n * 128 : n * 128 + 128] = tile
 
     for c in range(2):
         for k in range(4):
@@ -291,11 +300,11 @@
 
 
 def fill(v, target, at, count, x):
-    for r in range(4):
-        for c in range(count):
-            target[x, c, r, 0:8, :] = v.low[x, at + c, r]
-            target[x, c, r, 8:16, :] = v.mid[x, at + c, r]
-            target[x, c, r, 16:24, :] = v.high[x, at + c, r]
+    for c in range(count):
+        for tile, ref in enumerate((v.low, v.mid, v.high)):
+            parts = loose([ref[x, at + c, n] for n in range(3)], at + c == 2)
+            for r in range(4):
+                target[x, c, r, 8 * tile : 8 * tile + 8, :] = parts[r]
 
 
 def clear_down(v):
@@ -318,7 +327,7 @@
         return 0
 
     lax.fori_loop(0, 16, filled, 0)
-    copies = [keep(v, 0, v.source, v.out_source), keep(v, 1, v.weight, v.out_weight)]
+    copies = [keep(v, 0, v.source.at[4:12], v.out_source), keep(v, 1, v.weight, v.out_weight)]
 
     def coarse(k, _):
         for s in range(2):
@@ -346,7 +355,7 @@
         return 0
 
     lax.fori_loop(0, 16, turn, 0)
-    copies += [keep(v, 2, v.diag, v.out_diag), keep(v, 3, v.weight_one, v.out_weight_one),
+    copies += [keep(v, 2, v.diag.at[2:14], v.out_diag), keep(v, 3, v.weight_one, v.out_weight_one),
                keep(v, 4, v.diag_one, v.out_diag_one)]
     copies += down_body(v, v.source, v.weight, v.diag, v.weight_one, v.diag_one, 5, True)
     v.two[0:1, 384:768] = v.inverse_two[...]
@@ -359,8 +368,8 @@
         "down_first",
         down_first_kernel,
         dict(mid=(mid, VM), low=(low, VM), high=(high, VM), inverse_two=(inverse_two, VM)),
-        dict(out_source=(FINE, HB), out_weight=(FINE, HB), out_diag=(FINE, HB), out_weight_one=(COARSE, HB),
-             out_diag_one=(COARSE, HB), out_guess=(WIDE, HB), out_source_one=(COARSE, HB), out_guess_one=(COARSE_WIDE, HB),
+        dict(out_source=(PART, HB), out_weight=(FINE, HB), out_diag=(INNER, HB), out_weight_one=(COARSE, HB),
+             out_diag_one=(COARSE, HB), out_guess=(INNER, HB), out_source_one=(COARSE, HB), out_guess_one=(COARSE_WIDE, HB),
              two=((1, 768), VM), send_y=((8, 8, 128), VM), send_up=((16, 8, 128), VM), send_down=((16, 8, 128), VM),
              send_far_up=((2, 8, 128), VM), send_far_down=((2, 8, 128), VM)),
         dict(source=FINE, weight=FINE, diag=FINE, weight_one=COARSE, diag_one=COARSE, start=WIDE, guess=WIDE,
@@ -370,7 +379,7 @@
 
 
 def down_second_kernel(v):
-    loads = [keep(v, 0, v.in_weight, v.weight), keep(v, 1, v.in_diag, v.diag),
+    loads = [keep(v, 0, v.in_weight, v.weight), keep(v, 1, v.in_diag, v.diag.at[2:14]),
              keep(v, 2, v.in_weight_one, v.weight_one), keep(v, 3, v.in_diag_one, v.diag_one)]
     clear_down(v)
 
@@ -379,7 +388,7 @@
         return 0
 
     lax.fori_loop(0, 16, filled, 0)
-    copies = [keep(v, 4, v.source, v.out_source)]
+    copies = [keep(v, 4, v.source.at[4:12], v.out_source)]
     for load in loads:
         load.wait()
     copies += down_body(v, v.source, v.weight, v.diag, v.weight_one, v.diag_one, 5, False)
@@ -393,7 +402,7 @@
         down_second_kernel,
         dict(mid=(mid, VM), low=(low, VM), high=(high, VM), in_weight=(old.out_weight, HB), in_diag=(old.out_diag, HB),
              in_weight_one=(old.out_weight_one, HB), in_diag_one=(old.out_diag_one, HB)),
-        dict(out_source=(FINE, HB), out_guess=(WIDE, HB), out_source_one=(COARSE, HB), out_guess_one=(COARSE_WIDE, HB),
+        dict(out_source=(PART, HB), out_guess=(INNER, HB), out_source_one=(COARSE, HB), out_guess_one=(COARSE_WIDE, HB),
              two=((1, 384), VM), send_y=((8, 8, 128), VM), send_up=((12, 8, 128), VM), send_down=((12, 8, 128), VM)),
         dict(source=FINE, weight=FINE, diag=FINE, weight_one=COARSE, diag_one=COARSE, start=WIDE, guess=WIDE,
              start_one=COARSE_WIDE, source_one=COARSE, guess_one=COARSE_WIDE, temp=(2, 40, 128)),
@@ -401,38 +410,40 @@
     )
 
 
-def unpack_two(packed, first, target, planes):
-    def body(x, _):
-        for k, part in enumerate(loose(packed[x, :, first : first + 384])):
+def over(low, count, block, body):
+    def several(number, _):
+        for n in range(block):
+            body(low + number * block + n)
+        return 0
+
+    lax.fori_loop(0, count // block, several, 0)
+    for n in range(count - count % block, count):
+        body(low + n)
+
+
+def unpack_two(packed, first, begin, target, window, clean):
+    def body(x):
+        parts = [packed[begin + x, :, first + n * 128 : first + n * 128 + 128] for n in range(3)]
+        for k, part in enumerate(loose(parts, clean)):
             target[x, k] = part
-        return 0
-
-    lax.fori_loop(0, planes, body, 0)
-
-
-def solve_two(begin, source, weight, ping, pong, window, groups):
+
+    over(0, window, 7, body)
+
+
+def solve_two(own, source, weight, ping, pong, window, planes, groups):
     clear(ping, window + 8)
     clear(pong, window + 8)
     rows = slice(8, 8 + groups)
-    block = next(b for b in (7, 4, 1) if window % b == 0)
-
-    def over(body):
-        def several(number, _):
-            for n in range(block):
-                body(number * block + n)
-            return 0
-
-        lax.fori_loop(0, window // block, several, 0)
 
     def start(x):
         for k in range(2):
-            e = product([weight[begin + x, k], weight[begin + x, 2 + k]], [source[begin + x, k], source[begin + x, 2 + k]])
+            e = product([weight[x, k], weight[x, 2 + k]], [source[x, k], source[x, 2 + k]])
             for c in range(2):
                 ping[x + 4, c * 2 + k, rows, :] = e[c]
 
-    over(start)
-
-    def step(old, new):
+    over(0, window, 7, start)
+
+    def step(old, new, left):
         def body(x):
             here = [old[x + 4, n, rows, :] for n in range(4)]
             for k in range(2):
@@ -442,16 +453,17 @@
                     side = old[x + 4, other, 7 : 7 + groups, :] if k == 0 else old[x + 4, other, 9 : 9 + groups, :]
                     total = (old[x + 3, n, rows, :] + old[x + 5, n, rows, :]) + (here[other] + side)
                     total = total + (pltpu.roll(here[n], 1, 1) + pltpu.roll(here[n], 127, 1))
-                    parts.append(source[begin + x, n] + 0.0625 * total)
-                moved = product([weight[begin + x, k], weight[begin + x, 2 + k]], parts)
+                    parts.append(source[x, n] + 0.0625 * total)
+                moved = product([weight[x, k], weight[x, 2 + k]], parts)
                 for c in range(2):
                     new[x + 4, c * 2 + k, rows, :] = (1.0 - OMEGA) * here[c * 2 + k] + moved[c]
 
-        over(body)
+        count = min(window, 2 * (3 + left) + 1)
+        over(jnp.clip(own - 3 - left, 0, window - count), count, 4, body)
 
     pairs = (ping, pong)
     for number in range(NC - 1):
-        step(pairs[number % 2], pairs[(number + 1) % 2])
+        step(pairs[number % 2], pairs[(number + 1) % 2], NC - 2 - number)
     return pairs[(NC - 1) % 2]
 
 
@@ -478,30 +490,33 @@
 
 def up_kernel(v, planes, groups, far):
     count = 8 + 2 * far
-    loads = [keep(v, 0, v.in_source, v.source), keep(v, 1, v.in_weight, v.weight), keep(v, 2, v.in_guess, v.guess),
-             keep(v, 3, v.in_guess_one, v.guess_one),
-             keep(v, 4, v.in_source_one, v.source_one.at[2 * far : 6 + 2 * far]),
-             keep(v, 5, v.in_weight_one, v.weight_one.at[2 * far : 6 + 2 * far])]
+    loads = []
+    if not far:
+        loads.append(keep(v, 7, v.in_weight_two, v.weight_two))
+    loads += [keep(v, 0, v.in_source, v.source.at[4:12]), keep(v, 1, v.in_weight.at[4:12], v.weight.at[4:12]),
+              keep(v, 2, v.in_guess, v.guess.at[2:14]), keep(v, 3, v.in_guess_one, v.guess_one),
+              keep(v, 4, v.in_source_one, v.source_one.at[2 * far : 6 + 2 * far]),
+              keep(v, 5, v.in_weight_one, v.weight_one.at[2 * far : 6 + 2 * far])]
     if far:
-        loads.append(keep(v, 6, v.in_diag, v.diag))
+        loads.append(keep(v, 6, v.in_diag.at[4:8], v.diag.at[6:10]))
     else:
-        loads.append(keep(v, 6, v.in_weight_two, v.weight_two))
-        loads.append(keep(v, 7, v.in_first, v.first))
+        loads.append(keep(v, 6, v.in_first, v.first))
+        v.matrix[...] = sort_matrix(512, 384, True)
     window = min(planes, WINDOW)
     begin = jnp.clip(v.where[0] - 10, 0, planes - window)
-    unpack_two(v.gathered, 0, v.source_two, planes)
+    unpack_two(v.gathered, 0, begin, v.source_two, window, False)
     copies = []
     if far:
-        unpack_two(v.gathered, 384, v.weight_two, planes)
+        unpack_two(v.gathered, 384, begin, v.weight_two, window, True)
         copies.append(keep(v, 7, v.weight_two, v.out_weight_two))
     else:
-        loads[6].wait()
-    answer = solve_two(begin, v.source_two, v.weight_two, v.ping, v.pong, window, groups)
+        loads.pop(0).wait()
+    answer = solve_two(v.where[0] - begin, v.source_two, v.weight_two, v.ping, v.pong, window, planes, groups)
     clear_edges(v.one, count)
     clear_edges(v.one_next, count)
     clear_edges(v.ea, 16)
     clear_edges(v.eb, 16)
-    for load in loads[0:6]:
+    for load in loads:
         load.wait()
 
     for k in range(4):
@@ -538,30 +553,28 @@
             x = 2 * (j - far) + half
             for r in range(4):
                 for c in range(2):
-                    v.ea[x, c, r, 8:32, :] = v.guess[x, c, r, 8:32, :] + v.one[j, c, r // 2, 8:32, :]
+                    v.ea[x, c, r, 8:32, :] = v.guess[x, c, r] + v.one[j, c, r // 2, 8:32, :]
         return 0
 
     lax.fori_loop(2, count - 2, correct, 0)
     sweep(v.ea, v.eb, v.weight, 0, v.source, 0, 5 - far, 11 + far, 4, 1, 1.0)
     sweep(v.eb, v.ea, v.weight, 0, v.source, 0, 6 - far, 10 + far, 4, 1, 1.0)
-    loads[6].wait() if far else loads[7].wait()
     return copies
 
 
 def up_first_kernel(v, planes, groups):
     copies = up_kernel(v, planes, groups, 1)
     for x in range(4):
+        values = [[], []]
         for r in range(4):
-            e = [v.ea[x + 6, c, r, 8:32, :] for c in range(2)]
-            moved = product([v.diag[x + 6, c, r] for c in range(2)], e)
-            for c in range(2):
-                value = v.source[x + 6, c, r] + neighbour(v.ea, x + 6, c, r, 4, 1) - moved[c]
-                v.packed[x, c, r] = value[8:16]
-                if x < 2:
-                    v.front[x, c, r] = value[8:16]
-                else:
-                    v.back[x - 2, c, r] = value[8:16]
-                v.first[x, c, r] = e[c][8:16]
+            e = [v.ea[x + 6, c, r, 16:24, :] for c in range(2)]
+            moved = product([v.diag[x + 6, c, r, 8:16, :] for c in range(2)], e)
+            for c in range(2):
+                total = neighbour(v.ea, x + 6, c, r, 4, 1, 16, 24)
+                values[c].append(v.source[x + 6, c, r, 8:16, :] + total - moved[c])
+                v.first[x, c, r] = e[c]
+        for c in range(2):
+            put_dense(v, x, c, values[c])
     copies.append(keep(v, 8, v.first, v.out_first))
     for copy in copies:
         copy.wait()
@@ -576,15 +589,16 @@
                 jnp.concatenate([v.first[x, c, r] + v.ea[x + 6, c, r, 16:24, :] for r in range(4)], axis=1)
             )
     values = jnp.concatenate(blocks, axis=0)
-    v.result[...] = exact_dot(values, sort_matrix(512, 384, True)).reshape(2, 4, 8, 384)
+    v.result[...] = exact_dot(values, v.matrix[...]).reshape(2, 4, 8, 384)
 
 
 def up_scratch(planes, groups, far):
     level = (8 + 2 * far, 2, 2, 40, 128)
     source = (6 + 4 * far, 2, 2, 24, 128)
     two = (min(planes, WINDOW) + 8, 4, 16 + groups, 128)
-    return dict(source=FINE, weight=FINE, guess=WIDE, guess_one=COARSE_WIDE, source_one=source, weight_one=source,
-                source_two=(planes, 4, groups, 128), weight_two=(planes, 4, groups, 128), ping=two, pong=two,
+    return dict(source=FINE, weight=FINE, guess=FINE, guess_one=COARSE_WIDE, source_one=source, weight_one=source,
+                source_two=(min(planes, WINDOW), 4, groups, 128),
+                weight_two=(min(planes, WINDOW), 4, groups, 128), ping=two, pong=two,
                 one=level, one_next=level, ea=WIDE, eb=WIDE, first=(4, 2, 4, 8, 128))
 
 
@@ -601,8 +615,8 @@
         "up_first",
         lambda v: up_first_kernel(v, planes, groups),
         dict(**up_inputs(where, gathered, messages, down, down), in_diag=(down.out_diag, HB)),
-        dict(packed=((4, 2, 4, 8, 128), VM), front=((2, 2, 4, 8, 128), VM), back=((2, 2, 4, 8, 128), VM),
-             out_first=((4, 2, 4, 8, 128), HB), out_weight_two=((planes, 4, groups, 128), HB)),
+        dict(packed=((4, 2, 3, 8, 128), VM), front=((2, 2, 3, 8, 128), VM), back=((2, 2, 3, 8, 128), VM),
+             out_first=((4, 2, 4, 8, 128), HB), out_weight_two=((min(planes, WINDOW), 4, groups, 128), HB)),
         dict(**up_scratch(planes, groups, 1), diag=FINE),
         9,
     )
@@ -616,7 +630,7 @@
         dict(**up_inputs(where, gathered, messages, down, first_down), in_weight_two=(first_up.out_weight_two, HB),
              in_first=(first_up.out_first, HB)),
         dict(result=((2, 4, 8, 384), VM)),
-        up_scratch(planes, groups, 0),
+        dict(**up_scratch(planes, groups, 0), matrix=pltpu.VMEM((512, 384), BF16)),
         8,
     ).result
 

time: 213 us -> 172 us (0.81)
  local copies, waits for them, and re-layouts: 29.6 us -> 2.48 us
  Pallas kernels: 35.9 us -> 28.6 us
  starting transfers between devices: 95.5 us -> 92 us
    unnamed x76 -> x10, local copies, waits for them, and re-layouts: 27.3 us -> 0.16 us
    pallas_call x5, Pallas kernels: 35.9 us -> 28.6 us  [run(): pl.pallas_call(lambda *refs: kernel(SimpleNamespace(**dict(zip(names, ref...]
    ppermute x22, waiting for transfers between devices: 34.8 us -> 30.8 us  [shifted(): return lax.ppermute(block, axis, pairs)]
    ppermute x22, starting transfers between devices: 61.6 us -> 58.9 us  [shifted(): return lax.ppermute(block, axis, pairs)]
  transfers between devices with their start and end apart: 24 -> 24, of which waited for: 11 -> 11; matrix products, arithmetic and copies ran while one was open for 1% -> 0% of each run, Pallas kernels for 0% -> 0%
where the time goes in v4:
time: 172 us; the launch traced here: 171 us
  starting transfers between devices  92 us (53%)
  waiting for transfers between devices  47.4 us (28%)
  Pallas kernels  28.6 us (17%)
  local copies, waits for them, and re-layouts  2.48 us (1%)
    ppermute x22, starting transfers between devices, shifted(): return lax.ppermute(block, axis, pairs)  58.9 us
    all_to_all x2, starting transfers between devices, gather_two(): lax.all_to_all(sent, ('gx', 'gy'), 0, 0).reshape(count_x, count_y, width)  33.1 us
    ppermute x22, waiting for transfers between devices, shifted(): return lax.ppermute(block, axis, pairs)  30.8 us
    pallas_call x5, Pallas kernels, run(): pl.pallas_call(lambda *refs: kernel(SimpleNamespace(**dict(zip(names, ref...  28.6 us
    all_to_all x2, waiting for transfers between devices, gather_two(): lax.all_to_all(sent, ('gx', 'gy'), 0, 0).reshape(count_x, count_y, width)  16.6 us
  transfers between devices with their start and end apart: 24, of which 11 were waited for; matrix products, arithmetic and copies ran while one was open for 0% of the time, Pallas kernels for 0%

profile of v4, /device:TPU:1, one launch (start us, length us, event | category | flops | bytes accessed | tf_op | source)
XLA Modules:
  0.0 171.0 jit_solution(5262015468160568350)
XLA Ops:
  0.0 1.5 pack.1
  1.5 5.6 %collective-permute-start = (f32[2,4,3,8,128]{4,3,2,1,0:T(8,128)S(1)}, f32[2,4,3,8,128]{4,3,2,1,0:T(8,128)S(1)}, u32[]{:S(2)}, u32[]{:S(2)}) collective-permute-start(f32[2,4,3,8,128]{4,3,2,1,0:T(8,128)S(1)} %get-tuple-element.36), channel_id=1, source_target_pairs={{0,16},{8,24},{16,32},{24,40},{32,48},{40,56},{48,64},{56,72},{64,... | collective-permute-start | bytes 294920 | tf_op jit(solution)/shard_map/ppermute | solution.py:641
  7.2 2.3 %collective-permute-start.1 = (f32[4,4,3,8,128]{4,3,2,1,0:T(8,128)S(1)}, f32[4,4,3,8,128]{4,3,2,1,0:T(8,128)S(1)}, u32[]{:S(2)}, u32[]{:S(2)}) collective-permute-start(f32[4,4,3,8,128]{4,3,2,1,0:T(8,128)S(1)} %get-tuple-element.37), channel_id=1, source_target_pairs={{0,8},{8,16},{16,24},{24,32},{32,40},{40,48},{48,56},{56,64},{64,7... | collective-permute-start | bytes 589832 | tf_op jit(solution)/shard_map/ppermute | solution.py:641
  9.5 1.3 collective-permute-start.2
  10.8 1.3 collective-permute-start.3
  12.1 0.6 collective-permute-done.1
  12.8 3.8 %collective-permute-done.2 = f32[4,4,3,8,128]{4,3,2,1,0:T(8,128)S(1)} collective-permute-done((f32[4,4,3,8,128]{4,3,2,1,0:T(8,128)S(1)}, f32[4,4,3,8,128]{4,3,2,1,0:T(8,128)S(1)}, u32[]{:S(2)}, u32[]{:S(2)}) %collective-permute-start.2) | collective-permute-done | bytes 196640 | tf_op jit(solution)/shard_map/ppermute | solution.py:641
  16.7 2.0 %collective-permute-done.3 = f32[2,4,3,8,128]{4,3,2,1,0:T(8,128)S(1)} collective-permute-done((f32[2,4,3,8,128]{4,3,2,1,0:T(8,128)S(1)}, f32[2,4,3,8,128]{4,3,2,1,0:T(8,128)S(1)}, u32[]{:S(2)}, u32[]{:S(2)}) %collective-permute-start.3) | collective-permute-done | bytes 98336 | tf_op jit(solution)/shard_map/ppermute | solution.py:641
  18.6 4.8 %collective-permute-start.4 = (f32[16,4,3,8,128]{4,3,2,1,0:T(8,128)S(1)}, f32[16,4,3,8,128]{4,3,2,1,0:T(8,128)S(1)}, u32[]{:S(2)}, u32[]{:S(2)}) collective-permute-start(f32[16,4,3,8,128]{4,3,2,1,0:T(8,128)S(1)} %constant_dynamic-update-slice_fusion.refs_0_), channel_id=1, source_target_pairs={{0,1},{1,2},{2,3},{3,4},{4,5},{5,6},{6,7},{8,9},{9,10},{10,11},{11... | collective-permute-start | bytes 2359304 | tf_op jit(solution)/shard_map/ppermute | solution.py:641
  23.4 1.9 %collective-permute-start.5 = (f32[16,4,3,8,128]{4,3,2,1,0:T(8,128)S(1)}, f32[16,4,3,8,128]{4,3,2,1,0:T(8,128)S(1)}, u32[]{:S(2)}, u32[]{:S(2)}) collective-permute-start(f32[16,4,3,8,128]{4,3,2,1,0:T(8,128)S(1)} %constant_dynamic-update-slice_fusion.refs_0_), channel_id=1, source_target_pairs={{1,0},{2,1},{3,2},{4,3},{5,4},{6,5},{7,6},{9,8},{10,9},{11,10},{12... | collective-permute-start | bytes 2359304 | tf_op jit(solution)/shard_map/ppermute | solution.py:641
  25.3 7.0 %collective-permute-done.4.refs_1_ = f32[16,4,3,8,128]{4,3,2,1,0:T(8,128)S(1)} collective-permute-done((f32[16,4,3,8,128]{4,3,2,1,0:T(8,128)S(1)}, f32[16,4,3,8,128]{4,3,2,1,0:T(8,128)S(1)}, u32[]{:S(2)}, u32[]{:S(2)}) %collective-permute-start.4) | collective-permute-done | bytes 786464 | tf_op jit(solution)/shard_map/ppermute | solution.py:641
  32.3 4.4 %collective-permute-done.5.refs_2_ = f32[16,4,3,8,128]{4,3,2,1,0:T(8,128)S(1)} collective-permute-done((f32[16,4,3,8,128]{4,3,2,1,0:T(8,128)S(1)}, f32[16,4,3,8,128]{4,3,2,1,0:T(8,128)S(1)}, u32[]{:S(2)}, u32[]{:S(2)}) %collective-permute-start.5) | collective-permute-done | bytes 786464 | tf_op jit(solution)/shard_map/ppermute | solution.py:641
  36.7 6.2 %down_first.1 = (f32[8,2,4,24,128]{4,3,2,1,0:T(8,128)}, f32[16,2,4,24,128]{4,3,2,1,0:T(8,128)}, f32[12,2,4,24,128]{4,3,2,1,0:T(8,128)}, f32[6,2,2,24,128]{4,3,2,...) custom-call(f32[16,4,3,8,128]{4,3,2,1,0:T(8,128)S(1)} %constant_dyna, ...), custom_call_target="tpu_custom_call" | custom-call | tf_op jit(solution)/shard_map/down_first/pallas_call | solution.py:29
  43.0 1.3 broadcast_in_dim.17
  44.3 17.4 %all-to-all-start = ((f32[256,1,768]{2,1,0:T(1,128)}), f32[256,1,768]{2,1,0:T(1,128)S(1)}, u32[]{:S(2)}, u32[]{:S(2)}) async-start(f32[256,1,768]{2,1,0:T(1,128)} %broadcast_in_dim.17), calls=%async_computation | async-start | bytes 1572864 | tf_op jit(solution)/shard_map/all_to_all | solution.py:648
  61.7 4.8 %collective-permute-start.10 = (f32[2,8,128]{2,1,0:T(8,128)S(1)}, f32[2,8,128]{2,1,0:T(8,128)S(1)}, u32[]{:S(2)}, u32[]{:S(2)}) collective-permute-start(f32[2,8,128]{2,1,0:T(8,128)S(1)} %get-tuple-element.44), channel_id=1, source_target_pairs={{0,16},{8,24},{16,32},{24,40},{32,48},{40,56},{48,64},{56,72},{64,... | collective-permute-start | bytes 24584 | tf_op jit(solution)/shard_map/ppermute | solution.py:641
  66.5 3.7 %collective-permute-start.6 = (f32[8,8,128]{2,1,0:T(8,128)S(1)}, f32[8,8,128]{2,1,0:T(8,128)S(1)}, u32[]{:S(2)}, u32[]{:S(2)}) collective-permute-start(f32[8,8,128]{2,1,0:T(8,128)S(1)} %get-tuple-element.41), channel_id=1, source_target_pairs={{0,1},{1,2},{2,3},{3,4},{4,5},{5,6},{6,7},{8,9},{9,10},{10,11},{11... | collective-permute-start | bytes 98312 | tf_op jit(solution)/shard_map/ppermute | solution.py:641
  70.1 1.9 %collective-permute-start.7 = (f32[8,8,128]{2,1,0:T(8,128)S(1)}, f32[8,8,128]{2,1,0:T(8,128)S(1)}, u32[]{:S(2)}, u32[]{:S(2)}) collective-permute-start(f32[8,8,128]{2,1,0:T(8,128)S(1)} %get-tuple-element.41), channel_id=1, source_target_pairs={{1,0},{2,1},{3,2},{4,3},{5,4},{6,5},{7,6},{9,8},{10,9},{11,10},{12... | collective-permute-start | bytes 98312 | tf_op jit(solution)/shard_map/ppermute | solution.py:641
  72.1 2.3 %collective-permute-start.8 = (f32[16,8,128]{2,1,0:T(8,128)S(1)}, f32[16,8,128]{2,1,0:T(8,128)S(1)}, u32[]{:S(2)}, u32[]{:S(2)}) collective-permute-start(f32[16,8,128]{2,1,0:T(8,128)S(1)} %get-tuple-element.42), channel_id=1, source_target_pairs={{0,8},{8,16},{16,24},{24,32},{32,40},{40,48},{48,56},{56,64},{64,7... | collective-permute-start | bytes 196616 | tf_op jit(solution)/shard_map/ppermute | solution.py:641
  74.3 1.3 collective-permute-start.9
  75.6 0.0 collective-permute-done.10.refs_6_
  75.6 1.3 collective-permute-start.11
  76.9 0.1 pad_add_fusion.refs_0_
  77.0 9.7 %all-to-all-done = f32[256,1,768]{2,1,0:T(1,128)S(1)} async-done(((f32[256,1,768]{2,1,0:T(1,128)}), f32[256,1,768]{2,1,0:T(1,128)S(1)}, u32[]{:S(2)}, u32[]{:S(2)}) %all-to-all-start) | async-done | bytes 786464 | tf_op jit(solution)/shard_map/all_to_all | solution.py:648
  86.7 0.1 copy.9
  86.8 0.0 collective-permute-done.11.refs_7_
  86.8 0.0 collective-permute-done.6.refs_2_
  86.8 0.0 collective-permute-done.8.refs_4_
  86.8 7.9 %up_first.1 = (f32[4,2,3,8,128]{4,3,2,1,0:T(8,128)S(1)}, f32[2,2,3,8,128]{4,3,2,1,0:T(8,128)S(1)}, f32[2,2,3,8,128]{4,3,2,1,0:T(8,128)S(1)}, f32[4,2,4,8,128]{4,3,2,1,0:T(8,128)}, f32[21,4,8,128]{3,2,1,0:T(8,128)}) custom-call(s32[2]{0:T(128)S(1)} %pad_add_fusion.refs_0_, f32[32,8,768]{2,1,0:T(8,128)S(1)} %bitcast.8, ...), custom_call_target="tpu_custom_call" | custom-call | tf_op jit(solution)/shard_map/up_first/pallas_call | solution.py:29
  94.7 4.3 %collective-permute-start.12 = (f32[2,2,3,8,128]{4,3,2,1,0:T(8,128)S(1)}, f32[2,2,3,8,128]{4,3,2,1,0:T(8,128)S(1)}, u32[]{:S(2)}, u32[]{:S(2)}) collective-permute-start(f32[2,2,3,8,128]{4,3,2,1,0:T(8,128)S(1)} %get-tuple-element.53), channel_id=1, source_target_pairs={{0,16},{8,24},{16,32},{24,40},{32,48},{40,56},{48,64},{56,72},{64,... | collective-permute-start | bytes 147464 | tf_op jit(solution)/shard_map/ppermute | solution.py:641
  99.1 1.6 collective-permute-start.13
  100.7 1.3 collective-permute-start.14
  102.0 1.3 collective-permute-start.15
  103.4 2.7 %collective-permute-done.14 = f32[4,2,3,8,128]{4,3,2,1,0:T(8,128)S(1)} collective-permute-done((f32[4,2,3,8,128]{4,3,2,1,0:T(8,128)S(1)}, f32[4,2,3,8,128]{4,3,2,1,0:T(8,128)S(1)}, u32[]{:S(2)}, u32[]{:S(2)}) %collective-permute-start.14) | collective-permute-done | bytes 98336 | tf_op jit(solution)/shard_map/ppermute | solution.py:641
  106.1 3.1 %collective-permute-done.15 = f32[2,2,3,8,128]{4,3,2,1,0:T(8,128)S(1)} collective-permute-done((f32[2,2,3,8,128]{4,3,2,1,0:T(8,128)S(1)}, f32[2,2,3,8,128]{4,3,2,1,0:T(8,128)S(1)}, u32[]{:S(2)}, u32[]{:S(2)}) %collective-permute-start.15) | collective-permute-done | bytes 49184 | tf_op jit(solution)/shard_map/ppermute | solution.py:641
  109.2 5.9 %collective-permute-start.16 = (f32[16,2,3,8,128]{4,3,2,1,0:T(8,128)S(1)}, f32[16,2,3,8,128]{4,3,2,1,0:T(8,128)S(1)}, u32[]{:S(2)}, u32[]{:S(2)}) collective-permute-start(f32[16,2,3,8,128]{4,3,2,1,0:T(8,128)S(1)} %constant_dynamic-update-slice_fusion.5.refs_0_), channel_id=1, source_target_pairs={{0,1},{1,2},{2,3},{3,4},{4,5},{5,6},{6,7},{8,9},{9,10},{10,11},{11... | collective-permute-start | bytes 1179656 | tf_op jit(solution)/shard_map/ppermute | solution.py:641
  115.1 1.9 %collective-permute-start.17 = (f32[16,2,3,8,128]{4,3,2,1,0:T(8,128)S(1)}, f32[16,2,3,8,128]{4,3,2,1,0:T(8,128)S(1)}, u32[]{:S(2)}, u32[]{:S(2)}) collective-permute-start(f32[16,2,3,8,128]{4,3,2,1,0:T(8,128)S(1)} %constant_dynamic-update-slice_fusion.5.refs_0_), channel_id=1, source_target_pairs={{1,0},{2,1},{3,2},{4,3},{5,4},{6,5},{7,6},{9,8},{10,9},{11,10},{12... | collective-permute-start | bytes 1179656 | tf_op jit(solution)/shard_map/ppermute | solution.py:641
  117.0 2.8 %collective-permute-done.16.refs_1_ = f32[16,2,3,8,128]{4,3,2,1,0:T(8,128)S(1)} collective-permute-done((f32[16,2,3,8,128]{4,3,2,1,0:T(8,128)S(1)}, f32[16,2,3,8,128]{4,3,2,1,0:T(8,128)S(1)}, u32[]{:S(2)}, u32[]{:S(2)}) %collective-permute-start.16) | collective-permute-done | bytes 393248 | tf_op jit(solution)/shard_map/ppermute | solution.py:641
  119.8 4.4 %collective-permute-done.17.refs_2_ = f32[16,2,3,8,128]{4,3,2,1,0:T(8,128)S(1)} collective-permute-done((f32[16,2,3,8,128]{4,3,2,1,0:T(8,128)S(1)}, f32[16,2,3,8,128]{4,3,2,1,0:T(8,128)S(1)}, u32[]{:S(2)}, u32[]{:S(2)}) %collective-permute-start.17) | collective-permute-done | bytes 393248 | tf_op jit(solution)/shard_map/ppermute | solution.py:641
  124.2 5.3 %down_second.1 = (f32[8,2,4,24,128]{4,3,2,1,0:T(8,128)}, f32[12,2,4,24,128]{4,3,2,1,0:T(8,128)}, f32[6,2,2,24,128]{4,3,2,1,0:T(8,128)}, f32[6,2,2,40,128]{4,3,2,...) custom-call(f32[16,2,3,8,128]{4,3,2,1,0:T(8,128)S(1)} %constant_dyna, ...), custom_call_target="tpu_custom_call" | custom-call | tf_op jit(solution)/shard_map/down_second/pallas_call | solution.py:29
  129.5 1.0 broadcast_in_dim.19
  130.5 15.7 %all-to-all-start.1 = ((f32[256,1,384]{2,1,0:T(1,128)}), f32[256,1,384]{2,1,0:T(1,128)S(1)}, u32[]{:S(2)}, u32[]{:S(2)}) async-start(f32[256,1,384]{2,1,0:T(1,128)} %broadcast_in_dim.19), calls=%async_computation.1 | async-start | bytes 786432 | tf_op jit(solution)/shard_map/all_to_all | solution.py:648
  146.2 3.3 %collective-permute-start.20 = (f32[12,8,128]{2,1,0:T(8,128)S(1)}, f32[12,8,128]{2,1,0:T(8,128)S(1)}, u32[]{:S(2)}, u32[]{:S(2)}) collective-permute-start(f32[12,8,128]{2,1,0:T(8,128)S(1)} %get-tuple-element.59), channel_id=1, source_target_pairs={{0,8},{8,16},{16,24},{24,32},{32,40},{40,48},{48,56},{56,64},{64,7... | collective-permute-start | bytes 147464 | tf_op jit(solution)/shard_map/ppermute | solution.py:641
  149.5 1.3 collective-permute-start.21
  150.8 3.7 %collective-permute-start.18 = (f32[8,8,128]{2,1,0:T(8,128)S(1)}, f32[8,8,128]{2,1,0:T(8,128)S(1)}, u32[]{:S(2)}, u32[]{:S(2)}) collective-permute-start(f32[8,8,128]{2,1,0:T(8,128)S(1)} %get-tuple-element.58), channel_id=1, source_target_pairs={{0,1},{1,2},{2,3},{3,4},{4,5},{5,6},{6,7},{8,9},{9,10},{10,11},{11... | collective-permute-start | bytes 98312 | tf_op jit(solution)/shard_map/ppermute | solution.py:641
  154.4 1.9 %collective-permute-start.19 = (f32[8,8,128]{2,1,0:T(8,128)S(1)}, f32[8,8,128]{2,1,0:T(8,128)S(1)}, u32[]{:S(2)}, u32[]{:S(2)}) collective-permute-start(f32[8,8,128]{2,1,0:T(8,128)S(1)} %get-tuple-element.58), channel_id=1, source_target_pairs={{1,0},{2,1},{3,2},{4,3},{5,4},{6,5},{7,6},{9,8},{10,9},{11,10},{12... | collective-permute-start | bytes 98312 | tf_op jit(solution)/shard_map/ppermute | solution.py:641
  156.4 6.9 %all-to-all-done.1 = f32[256,1,384]{2,1,0:T(1,128)S(1)} async-done(((f32[256,1,384]{2,1,0:T(1,128)}), f32[256,1,384]{2,1,0:T(1,128)S(1)}, u32[]{:S(2)}, u32[]{:S(2)}) %all-to-all-start.1) | async-done | bytes 393248 | tf_op jit(solution)/shard_map/all_to_all | solution.py:648
  163.4 7.7 %up_second.1 = f32[2,4,8,384]{3,2,1,0:T(8,128)} custom-call(s32[2]{0:T(128)S(1)} %pad_add_fusion.refs_0_, f32[32,8,384]{2,1,0:T(8,128)S(1)} %bitcast.9, f32[8,8,128]{2,1,0:T(8,128)S(1)} %collective-permute-done.18.refs_2_, f32[8,8,128]{2,1,0:T(8,128)S(1)} %collective-permute-done.19.refs_3_, f32[12,8,128]{2,1,0:T(8,128)S(1)} %collective-permute-done.20.refs_4_, ...), custom_call_target="tpu_custom_call" | custom-call | tf_op jit(solution)/shard_map/up_second/pallas_call | solution.py:29
  (22 shorter events, 0.2 us)
Async XLA Ops:
  1.5 10.6 %collective-permute-start = (f32[2,4,3,8,128]{4,3,2,1,0:T(8,128)S(1)}, f32[2,4,3,8,128]{4,3,2,1,0:T(8,128)S(1)}, u32[]{:S(2)}, u32[]{:S(2)}) collective-permute-start(f32[2,4,3,8,128]{4,3,2,1,0:T(8,128)S(1)} %get-tuple-element.36), channel_id=1, source_target_pairs={{0,16},{8,24},{16,32},{24,40},{32,48},{40,56},{48,64},{56,72},{64,... | collective-permute-start | bytes 294920 | tf_op jit(solution)/shard_map/ppermute | solution.py:641
  7.2 5.6 %collective-permute-start.1 = (f32[4,4,3,8,128]{4,3,2,1,0:T(8,128)S(1)}, f32[4,4,3,8,128]{4,3,2,1,0:T(8,128)S(1)}, u32[]{:S(2)}, u32[]{:S(2)}) collective-permute-start(f32[4,4,3,8,128]{4,3,2,1,0:T(8,128)S(1)} %get-tuple-element.37), channel_id=1, source_target_pairs={{0,8},{8,16},{16,24},{24,32},{32,40},{40,48},{48,56},{56,64},{64,7... | collective-permute-start | bytes 589832 | tf_op jit(solution)/shard_map/ppermute | solution.py:641
  9.5 7.1 %collective-permute-start.2 = (f32[4,4,3,8,128]{4,3,2,1,0:T(8,128)S(1)}, f32[4,4,3,8,128]{4,3,2,1,0:T(8,128)S(1)}, u32[]{:S(2)}, u32[]{:S(2)}) collective-permute-start(f32[4,4,3,8,128]{4,3,2,1,0:T(8,128)S(1)} %get-tuple-element.37), channel_id=1, source_target_pairs={{8,0},{16,8},{24,16},{32,24},{40,32},{48,40},{56,48},{64,56},{72,6... | collective-permute-start | bytes 589832 | tf_op jit(solution)/shard_map/ppermute | solution.py:641
  10.8 7.8 %collective-permute-start.3 = (f32[2,4,3,8,128]{4,3,2,1,0:T(8,128)S(1)}, f32[2,4,3,8,128]{4,3,2,1,0:T(8,128)S(1)}, u32[]{:S(2)}, u32[]{:S(2)}) collective-permute-start(f32[2,4,3,8,128]{4,3,2,1,0:T(8,128)S(1)} %get-tuple-element.38), channel_id=1, source_target_pairs={{16,0},{24,8},{32,16},{40,24},{48,32},{56,40},{64,48},{72,56},{80,... | collective-permute-start | bytes 294920 | tf_op jit(solution)/shard_map/ppermute | solution.py:641
  18.6 13.7 %collective-permute-start.4 = (f32[16,4,3,8,128]{4,3,2,1,0:T(8,128)S(1)}, f32[16,4,3,8,128]{4,3,2,1,0:T(8,128)S(1)}, u32[]{:S(2)}, u32[]{:S(2)}) collective-permute-start(f32[16,4,3,8,128]{4,3,2,1,0:T(8,128)S(1)} %constant_dynamic-update-slice_fusion.refs_0_), channel_id=1, source_target_pairs={{0,1},{1,2},{2,3},{3,4},{4,5},{5,6},{6,7},{8,9},{9,10},{10,11},{11... | collective-permute-start | bytes 2359304 | tf_op jit(solution)/shard_map/ppermute | solution.py:641
  23.4 13.3 %collective-permute-start.5 = (f32[16,4,3,8,128]{4,3,2,1,0:T(8,128)S(1)}, f32[16,4,3,8,128]{4,3,2,1,0:T(8,128)S(1)}, u32[]{:S(2)}, u32[]{:S(2)}) collective-permute-start(f32[16,4,3,8,128]{4,3,2,1,0:T(8,128)S(1)} %constant_dynamic-update-slice_fusion.refs_0_), channel_id=1, source_target_pairs={{1,0},{2,1},{3,2},{4,3},{5,4},{6,5},{7,6},{9,8},{10,9},{11,10},{12... | collective-permute-start | bytes 2359304 | tf_op jit(solution)/shard_map/ppermute | solution.py:641
  44.3 42.5 %all-to-all-start = ((f32[256,1,768]{2,1,0:T(1,128)}), f32[256,1,768]{2,1,0:T(1,128)S(1)}, u32[]{:S(2)}, u32[]{:S(2)}) async-start(f32[256,1,768]{2,1,0:T(1,128)} %broadcast_in_dim.17), calls=%async_computation | async-start | bytes 1572864 | tf_op jit(solution)/shard_map/all_to_all | solution.py:648
  61.7 13.9 %collective-permute-start.10 = (f32[2,8,128]{2,1,0:T(8,128)S(1)}, f32[2,8,128]{2,1,0:T(8,128)S(1)}, u32[]{:S(2)}, u32[]{:S(2)}) collective-permute-start(f32[2,8,128]{2,1,0:T(8,128)S(1)} %get-tuple-element.44), channel_id=1, source_target_pairs={{0,16},{8,24},{16,32},{24,40},{32,48},{40,56},{48,64},{56,72},{64,... | collective-permute-start | bytes 24584 | tf_op jit(solution)/shard_map/ppermute | solution.py:641
  66.5 20.3 %collective-permute-start.6 = (f32[8,8,128]{2,1,0:T(8,128)S(1)}, f32[8,8,128]{2,1,0:T(8,128)S(1)}, u32[]{:S(2)}, u32[]{:S(2)}) collective-permute-start(f32[8,8,128]{2,1,0:T(8,128)S(1)} %get-tuple-element.41), channel_id=1, source_target_pairs={{0,1},{1,2},{2,3},{3,4},{4,5},{5,6},{6,7},{8,9},{9,10},{10,11},{11... | collective-permute-start | bytes 98312 | tf_op jit(solution)/shard_map/ppermute | solution.py:641
  70.1 16.7 %collective-permute-start.7 = (f32[8,8,128]{2,1,0:T(8,128)S(1)}, f32[8,8,128]{2,1,0:T(8,128)S(1)}, u32[]{:S(2)}, u32[]{:S(2)}) collective-permute-start(f32[8,8,128]{2,1,0:T(8,128)S(1)} %get-tuple-element.41), channel_id=1, source_target_pairs={{1,0},{2,1},{3,2},{4,3},{5,4},{6,5},{7,6},{9,8},{10,9},{11,10},{12... | collective-permute-start | bytes 98312 | tf_op jit(solution)/shard_map/ppermute | solution.py:641
  72.1 14.8 %collective-permute-start.8 = (f32[16,8,128]{2,1,0:T(8,128)S(1)}, f32[16,8,128]{2,1,0:T(8,128)S(1)}, u32[]{:S(2)}, u32[]{:S(2)}) collective-permute-start(f32[16,8,128]{2,1,0:T(8,128)S(1)} %get-tuple-element.42), channel_id=1, source_target_pairs={{0,8},{8,16},{16,24},{24,32},{32,40},{40,48},{48,56},{56,64},{64,7... | collective-permute-start | bytes 196616 | tf_op jit(solution)/shard_map/ppermute | solution.py:641
  74.3 12.5 %collective-permute-start.9 = (f32[16,8,128]{2,1,0:T(8,128)S(1)}, f32[16,8,128]{2,1,0:T(8,128)S(1)}, u32[]{:S(2)}, u32[]{:S(2)}) collective-permute-start(f32[16,8,128]{2,1,0:T(8,128)S(1)} %get-tuple-element.43), channel_id=1, source_target_pairs={{8,0},{16,8},{24,16},{32,24},{40,32},{48,40},{56,48},{64,56},{72,6... | collective-permute-start | bytes 196616 | tf_op jit(solution)/shard_map/ppermute | solution.py:641
  75.6 11.2 %collective-permute-start.11 = (f32[2,8,128]{2,1,0:T(8,128)S(1)}, f32[2,8,128]{2,1,0:T(8,128)S(1)}, u32[]{:S(2)}, u32[]{:S(2)}) collective-permute-start(f32[2,8,128]{2,1,0:T(8,128)S(1)} %get-tuple-element.45), channel_id=1, source_target_pairs={{16,0},{24,8},{32,16},{40,24},{48,32},{56,40},{64,48},{72,56},{80,... | collective-permute-start | bytes 24584 | tf_op jit(solution)/shard_map/ppermute | solution.py:641
  94.7 8.6 %collective-permute-start.12 = (f32[2,2,3,8,128]{4,3,2,1,0:T(8,128)S(1)}, f32[2,2,3,8,128]{4,3,2,1,0:T(8,128)S(1)}, u32[]{:S(2)}, u32[]{:S(2)}) collective-permute-start(f32[2,2,3,8,128]{4,3,2,1,0:T(8,128)S(1)} %get-tuple-element.53), channel_id=1, source_target_pairs={{0,16},{8,24},{16,32},{24,40},{32,48},{40,56},{48,64},{56,72},{64,... | collective-permute-start | bytes 147464 | tf_op jit(solution)/shard_map/ppermute | solution.py:641
  99.1 4.2 %collective-permute-start.13 = (f32[4,2,3,8,128]{4,3,2,1,0:T(8,128)S(1)}, f32[4,2,3,8,128]{4,3,2,1,0:T(8,128)S(1)}, u32[]{:S(2)}, u32[]{:S(2)}) collective-permute-start(f32[4,2,3,8,128]{4,3,2,1,0:T(8,128)S(1)} %get-tuple-element.54), channel_id=1, source_target_pairs={{0,8},{8,16},{16,24},{24,32},{32,40},{40,48},{48,56},{56,64},{64,7... | collective-permute-start | bytes 294920 | tf_op jit(solution)/shard_map/ppermute | solution.py:641
  100.7 5.4 %collective-permute-start.14 = (f32[4,2,3,8,128]{4,3,2,1,0:T(8,128)S(1)}, f32[4,2,3,8,128]{4,3,2,1,0:T(8,128)S(1)}, u32[]{:S(2)}, u32[]{:S(2)}) collective-permute-start(f32[4,2,3,8,128]{4,3,2,1,0:T(8,128)S(1)} %get-tuple-element.54), channel_id=1, source_target_pairs={{8,0},{16,8},{24,16},{32,24},{40,32},{48,40},{56,48},{64,56},{72,6... | collective-permute-start | bytes 294920 | tf_op jit(solution)/shard_map/ppermute | solution.py:641
  102.0 7.2 %collective-permute-start.15 = (f32[2,2,3,8,128]{4,3,2,1,0:T(8,128)S(1)}, f32[2,2,3,8,128]{4,3,2,1,0:T(8,128)S(1)}, u32[]{:S(2)}, u32[]{:S(2)}) collective-permute-start(f32[2,2,3,8,128]{4,3,2,1,0:T(8,128)S(1)} %get-tuple-element.55), channel_id=1, source_target_pairs={{16,0},{24,8},{32,16},{40,24},{48,32},{56,40},{64,48},{72,56},{80,... | collective-permute-start | bytes 147464 | tf_op jit(solution)/shard_map/ppermute | solution.py:641
  109.2 10.6 %collective-permute-start.16 = (f32[16,2,3,8,128]{4,3,2,1,0:T(8,128)S(1)}, f32[16,2,3,8,128]{4,3,2,1,0:T(8,128)S(1)}, u32[]{:S(2)}, u32[]{:S(2)}) collective-permute-start(f32[16,2,3,8,128]{4,3,2,1,0:T(8,128)S(1)} %constant_dynamic-update-slice_fusion.5.refs_0_), channel_id=1, source_target_pairs={{0,1},{1,2},{2,3},{3,4},{4,5},{5,6},{6,7},{8,9},{9,10},{10,11},{11... | collective-permute-start | bytes 1179656 | tf_op jit(solution)/shard_map/ppermute | solution.py:641
  115.1 9.1 %collective-permute-start.17 = (f32[16,2,3,8,128]{4,3,2,1,0:T(8,128)S(1)}, f32[16,2,3,8,128]{4,3,2,1,0:T(8,128)S(1)}, u32[]{:S(2)}, u32[]{:S(2)}) collective-permute-start(f32[16,2,3,8,128]{4,3,2,1,0:T(8,128)S(1)} %constant_dynamic-update-slice_fusion.5.refs_0_), channel_id=1, source_target_pairs={{1,0},{2,1},{3,2},{4,3},{5,4},{6,5},{7,6},{9,8},{10,9},{11,10},{12... | collective-permute-start | bytes 1179656 | tf_op jit(solution)/shard_map/ppermute | solution.py:641
  130.5 32.8 %all-to-all-start.1 = ((f32[256,1,384]{2,1,0:T(1,128)}), f32[256,1,384]{2,1,0:T(1,128)S(1)}, u32[]{:S(2)}, u32[]{:S(2)}) async-start(f32[256,1,384]{2,1,0:T(1,128)} %broadcast_in_dim.19), calls=%async_computation.1 | async-start | bytes 786432 | tf_op jit(solution)/shard_map/all_to_all | solution.py:648
  146.2 17.1 %collective-permute-start.20 = (f32[12,8,128]{2,1,0:T(8,128)S(1)}, f32[12,8,128]{2,1,0:T(8,128)S(1)}, u32[]{:S(2)}, u32[]{:S(2)}) collective-permute-start(f32[12,8,128]{2,1,0:T(8,128)S(1)} %get-tuple-element.59), channel_id=1, source_target_pairs={{0,8},{8,16},{16,24},{24,32},{32,40},{40,48},{48,56},{56,64},{64,7... | collective-permute-start | bytes 147464 | tf_op jit(solution)/shard_map/ppermute | solution.py:641
  149.5 13.9 %collective-permute-start.21 = (f32[12,8,128]{2,1,0:T(8,128)S(1)}, f32[12,8,128]{2,1,0:T(8,128)S(1)}, u32[]{:S(2)}, u32[]{:S(2)}) collective-permute-start(f32[12,8,128]{2,1,0:T(8,128)S(1)} %get-tuple-element.60), channel_id=1, source_target_pairs={{8,0},{16,8},{24,16},{32,24},{40,32},{48,40},{56,48},{64,56},{72,6... | collective-permute-start | bytes 147464 | tf_op jit(solution)/shard_map/ppermute | solution.py:641
  150.8 12.6 %collective-permute-start.18 = (f32[8,8,128]{2,1,0:T(8,128)S(1)}, f32[8,8,128]{2,1,0:T(8,128)S(1)}, u32[]{:S(2)}, u32[]{:S(2)}) collective-permute-start(f32[8,8,128]{2,1,0:T(8,128)S(1)} %get-tuple-element.58), channel_id=1, source_target_pairs={{0,1},{1,2},{2,3},{3,4},{4,5},{5,6},{6,7},{8,9},{9,10},{10,11},{11... | collective-permute-start | bytes 98312 | tf_op jit(solution)/shard_map/ppermute | solution.py:641
  154.4 8.9 %collective-permute-start.19 = (f32[8,8,128]{2,1,0:T(8,128)S(1)}, f32[8,8,128]{2,1,0:T(8,128)S(1)}, u32[]{:S(2)}, u32[]{:S(2)}) collective-permute-start(f32[8,8,128]{2,1,0:T(8,128)S(1)} %get-tuple-element.58), channel_id=1, source_target_pairs={{1,0},{2,1},{3,2},{4,3},{5,4},{6,5},{7,6},{9,8},{10,9},{11,10},{12... | collective-permute-start | bytes 98312 | tf_op jit(solution)/shard_map/ppermute | solution.py:641

commit v5 on v4

--- a/solution.py
+++ b/solution.py
@@ -145,10 +145,11 @@
 def put_dense(v, x, c, parts):
     for n, tile in enumerate(dense(parts)):
         v.packed[x, c, n] = tile
-        if x < 2:
+        depth = v.front.shape[0]
+        if x < depth:
             v.front[x, c, n] = tile
-        else:
-            v.back[x - 2, c, n] = tile
+        if x >= 4 - depth:
+            v.back[x - 4 + depth, c, n] = tile
 
 
 def pack_kernel(v):
@@ -230,7 +231,7 @@
         target[n, s * 4 : s * 4 + 4, :] = source[k, c, s, pl.ds(top + 8 * tile, 4, 2), :]
 
 
-def down_body(v, source, weight, diag, weight_one, diag_one, first_copy, sends_weight):
+def down_body(v, source, weight, diag, weight_one, diag_one, first_copy):
     def first(x, _):
         for r in range(4):
             e = product([weight[x, c, r] for c in range(2)], [source[x, c, r] for c in range(2)])
@@ -290,12 +291,6 @@
                 n = (k * 3 + tile) * 2 + c
                 squeeze_rows(v.send_up, n, v.guess_one, k + 1, c, tile, 8)
                 squeeze_rows(v.send_down, n, v.guess_one, k + 3, c, tile, 8)
-        if sends_weight:
-            for target, k in ((v.send_up, 1), (v.send_down, 4)):
-                squeeze_rows(target, 12 + c, v.source_one, k, c, 1, 0)
-                squeeze_rows(target, 14 + c, weight_one, k, c, 1, 0)
-            squeeze_rows(v.send_far_up, c, v.guess_one, 2, c, 1, 8)
-            squeeze_rows(v.send_far_down, c, v.guess_one, 3, c, 1, 8)
     return copies
 
 
@@ -327,7 +322,7 @@
         return 0
 
     lax.fori_loop(0, 16, filled, 0)
-    copies = [keep(v, 0, v.source.at[4:12], v.out_source), keep(v, 1, v.weight, v.out_weight)]
+    copies = [keep(v, 0, v.source, v.out_source), keep(v, 1, v.weight, v.out_weight)]
 
     def coarse(k, _):
         for s in range(2):
@@ -355,9 +350,9 @@
         return 0
 
     lax.fori_loop(0, 16, turn, 0)
-    copies += [keep(v, 2, v.diag.at[2:14], v.out_diag), keep(v, 3, v.weight_one, v.out_weight_one),
+    copies += [keep(v, 2, v.diag, v.out_diag), keep(v, 3, v.weight_one, v.out_weight_one),
                keep(v, 4, v.diag_one, v.out_diag_one)]
-    copies += down_body(v, v.source, v.weight, v.diag, v.weight_one, v.diag_one, 5, True)
+    copies += down_body(v, v.source, v.weight, v.diag, v.weight_one, v.diag_one, 5)
     v.two[0:1, 384:768] = v.inverse_two[...]
     for copy in copies:
         copy.wait()
@@ -368,30 +363,52 @@
         "down_first",
         down_first_kernel,
         dict(mid=(mid, VM), low=(low, VM), high=(high, VM), inverse_two=(inverse_two, VM)),
-        dict(out_source=(PART, HB), out_weight=(FINE, HB), out_diag=(INNER, HB), out_weight_one=(COARSE, HB),
+        dict(out_source=(FINE, HB), out_weight=(FINE, HB), out_diag=(FINE, HB), out_weight_one=(COARSE, HB),
              out_diag_one=(COARSE, HB), out_guess=(INNER, HB), out_source_one=(COARSE, HB), out_guess_one=(COARSE_WIDE, HB),
-             two=((1, 768), VM), send_y=((8, 8, 128), VM), send_up=((16, 8, 128), VM), send_down=((16, 8, 128), VM),
-             send_far_up=((2, 8, 128), VM), send_far_down=((2, 8, 128), VM)),
+             two=((1, 768), VM), send_y=((8, 8, 128), VM), send_up=((12, 8, 128), VM), send_down=((12, 8, 128), VM)),
         dict(source=FINE, weight=FINE, diag=FINE, weight_one=COARSE, diag_one=COARSE, start=WIDE, guess=WIDE,
              start_one=COARSE_WIDE, source_one=COARSE, guess_one=COARSE_WIDE, temp=(2, 40, 128)),
         8,
     )
 
 
+EDGE = 18 * 2 * 3
+
+
 def down_second_kernel(v):
-    loads = [keep(v, 0, v.in_weight, v.weight), keep(v, 1, v.in_diag, v.diag.at[2:14]),
-             keep(v, 2, v.in_weight_one, v.weight_one), keep(v, 3, v.in_diag_one, v.diag_one)]
+    loads = [keep(v, 0, v.in_right, v.right), keep(v, 1, v.in_diag, v.diag), keep(v, 2, v.in_weight, v.weight),
+             keep(v, 3, v.in_weight_one, v.weight_one), keep(v, 4, v.in_diag_one, v.diag_one)]
     clear_down(v)
+    clear_edges(v.first, 18)
 
     def filled(x, _):
-        fill(v, v.source, 0, 2, x)
-        return 0
-
-    lax.fori_loop(0, 16, filled, 0)
-    copies = [keep(v, 4, v.source.at[4:12], v.out_source)]
+        for c in range(2):
+            for tile, ref in enumerate((v.low, v.mid, v.high)):
+                parts = loose([ref[(x * 2 + c) * 3 + n] for n in range(3)], True)
+                for r in range(4):
+                    v.first[x, c, r, 8 + 8 * tile : 16 + 8 * tile, :] = parts[r]
+        return 0
+
+    lax.fori_loop(0, 18, filled, 0)
+    for x in range(4):
+        for c in range(2):
+            for r in range(4):
+                row = slice(c * 4 + r, c * 4 + r + 1)
+                v.first[x + 7, c, r, 7:8, :] = v.low[EDGE + x, row]
+                v.first[x + 7, c, r, 32:33, :] = v.high[EDGE + 4 + x, row]
     for load in loads:
         load.wait()
-    copies += down_body(v, v.source, v.weight, v.diag, v.weight_one, v.diag_one, 5, False)
+
+    def residual(x, _):
+        for r in range(4):
+            moved = product([v.diag[x, c, r] for c in range(2)], [v.first[x + 1, c, r, 8:32, :] for c in range(2)])
+            for c in range(2):
+                v.source[x, c, r] = v.right[x, c, r] + neighbour(v.first, x + 1, c, r, 4, 1) - moved[c]
+        return 0
+
+    lax.fori_loop(0, 16, residual, 0)
+    copies = [keep(v, 8, v.source.at[4:12], v.out_source)]
+    copies += down_body(v, v.source, v.weight, v.diag, v.weight_one, v.diag_one, 5)
     for copy in copies:
         copy.wait()
 
@@ -400,13 +417,14 @@
     return run(
         "down_second",
         down_second_kernel,
-        dict(mid=(mid, VM), low=(low, VM), high=(high, VM), in_weight=(old.out_weight, HB), in_diag=(old.out_diag, HB),
-             in_weight_one=(old.out_weight_one, HB), in_diag_one=(old.out_diag_one, HB)),
+        dict(mid=(mid, VM), low=(low, VM), high=(high, VM), in_right=(old.out_source, HB), in_weight=(old.out_weight, HB),
+             in_diag=(old.out_diag, HB), in_weight_one=(old.out_weight_one, HB), in_diag_one=(old.out_diag_one, HB)),
         dict(out_source=(PART, HB), out_guess=(INNER, HB), out_source_one=(COARSE, HB), out_guess_one=(COARSE_WIDE, HB),
              two=((1, 384), VM), send_y=((8, 8, 128), VM), send_up=((12, 8, 128), VM), send_down=((12, 8, 128), VM)),
         dict(source=FINE, weight=FINE, diag=FINE, weight_one=COARSE, diag_one=COARSE, start=WIDE, guess=WIDE,
-             start_one=COARSE_WIDE, source_one=COARSE, guess_one=COARSE_WIDE, temp=(2, 40, 128)),
-        8,
+             start_one=COARSE_WIDE, source_one=COARSE, guess_one=COARSE_WIDE, temp=(2, 40, 128),
+             right=FINE, first=(18, 2, 4, 40, 128)),
+        9,
     )
 
 
@@ -488,29 +506,27 @@
                     one[j, c, s, at, :] = one[j, c, s, at, :] + value
 
 
-def up_kernel(v, planes, groups, far):
-    count = 8 + 2 * far
+def up_kernel(v, planes, groups, second):
+    count = 8
     loads = []
-    if not far:
+    if second:
         loads.append(keep(v, 7, v.in_weight_two, v.weight_two))
-    loads += [keep(v, 0, v.in_source, v.source.at[4:12]), keep(v, 1, v.in_weight.at[4:12], v.weight.at[4:12]),
+    own = v.in_source if second else v.in_source.at[4:12]
+    loads += [keep(v, 0, own, v.source.at[4:12]), keep(v, 1, v.in_weight.at[4:12], v.weight.at[4:12]),
               keep(v, 2, v.in_guess, v.guess.at[2:14]), keep(v, 3, v.in_guess_one, v.guess_one),
-              keep(v, 4, v.in_source_one, v.source_one.at[2 * far : 6 + 2 * far]),
-              keep(v, 5, v.in_weight_one, v.weight_one.at[2 * far : 6 + 2 * far])]
-    if far:
-        loads.append(keep(v, 6, v.in_diag.at[4:8], v.diag.at[6:10]))
-    else:
+              keep(v, 4, v.in_source_one, v.source_one), keep(v, 5, v.in_weight_one, v.weight_one)]
+    if second:
         loads.append(keep(v, 6, v.in_first, v.first))
         v.matrix[...] = sort_matrix(512, 384, True)
     window = min(planes, WINDOW)
     begin = jnp.clip(v.where[0] - 10, 0, planes - window)
     unpack_two(v.gathered, 0, begin, v.source_two, window, False)
     copies = []
-    if far:
+    if second:
+        loads.pop(0).wait()
+    else:
         unpack_two(v.gathered, 384, begin, v.weight_two, window, True)
         copies.append(keep(v, 7, v.weight_two, v.out_weight_two))
-    else:
-        loads.pop(0).wait()
     answer = solve_two(v.where[0] - begin, v.source_two, v.weight_two, v.ping, v.pong, window, planes, groups)
     clear_edges(v.one, count)
     clear_edges(v.one_next, count)
@@ -522,66 +538,50 @@
     for k in range(4):
         for c in range(2):
             for s in range(2):
-                v.one[k + 2 + far, c, s, 16:24, :] = v.guess_one[k + 1, c, s, 16:24, :]
-            spread_rows(v.one, 8, k + 2 + far, c, 0, v.from_y_low[k * 2 + c])
-            spread_rows(v.one, 8, k + 2 + far, c, 2, v.from_y_high[k * 2 + c])
+                v.one[k + 2, c, s, 16:24, :] = v.guess_one[k + 1, c, s, 16:24, :]
+            spread_rows(v.one, 8, k + 2, c, 0, v.from_y_low[k * 2 + c])
+            spread_rows(v.one, 8, k + 2, c, 2, v.from_y_high[k * 2 + c])
     for c in range(2):
         for tile in range(3):
             for k in range(2):
                 n = (k * 3 + tile) * 2 + c
-                spread_rows(v.one, 8, far + k, c, tile, v.from_low[n])
-                spread_rows(v.one, 8, 6 + far + k, c, tile, v.from_high[n])
-    if far:
-        zero = jnp.zeros((24, 128), F32)
-        for c in range(2):
-            for ref, edge, plane in ((v.from_low, v.from_far_low, 0), (v.from_high, v.from_far_high, 9)):
-                inner = 1 if plane == 0 else 8
-                for s in range(2):
-                    v.one[plane, c, s, 8:32, :] = zero
-                    v.source_one[inner, c, s] = zero
-                    v.weight_one[inner, c, s] = zero
-                spread_rows(v.one, 8, plane, c, 1, edge[c])
-                spread_rows(v.source_one, 0, inner, c, 1, ref[12 + c])
-                spread_rows(v.weight_one, 0, inner, c, 1, ref[14 + c])
-    add_two(answer, v.where[0] - begin, v.where[1], v.one, -3 - far, count)
-    shift = 0 if far else -1
-    sweep(v.one, v.one_next, v.weight_one, shift, v.source_one, shift, 1, count - 1, 2, 2, 0.25)
-    sweep(v.one_next, v.one, v.weight_one, shift, v.source_one, shift, 2, count - 2, 2, 2, 0.25)
+                spread_rows(v.one, 8, k, c, tile, v.from_low[n])
+                spread_rows(v.one, 8, 6 + k, c, tile, v.from_high[n])
+    add_two(answer, v.where[0] - begin, v.where[1], v.one, -3, count)
+    sweep(v.one, v.one_next, v.weight_one, -1, v.source_one, -1, 1, 7, 2, 2, 0.25)
+    sweep(v.one_next, v.one, v.weight_one, -1, v.source_one, -1, 2, 6, 2, 2, 0.25)
 
     def correct(j, _):
         for half in range(2):
-            x = 2 * (j - far) + half
+            x = 2 * j + half
             for r in range(4):
                 for c in range(2):
                     v.ea[x, c, r, 8:32, :] = v.guess[x, c, r] + v.one[j, c, r // 2, 8:32, :]
         return 0
 
-    lax.fori_loop(2, count - 2, correct, 0)
-    sweep(v.ea, v.eb, v.weight, 0, v.source, 0, 5 - far, 11 + far, 4, 1, 1.0)
-    sweep(v.eb, v.ea, v.weight, 0, v.source, 0, 6 - far, 10 + far, 4, 1, 1.0)
+    lax.fori_loop(2, 6, correct, 0)
+    sweep(v.ea, v.eb, v.weight, 0, v.source, 0, 5, 11, 4, 1, 1.0)
+    sweep(v.eb, v.ea, v.weight, 0, v.source, 0, 6, 10, 4, 1, 1.0)
     return copies
 
 
 def up_first_kernel(v, planes, groups):
-    copies = up_kernel(v, planes, groups, 1)
+    copies = up_kernel(v, planes, groups, False)
     for x in range(4):
-        values = [[], []]
-        for r in range(4):
-            e = [v.ea[x + 6, c, r, 16:24, :] for c in range(2)]
-            moved = product([v.diag[x + 6, c, r, 8:16, :] for c in range(2)], e)
-            for c in range(2):
-                total = neighbour(v.ea, x + 6, c, r, 4, 1, 16, 24)
-                values[c].append(v.source[x + 6, c, r, 8:16, :] + total - moved[c])
-                v.first[x, c, r] = e[c]
         for c in range(2):
-            put_dense(v, x, c, values[c])
+            for r in range(4):
+                v.first[x, c, r] = v.ea[x + 6, c, r, 16:24, :]
+                row = slice(c * 4 + r, c * 4 + r + 1)
+                v.edges[x, row] = v.ea[x + 6, c, r, 15:16, :]
+                v.edges[x + 4, row] = v.ea[x + 6, c, r, 24:25, :]
+            put_dense(v, x, c, [v.ea[x + 6, c, r, 16:24, :] for r in range(4)])
     copies.append(keep(v, 8, v.first, v.out_first))
     for copy in copies:
         copy.wait()
 
 
 def up_second_kernel(v, planes, groups):
-    up_kernel(v, planes, groups, 0)
+    up_kernel(v, planes, groups, True)
     blocks = []
     for c in range(2):
         for x in range(4):
@@ -592,13 +592,12 @@
     v.result[...] = exact_dot(values, v.matrix[...]).reshape(2, 4, 8, 384)
 
 
-def up_scratch(planes, groups, far):
-    level = (8 + 2 * far, 2, 2, 40, 128)
-    source = (6 + 4 * far, 2, 2, 24, 128)
+def up_scratch(planes, groups):
+    level = (8, 2, 2, 40, 128)
     two = (min(planes, WINDOW) + 8, 4, 16 + groups, 128)
-    return dict(source=FINE, weight=FINE, guess=FINE, guess_one=COARSE_WIDE, source_one=source, weight_one=source,
-                source_two=(min(planes, WINDOW), 4, groups, 128),
-                weight_two=(min(planes, WINDOW), 4, groups, 128), ping=two, pong=two,
+    source = (min(planes, WINDOW), 4, groups, 128)
+    return dict(source=FINE, weight=FINE, guess=FINE, guess_one=COARSE_WIDE, source_one=COARSE, weight_one=COARSE,
+                source_two=source, weight_two=source, ping=two, pong=two,
                 one=level, one_next=level, ea=WIDE, eb=WIDE, first=(4, 2, 4, 8, 128))
 
 
@@ -614,10 +613,10 @@
     return run(
         "up_first",
         lambda v: up_first_kernel(v, planes, groups),
-        dict(**up_inputs(where, gathered, messages, down, down), in_diag=(down.out_diag, HB)),
-        dict(packed=((4, 2, 3, 8, 128), VM), front=((2, 2, 3, 8, 128), VM), back=((2, 2, 3, 8, 128), VM),
-             out_first=((4, 2, 4, 8, 128), HB), out_weight_two=((min(planes, WINDOW), 4, groups, 128), HB)),
-        dict(**up_scratch(planes, groups, 1), diag=FINE),
+        up_inputs(where, gathered, messages, down, down),
+        dict(packed=((4, 2, 3, 8, 128), VM), front=((3, 2, 3, 8, 128), VM), back=((3, 2, 3, 8, 128), VM),
+             edges=((8, 8, 128), VM), out_first=((4, 2, 4, 8, 128), HB), out_weight_two=((min(planes, WINDOW), 4, groups, 128), HB)),
+        up_scratch(planes, groups),
         9,
     )
 
@@ -630,7 +629,7 @@
         dict(**up_inputs(where, gathered, messages, down, first_down), in_weight_two=(first_up.out_weight_two, HB),
              in_first=(first_up.out_first, HB)),
         dict(result=((2, 4, 8, 384), VM)),
-        dict(**up_scratch(planes, groups, 0), matrix=pltpu.VMEM((512, 384), BF16)),
+        dict(**up_scratch(planes, groups), matrix=pltpu.VMEM((512, 384), BF16)),
         8,
     ).result
 
@@ -648,8 +647,8 @@
     return lax.all_to_all(sent, ("gx", "gy"), 0, 0).reshape(count_x, count_y, width)
 
 
-def surround(own):
-    mid = jnp.concatenate(
+def beside(own):
+    return jnp.concatenate(
         [
             shifted(own.back, "gx", 2),
             shifted(own.packed, "gx", 1),
@@ -658,28 +657,28 @@
             shifted(own.front, "gx", -2),
         ]
     )
+
+
+def surround(mid):
     return mid, shifted(mid, "gy", 1), shifted(mid, "gy", -1)
 
 
 def exchange_one(down):
-    messages = dict(
+    return dict(
         from_y_low=shifted(down.send_y, "gy", 1),
         from_y_high=shifted(down.send_y, "gy", -1),
         from_low=shifted(down.send_up, "gx", 1),
         from_high=shifted(down.send_down, "gx", -1),
     )
-    if hasattr(down, "send_far_up"):
-        messages["from_far_low"] = shifted(down.send_far_up, "gx", 2)
-        messages["from_far_high"] = shifted(down.send_far_down, "gx", -2)
-    return messages
 
 
 def local(right_side, velocity_table, layer_index, absorb_level):
     where = jnp.stack([lax.axis_index("gx"), lax.axis_index("gy")]).astype(jnp.int32)
     packed = pack(velocity_table, right_side, layer_index, absorb_level)
-    down = down_first(*surround(packed), packed.inverse_two)
+    down = down_first(*surround(beside(packed)), packed.inverse_two)
     middle = up_first(where, gather_two(down.two), exchange_one(down), down)
-    again = down_second(*surround(middle), down)
+    rows = jnp.concatenate([beside(middle).reshape(EDGE, 8, 128), middle.edges])
+    again = down_second(*surround(rows), down)
     return up_second(where, gather_two(again.two), exchange_one(again), again, down, middle)
 
 

time: 172 us -> 168 us (0.977)
  starting transfers between devices: 92 us -> 86.2 us
    all_to_all x2, waiting for transfers between devices: 16.6 us -> 22 us  [gather_two(): lax.all_to_all(sent, ('gx', 'gy'), 0, 0).reshape(count_x, count_y, width)]
    ppermute x22 -> x20, waiting for transfers between devices: 30.8 us -> 26.2 us  [shifted(): return lax.ppermute(block, axis, pairs)]
    ppermute x22 -> x20, starting transfers between devices: 58.9 us -> 55.6 us  [shifted(): return lax.ppermute(block, axis, pairs)]
    all_to_all x2, starting transfers between devices: 33.1 us -> 30.7 us  [gather_two(): lax.all_to_all(sent, ('gx', 'gy'), 0, 0).reshape(count_x, count_y, width)]
  transfers between devices with their start and end apart: 24 -> 22, of which waited for: 11 -> 11; matrix products, arithmetic and copies ran while one was open for 0% -> 0% of each run, Pallas kernels for 0% -> 0%
where the time goes in v5:
time: 168 us; the launch traced here: 167 us
  starting transfers between devices  86.2 us (51%)
  waiting for transfers between devices  48.2 us (29%)
  Pallas kernels  29.7 us (18%)
  local copies, waits for them, and re-layouts  2.42 us (1%)
    ppermute x20, starting transfers between devices, shifted(): return lax.ppermute(block, axis, pairs)  55.6 us
    all_to_all x2, starting transfers between devices, gather_two(): lax.all_to_all(sent, ('gx', 'gy'), 0, 0).reshape(count_x, count_y, width)  30.7 us
    pallas_call x5, Pallas kernels, run(): pl.pallas_call(lambda *refs: kernel(SimpleNamespace(**dict(zip(names, ref...  29.7 us
    ppermute x20, waiting for transfers between devices, shifted(): return lax.ppermute(block, axis, pairs)  26.2 us
    all_to_all x2, waiting for transfers between devices, gather_two(): lax.all_to_all(sent, ('gx', 'gy'), 0, 0).reshape(count_x, count_y, width)  22 us
  transfers between devices with their start and end apart: 22, of which 11 were waited for; matrix products, arithmetic and copies ran while one was open for 0% of the time, Pallas kernels for 0%

profile of v5, /device:TPU:1, one launch (start us, length us, event | category | flops | bytes accessed | tf_op | source)
XLA Modules:
  0.0 167.0 jit_solution(8800157171971150597)
XLA Ops:
  0.0 1.5 pack.1
  1.5 5.6 %collective-permute-start = (f32[2,4,3,8,128]{4,3,2,1,0:T(8,128)S(1)}, f32[2,4,3,8,128]{4,3,2,1,0:T(8,128)S(1)}, u32[]{:S(2)}, u32[]{:S(2)}) collective-permute-start(f32[2,4,3,8,128]{4,3,2,1,0:T(8,128)S(1)} %get-tuple-element.35), channel_id=1, source_target_pairs={{0,16},{8,24},{16,32},{24,40},{32,48},{40,56},{48,64},{56,72},{64,... | collective-permute-start | bytes 294920 | tf_op jit(solution)/shard_map/ppermute | solution.py:640
  7.2 2.3 %collective-permute-start.1 = (f32[4,4,3,8,128]{4,3,2,1,0:T(8,128)S(1)}, f32[4,4,3,8,128]{4,3,2,1,0:T(8,128)S(1)}, u32[]{:S(2)}, u32[]{:S(2)}) collective-permute-start(f32[4,4,3,8,128]{4,3,2,1,0:T(8,128)S(1)} %get-tuple-element.36), channel_id=1, source_target_pairs={{0,8},{8,16},{16,24},{24,32},{32,40},{40,48},{48,56},{56,64},{64,7... | collective-permute-start | bytes 589832 | tf_op jit(solution)/shard_map/ppermute | solution.py:640
  9.5 1.3 collective-permute-start.2
  10.8 1.3 collective-permute-start.3
  12.1 0.0 collective-permute-done
  12.1 0.6 collective-permute-done.1
  12.8 3.8 %collective-permute-done.2 = f32[4,4,3,8,128]{4,3,2,1,0:T(8,128)S(1)} collective-permute-done((f32[4,4,3,8,128]{4,3,2,1,0:T(8,128)S(1)}, f32[4,4,3,8,128]{4,3,2,1,0:T(8,128)S(1)}, u32[]{:S(2)}, u32[]{:S(2)}) %collective-permute-start.2) | collective-permute-done | bytes 196640 | tf_op jit(solution)/shard_map/ppermute | solution.py:640
  16.7 2.0 %collective-permute-done.3 = f32[2,4,3,8,128]{4,3,2,1,0:T(8,128)S(1)} collective-permute-done((f32[2,4,3,8,128]{4,3,2,1,0:T(8,128)S(1)}, f32[2,4,3,8,128]{4,3,2,1,0:T(8,128)S(1)}, u32[]{:S(2)}, u32[]{:S(2)}) %collective-permute-start.3) | collective-permute-done | bytes 98336 | tf_op jit(solution)/shard_map/ppermute | solution.py:640
  18.6 3.7 %collective-permute-start.5 = (f32[16,4,3,8,128]{4,3,2,1,0:T(8,128)S(1)}, f32[16,4,3,8,128]{4,3,2,1,0:T(8,128)S(1)}, u32[]{:S(2)}, u32[]{:S(2)}) collective-permute-start(f32[16,4,3,8,128]{4,3,2,1,0:T(8,128)S(1)} %constant_dynamic-update-slice_fusion.refs_0_), channel_id=1, source_target_pairs={{1,0},{2,1},{3,2},{4,3},{5,4},{6,5},{7,6},{9,8},{10,9},{11,10},{12... | collective-permute-start | bytes 2359304 | tf_op jit(solution)/shard_map/ppermute | solution.py:640
  22.3 3.0 %collective-permute-start.4 = (f32[16,4,3,8,128]{4,3,2,1,0:T(8,128)S(1)}, f32[16,4,3,8,128]{4,3,2,1,0:T(8,128)S(1)}, u32[]{:S(2)}, u32[]{:S(2)}) collective-permute-start(f32[16,4,3,8,128]{4,3,2,1,0:T(8,128)S(1)} %constant_dynamic-update-slice_fusion.refs_0_), channel_id=1, source_target_pairs={{0,1},{1,2},{2,3},{3,4},{4,5},{5,6},{6,7},{8,9},{9,10},{10,11},{11... | collective-permute-start | bytes 2359304 | tf_op jit(solution)/shard_map/ppermute | solution.py:640
  25.3 7.7 %collective-permute-done.5.refs_2_ = f32[16,4,3,8,128]{4,3,2,1,0:T(8,128)S(1)} collective-permute-done((f32[16,4,3,8,128]{4,3,2,1,0:T(8,128)S(1)}, f32[16,4,3,8,128]{4,3,2,1,0:T(8,128)S(1)}, u32[]{:S(2)}, u32[]{:S(2)}) %collective-permute-start.5) | collective-permute-done | bytes 786464 | tf_op jit(solution)/shard_map/ppermute | solution.py:640
  33.0 1.2 collective-permute-done.4.refs_1_
  34.2 6.2 %down_first.1 = (f32[16,2,4,24,128]{4,3,2,1,0:T(8,128)}, f32[16,2,4,24,128]{4,3,2,1,0:T(8,128)}, f32[16,2,4,24,128]{4,3,2,1,0:T(8,128)}, f32[6,2,2,24,128]{4,3,2...) custom-call(f32[16,4,3,8,128]{4,3,2,1,0:T(8,128)S(1)} %constant_dyna, ...), custom_call_target="tpu_custom_call" | custom-call | tf_op jit(solution)/shard_map/down_first/pallas_call | solution.py:29
  40.5 1.3 broadcast_in_dim.17
  41.7 19.0 %all-to-all-start = ((f32[256,1,768]{2,1,0:T(1,128)}), f32[256,1,768]{2,1,0:T(1,128)S(1)}, u32[]{:S(2)}, u32[]{:S(2)}) async-start(f32[256,1,768]{2,1,0:T(1,128)} %broadcast_in_dim.17), calls=%async_computation | async-start | bytes 1572864 | tf_op jit(solution)/shard_map/all_to_all | solution.py:647
  60.7 4.1 %collective-permute-start.7 = (f32[8,8,128]{2,1,0:T(8,128)S(1)}, f32[8,8,128]{2,1,0:T(8,128)S(1)}, u32[]{:S(2)}, u32[]{:S(2)}) collective-permute-start(f32[8,8,128]{2,1,0:T(8,128)S(1)} %get-tuple-element.40), channel_id=1, source_target_pairs={{1,0},{2,1},{3,2},{4,3},{5,4},{6,5},{7,6},{9,8},{10,9},{11,10},{12... | collective-permute-start | bytes 98312 | tf_op jit(solution)/shard_map/ppermute | solution.py:640
  64.8 1.9 %collective-permute-start.6 = (f32[8,8,128]{2,1,0:T(8,128)S(1)}, f32[8,8,128]{2,1,0:T(8,128)S(1)}, u32[]{:S(2)}, u32[]{:S(2)}) collective-permute-start(f32[8,8,128]{2,1,0:T(8,128)S(1)} %get-tuple-element.40), channel_id=1, source_target_pairs={{0,1},{1,2},{2,3},{3,4},{4,5},{5,6},{6,7},{8,9},{9,10},{10,11},{11... | collective-permute-start | bytes 98312 | tf_op jit(solution)/shard_map/ppermute | solution.py:640
  66.7 2.9 %collective-permute-start.8 = (f32[12,8,128]{2,1,0:T(8,128)S(1)}, f32[12,8,128]{2,1,0:T(8,128)S(1)}, u32[]{:S(2)}, u32[]{:S(2)}) collective-permute-start(f32[12,8,128]{2,1,0:T(8,128)S(1)} %get-tuple-element.41), channel_id=1, source_target_pairs={{0,8},{8,16},{16,24},{24,32},{32,40},{40,48},{48,56},{56,64},{64,7... | collective-permute-start | bytes 147464 | tf_op jit(solution)/shard_map/ppermute | solution.py:640
  69.6 1.3 collective-permute-start.9
  70.9 0.1 pad_add_fusion.refs_0_
  71.0 15.1 %all-to-all-done = f32[256,1,768]{2,1,0:T(1,128)S(1)} async-done(((f32[256,1,768]{2,1,0:T(1,128)}), f32[256,1,768]{2,1,0:T(1,128)S(1)}, u32[]{:S(2)}, u32[]{:S(2)}) %all-to-all-start) | async-done | bytes 786464 | tf_op jit(solution)/shard_map/all_to_all | solution.py:647
  86.1 0.1 copy.9
  86.1 0.0 collective-permute-done.7.refs_3_
  86.2 0.0 collective-permute-done.9.refs_5_
  86.2 7.1 %up_first.1 = (f32[4,2,3,8,128]{4,3,2,1,0:T(8,128)S(1)}, f32[3,2,3,8,128]{4,3,2,1,0:T(8,128)S(1)}, f32[3,2,3,8,128]{4,3,2,1,0:T(8,128)S(1)}, f32[8,8,128]{2,1,0:...) custom-call(s32[2]{0:T(128)S(1)} %pad_add_fusion.refs_0_, f32[32,8,768]{2,1,0:T(8,128)S(1)} %bitcast.9, ...), custom_call_target="tpu_custom_call" | custom-call | tf_op jit(solution)/shard_map/up_first/pallas_call | solution.py:29
  93.2 4.0 %collective-permute-start.10 = (f32[3,2,3,8,128]{4,3,2,1,0:T(8,128)S(1)}, f32[3,2,3,8,128]{4,3,2,1,0:T(8,128)S(1)}, u32[]{:S(2)}, u32[]{:S(2)}) collective-permute-start(f32[3,2,3,8,128]{4,3,2,1,0:T(8,128)S(1)} %get-tuple-element.49), channel_id=1, source_target_pairs={{0,16},{8,24},{16,32},{24,40},{32,48},{40,56},{48,64},{56,72},{64,... | collective-permute-start | bytes 221192 | tf_op jit(solution)/shard_map/ppermute | solution.py:640
  97.3 1.3 collective-permute-start.12
  98.6 4.0 %collective-permute-start.11 = (f32[4,2,3,8,128]{4,3,2,1,0:T(8,128)S(1)}, f32[4,2,3,8,128]{4,3,2,1,0:T(8,128)S(1)}, u32[]{:S(2)}, u32[]{:S(2)}) collective-permute-start(f32[4,2,3,8,128]{4,3,2,1,0:T(8,128)S(1)} %get-tuple-element.50), channel_id=1, source_target_pairs={{0,8},{8,16},{16,24},{24,32},{32,40},{40,48},{48,56},{56,64},{64,7... | collective-permute-start | bytes 294920 | tf_op jit(solution)/shard_map/ppermute | solution.py:640
  102.6 1.3 collective-permute-start.13
  103.9 0.3 collective-permute-done.11
  104.3 4.9 %collective-permute-done.13 = f32[3,2,3,8,128]{4,3,2,1,0:T(8,128)S(1)} collective-permute-done((f32[3,2,3,8,128]{4,3,2,1,0:T(8,128)S(1)}, f32[3,2,3,8,128]{4,3,2,1,0:T(8,128)S(1)}, u32[]{:S(2)}, u32[]{:S(2)}) %collective-permute-start.13) | collective-permute-done | bytes 73760 | tf_op jit(solution)/shard_map/ppermute | solution.py:640
  109.2 5.3 %collective-permute-start.15 = (f32[116,8,128]{2,1,0:T(8,128)S(1)}, f32[116,8,128]{2,1,0:T(8,128)S(1)}, u32[]{:S(2)}, u32[]{:S(2)}) collective-permute-start(f32[116,8,128]{2,1,0:T(8,128)S(1)} %pad_maximum_fusion.refs_0_), channel_id=1, source_target_pairs={{1,0},{2,1},{3,2},{4,3},{5,4},{6,5},{7,6},{9,8},{10,9},{11,10},{12... | collective-permute-start | bytes 1425416 | tf_op jit(solution)/shard_map/ppermute | solution.py:640
  114.6 2.1 %collective-permute-start.14 = (f32[116,8,128]{2,1,0:T(8,128)S(1)}, f32[116,8,128]{2,1,0:T(8,128)S(1)}, u32[]{:S(2)}, u32[]{:S(2)}) collective-permute-start(f32[116,8,128]{2,1,0:T(8,128)S(1)} %pad_maximum_fusion.refs_0_), channel_id=1, source_target_pairs={{0,1},{1,2},{2,3},{3,4},{4,5},{5,6},{6,7},{8,9},{9,10},{10,11},{11... | collective-permute-start | bytes 1425416 | tf_op jit(solution)/shard_map/ppermute | solution.py:640
  116.7 4.4 %collective-permute-done.15.refs_2_ = f32[116,8,128]{2,1,0:T(8,128)S(1)} collective-permute-done((f32[116,8,128]{2,1,0:T(8,128)S(1)}, f32[116,8,128]{2,1,0:T(8,128)S(1)}, u32[]{:S(2)}, u32[]{:S(2)}) %collective-permute-start.15) | collective-permute-done | bytes 475168 | tf_op jit(solution)/shard_map/ppermute | solution.py:640
  121.1 1.2 collective-permute-done.14.refs_1_
  122.3 7.2 %down_second.1 = (f32[8,2,4,24,128]{4,3,2,1,0:T(8,128)}, f32[12,2,4,24,128]{4,3,2,1,0:T(8,128)}, f32[6,2,2,24,128]{4,3,2,1,0:T(8,128)}, f32[6,2,2,40,128]{4,3,2,...) custom-call(f32[116,8,128]{2,1,0:T(8,128)S(1)} %pad_maximum_fusion.r, ...), custom_call_target="tpu_custom_call" | custom-call | tf_op jit(solution)/shard_map/down_second/pallas_call | solution.py:29
  129.6 1.0 broadcast_in_dim.19
  130.5 11.7 %all-to-all-start.1 = ((f32[256,1,384]{2,1,0:T(1,128)}), f32[256,1,384]{2,1,0:T(1,128)S(1)}, u32[]{:S(2)}, u32[]{:S(2)}) async-start(f32[256,1,384]{2,1,0:T(1,128)} %broadcast_in_dim.19), calls=%async_computation.1 | async-start | bytes 786432 | tf_op jit(solution)/shard_map/all_to_all | solution.py:647
  142.2 3.3 %collective-permute-start.18 = (f32[12,8,128]{2,1,0:T(8,128)S(1)}, f32[12,8,128]{2,1,0:T(8,128)S(1)}, u32[]{:S(2)}, u32[]{:S(2)}) collective-permute-start(f32[12,8,128]{2,1,0:T(8,128)S(1)} %get-tuple-element.57), channel_id=1, source_target_pairs={{0,8},{8,16},{16,24},{24,32},{32,40},{40,48},{48,56},{56,64},{64,7... | collective-permute-start | bytes 147464 | tf_op jit(solution)/shard_map/ppermute | solution.py:640
  145.5 1.3 collective-permute-start.19
  146.8 2.6 %collective-permute-start.17 = (f32[8,8,128]{2,1,0:T(8,128)S(1)}, f32[8,8,128]{2,1,0:T(8,128)S(1)}, u32[]{:S(2)}, u32[]{:S(2)}) collective-permute-start(f32[8,8,128]{2,1,0:T(8,128)S(1)} %get-tuple-element.56), channel_id=1, source_target_pairs={{1,0},{2,1},{3,2},{4,3},{5,4},{6,5},{7,6},{9,8},{10,9},{11,10},{12... | collective-permute-start | bytes 98312 | tf_op jit(solution)/shard_map/ppermute | solution.py:640
  149.4 3.0 %collective-permute-start.16 = (f32[8,8,128]{2,1,0:T(8,128)S(1)}, f32[8,8,128]{2,1,0:T(8,128)S(1)}, u32[]{:S(2)}, u32[]{:S(2)}) collective-permute-start(f32[8,8,128]{2,1,0:T(8,128)S(1)} %get-tuple-element.56), channel_id=1, source_target_pairs={{0,1},{1,2},{2,3},{3,4},{4,5},{5,6},{6,7},{8,9},{9,10},{10,11},{11... | collective-permute-start | bytes 98312 | tf_op jit(solution)/shard_map/ppermute | solution.py:640
  152.4 6.9 %all-to-all-done.1 = f32[256,1,384]{2,1,0:T(1,128)S(1)} async-done(((f32[256,1,384]{2,1,0:T(1,128)}), f32[256,1,384]{2,1,0:T(1,128)S(1)}, u32[]{:S(2)}, u32[]{:S(2)}) %all-to-all-start.1) | async-done | bytes 393248 | tf_op jit(solution)/shard_map/all_to_all | solution.py:647
  159.3 0.0 collective-permute-done.17.refs_3_
  159.3 0.0 collective-permute-done.16.refs_2_
  159.3 0.0 collective-permute-done.19.refs_5_
  159.4 7.7 %up_second.1 = f32[2,4,8,384]{3,2,1,0:T(8,128)} custom-call(s32[2]{0:T(128)S(1)} %pad_add_fusion.refs_0_, f32[32,8,384]{2,1,0:T(8,128)S(1)} %bitcast.10, f32[8,8,128]{2,1,0:T(8,128)S(1)} %collective-permute-done.16.refs_2_, f32[8,8,128]{2,1,0:T(8,128)S(1)} %collective-permute-done.17.refs_3_, f32[12,8,128]{2,1,0:T(8,128)S(1)} %collective-permute-done.18.refs_4_, ...), custom_call_target="tpu_custom_call" | custom-call | tf_op jit(solution)/shard_map/up_second/pallas_call | solution.py:29
  (19 shorter events, 0.2 us)
Async XLA Ops:
  1.5 10.6 %collective-permute-start = (f32[2,4,3,8,128]{4,3,2,1,0:T(8,128)S(1)}, f32[2,4,3,8,128]{4,3,2,1,0:T(8,128)S(1)}, u32[]{:S(2)}, u32[]{:S(2)}) collective-permute-start(f32[2,4,3,8,128]{4,3,2,1,0:T(8,128)S(1)} %get-tuple-element.35), channel_id=1, source_target_pairs={{0,16},{8,24},{16,32},{24,40},{32,48},{40,56},{48,64},{56,72},{64,... | collective-permute-start | bytes 294920 | tf_op jit(solution)/shard_map/ppermute | solution.py:640
  7.2 5.6 %collective-permute-start.1 = (f32[4,4,3,8,128]{4,3,2,1,0:T(8,128)S(1)}, f32[4,4,3,8,128]{4,3,2,1,0:T(8,128)S(1)}, u32[]{:S(2)}, u32[]{:S(2)}) collective-permute-start(f32[4,4,3,8,128]{4,3,2,1,0:T(8,128)S(1)} %get-tuple-element.36), channel_id=1, source_target_pairs={{0,8},{8,16},{16,24},{24,32},{32,40},{40,48},{48,56},{56,64},{64,7... | collective-permute-start | bytes 589832 | tf_op jit(solution)/shard_map/ppermute | solution.py:640
  9.5 7.1 %collective-permute-start.2 = (f32[4,4,3,8,128]{4,3,2,1,0:T(8,128)S(1)}, f32[4,4,3,8,128]{4,3,2,1,0:T(8,128)S(1)}, u32[]{:S(2)}, u32[]{:S(2)}) collective-permute-start(f32[4,4,3,8,128]{4,3,2,1,0:T(8,128)S(1)} %get-tuple-element.36), channel_id=1, source_target_pairs={{8,0},{16,8},{24,16},{32,24},{40,32},{48,40},{56,48},{64,56},{72,6... | collective-permute-start | bytes 589832 | tf_op jit(solution)/shard_map/ppermute | solution.py:640
  10.8 7.8 %collective-permute-start.3 = (f32[2,4,3,8,128]{4,3,2,1,0:T(8,128)S(1)}, f32[2,4,3,8,128]{4,3,2,1,0:T(8,128)S(1)}, u32[]{:S(2)}, u32[]{:S(2)}) collective-permute-start(f32[2,4,3,8,128]{4,3,2,1,0:T(8,128)S(1)} %get-tuple-element.37), channel_id=1, source_target_pairs={{16,0},{24,8},{32,16},{40,24},{48,32},{56,40},{64,48},{72,56},{80,... | collective-permute-start | bytes 294920 | tf_op jit(solution)/shard_map/ppermute | solution.py:640
  18.6 14.4 %collective-permute-start.5 = (f32[16,4,3,8,128]{4,3,2,1,0:T(8,128)S(1)}, f32[16,4,3,8,128]{4,3,2,1,0:T(8,128)S(1)}, u32[]{:S(2)}, u32[]{:S(2)}) collective-permute-start(f32[16,4,3,8,128]{4,3,2,1,0:T(8,128)S(1)} %constant_dynamic-update-slice_fusion.refs_0_), channel_id=1, source_target_pairs={{1,0},{2,1},{3,2},{4,3},{5,4},{6,5},{7,6},{9,8},{10,9},{11,10},{12... | collective-permute-start | bytes 2359304 | tf_op jit(solution)/shard_map/ppermute | solution.py:640
  22.3 11.9 %collective-permute-start.4 = (f32[16,4,3,8,128]{4,3,2,1,0:T(8,128)S(1)}, f32[16,4,3,8,128]{4,3,2,1,0:T(8,128)S(1)}, u32[]{:S(2)}, u32[]{:S(2)}) collective-permute-start(f32[16,4,3,8,128]{4,3,2,1,0:T(8,128)S(1)} %constant_dynamic-update-slice_fusion.refs_0_), channel_id=1, source_target_pairs={{0,1},{1,2},{2,3},{3,4},{4,5},{5,6},{6,7},{8,9},{9,10},{10,11},{11... | collective-permute-start | bytes 2359304 | tf_op jit(solution)/shard_map/ppermute | solution.py:640
  41.7 44.3 %all-to-all-start = ((f32[256,1,768]{2,1,0:T(1,128)}), f32[256,1,768]{2,1,0:T(1,128)S(1)}, u32[]{:S(2)}, u32[]{:S(2)}) async-start(f32[256,1,768]{2,1,0:T(1,128)} %broadcast_in_dim.17), calls=%async_computation | async-start | bytes 1572864 | tf_op jit(solution)/shard_map/all_to_all | solution.py:647
  60.7 25.4 %collective-permute-start.7 = (f32[8,8,128]{2,1,0:T(8,128)S(1)}, f32[8,8,128]{2,1,0:T(8,128)S(1)}, u32[]{:S(2)}, u32[]{:S(2)}) collective-permute-start(f32[8,8,128]{2,1,0:T(8,128)S(1)} %get-tuple-element.40), channel_id=1, source_target_pairs={{1,0},{2,1},{3,2},{4,3},{5,4},{6,5},{7,6},{9,8},{10,9},{11,10},{12... | collective-permute-start | bytes 98312 | tf_op jit(solution)/shard_map/ppermute | solution.py:640
  64.8 21.3 %collective-permute-start.6 = (f32[8,8,128]{2,1,0:T(8,128)S(1)}, f32[8,8,128]{2,1,0:T(8,128)S(1)}, u32[]{:S(2)}, u32[]{:S(2)}) collective-permute-start(f32[8,8,128]{2,1,0:T(8,128)S(1)} %get-tuple-element.40), channel_id=1, source_target_pairs={{0,1},{1,2},{2,3},{3,4},{4,5},{5,6},{6,7},{8,9},{9,10},{10,11},{11... | collective-permute-start | bytes 98312 | tf_op jit(solution)/shard_map/ppermute | solution.py:640
  66.7 19.4 %collective-permute-start.8 = (f32[12,8,128]{2,1,0:T(8,128)S(1)}, f32[12,8,128]{2,1,0:T(8,128)S(1)}, u32[]{:S(2)}, u32[]{:S(2)}) collective-permute-start(f32[12,8,128]{2,1,0:T(8,128)S(1)} %get-tuple-element.41), channel_id=1, source_target_pairs={{0,8},{8,16},{16,24},{24,32},{32,40},{40,48},{48,56},{56,64},{64,7... | collective-permute-start | bytes 147464 | tf_op jit(solution)/shard_map/ppermute | solution.py:640
  69.6 16.6 %collective-permute-start.9 = (f32[12,8,128]{2,1,0:T(8,128)S(1)}, f32[12,8,128]{2,1,0:T(8,128)S(1)}, u32[]{:S(2)}, u32[]{:S(2)}) collective-permute-start(f32[12,8,128]{2,1,0:T(8,128)S(1)} %get-tuple-element.42), channel_id=1, source_target_pairs={{8,0},{16,8},{24,16},{32,24},{40,32},{48,40},{56,48},{64,56},{72,6... | collective-permute-start | bytes 147464 | tf_op jit(solution)/shard_map/ppermute | solution.py:640
  93.2 10.7 %collective-permute-start.10 = (f32[3,2,3,8,128]{4,3,2,1,0:T(8,128)S(1)}, f32[3,2,3,8,128]{4,3,2,1,0:T(8,128)S(1)}, u32[]{:S(2)}, u32[]{:S(2)}) collective-permute-start(f32[3,2,3,8,128]{4,3,2,1,0:T(8,128)S(1)} %get-tuple-element.49), channel_id=1, source_target_pairs={{0,16},{8,24},{16,32},{24,40},{32,48},{40,56},{48,64},{56,72},{64,... | collective-permute-start | bytes 221192 | tf_op jit(solution)/shard_map/ppermute | solution.py:640
  97.3 6.9 %collective-permute-start.12 = (f32[4,2,3,8,128]{4,3,2,1,0:T(8,128)S(1)}, f32[4,2,3,8,128]{4,3,2,1,0:T(8,128)S(1)}, u32[]{:S(2)}, u32[]{:S(2)}) collective-permute-start(f32[4,2,3,8,128]{4,3,2,1,0:T(8,128)S(1)} %get-tuple-element.50), channel_id=1, source_target_pairs={{8,0},{16,8},{24,16},{32,24},{40,32},{48,40},{56,48},{64,56},{72,6... | collective-permute-start | bytes 294920 | tf_op jit(solution)/shard_map/ppermute | solution.py:640
  98.6 5.6 %collective-permute-start.11 = (f32[4,2,3,8,128]{4,3,2,1,0:T(8,128)S(1)}, f32[4,2,3,8,128]{4,3,2,1,0:T(8,128)S(1)}, u32[]{:S(2)}, u32[]{:S(2)}) collective-permute-start(f32[4,2,3,8,128]{4,3,2,1,0:T(8,128)S(1)} %get-tuple-element.50), channel_id=1, source_target_pairs={{0,8},{8,16},{16,24},{24,32},{32,40},{40,48},{48,56},{56,64},{64,7... | collective-permute-start | bytes 294920 | tf_op jit(solution)/shard_map/ppermute | solution.py:640
  102.6 6.6 %collective-permute-start.13 = (f32[3,2,3,8,128]{4,3,2,1,0:T(8,128)S(1)}, f32[3,2,3,8,128]{4,3,2,1,0:T(8,128)S(1)}, u32[]{:S(2)}, u32[]{:S(2)}) collective-permute-start(f32[3,2,3,8,128]{4,3,2,1,0:T(8,128)S(1)} %get-tuple-element.51), channel_id=1, source_target_pairs={{16,0},{24,8},{32,16},{40,24},{48,32},{56,40},{64,48},{72,56},{80,... | collective-permute-start | bytes 221192 | tf_op jit(solution)/shard_map/ppermute | solution.py:640
  109.2 11.9 %collective-permute-start.15 = (f32[116,8,128]{2,1,0:T(8,128)S(1)}, f32[116,8,128]{2,1,0:T(8,128)S(1)}, u32[]{:S(2)}, u32[]{:S(2)}) collective-permute-start(f32[116,8,128]{2,1,0:T(8,128)S(1)} %pad_maximum_fusion.refs_0_), channel_id=1, source_target_pairs={{1,0},{2,1},{3,2},{4,3},{5,4},{6,5},{7,6},{9,8},{10,9},{11,10},{12... | collective-permute-start | bytes 1425416 | tf_op jit(solution)/shard_map/ppermute | solution.py:640
  114.6 7.7 %collective-permute-start.14 = (f32[116,8,128]{2,1,0:T(8,128)S(1)}, f32[116,8,128]{2,1,0:T(8,128)S(1)}, u32[]{:S(2)}, u32[]{:S(2)}) collective-permute-start(f32[116,8,128]{2,1,0:T(8,128)S(1)} %pad_maximum_fusion.refs_0_), channel_id=1, source_target_pairs={{0,1},{1,2},{2,3},{3,4},{4,5},{5,6},{6,7},{8,9},{9,10},{10,11},{11... | collective-permute-start | bytes 1425416 | tf_op jit(solution)/shard_map/ppermute | solution.py:640
  130.5 28.7 %all-to-all-start.1 = ((f32[256,1,384]{2,1,0:T(1,128)}), f32[256,1,384]{2,1,0:T(1,128)S(1)}, u32[]{:S(2)}, u32[]{:S(2)}) async-start(f32[256,1,384]{2,1,0:T(1,128)} %broadcast_in_dim.19), calls=%async_computation.1 | async-start | bytes 786432 | tf_op jit(solution)/shard_map/all_to_all | solution.py:647
  142.2 17.1 %collective-permute-start.18 = (f32[12,8,128]{2,1,0:T(8,128)S(1)}, f32[12,8,128]{2,1,0:T(8,128)S(1)}, u32[]{:S(2)}, u32[]{:S(2)}) collective-permute-start(f32[12,8,128]{2,1,0:T(8,128)S(1)} %get-tuple-element.57), channel_id=1, source_target_pairs={{0,8},{8,16},{16,24},{24,32},{32,40},{40,48},{48,56},{56,64},{64,7... | collective-permute-start | bytes 147464 | tf_op jit(solution)/shard_map/ppermute | solution.py:640
  145.5 13.8 %collective-permute-start.19 = (f32[12,8,128]{2,1,0:T(8,128)S(1)}, f32[12,8,128]{2,1,0:T(8,128)S(1)}, u32[]{:S(2)}, u32[]{:S(2)}) collective-permute-start(f32[12,8,128]{2,1,0:T(8,128)S(1)} %get-tuple-element.58), channel_id=1, source_target_pairs={{8,0},{16,8},{24,16},{32,24},{40,32},{48,40},{56,48},{64,56},{72,6... | collective-permute-start | bytes 147464 | tf_op jit(solution)/shard_map/ppermute | solution.py:640
  146.8 12.5 %collective-permute-start.17 = (f32[8,8,128]{2,1,0:T(8,128)S(1)}, f32[8,8,128]{2,1,0:T(8,128)S(1)}, u32[]{:S(2)}, u32[]{:S(2)}) collective-permute-start(f32[8,8,128]{2,1,0:T(8,128)S(1)} %get-tuple-element.56), channel_id=1, source_target_pairs={{1,0},{2,1},{3,2},{4,3},{5,4},{6,5},{7,6},{9,8},{10,9},{11,10},{12... | collective-permute-start | bytes 98312 | tf_op jit(solution)/shard_map/ppermute | solution.py:640
  149.4 9.9 %collective-permute-start.16 = (f32[8,8,128]{2,1,0:T(8,128)S(1)}, f32[8,8,128]{2,1,0:T(8,128)S(1)}, u32[]{:S(2)}, u32[]{:S(2)}) collective-permute-start(f32[8,8,128]{2,1,0:T(8,128)S(1)} %get-tuple-element.56), channel_id=1, source_target_pairs={{0,1},{1,2},{2,3},{3,4},{4,5},{5,6},{6,7},{8,9},{9,10},{10,11},{11... | collective-permute-start | bytes 98312 | tf_op jit(solution)/shard_map/ppermute | solution.py:640

commit v6 on v5

--- a/solution.py
+++ b/solution.py
@@ -111,7 +111,7 @@
     lax.fori_loop(0, count, body, 0)
 
 
-def clear_edges(ref, count):
+def clear_edges(ref, count, begin=0):
     zero = jnp.zeros((8, 128), F32)
 
     def body(x, _):
@@ -121,7 +121,7 @@
                 ref[x, c, r, 32:40, :] = zero
         return 0
 
-    lax.fori_loop(0, count, body, 0)
+    lax.fori_loop(begin, count, body, 0)
 
 
 def dense(parts):
@@ -353,19 +353,18 @@
     copies += [keep(v, 2, v.diag, v.out_diag), keep(v, 3, v.weight_one, v.out_weight_one),
                keep(v, 4, v.diag_one, v.out_diag_one)]
     copies += down_body(v, v.source, v.weight, v.diag, v.weight_one, v.diag_one, 5)
-    v.two[0:1, 384:768] = v.inverse_two[...]
     for copy in copies:
         copy.wait()
 
 
-def down_first(mid, low, high, inverse_two):
+def down_first(mid, low, high):
     return run(
         "down_first",
         down_first_kernel,
-        dict(mid=(mid, VM), low=(low, VM), high=(high, VM), inverse_two=(inverse_two, VM)),
+        dict(mid=(mid, VM), low=(low, VM), high=(high, VM)),
         dict(out_source=(FINE, HB), out_weight=(FINE, HB), out_diag=(FINE, HB), out_weight_one=(COARSE, HB),
              out_diag_one=(COARSE, HB), out_guess=(INNER, HB), out_source_one=(COARSE, HB), out_guess_one=(COARSE_WIDE, HB),
-             two=((1, 768), VM), send_y=((8, 8, 128), VM), send_up=((12, 8, 128), VM), send_down=((12, 8, 128), VM)),
+             two=((1, 384), VM), send_y=((8, 8, 128), VM), send_up=((12, 8, 128), VM), send_down=((12, 8, 128), VM)),
         dict(source=FINE, weight=FINE, diag=FINE, weight_one=COARSE, diag_one=COARSE, start=WIDE, guess=WIDE,
              start_one=COARSE_WIDE, source_one=COARSE, guess_one=COARSE_WIDE, temp=(2, 40, 128)),
         8,
@@ -396,7 +395,7 @@
                 row = slice(c * 4 + r, c * 4 + r + 1)
                 v.first[x + 7, c, r, 7:8, :] = v.low[EDGE + x, row]
                 v.first[x + 7, c, r, 32:33, :] = v.high[EDGE + 4 + x, row]
-    for load in loads:
+    for load in loads[0:2]:
         load.wait()
 
     def residual(x, _):
@@ -407,6 +406,8 @@
         return 0
 
     lax.fori_loop(0, 16, residual, 0)
+    for load in loads[2:5]:
+        load.wait()
     copies = [keep(v, 8, v.source.at[4:12], v.out_source)]
     copies += down_body(v, v.source, v.weight, v.diag, v.weight_one, v.diag_one, 5)
     for copy in copies:
@@ -439,9 +440,9 @@
         body(low + n)
 
 
-def unpack_two(packed, first, begin, target, window, clean):
+def unpack_two(packed, begin, target, window, clean):
     def body(x):
-        parts = [packed[begin + x, :, first + n * 128 : first + n * 128 + 128] for n in range(3)]
+        parts = [packed[begin + x, :, n * 128 : n * 128 + 128] for n in range(3)]
         for k, part in enumerate(loose(parts, clean)):
             target[x, k] = part
 
@@ -520,18 +521,18 @@
         v.matrix[...] = sort_matrix(512, 384, True)
     window = min(planes, WINDOW)
     begin = jnp.clip(v.where[0] - 10, 0, planes - window)
-    unpack_two(v.gathered, 0, begin, v.source_two, window, False)
+    unpack_two(v.gathered, begin, v.source_two, window, False)
     copies = []
     if second:
         loads.pop(0).wait()
     else:
-        unpack_two(v.gathered, 384, begin, v.weight_two, window, True)
+        unpack_two(v.gathered_weight, begin, v.weight_two, window, True)
         copies.append(keep(v, 7, v.weight_two, v.out_weight_two))
     answer = solve_two(v.where[0] - begin, v.source_two, v.weight_two, v.ping, v.pong, window, planes, groups)
     clear_edges(v.one, count)
     clear_edges(v.one_next, count)
-    clear_edges(v.ea, 16)
-    clear_edges(v.eb, 16)
+    clear_edges(v.ea, 12, 4)
+    clear_edges(v.eb, 11, 5)
     for load in loads:
         load.wait()
 
@@ -608,12 +609,12 @@
                 in_weight_one=(first_down.out_weight_one, HB))
 
 
-def up_first(where, gathered, messages, down):
+def up_first(where, gathered, gathered_weight, messages, down):
     planes, groups = gathered.shape[0], gathered.shape[1]
     return run(
         "up_first",
         lambda v: up_first_kernel(v, planes, groups),
-        up_inputs(where, gathered, messages, down, down),
+        dict(**up_inputs(where, gathered, messages, down, down), gathered_weight=(gathered_weight, VM)),
         dict(packed=((4, 2, 3, 8, 128), VM), front=((3, 2, 3, 8, 128), VM), back=((3, 2, 3, 8, 128), VM),
              edges=((8, 8, 128), VM), out_first=((4, 2, 4, 8, 128), HB), out_weight_two=((min(planes, WINDOW), 4, groups, 128), HB)),
         up_scratch(planes, groups),
@@ -675,8 +676,9 @@
 def local(right_side, velocity_table, layer_index, absorb_level):
     where = jnp.stack([lax.axis_index("gx"), lax.axis_index("gy")]).astype(jnp.int32)
     packed = pack(velocity_table, right_side, layer_index, absorb_level)
-    down = down_first(*surround(beside(packed)), packed.inverse_two)
-    middle = up_first(where, gather_two(down.two), exchange_one(down), down)
+    weight_two = gather_two(packed.inverse_two)
+    down = down_first(*surround(beside(packed)))
+    middle = up_first(where, gather_two(down.two), weight_two, exchange_one(down), down)
     rows = jnp.concatenate([beside(middle).reshape(EDGE, 8, 128), middle.edges])
     again = down_second(*surround(rows), down)
     return up_second(where, gather_two(again.two), exchange_one(again), again, down, middle)

time: 168 us -> 171 us (1.018)
  starting transfers between devices: 86.2 us -> 92.9 us
  waiting for transfers between devices: 48.2 us -> 44.7 us
    all_to_all x2 -> x3, starting transfers between devices: 30.7 us -> 39.4 us  [gather_two(): lax.all_to_all(sent, ('gx', 'gy'), 0, 0).reshape(count_x, count_y, width)]
    ppermute x20, waiting for transfers between devices: 26.2 us -> 20 us  [shifted(): return lax.ppermute(block, axis, pairs)]
    all_to_all x2 -> x3, waiting for transfers between devices: 22 us -> 24.7 us  [gather_two(): lax.all_to_all(sent, ('gx', 'gy'), 0, 0).reshape(count_x, count_y, width)]
    ppermute x20, starting transfers between devices: 55.6 us -> 53.5 us  [shifted(): return lax.ppermute(block, axis, pairs)]
  transfers between devices with their start and end apart: 22 -> 23, of which waited for: 11 -> 10; matrix products, arithmetic and copies ran while one was open for 0% -> 1% of each run, Pallas kernels for 0% -> 4%
where the time goes in v6:
time: 171 us
  starting transfers between devices  92.9 us (54%)
  waiting for transfers between devices  44.7 us (26%)
  Pallas kernels  29.3 us (17%)
  local copies, waits for them, and re-layouts  3.07 us (2%)
    ppermute x20, starting transfers between devices, shifted(): return lax.ppermute(block, axis, pairs)  53.5 us
    all_to_all x3, starting transfers between devices, gather_two(): lax.all_to_all(sent, ('gx', 'gy'), 0, 0).reshape(count_x, count_y, width)  39.4 us
    pallas_call x5, Pallas kernels, run(): pl.pallas_call(lambda *refs: kernel(SimpleNamespace(**dict(zip(names, ref...  29.3 us
    all_to_all x3, waiting for transfers between devices, gather_two(): lax.all_to_all(sent, ('gx', 'gy'), 0, 0).reshape(count_x, count_y, width)  24.7 us
    ppermute x20, waiting for transfers between devices, shifted(): return lax.ppermute(block, axis, pairs)  20 us
  transfers between devices with their start and end apart: 23, of which 10 were waited for; matrix products, arithmetic and copies ran while one was open for 1% of the time, Pallas kernels for 4%

profile of v6, /device:TPU:1, one launch (start us, length us, event | category | flops | bytes accessed | tf_op | source)
XLA Modules:
  0.0 170.5 jit_solution(10419130760821875196)
XLA Ops:
  0.0 1.5 pack.1
  1.5 5.6 %collective-permute-start = (f32[2,4,3,8,128]{4,3,2,1,0:T(8,128)S(1)}, f32[2,4,3,8,128]{4,3,2,1,0:T(8,128)S(1)}, u32[]{:S(2)}, u32[]{:S(2)}) collective-permute-start(f32[2,4,3,8,128]{4,3,2,1,0:T(8,128)S(1)} %get-tuple-element.35), channel_id=1, source_target_pairs={{0,16},{8,24},{16,32},{24,40},{32,48},{40,56},{48,64},{56,72},{64,... | collective-permute-start | bytes 294920 | tf_op jit(solution)/shard_map/ppermute | solution.py:641
  7.2 2.3 %collective-permute-start.1 = (f32[4,4,3,8,128]{4,3,2,1,0:T(8,128)S(1)}, f32[4,4,3,8,128]{4,3,2,1,0:T(8,128)S(1)}, u32[]{:S(2)}, u32[]{:S(2)}) collective-permute-start(f32[4,4,3,8,128]{4,3,2,1,0:T(8,128)S(1)} %get-tuple-element.36), channel_id=1, source_target_pairs={{0,8},{8,16},{16,24},{24,32},{32,40},{40,48},{48,56},{56,64},{64,7... | collective-permute-start | bytes 589832 | tf_op jit(solution)/shard_map/ppermute | solution.py:641
  9.5 1.3 collective-permute-start.2
  10.8 1.3 collective-permute-start.3
  12.1 0.6 collective-permute-done.1
  12.8 3.8 %collective-permute-done.2 = f32[4,4,3,8,128]{4,3,2,1,0:T(8,128)S(1)} collective-permute-done((f32[4,4,3,8,128]{4,3,2,1,0:T(8,128)S(1)}, f32[4,4,3,8,128]{4,3,2,1,0:T(8,128)S(1)}, u32[]{:S(2)}, u32[]{:S(2)}) %collective-permute-start.2) | collective-permute-done | bytes 196640 | tf_op jit(solution)/shard_map/ppermute | solution.py:641
  16.7 2.0 %collective-permute-done.3 = f32[2,4,3,8,128]{4,3,2,1,0:T(8,128)S(1)} collective-permute-done((f32[2,4,3,8,128]{4,3,2,1,0:T(8,128)S(1)}, f32[2,4,3,8,128]{4,3,2,1,0:T(8,128)S(1)}, u32[]{:S(2)}, u32[]{:S(2)}) %collective-permute-start.3) | collective-permute-done | bytes 98336 | tf_op jit(solution)/shard_map/ppermute | solution.py:641
  18.6 4.8 %collective-permute-start.4 = (f32[16,4,3,8,128]{4,3,2,1,0:T(8,128)S(1)}, f32[16,4,3,8,128]{4,3,2,1,0:T(8,128)S(1)}, u32[]{:S(2)}, u32[]{:S(2)}) collective-permute-start(f32[16,4,3,8,128]{4,3,2,1,0:T(8,128)S(1)} %constant_dynamic-update-slice_fusion.refs_0_), channel_id=1, source_target_pairs={{0,1},{1,2},{2,3},{3,4},{4,5},{5,6},{6,7},{8,9},{9,10},{10,11},{11... | collective-permute-start | bytes 2359304 | tf_op jit(solution)/shard_map/ppermute | solution.py:641
  23.4 1.9 %collective-permute-start.5 = (f32[16,4,3,8,128]{4,3,2,1,0:T(8,128)S(1)}, f32[16,4,3,8,128]{4,3,2,1,0:T(8,128)S(1)}, u32[]{:S(2)}, u32[]{:S(2)}) collective-permute-start(f32[16,4,3,8,128]{4,3,2,1,0:T(8,128)S(1)} %constant_dynamic-update-slice_fusion.refs_0_), channel_id=1, source_target_pairs={{1,0},{2,1},{3,2},{4,3},{5,4},{6,5},{7,6},{9,8},{10,9},{11,10},{12... | collective-permute-start | bytes 2359304 | tf_op jit(solution)/shard_map/ppermute | solution.py:641
  25.3 1.0 broadcast_in_dim.27
  26.3 18.2 %all-to-all-start.1 = ((f32[256,1,384]{2,1,0:T(1,128)}), f32[256,1,384]{2,1,0:T(1,128)S(1)}, u32[]{:S(2)}, u32[]{:S(2)}) async-start(f32[256,1,384]{2,1,0:T(1,128)} %broadcast_in_dim.27), calls=%async_computation.1 | async-start | bytes 786432 | tf_op jit(solution)/shard_map/all_to_all | solution.py:648
  44.5 0.0 collective-permute-done.4.refs_1_
  44.6 6.2 %down_first.1 = (f32[16,2,4,24,128]{4,3,2,1,0:T(8,128)}, f32[16,2,4,24,128]{4,3,2,1,0:T(8,128)}, f32[16,2,4,24,128]{4,3,2,1,0:T(8,128)}, f32[6,2,2,24,128]{4,3,2...) custom-call(f32[16,4,3,8,128]{4,3,2,1,0:T(8,128)S(1)} %constant_dyna, ...), custom_call_target="tpu_custom_call" | custom-call | tf_op jit(solution)/shard_map/down_first/pallas_call | solution.py:29
  50.8 10.8 %all-to-all-done.1 = f32[256,1,384]{2,1,0:T(1,128)S(1)} async-done(((f32[256,1,384]{2,1,0:T(1,128)}), f32[256,1,384]{2,1,0:T(1,128)S(1)}, u32[]{:S(2)}, u32[]{:S(2)}) %all-to-all-start.1) | async-done | bytes 393248 | tf_op jit(solution)/shard_map/all_to_all | solution.py:648
  61.5 1.0 broadcast_in_dim.25
  62.5 6.3 %all-to-all-start = ((f32[256,1,384]{2,1,0:T(1,128)}), f32[256,1,384]{2,1,0:T(1,128)S(1)}, u32[]{:S(2)}, u32[]{:S(2)}) async-start(f32[256,1,384]{2,1,0:T(1,128)} %broadcast_in_dim.25), calls=%async_computation | async-start | bytes 786432 | tf_op jit(solution)/shard_map/all_to_all | solution.py:648
  68.8 3.5 %collective-permute-start.6 = (f32[8,8,128]{2,1,0:T(8,128)S(1)}, f32[8,8,128]{2,1,0:T(8,128)S(1)}, u32[]{:S(2)}, u32[]{:S(2)}) collective-permute-start(f32[8,8,128]{2,1,0:T(8,128)S(1)} %get-tuple-element.39), channel_id=1, source_target_pairs={{0,1},{1,2},{2,3},{3,4},{4,5},{5,6},{6,7},{8,9},{9,10},{10,11},{11... | collective-permute-start | bytes 98312 | tf_op jit(solution)/shard_map/ppermute | solution.py:641
  72.4 1.9 %collective-permute-start.7 = (f32[8,8,128]{2,1,0:T(8,128)S(1)}, f32[8,8,128]{2,1,0:T(8,128)S(1)}, u32[]{:S(2)}, u32[]{:S(2)}) collective-permute-start(f32[8,8,128]{2,1,0:T(8,128)S(1)} %get-tuple-element.39), channel_id=1, source_target_pairs={{1,0},{2,1},{3,2},{4,3},{5,4},{6,5},{7,6},{9,8},{10,9},{11,10},{12... | collective-permute-start | bytes 98312 | tf_op jit(solution)/shard_map/ppermute | solution.py:641
  74.3 3.1 %collective-permute-start.8 = (f32[12,8,128]{2,1,0:T(8,128)S(1)}, f32[12,8,128]{2,1,0:T(8,128)S(1)}, u32[]{:S(2)}, u32[]{:S(2)}) collective-permute-start(f32[12,8,128]{2,1,0:T(8,128)S(1)} %get-tuple-element.40), channel_id=1, source_target_pairs={{0,8},{8,16},{16,24},{24,32},{32,40},{40,48},{48,56},{56,64},{64,7... | collective-permute-start | bytes 147464 | tf_op jit(solution)/shard_map/ppermute | solution.py:641
  77.4 1.3 collective-permute-start.9
  78.7 0.1 pad_add_fusion.refs_0_
  78.8 7.0 %all-to-all-done = f32[256,1,384]{2,1,0:T(1,128)S(1)} async-done(((f32[256,1,384]{2,1,0:T(1,128)}), f32[256,1,384]{2,1,0:T(1,128)S(1)}, u32[]{:S(2)}, u32[]{:S(2)}) %all-to-all-start) | async-done | bytes 393248 | tf_op jit(solution)/shard_map/all_to_all | solution.py:648
  85.9 0.0 collective-permute-done.6.refs_2_
  85.9 0.0 collective-permute-done.8.refs_4_
  85.9 0.0 collective-permute-done.9.refs_5_
  85.9 7.0 %up_first.1 = (f32[4,2,3,8,128]{4,3,2,1,0:T(8,128)S(1)}, f32[3,2,3,8,128]{4,3,2,1,0:T(8,128)S(1)}, f32[3,2,3,8,128]{4,3,2,1,0:T(8,128)S(1)}, f32[8,8,128]{2,1,0:...) custom-call(s32[2]{0:T(128)S(1)} %pad_add_fusion.refs_0_, f32[32,8,384]{2,1,0:T(8,128)S(1)} %bitcast.14, ...), custom_call_target="tpu_custom_call" | custom-call | tf_op jit(solution)/shard_map/up_first/pallas_call | solution.py:29
  92.9 4.2 %collective-permute-start.10 = (f32[3,2,3,8,128]{4,3,2,1,0:T(8,128)S(1)}, f32[3,2,3,8,128]{4,3,2,1,0:T(8,128)S(1)}, u32[]{:S(2)}, u32[]{:S(2)}) collective-permute-start(f32[3,2,3,8,128]{4,3,2,1,0:T(8,128)S(1)} %get-tuple-element.49), channel_id=1, source_target_pairs={{0,16},{8,24},{16,32},{24,40},{32,48},{40,56},{48,64},{56,72},{64,... | collective-permute-start | bytes 221192 | tf_op jit(solution)/shard_map/ppermute | solution.py:641
  97.1 2.1 %collective-permute-start.11 = (f32[4,2,3,8,128]{4,3,2,1,0:T(8,128)S(1)}, f32[4,2,3,8,128]{4,3,2,1,0:T(8,128)S(1)}, u32[]{:S(2)}, u32[]{:S(2)}) collective-permute-start(f32[4,2,3,8,128]{4,3,2,1,0:T(8,128)S(1)} %get-tuple-element.50), channel_id=1, source_target_pairs={{0,8},{8,16},{16,24},{24,32},{32,40},{40,48},{48,56},{56,64},{64,7... | collective-permute-start | bytes 294920 | tf_op jit(solution)/shard_map/ppermute | solution.py:641
  99.2 1.3 collective-permute-start.12
  100.5 1.3 collective-permute-start.13
  101.8 0.0 collective-permute-done.10
  101.8 0.0 collective-permute-done.11
  101.9 2.7 %collective-permute-done.12 = f32[4,2,3,8,128]{4,3,2,1,0:T(8,128)S(1)} collective-permute-done((f32[4,2,3,8,128]{4,3,2,1,0:T(8,128)S(1)}, f32[4,2,3,8,128]{4,3,2,1,0:T(8,128)S(1)}, u32[]{:S(2)}, u32[]{:S(2)}) %collective-permute-start.12) | collective-permute-done | bytes 98336 | tf_op jit(solution)/shard_map/ppermute | solution.py:641
  104.6 2.9 %collective-permute-done.13 = f32[3,2,3,8,128]{4,3,2,1,0:T(8,128)S(1)} collective-permute-done((f32[3,2,3,8,128]{4,3,2,1,0:T(8,128)S(1)}, f32[3,2,3,8,128]{4,3,2,1,0:T(8,128)S(1)}, u32[]{:S(2)}, u32[]{:S(2)}) %collective-permute-start.13) | collective-permute-done | bytes 73760 | tf_op jit(solution)/shard_map/ppermute | solution.py:641
  107.5 5.5 %collective-permute-start.14 = (f32[116,8,128]{2,1,0:T(8,128)S(1)}, f32[116,8,128]{2,1,0:T(8,128)S(1)}, u32[]{:S(2)}, u32[]{:S(2)}) collective-permute-start(f32[116,8,128]{2,1,0:T(8,128)S(1)} %pad_maximum_fusion.refs_0_), channel_id=1, source_target_pairs={{0,1},{1,2},{2,3},{3,4},{4,5},{5,6},{6,7},{8,9},{9,10},{10,11},{11... | collective-permute-start | bytes 1425416 | tf_op jit(solution)/shard_map/ppermute | solution.py:641
  113.0 1.9 %collective-permute-start.15 = (f32[116,8,128]{2,1,0:T(8,128)S(1)}, f32[116,8,128]{2,1,0:T(8,128)S(1)}, u32[]{:S(2)}, u32[]{:S(2)}) collective-permute-start(f32[116,8,128]{2,1,0:T(8,128)S(1)} %pad_maximum_fusion.refs_0_), channel_id=1, source_target_pairs={{1,0},{2,1},{3,2},{4,3},{5,4},{6,5},{7,6},{9,8},{10,9},{11,10},{12... | collective-permute-start | bytes 1425416 | tf_op jit(solution)/shard_map/ppermute | solution.py:641
  114.9 3.6 %collective-permute-done.14.refs_1_ = f32[116,8,128]{2,1,0:T(8,128)S(1)} collective-permute-done((f32[116,8,128]{2,1,0:T(8,128)S(1)}, f32[116,8,128]{2,1,0:T(8,128)S(1)}, u32[]{:S(2)}, u32[]{:S(2)}) %collective-permute-start.14) | collective-permute-done | bytes 475168 | tf_op jit(solution)/shard_map/ppermute | solution.py:641
  118.6 4.4 %collective-permute-done.15.refs_2_ = f32[116,8,128]{2,1,0:T(8,128)S(1)} collective-permute-done((f32[116,8,128]{2,1,0:T(8,128)S(1)}, f32[116,8,128]{2,1,0:T(8,128)S(1)}, u32[]{:S(2)}, u32[]{:S(2)}) %collective-permute-start.15) | collective-permute-done | bytes 475168 | tf_op jit(solution)/shard_map/ppermute | solution.py:641
  123.0 7.0 %down_second.1 = (f32[8,2,4,24,128]{4,3,2,1,0:T(8,128)}, f32[12,2,4,24,128]{4,3,2,1,0:T(8,128)}, f32[6,2,2,24,128]{4,3,2,1,0:T(8,128)}, f32[6,2,2,40,128]{4,3,2,...) custom-call(f32[116,8,128]{2,1,0:T(8,128)S(1)} %pad_maximum_fusion.r, ...), custom_call_target="tpu_custom_call" | custom-call | tf_op jit(solution)/shard_map/down_second/pallas_call | solution.py:29
  130.0 1.0 broadcast_in_dim.29
  131.0 14.9 %all-to-all-start.2 = ((f32[256,1,384]{2,1,0:T(1,128)}), f32[256,1,384]{2,1,0:T(1,128)S(1)}, u32[]{:S(2)}, u32[]{:S(2)}) async-start(f32[256,1,384]{2,1,0:T(1,128)} %broadcast_in_dim.29), calls=%async_computation.2 | async-start | bytes 786432 | tf_op jit(solution)/shard_map/all_to_all | solution.py:648
  145.8 3.3 %collective-permute-start.18 = (f32[12,8,128]{2,1,0:T(8,128)S(1)}, f32[12,8,128]{2,1,0:T(8,128)S(1)}, u32[]{:S(2)}, u32[]{:S(2)}) collective-permute-start(f32[12,8,128]{2,1,0:T(8,128)S(1)} %get-tuple-element.57), channel_id=1, source_target_pairs={{0,8},{8,16},{16,24},{24,32},{32,40},{40,48},{48,56},{56,64},{64,7... | collective-permute-start | bytes 147464 | tf_op jit(solution)/shard_map/ppermute | solution.py:641
  149.1 1.3 collective-permute-start.19
  150.4 3.7 %collective-permute-start.16 = (f32[8,8,128]{2,1,0:T(8,128)S(1)}, f32[8,8,128]{2,1,0:T(8,128)S(1)}, u32[]{:S(2)}, u32[]{:S(2)}) collective-permute-start(f32[8,8,128]{2,1,0:T(8,128)S(1)} %get-tuple-element.56), channel_id=1, source_target_pairs={{0,1},{1,2},{2,3},{3,4},{4,5},{5,6},{6,7},{8,9},{9,10},{10,11},{11... | collective-permute-start | bytes 98312 | tf_op jit(solution)/shard_map/ppermute | solution.py:641
  154.1 1.9 %collective-permute-start.17 = (f32[8,8,128]{2,1,0:T(8,128)S(1)}, f32[8,8,128]{2,1,0:T(8,128)S(1)}, u32[]{:S(2)}, u32[]{:S(2)}) collective-permute-start(f32[8,8,128]{2,1,0:T(8,128)S(1)} %get-tuple-element.56), channel_id=1, source_target_pairs={{1,0},{2,1},{3,2},{4,3},{5,4},{6,5},{7,6},{9,8},{10,9},{11,10},{12... | collective-permute-start | bytes 98312 | tf_op jit(solution)/shard_map/ppermute | solution.py:641
  156.0 6.9 %all-to-all-done.2 = f32[256,1,384]{2,1,0:T(1,128)S(1)} async-done(((f32[256,1,384]{2,1,0:T(1,128)}), f32[256,1,384]{2,1,0:T(1,128)S(1)}, u32[]{:S(2)}, u32[]{:S(2)}) %all-to-all-start.2) | async-done | bytes 393248 | tf_op jit(solution)/shard_map/all_to_all | solution.py:648
  163.0 7.6 %up_second.1 = f32[2,4,8,384]{3,2,1,0:T(8,128)} custom-call(s32[2]{0:T(128)S(1)} %pad_add_fusion.refs_0_, f32[32,8,384]{2,1,0:T(8,128)S(1)} %bitcast.13, f32[8,8,128]{2,1,0:T(8,128)S(1)} %collective-permute-done.16.refs_2_, f32[8,8,128]{2,1,0:T(8,128)S(1)} %collective-permute-done.17.refs_3_, f32[12,8,128]{2,1,0:T(8,128)S(1)} %collective-permute-done.18.refs_4_, ...), custom_call_target="tpu_custom_call" | custom-call | tf_op jit(solution)/shard_map/up_second/pallas_call | solution.py:29
  (24 shorter events, 0.3 us)
Async XLA Ops:
  1.5 10.6 %collective-permute-start = (f32[2,4,3,8,128]{4,3,2,1,0:T(8,128)S(1)}, f32[2,4,3,8,128]{4,3,2,1,0:T(8,128)S(1)}, u32[]{:S(2)}, u32[]{:S(2)}) collective-permute-start(f32[2,4,3,8,128]{4,3,2,1,0:T(8,128)S(1)} %get-tuple-element.35), channel_id=1, source_target_pairs={{0,16},{8,24},{16,32},{24,40},{32,48},{40,56},{48,64},{56,72},{64,... | collective-permute-start | bytes 294920 | tf_op jit(solution)/shard_map/ppermute | solution.py:641
  7.2 5.6 %collective-permute-start.1 = (f32[4,4,3,8,128]{4,3,2,1,0:T(8,128)S(1)}, f32[4,4,3,8,128]{4,3,2,1,0:T(8,128)S(1)}, u32[]{:S(2)}, u32[]{:S(2)}) collective-permute-start(f32[4,4,3,8,128]{4,3,2,1,0:T(8,128)S(1)} %get-tuple-element.36), channel_id=1, source_target_pairs={{0,8},{8,16},{16,24},{24,32},{32,40},{40,48},{48,56},{56,64},{64,7... | collective-permute-start | bytes 589832 | tf_op jit(solution)/shard_map/ppermute | solution.py:641
  9.5 7.1 %collective-permute-start.2 = (f32[4,4,3,8,128]{4,3,2,1,0:T(8,128)S(1)}, f32[4,4,3,8,128]{4,3,2,1,0:T(8,128)S(1)}, u32[]{:S(2)}, u32[]{:S(2)}) collective-permute-start(f32[4,4,3,8,128]{4,3,2,1,0:T(8,128)S(1)} %get-tuple-element.36), channel_id=1, source_target_pairs={{8,0},{16,8},{24,16},{32,24},{40,32},{48,40},{56,48},{64,56},{72,6... | collective-permute-start | bytes 589832 | tf_op jit(solution)/shard_map/ppermute | solution.py:641
  10.8 7.8 %collective-permute-start.3 = (f32[2,4,3,8,128]{4,3,2,1,0:T(8,128)S(1)}, f32[2,4,3,8,128]{4,3,2,1,0:T(8,128)S(1)}, u32[]{:S(2)}, u32[]{:S(2)}) collective-permute-start(f32[2,4,3,8,128]{4,3,2,1,0:T(8,128)S(1)} %get-tuple-element.37), channel_id=1, source_target_pairs={{16,0},{24,8},{32,16},{40,24},{48,32},{56,40},{64,48},{72,56},{80,... | collective-permute-start | bytes 294920 | tf_op jit(solution)/shard_map/ppermute | solution.py:641
  18.6 25.9 %collective-permute-start.4 = (f32[16,4,3,8,128]{4,3,2,1,0:T(8,128)S(1)}, f32[16,4,3,8,128]{4,3,2,1,0:T(8,128)S(1)}, u32[]{:S(2)}, u32[]{:S(2)}) collective-permute-start(f32[16,4,3,8,128]{4,3,2,1,0:T(8,128)S(1)} %constant_dynamic-update-slice_fusion.refs_0_), channel_id=1, source_target_pairs={{0,1},{1,2},{2,3},{3,4},{4,5},{5,6},{6,7},{8,9},{9,10},{10,11},{11... | collective-permute-start | bytes 2359304 | tf_op jit(solution)/shard_map/ppermute | solution.py:641
  23.4 21.2 %collective-permute-start.5 = (f32[16,4,3,8,128]{4,3,2,1,0:T(8,128)S(1)}, f32[16,4,3,8,128]{4,3,2,1,0:T(8,128)S(1)}, u32[]{:S(2)}, u32[]{:S(2)}) collective-permute-start(f32[16,4,3,8,128]{4,3,2,1,0:T(8,128)S(1)} %constant_dynamic-update-slice_fusion.refs_0_), channel_id=1, source_target_pairs={{1,0},{2,1},{3,2},{4,3},{5,4},{6,5},{7,6},{9,8},{10,9},{11,10},{12... | collective-permute-start | bytes 2359304 | tf_op jit(solution)/shard_map/ppermute | solution.py:641
  26.3 35.3 %all-to-all-start.1 = ((f32[256,1,384]{2,1,0:T(1,128)}), f32[256,1,384]{2,1,0:T(1,128)S(1)}, u32[]{:S(2)}, u32[]{:S(2)}) async-start(f32[256,1,384]{2,1,0:T(1,128)} %broadcast_in_dim.27), calls=%async_computation.1 | async-start | bytes 786432 | tf_op jit(solution)/shard_map/all_to_all | solution.py:648
  62.5 23.3 %all-to-all-start = ((f32[256,1,384]{2,1,0:T(1,128)}), f32[256,1,384]{2,1,0:T(1,128)S(1)}, u32[]{:S(2)}, u32[]{:S(2)}) async-start(f32[256,1,384]{2,1,0:T(1,128)} %broadcast_in_dim.25), calls=%async_computation | async-start | bytes 786432 | tf_op jit(solution)/shard_map/all_to_all | solution.py:648
  68.8 17.0 %collective-permute-start.6 = (f32[8,8,128]{2,1,0:T(8,128)S(1)}, f32[8,8,128]{2,1,0:T(8,128)S(1)}, u32[]{:S(2)}, u32[]{:S(2)}) collective-permute-start(f32[8,8,128]{2,1,0:T(8,128)S(1)} %get-tuple-element.39), channel_id=1, source_target_pairs={{0,1},{1,2},{2,3},{3,4},{4,5},{5,6},{6,7},{8,9},{9,10},{10,11},{11... | collective-permute-start | bytes 98312 | tf_op jit(solution)/shard_map/ppermute | solution.py:641
  72.4 13.5 %collective-permute-start.7 = (f32[8,8,128]{2,1,0:T(8,128)S(1)}, f32[8,8,128]{2,1,0:T(8,128)S(1)}, u32[]{:S(2)}, u32[]{:S(2)}) collective-permute-start(f32[8,8,128]{2,1,0:T(8,128)S(1)} %get-tuple-element.39), channel_id=1, source_target_pairs={{1,0},{2,1},{3,2},{4,3},{5,4},{6,5},{7,6},{9,8},{10,9},{11,10},{12... | collective-permute-start | bytes 98312 | tf_op jit(solution)/shard_map/ppermute | solution.py:641
  74.3 11.6 %collective-permute-start.8 = (f32[12,8,128]{2,1,0:T(8,128)S(1)}, f32[12,8,128]{2,1,0:T(8,128)S(1)}, u32[]{:S(2)}, u32[]{:S(2)}) collective-permute-start(f32[12,8,128]{2,1,0:T(8,128)S(1)} %get-tuple-element.40), channel_id=1, source_target_pairs={{0,8},{8,16},{16,24},{24,32},{32,40},{40,48},{48,56},{56,64},{64,7... | collective-permute-start | bytes 147464 | tf_op jit(solution)/shard_map/ppermute | solution.py:641
  77.4 8.5 %collective-permute-start.9 = (f32[12,8,128]{2,1,0:T(8,128)S(1)}, f32[12,8,128]{2,1,0:T(8,128)S(1)}, u32[]{:S(2)}, u32[]{:S(2)}) collective-permute-start(f32[12,8,128]{2,1,0:T(8,128)S(1)} %get-tuple-element.41), channel_id=1, source_target_pairs={{8,0},{16,8},{24,16},{32,24},{40,32},{48,40},{56,48},{64,56},{72,6... | collective-permute-start | bytes 147464 | tf_op jit(solution)/shard_map/ppermute | solution.py:641
  92.9 8.9 %collective-permute-start.10 = (f32[3,2,3,8,128]{4,3,2,1,0:T(8,128)S(1)}, f32[3,2,3,8,128]{4,3,2,1,0:T(8,128)S(1)}, u32[]{:S(2)}, u32[]{:S(2)}) collective-permute-start(f32[3,2,3,8,128]{4,3,2,1,0:T(8,128)S(1)} %get-tuple-element.49), channel_id=1, source_target_pairs={{0,16},{8,24},{16,32},{24,40},{32,48},{40,56},{48,64},{56,72},{64,... | collective-permute-start | bytes 221192 | tf_op jit(solution)/shard_map/ppermute | solution.py:641
  97.1 4.7 %collective-permute-start.11 = (f32[4,2,3,8,128]{4,3,2,1,0:T(8,128)S(1)}, f32[4,2,3,8,128]{4,3,2,1,0:T(8,128)S(1)}, u32[]{:S(2)}, u32[]{:S(2)}) collective-permute-start(f32[4,2,3,8,128]{4,3,2,1,0:T(8,128)S(1)} %get-tuple-element.50), channel_id=1, source_target_pairs={{0,8},{8,16},{16,24},{24,32},{32,40},{40,48},{48,56},{56,64},{64,7... | collective-permute-start | bytes 294920 | tf_op jit(solution)/shard_map/ppermute | solution.py:641
  99.2 5.4 %collective-permute-start.12 = (f32[4,2,3,8,128]{4,3,2,1,0:T(8,128)S(1)}, f32[4,2,3,8,128]{4,3,2,1,0:T(8,128)S(1)}, u32[]{:S(2)}, u32[]{:S(2)}) collective-permute-start(f32[4,2,3,8,128]{4,3,2,1,0:T(8,128)S(1)} %get-tuple-element.50), channel_id=1, source_target_pairs={{8,0},{16,8},{24,16},{32,24},{40,32},{48,40},{56,48},{64,56},{72,6... | collective-permute-start | bytes 294920 | tf_op jit(solution)/shard_map/ppermute | solution.py:641
  100.5 6.9 %collective-permute-start.13 = (f32[3,2,3,8,128]{4,3,2,1,0:T(8,128)S(1)}, f32[3,2,3,8,128]{4,3,2,1,0:T(8,128)S(1)}, u32[]{:S(2)}, u32[]{:S(2)}) collective-permute-start(f32[3,2,3,8,128]{4,3,2,1,0:T(8,128)S(1)} %get-tuple-element.51), channel_id=1, source_target_pairs={{16,0},{24,8},{32,16},{40,24},{48,32},{56,40},{64,48},{72,56},{80,... | collective-permute-start | bytes 221192 | tf_op jit(solution)/shard_map/ppermute | solution.py:641
  107.5 11.1 %collective-permute-start.14 = (f32[116,8,128]{2,1,0:T(8,128)S(1)}, f32[116,8,128]{2,1,0:T(8,128)S(1)}, u32[]{:S(2)}, u32[]{:S(2)}) collective-permute-start(f32[116,8,128]{2,1,0:T(8,128)S(1)} %pad_maximum_fusion.refs_0_), channel_id=1, source_target_pairs={{0,1},{1,2},{2,3},{3,4},{4,5},{5,6},{6,7},{8,9},{9,10},{10,11},{11... | collective-permute-start | bytes 1425416 | tf_op jit(solution)/shard_map/ppermute | solution.py:641
  113.0 10.0 %collective-permute-start.15 = (f32[116,8,128]{2,1,0:T(8,128)S(1)}, f32[116,8,128]{2,1,0:T(8,128)S(1)}, u32[]{:S(2)}, u32[]{:S(2)}) collective-permute-start(f32[116,8,128]{2,1,0:T(8,128)S(1)} %pad_maximum_fusion.refs_0_), channel_id=1, source_target_pairs={{1,0},{2,1},{3,2},{4,3},{5,4},{6,5},{7,6},{9,8},{10,9},{11,10},{12... | collective-permute-start | bytes 1425416 | tf_op jit(solution)/shard_map/ppermute | solution.py:641
  131.0 31.9 %all-to-all-start.2 = ((f32[256,1,384]{2,1,0:T(1,128)}), f32[256,1,384]{2,1,0:T(1,128)S(1)}, u32[]{:S(2)}, u32[]{:S(2)}) async-start(f32[256,1,384]{2,1,0:T(1,128)} %broadcast_in_dim.29), calls=%async_computation.2 | async-start | bytes 786432 | tf_op jit(solution)/shard_map/all_to_all | solution.py:648
  145.8 17.1 %collective-permute-start.18 = (f32[12,8,128]{2,1,0:T(8,128)S(1)}, f32[12,8,128]{2,1,0:T(8,128)S(1)}, u32[]{:S(2)}, u32[]{:S(2)}) collective-permute-start(f32[12,8,128]{2,1,0:T(8,128)S(1)} %get-tuple-element.57), channel_id=1, source_target_pairs={{0,8},{8,16},{16,24},{24,32},{32,40},{40,48},{48,56},{56,64},{64,7... | collective-permute-start | bytes 147464 | tf_op jit(solution)/shard_map/ppermute | solution.py:641
  149.1 13.8 %collective-permute-start.19 = (f32[12,8,128]{2,1,0:T(8,128)S(1)}, f32[12,8,128]{2,1,0:T(8,128)S(1)}, u32[]{:S(2)}, u32[]{:S(2)}) collective-permute-start(f32[12,8,128]{2,1,0:T(8,128)S(1)} %get-tuple-element.58), channel_id=1, source_target_pairs={{8,0},{16,8},{24,16},{32,24},{40,32},{48,40},{56,48},{64,56},{72,6... | collective-permute-start | bytes 147464 | tf_op jit(solution)/shard_map/ppermute | solution.py:641
  150.4 12.5 %collective-permute-start.16 = (f32[8,8,128]{2,1,0:T(8,128)S(1)}, f32[8,8,128]{2,1,0:T(8,128)S(1)}, u32[]{:S(2)}, u32[]{:S(2)}) collective-permute-start(f32[8,8,128]{2,1,0:T(8,128)S(1)} %get-tuple-element.56), channel_id=1, source_target_pairs={{0,1},{1,2},{2,3},{3,4},{4,5},{5,6},{6,7},{8,9},{9,10},{10,11},{11... | collective-permute-start | bytes 98312 | tf_op jit(solution)/shard_map/ppermute | solution.py:641
  154.1 8.9 %collective-permute-start.17 = (f32[8,8,128]{2,1,0:T(8,128)S(1)}, f32[8,8,128]{2,1,0:T(8,128)S(1)}, u32[]{:S(2)}, u32[]{:S(2)}) collective-permute-start(f32[8,8,128]{2,1,0:T(8,128)S(1)} %get-tuple-element.56), channel_id=1, source_target_pairs={{1,0},{2,1},{3,2},{4,3},{5,4},{6,5},{7,6},{9,8},{10,9},{11,10},{12... | collective-permute-start | bytes 98312 | tf_op jit(solution)/shard_map/ppermute | solution.py:641

commit v7 on v6

--- a/solution.py
+++ b/solution.py
@@ -24,11 +24,10 @@
 PARAMS = pltpu.CompilerParams(vmem_limit_bytes=32 * 1024 * 1024)
 
 
-def run(name, kernel, inputs, outputs, scratch, copies):
+def run(kernel, inputs, outputs, scratch, copies):
     names = list(inputs) + list(outputs) + list(scratch) + ["sem"]
     result = pl.pallas_call(
         lambda *refs: kernel(SimpleNamespace(**dict(zip(names, refs)))),
-        name=name,
         out_shape=tuple(HB(dims, F32) if space is HB else jax.ShapeDtypeStruct(dims, F32) for dims, space in outputs.values()),
         in_specs=[pl.BlockSpec(memory_space=space) for _, space in inputs.values()],
         out_specs=tuple(pl.BlockSpec(memory_space=space) for _, space in outputs.values()),
@@ -201,7 +200,6 @@
 
 def pack(table, right_side, layer_index, absorb_level):
     return run(
-        "pack",
         pack_kernel,
         dict(speeds=(table, HB), right_side=(right_side, HB), layer_index=(layer_index, HB), absorb_level=(absorb_level, HB)),
         dict(packed=((4, 4, 3, 8, 128), VM), front=((2, 4, 3, 8, 128), VM), back=((2, 4, 3, 8, 128), VM),
@@ -359,7 +357,6 @@
 
 def down_first(mid, low, high):
     return run(
-        "down_first",
         down_first_kernel,
         dict(mid=(mid, VM), low=(low, VM), high=(high, VM)),
         dict(out_source=(FINE, HB), out_weight=(FINE, HB), out_diag=(FINE, HB), out_weight_one=(COARSE, HB),
@@ -416,7 +413,6 @@
 
 def down_second(mid, low, high, old):
     return run(
-        "down_second",
         down_second_kernel,
         dict(mid=(mid, VM), low=(low, VM), high=(high, VM), in_right=(old.out_source, HB), in_weight=(old.out_weight, HB),
              in_diag=(old.out_diag, HB), in_weight_one=(old.out_weight_one, HB), in_diag_one=(old.out_diag_one, HB)),
@@ -449,7 +445,7 @@
     over(0, window, 7, body)
 
 
-def solve_two(own, source, weight, ping, pong, window, planes, groups):
+def solve_two(own, source, weight, ping, pong, window, groups):
     clear(ping, window + 8)
     clear(pong, window + 8)
     rows = slice(8, 8 + groups)
@@ -528,7 +524,7 @@
     else:
         unpack_two(v.gathered_weight, begin, v.weight_two, window, True)
         copies.append(keep(v, 7, v.weight_two, v.out_weight_two))
-    answer = solve_two(v.where[0] - begin, v.source_two, v.weight_two, v.ping, v.pong, window, planes, groups)
+    answer = solve_two(v.where[0] - begin, v.source_two, v.weight_two, v.ping, v.pong, window, groups)
     clear_edges(v.one, count)
     clear_edges(v.one_next, count)
     clear_edges(v.ea, 12, 4)
@@ -612,7 +608,6 @@
 def up_first(where, gathered, gathered_weight, messages, down):
     planes, groups = gathered.shape[0], gathered.shape[1]
     return run(
-        "up_first",
         lambda v: up_first_kernel(v, planes, groups),
         dict(**up_inputs(where, gathered, messages, down, down), gathered_weight=(gathered_weight, VM)),
         dict(packed=((4, 2, 3, 8, 128), VM), front=((3, 2, 3, 8, 128), VM), back=((3, 2, 3, 8, 128), VM),
@@ -625,7 +620,6 @@
 def up_second(where, gathered, messages, down, first_down, first_up):
     planes, groups = gathered.shape[0], gathered.shape[1]
     return run(
-        "up_second",
         lambda v: up_second_kernel(v, planes, groups),
         dict(**up_inputs(where, gathered, messages, down, first_down), in_weight_two=(first_up.out_weight_two, HB),
              in_first=(first_up.out_first, HB)),
@@ -649,13 +643,14 @@
 
 
 def beside(own):
+    after = shifted(own.front, "gx", -2)
     return jnp.concatenate(
         [
             shifted(own.back, "gx", 2),
             shifted(own.packed, "gx", 1),
             own.packed,
             shifted(own.packed, "gx", -1),
-            shifted(own.front, "gx", -2),
+            after,
         ]
     )
 
@@ -677,7 +672,8 @@
     where = jnp.stack([lax.axis_index("gx"), lax.axis_index("gy")]).astype(jnp.int32)
     packed = pack(velocity_table, right_side, layer_index, absorb_level)
     weight_two = gather_two(packed.inverse_two)
-    down = down_first(*surround(beside(packed)))
+    mid = beside(packed)
+    down = down_first(*surround(mid))
     middle = up_first(where, gather_two(down.two), weight_two, exchange_one(down), down)
     rows = jnp.concatenate([beside(middle).reshape(EDGE, 8, 128), middle.edges])
     again = down_second(*surround(rows), down)

time: 171 us -> 171 us (level)
  no operation moved by 1% of the time
where the time goes in v7:
time: 171 us
  starting transfers between devices  92.9 us (54%)
  waiting for transfers between devices  44.7 us (26%)
  Pallas kernels  29.3 us (17%)
  local copies, waits for them, and re-layouts  3.07 us (2%)
    ppermute x20, starting transfers between devices, shifted(): return lax.ppermute(block, axis, pairs)  53.5 us
    all_to_all x3, starting transfers between devices, gather_two(): lax.all_to_all(sent, ('gx', 'gy'), 0, 0).reshape(count_x, count_y, width)  39.4 us
    pallas_call x5, Pallas kernels, run(): pl.pallas_call(lambda *refs: kernel(SimpleNamespace(**dict(zip(names, ref...  29.3 us
    all_to_all x3, waiting for transfers between devices, gather_two(): lax.all_to_all(sent, ('gx', 'gy'), 0, 0).reshape(count_x, count_y, width)  24.7 us
    ppermute x20, waiting for transfers between devices, shifted(): return lax.ppermute(block, axis, pairs)  20 us
  transfers between devices with their start and end apart: 23, of which 10 were waited for; matrix products, arithmetic and copies ran while one was open for 1% of the time, Pallas kernels for 4%

profile of v7, /device:TPU:1, one launch (start us, length us, event | category | flops | bytes accessed | tf_op | source)
XLA Modules:
  0.0 170.5 jit_solution(10419130760821875196)
XLA Ops:
  0.0 1.5 shard_map.46
  1.5 5.6 %collective-permute-start = (f32[2,4,3,8,128]{4,3,2,1,0:T(8,128)S(1)}, f32[2,4,3,8,128]{4,3,2,1,0:T(8,128)S(1)}, u32[]{:S(2)}, u32[]{:S(2)}) collective-permute-start(f32[2,4,3,8,128]{4,3,2,1,0:T(8,128)S(1)} %get-tuple-element.35), channel_id=1, source_target_pairs={{0,16},{8,24},{16,32},{24,40},{32,48},{40,56},{48,64},{56,72},{64,... | collective-permute-start | bytes 294920 | tf_op jit(solution)/shard_map/ppermute | solution.py:635
  7.2 2.3 %collective-permute-start.1 = (f32[4,4,3,8,128]{4,3,2,1,0:T(8,128)S(1)}, f32[4,4,3,8,128]{4,3,2,1,0:T(8,128)S(1)}, u32[]{:S(2)}, u32[]{:S(2)}) collective-permute-start(f32[4,4,3,8,128]{4,3,2,1,0:T(8,128)S(1)} %get-tuple-element.36), channel_id=1, source_target_pairs={{0,8},{8,16},{16,24},{24,32},{32,40},{40,48},{48,56},{56,64},{64,7... | collective-permute-start | bytes 589832 | tf_op jit(solution)/shard_map/ppermute | solution.py:635
  9.5 1.3 collective-permute-start.2
  10.8 1.3 collective-permute-start.3
  12.1 0.6 collective-permute-done.1
  12.8 3.8 %collective-permute-done.2 = f32[4,4,3,8,128]{4,3,2,1,0:T(8,128)S(1)} collective-permute-done((f32[4,4,3,8,128]{4,3,2,1,0:T(8,128)S(1)}, f32[4,4,3,8,128]{4,3,2,1,0:T(8,128)S(1)}, u32[]{:S(2)}, u32[]{:S(2)}) %collective-permute-start.2) | collective-permute-done | bytes 196640 | tf_op jit(solution)/shard_map/ppermute | solution.py:635
  16.7 2.0 %collective-permute-done.3 = f32[2,4,3,8,128]{4,3,2,1,0:T(8,128)S(1)} collective-permute-done((f32[2,4,3,8,128]{4,3,2,1,0:T(8,128)S(1)}, f32[2,4,3,8,128]{4,3,2,1,0:T(8,128)S(1)}, u32[]{:S(2)}, u32[]{:S(2)}) %collective-permute-start.3) | collective-permute-done | bytes 98336 | tf_op jit(solution)/shard_map/ppermute | solution.py:635
  18.6 4.8 %collective-permute-start.4 = (f32[16,4,3,8,128]{4,3,2,1,0:T(8,128)S(1)}, f32[16,4,3,8,128]{4,3,2,1,0:T(8,128)S(1)}, u32[]{:S(2)}, u32[]{:S(2)}) collective-permute-start(f32[16,4,3,8,128]{4,3,2,1,0:T(8,128)S(1)} %constant_dynamic-update-slice_fusion.refs_0_), channel_id=1, source_target_pairs={{0,1},{1,2},{2,3},{3,4},{4,5},{5,6},{6,7},{8,9},{9,10},{10,11},{11... | collective-permute-start | bytes 2359304 | tf_op jit(solution)/shard_map/ppermute | solution.py:635
  23.4 1.9 %collective-permute-start.5 = (f32[16,4,3,8,128]{4,3,2,1,0:T(8,128)S(1)}, f32[16,4,3,8,128]{4,3,2,1,0:T(8,128)S(1)}, u32[]{:S(2)}, u32[]{:S(2)}) collective-permute-start(f32[16,4,3,8,128]{4,3,2,1,0:T(8,128)S(1)} %constant_dynamic-update-slice_fusion.refs_0_), channel_id=1, source_target_pairs={{1,0},{2,1},{3,2},{4,3},{5,4},{6,5},{7,6},{9,8},{10,9},{11,10},{12... | collective-permute-start | bytes 2359304 | tf_op jit(solution)/shard_map/ppermute | solution.py:635
  25.3 1.0 broadcast_in_dim.27
  26.3 18.2 %all-to-all-start.1 = ((f32[256,1,384]{2,1,0:T(1,128)}), f32[256,1,384]{2,1,0:T(1,128)S(1)}, u32[]{:S(2)}, u32[]{:S(2)}) async-start(f32[256,1,384]{2,1,0:T(1,128)} %broadcast_in_dim.27), calls=%async_computation.1 | async-start | bytes 786432 | tf_op jit(solution)/shard_map/all_to_all | solution.py:642
  44.5 0.0 collective-permute-done.5.refs_2_
  44.6 6.2 %shard_map.47 = (f32[16,2,4,24,128]{4,3,2,1,0:T(8,128)}, f32[16,2,4,24,128]{4,3,2,1,0:T(8,128)}, f32[16,2,4,24,128]{4,3,2,1,0:T(8,128)}, f32[6,2,2,24,128]{4,3,2...) custom-call(f32[16,4,3,8,128]{4,3,2,1,0:T(8,128)S(1)} %constant_dyna, ...), custom_call_target="tpu_custom_call" | custom-call | tf_op jit(solution)/shard_map/pallas_call | solution.py:29
  50.8 10.8 %all-to-all-done.1 = f32[256,1,384]{2,1,0:T(1,128)S(1)} async-done(((f32[256,1,384]{2,1,0:T(1,128)}), f32[256,1,384]{2,1,0:T(1,128)S(1)}, u32[]{:S(2)}, u32[]{:S(2)}) %all-to-all-start.1) | async-done | bytes 393248 | tf_op jit(solution)/shard_map/all_to_all | solution.py:642
  61.5 1.0 broadcast_in_dim.25
  62.5 6.3 %all-to-all-start = ((f32[256,1,384]{2,1,0:T(1,128)}), f32[256,1,384]{2,1,0:T(1,128)S(1)}, u32[]{:S(2)}, u32[]{:S(2)}) async-start(f32[256,1,384]{2,1,0:T(1,128)} %broadcast_in_dim.25), calls=%async_computation | async-start | bytes 786432 | tf_op jit(solution)/shard_map/all_to_all | solution.py:642
  68.8 3.5 %collective-permute-start.6 = (f32[8,8,128]{2,1,0:T(8,128)S(1)}, f32[8,8,128]{2,1,0:T(8,128)S(1)}, u32[]{:S(2)}, u32[]{:S(2)}) collective-permute-start(f32[8,8,128]{2,1,0:T(8,128)S(1)} %get-tuple-element.39), channel_id=1, source_target_pairs={{0,1},{1,2},{2,3},{3,4},{4,5},{5,6},{6,7},{8,9},{9,10},{10,11},{11... | collective-permute-start | bytes 98312 | tf_op jit(solution)/shard_map/ppermute | solution.py:635
  72.4 1.9 %collective-permute-start.7 = (f32[8,8,128]{2,1,0:T(8,128)S(1)}, f32[8,8,128]{2,1,0:T(8,128)S(1)}, u32[]{:S(2)}, u32[]{:S(2)}) collective-permute-start(f32[8,8,128]{2,1,0:T(8,128)S(1)} %get-tuple-element.39), channel_id=1, source_target_pairs={{1,0},{2,1},{3,2},{4,3},{5,4},{6,5},{7,6},{9,8},{10,9},{11,10},{12... | collective-permute-start | bytes 98312 | tf_op jit(solution)/shard_map/ppermute | solution.py:635
  74.3 3.1 %collective-permute-start.8 = (f32[12,8,128]{2,1,0:T(8,128)S(1)}, f32[12,8,128]{2,1,0:T(8,128)S(1)}, u32[]{:S(2)}, u32[]{:S(2)}) collective-permute-start(f32[12,8,128]{2,1,0:T(8,128)S(1)} %get-tuple-element.40), channel_id=1, source_target_pairs={{0,8},{8,16},{16,24},{24,32},{32,40},{40,48},{48,56},{56,64},{64,7... | collective-permute-start | bytes 147464 | tf_op jit(solution)/shard_map/ppermute | solution.py:635
  77.4 1.3 collective-permute-start.9
  78.7 0.1 pad_add_fusion.refs_0_
  78.8 7.0 %all-to-all-done = f32[256,1,384]{2,1,0:T(1,128)S(1)} async-done(((f32[256,1,384]{2,1,0:T(1,128)}), f32[256,1,384]{2,1,0:T(1,128)S(1)}, u32[]{:S(2)}, u32[]{:S(2)}) %all-to-all-start) | async-done | bytes 393248 | tf_op jit(solution)/shard_map/all_to_all | solution.py:642
  85.9 0.0 collective-permute-done.8.refs_4_
  85.9 0.0 collective-permute-done.9.refs_5_
  85.9 7.0 %shard_map.48 = (f32[4,2,3,8,128]{4,3,2,1,0:T(8,128)S(1)}, f32[3,2,3,8,128]{4,3,2,1,0:T(8,128)S(1)}, f32[3,2,3,8,128]{4,3,2,1,0:T(8,128)S(1)}, f32[8,8,128]{2,1,...) custom-call(s32[2]{0:T(128)S(1)} %pad_add_fusion.refs_0_, f32[32,8,384]{2,1,0:T(8,128)S(1)} %bitcast.14, ...), custom_call_target="tpu_custom_call" | custom-call | tf_op jit(solution)/shard_map/pallas_call | solution.py:29
  92.9 4.2 %collective-permute-start.10 = (f32[3,2,3,8,128]{4,3,2,1,0:T(8,128)S(1)}, f32[3,2,3,8,128]{4,3,2,1,0:T(8,128)S(1)}, u32[]{:S(2)}, u32[]{:S(2)}) collective-permute-start(f32[3,2,3,8,128]{4,3,2,1,0:T(8,128)S(1)} %get-tuple-element.49), channel_id=1, source_target_pairs={{0,16},{8,24},{16,32},{24,40},{32,48},{40,56},{48,64},{56,72},{64,... | collective-permute-start | bytes 221192 | tf_op jit(solution)/shard_map/ppermute | solution.py:635
  97.1 2.1 %collective-permute-start.11 = (f32[4,2,3,8,128]{4,3,2,1,0:T(8,128)S(1)}, f32[4,2,3,8,128]{4,3,2,1,0:T(8,128)S(1)}, u32[]{:S(2)}, u32[]{:S(2)}) collective-permute-start(f32[4,2,3,8,128]{4,3,2,1,0:T(8,128)S(1)} %get-tuple-element.50), channel_id=1, source_target_pairs={{0,8},{8,16},{16,24},{24,32},{32,40},{40,48},{48,56},{56,64},{64,7... | collective-permute-start | bytes 294920 | tf_op jit(solution)/shard_map/ppermute | solution.py:635
  99.2 1.3 collective-permute-start.12
  100.5 1.3 collective-permute-start.13
  101.8 0.0 collective-permute-done.10
  101.8 0.0 collective-permute-done.11
  101.9 2.7 %collective-permute-done.12 = f32[4,2,3,8,128]{4,3,2,1,0:T(8,128)S(1)} collective-permute-done((f32[4,2,3,8,128]{4,3,2,1,0:T(8,128)S(1)}, f32[4,2,3,8,128]{4,3,2,1,0:T(8,128)S(1)}, u32[]{:S(2)}, u32[]{:S(2)}) %collective-permute-start.12) | collective-permute-done | bytes 98336 | tf_op jit(solution)/shard_map/ppermute | solution.py:635
  104.6 2.9 %collective-permute-done.13 = f32[3,2,3,8,128]{4,3,2,1,0:T(8,128)S(1)} collective-permute-done((f32[3,2,3,8,128]{4,3,2,1,0:T(8,128)S(1)}, f32[3,2,3,8,128]{4,3,2,1,0:T(8,128)S(1)}, u32[]{:S(2)}, u32[]{:S(2)}) %collective-permute-start.13) | collective-permute-done | bytes 73760 | tf_op jit(solution)/shard_map/ppermute | solution.py:635
  107.5 5.5 %collective-permute-start.14 = (f32[116,8,128]{2,1,0:T(8,128)S(1)}, f32[116,8,128]{2,1,0:T(8,128)S(1)}, u32[]{:S(2)}, u32[]{:S(2)}) collective-permute-start(f32[116,8,128]{2,1,0:T(8,128)S(1)} %pad_maximum_fusion.refs_0_), channel_id=1, source_target_pairs={{0,1},{1,2},{2,3},{3,4},{4,5},{5,6},{6,7},{8,9},{9,10},{10,11},{11... | collective-permute-start | bytes 1425416 | tf_op jit(solution)/shard_map/ppermute | solution.py:635
  113.0 1.9 %collective-permute-start.15 = (f32[116,8,128]{2,1,0:T(8,128)S(1)}, f32[116,8,128]{2,1,0:T(8,128)S(1)}, u32[]{:S(2)}, u32[]{:S(2)}) collective-permute-start(f32[116,8,128]{2,1,0:T(8,128)S(1)} %pad_maximum_fusion.refs_0_), channel_id=1, source_target_pairs={{1,0},{2,1},{3,2},{4,3},{5,4},{6,5},{7,6},{9,8},{10,9},{11,10},{12... | collective-permute-start | bytes 1425416 | tf_op jit(solution)/shard_map/ppermute | solution.py:635
  114.9 3.6 %collective-permute-done.14.refs_1_ = f32[116,8,128]{2,1,0:T(8,128)S(1)} collective-permute-done((f32[116,8,128]{2,1,0:T(8,128)S(1)}, f32[116,8,128]{2,1,0:T(8,128)S(1)}, u32[]{:S(2)}, u32[]{:S(2)}) %collective-permute-start.14) | collective-permute-done | bytes 475168 | tf_op jit(solution)/shard_map/ppermute | solution.py:635
  118.6 4.4 %collective-permute-done.15.refs_2_ = f32[116,8,128]{2,1,0:T(8,128)S(1)} collective-permute-done((f32[116,8,128]{2,1,0:T(8,128)S(1)}, f32[116,8,128]{2,1,0:T(8,128)S(1)}, u32[]{:S(2)}, u32[]{:S(2)}) %collective-permute-start.15) | collective-permute-done | bytes 475168 | tf_op jit(solution)/shard_map/ppermute | solution.py:635
  123.0 7.0 %shard_map.49 = (f32[8,2,4,24,128]{4,3,2,1,0:T(8,128)}, f32[12,2,4,24,128]{4,3,2,1,0:T(8,128)}, f32[6,2,2,24,128]{4,3,2,1,0:T(8,128)}, f32[6,2,2,40,128]{4,3,2,1...) custom-call(f32[116,8,128]{2,1,0:T(8,128)S(1)} %pad_maximum_fusion.r, ...), custom_call_target="tpu_custom_call" | custom-call | tf_op jit(solution)/shard_map/pallas_call | solution.py:29
  130.0 1.0 broadcast_in_dim.29
  131.0 14.9 %all-to-all-start.2 = ((f32[256,1,384]{2,1,0:T(1,128)}), f32[256,1,384]{2,1,0:T(1,128)S(1)}, u32[]{:S(2)}, u32[]{:S(2)}) async-start(f32[256,1,384]{2,1,0:T(1,128)} %broadcast_in_dim.29), calls=%async_computation.2 | async-start | bytes 786432 | tf_op jit(solution)/shard_map/all_to_all | solution.py:642
  145.8 3.3 %collective-permute-start.18 = (f32[12,8,128]{2,1,0:T(8,128)S(1)}, f32[12,8,128]{2,1,0:T(8,128)S(1)}, u32[]{:S(2)}, u32[]{:S(2)}) collective-permute-start(f32[12,8,128]{2,1,0:T(8,128)S(1)} %get-tuple-element.57), channel_id=1, source_target_pairs={{0,8},{8,16},{16,24},{24,32},{32,40},{40,48},{48,56},{56,64},{64,7... | collective-permute-start | bytes 147464 | tf_op jit(solution)/shard_map/ppermute | solution.py:635
  149.1 1.3 collective-permute-start.19
  150.4 3.7 %collective-permute-start.16 = (f32[8,8,128]{2,1,0:T(8,128)S(1)}, f32[8,8,128]{2,1,0:T(8,128)S(1)}, u32[]{:S(2)}, u32[]{:S(2)}) collective-permute-start(f32[8,8,128]{2,1,0:T(8,128)S(1)} %get-tuple-element.56), channel_id=1, source_target_pairs={{0,1},{1,2},{2,3},{3,4},{4,5},{5,6},{6,7},{8,9},{9,10},{10,11},{11... | collective-permute-start | bytes 98312 | tf_op jit(solution)/shard_map/ppermute | solution.py:635
  154.1 1.9 %collective-permute-start.17 = (f32[8,8,128]{2,1,0:T(8,128)S(1)}, f32[8,8,128]{2,1,0:T(8,128)S(1)}, u32[]{:S(2)}, u32[]{:S(2)}) collective-permute-start(f32[8,8,128]{2,1,0:T(8,128)S(1)} %get-tuple-element.56), channel_id=1, source_target_pairs={{1,0},{2,1},{3,2},{4,3},{5,4},{6,5},{7,6},{9,8},{10,9},{11,10},{12... | collective-permute-start | bytes 98312 | tf_op jit(solution)/shard_map/ppermute | solution.py:635
  156.0 6.9 %all-to-all-done.2 = f32[256,1,384]{2,1,0:T(1,128)S(1)} async-done(((f32[256,1,384]{2,1,0:T(1,128)}), f32[256,1,384]{2,1,0:T(1,128)S(1)}, u32[]{:S(2)}, u32[]{:S(2)}) %all-to-all-start.2) | async-done | bytes 393248 | tf_op jit(solution)/shard_map/all_to_all | solution.py:642
  162.9 0.0 collective-permute-done.16.refs_2_
  163.0 7.6 %shard_map.50 = f32[2,4,8,384]{3,2,1,0:T(8,128)} custom-call(s32[2]{0:T(128)S(1)} %pad_add_fusion.refs_0_, f32[32,8,384]{2,1,0:T(8,128)S(1)} %bitcast.13, f32[8,8,128]{2,1,0:T(8,128)S(1)} %collective-permute-done.16.refs_2_, f32[8,8,128]{2,1,0:T(8,128)S(1)} %collective-permute-done.17.refs_3_, f32[12,8,128]{2,1,0:T(8,128)S(1)} %collective-permute-done.18.refs_4_, ...), custom_call_target="tpu_custom_call" | custom-call | tf_op jit(solution)/shard_map/pallas_call | solution.py:29
  (24 shorter events, 0.3 us)
Async XLA Ops:
  1.5 10.6 %collective-permute-start = (f32[2,4,3,8,128]{4,3,2,1,0:T(8,128)S(1)}, f32[2,4,3,8,128]{4,3,2,1,0:T(8,128)S(1)}, u32[]{:S(2)}, u32[]{:S(2)}) collective-permute-start(f32[2,4,3,8,128]{4,3,2,1,0:T(8,128)S(1)} %get-tuple-element.35), channel_id=1, source_target_pairs={{0,16},{8,24},{16,32},{24,40},{32,48},{40,56},{48,64},{56,72},{64,... | collective-permute-start | bytes 294920 | tf_op jit(solution)/shard_map/ppermute | solution.py:635
  7.2 5.6 %collective-permute-start.1 = (f32[4,4,3,8,128]{4,3,2,1,0:T(8,128)S(1)}, f32[4,4,3,8,128]{4,3,2,1,0:T(8,128)S(1)}, u32[]{:S(2)}, u32[]{:S(2)}) collective-permute-start(f32[4,4,3,8,128]{4,3,2,1,0:T(8,128)S(1)} %get-tuple-element.36), channel_id=1, source_target_pairs={{0,8},{8,16},{16,24},{24,32},{32,40},{40,48},{48,56},{56,64},{64,7... | collective-permute-start | bytes 589832 | tf_op jit(solution)/shard_map/ppermute | solution.py:635
  9.5 7.1 %collective-permute-start.2 = (f32[4,4,3,8,128]{4,3,2,1,0:T(8,128)S(1)}, f32[4,4,3,8,128]{4,3,2,1,0:T(8,128)S(1)}, u32[]{:S(2)}, u32[]{:S(2)}) collective-permute-start(f32[4,4,3,8,128]{4,3,2,1,0:T(8,128)S(1)} %get-tuple-element.36), channel_id=1, source_target_pairs={{8,0},{16,8},{24,16},{32,24},{40,32},{48,40},{56,48},{64,56},{72,6... | collective-permute-start | bytes 589832 | tf_op jit(solution)/shard_map/ppermute | solution.py:635
  10.8 7.8 %collective-permute-start.3 = (f32[2,4,3,8,128]{4,3,2,1,0:T(8,128)S(1)}, f32[2,4,3,8,128]{4,3,2,1,0:T(8,128)S(1)}, u32[]{:S(2)}, u32[]{:S(2)}) collective-permute-start(f32[2,4,3,8,128]{4,3,2,1,0:T(8,128)S(1)} %get-tuple-element.37), channel_id=1, source_target_pairs={{16,0},{24,8},{32,16},{40,24},{48,32},{56,40},{64,48},{72,56},{80,... | collective-permute-start | bytes 294920 | tf_op jit(solution)/shard_map/ppermute | solution.py:635
  18.6 25.9 %collective-permute-start.4 = (f32[16,4,3,8,128]{4,3,2,1,0:T(8,128)S(1)}, f32[16,4,3,8,128]{4,3,2,1,0:T(8,128)S(1)}, u32[]{:S(2)}, u32[]{:S(2)}) collective-permute-start(f32[16,4,3,8,128]{4,3,2,1,0:T(8,128)S(1)} %constant_dynamic-update-slice_fusion.refs_0_), channel_id=1, source_target_pairs={{0,1},{1,2},{2,3},{3,4},{4,5},{5,6},{6,7},{8,9},{9,10},{10,11},{11... | collective-permute-start | bytes 2359304 | tf_op jit(solution)/shard_map/ppermute | solution.py:635
  23.4 21.2 %collective-permute-start.5 = (f32[16,4,3,8,128]{4,3,2,1,0:T(8,128)S(1)}, f32[16,4,3,8,128]{4,3,2,1,0:T(8,128)S(1)}, u32[]{:S(2)}, u32[]{:S(2)}) collective-permute-start(f32[16,4,3,8,128]{4,3,2,1,0:T(8,128)S(1)} %constant_dynamic-update-slice_fusion.refs_0_), channel_id=1, source_target_pairs={{1,0},{2,1},{3,2},{4,3},{5,4},{6,5},{7,6},{9,8},{10,9},{11,10},{12... | collective-permute-start | bytes 2359304 | tf_op jit(solution)/shard_map/ppermute | solution.py:635
  26.3 35.3 %all-to-all-start.1 = ((f32[256,1,384]{2,1,0:T(1,128)}), f32[256,1,384]{2,1,0:T(1,128)S(1)}, u32[]{:S(2)}, u32[]{:S(2)}) async-start(f32[256,1,384]{2,1,0:T(1,128)} %broadcast_in_dim.27), calls=%async_computation.1 | async-start | bytes 786432 | tf_op jit(solution)/shard_map/all_to_all | solution.py:642
  62.5 23.3 %all-to-all-start = ((f32[256,1,384]{2,1,0:T(1,128)}), f32[256,1,384]{2,1,0:T(1,128)S(1)}, u32[]{:S(2)}, u32[]{:S(2)}) async-start(f32[256,1,384]{2,1,0:T(1,128)} %broadcast_in_dim.25), calls=%async_computation | async-start | bytes 786432 | tf_op jit(solution)/shard_map/all_to_all | solution.py:642
  68.8 17.0 %collective-permute-start.6 = (f32[8,8,128]{2,1,0:T(8,128)S(1)}, f32[8,8,128]{2,1,0:T(8,128)S(1)}, u32[]{:S(2)}, u32[]{:S(2)}) collective-permute-start(f32[8,8,128]{2,1,0:T(8,128)S(1)} %get-tuple-element.39), channel_id=1, source_target_pairs={{0,1},{1,2},{2,3},{3,4},{4,5},{5,6},{6,7},{8,9},{9,10},{10,11},{11... | collective-permute-start | bytes 98312 | tf_op jit(solution)/shard_map/ppermute | solution.py:635
  72.4 13.5 %collective-permute-start.7 = (f32[8,8,128]{2,1,0:T(8,128)S(1)}, f32[8,8,128]{2,1,0:T(8,128)S(1)}, u32[]{:S(2)}, u32[]{:S(2)}) collective-permute-start(f32[8,8,128]{2,1,0:T(8,128)S(1)} %get-tuple-element.39), channel_id=1, source_target_pairs={{1,0},{2,1},{3,2},{4,3},{5,4},{6,5},{7,6},{9,8},{10,9},{11,10},{12... | collective-permute-start | bytes 98312 | tf_op jit(solution)/shard_map/ppermute | solution.py:635
  74.3 11.6 %collective-permute-start.8 = (f32[12,8,128]{2,1,0:T(8,128)S(1)}, f32[12,8,128]{2,1,0:T(8,128)S(1)}, u32[]{:S(2)}, u32[]{:S(2)}) collective-permute-start(f32[12,8,128]{2,1,0:T(8,128)S(1)} %get-tuple-element.40), channel_id=1, source_target_pairs={{0,8},{8,16},{16,24},{24,32},{32,40},{40,48},{48,56},{56,64},{64,7... | collective-permute-start | bytes 147464 | tf_op jit(solution)/shard_map/ppermute | solution.py:635
  77.4 8.5 %collective-permute-start.9 = (f32[12,8,128]{2,1,0:T(8,128)S(1)}, f32[12,8,128]{2,1,0:T(8,128)S(1)}, u32[]{:S(2)}, u32[]{:S(2)}) collective-permute-start(f32[12,8,128]{2,1,0:T(8,128)S(1)} %get-tuple-element.41), channel_id=1, source_target_pairs={{8,0},{16,8},{24,16},{32,24},{40,32},{48,40},{56,48},{64,56},{72,6... | collective-permute-start | bytes 147464 | tf_op jit(solution)/shard_map/ppermute | solution.py:635
  92.9 8.9 %collective-permute-start.10 = (f32[3,2,3,8,128]{4,3,2,1,0:T(8,128)S(1)}, f32[3,2,3,8,128]{4,3,2,1,0:T(8,128)S(1)}, u32[]{:S(2)}, u32[]{:S(2)}) collective-permute-start(f32[3,2,3,8,128]{4,3,2,1,0:T(8,128)S(1)} %get-tuple-element.49), channel_id=1, source_target_pairs={{0,16},{8,24},{16,32},{24,40},{32,48},{40,56},{48,64},{56,72},{64,... | collective-permute-start | bytes 221192 | tf_op jit(solution)/shard_map/ppermute | solution.py:635
  97.1 4.7 %collective-permute-start.11 = (f32[4,2,3,8,128]{4,3,2,1,0:T(8,128)S(1)}, f32[4,2,3,8,128]{4,3,2,1,0:T(8,128)S(1)}, u32[]{:S(2)}, u32[]{:S(2)}) collective-permute-start(f32[4,2,3,8,128]{4,3,2,1,0:T(8,128)S(1)} %get-tuple-element.50), channel_id=1, source_target_pairs={{0,8},{8,16},{16,24},{24,32},{32,40},{40,48},{48,56},{56,64},{64,7... | collective-permute-start | bytes 294920 | tf_op jit(solution)/shard_map/ppermute | solution.py:635
  99.2 5.4 %collective-permute-start.12 = (f32[4,2,3,8,128]{4,3,2,1,0:T(8,128)S(1)}, f32[4,2,3,8,128]{4,3,2,1,0:T(8,128)S(1)}, u32[]{:S(2)}, u32[]{:S(2)}) collective-permute-start(f32[4,2,3,8,128]{4,3,2,1,0:T(8,128)S(1)} %get-tuple-element.50), channel_id=1, source_target_pairs={{8,0},{16,8},{24,16},{32,24},{40,32},{48,40},{56,48},{64,56},{72,6... | collective-permute-start | bytes 294920 | tf_op jit(solution)/shard_map/ppermute | solution.py:635
  100.5 6.9 %collective-permute-start.13 = (f32[3,2,3,8,128]{4,3,2,1,0:T(8,128)S(1)}, f32[3,2,3,8,128]{4,3,2,1,0:T(8,128)S(1)}, u32[]{:S(2)}, u32[]{:S(2)}) collective-permute-start(f32[3,2,3,8,128]{4,3,2,1,0:T(8,128)S(1)} %get-tuple-element.51), channel_id=1, source_target_pairs={{16,0},{24,8},{32,16},{40,24},{48,32},{56,40},{64,48},{72,56},{80,... | collective-permute-start | bytes 221192 | tf_op jit(solution)/shard_map/ppermute | solution.py:635
  107.5 11.1 %collective-permute-start.14 = (f32[116,8,128]{2,1,0:T(8,128)S(1)}, f32[116,8,128]{2,1,0:T(8,128)S(1)}, u32[]{:S(2)}, u32[]{:S(2)}) collective-permute-start(f32[116,8,128]{2,1,0:T(8,128)S(1)} %pad_maximum_fusion.refs_0_), channel_id=1, source_target_pairs={{0,1},{1,2},{2,3},{3,4},{4,5},{5,6},{6,7},{8,9},{9,10},{10,11},{11... | collective-permute-start | bytes 1425416 | tf_op jit(solution)/shard_map/ppermute | solution.py:635
  113.0 10.0 %collective-permute-start.15 = (f32[116,8,128]{2,1,0:T(8,128)S(1)}, f32[116,8,128]{2,1,0:T(8,128)S(1)}, u32[]{:S(2)}, u32[]{:S(2)}) collective-permute-start(f32[116,8,128]{2,1,0:T(8,128)S(1)} %pad_maximum_fusion.refs_0_), channel_id=1, source_target_pairs={{1,0},{2,1},{3,2},{4,3},{5,4},{6,5},{7,6},{9,8},{10,9},{11,10},{12... | collective-permute-start | bytes 1425416 | tf_op jit(solution)/shard_map/ppermute | solution.py:635
  131.0 31.9 %all-to-all-start.2 = ((f32[256,1,384]{2,1,0:T(1,128)}), f32[256,1,384]{2,1,0:T(1,128)S(1)}, u32[]{:S(2)}, u32[]{:S(2)}) async-start(f32[256,1,384]{2,1,0:T(1,128)} %broadcast_in_dim.29), calls=%async_computation.2 | async-start | bytes 786432 | tf_op jit(solution)/shard_map/all_to_all | solution.py:642
  145.8 17.1 %collective-permute-start.18 = (f32[12,8,128]{2,1,0:T(8,128)S(1)}, f32[12,8,128]{2,1,0:T(8,128)S(1)}, u32[]{:S(2)}, u32[]{:S(2)}) collective-permute-start(f32[12,8,128]{2,1,0:T(8,128)S(1)} %get-tuple-element.57), channel_id=1, source_target_pairs={{0,8},{8,16},{16,24},{24,32},{32,40},{40,48},{48,56},{56,64},{64,7... | collective-permute-start | bytes 147464 | tf_op jit(solution)/shard_map/ppermute | solution.py:635
  149.1 13.8 %collective-permute-start.19 = (f32[12,8,128]{2,1,0:T(8,128)S(1)}, f32[12,8,128]{2,1,0:T(8,128)S(1)}, u32[]{:S(2)}, u32[]{:S(2)}) collective-permute-start(f32[12,8,128]{2,1,0:T(8,128)S(1)} %get-tuple-element.58), channel_id=1, source_target_pairs={{8,0},{16,8},{24,16},{32,24},{40,32},{48,40},{56,48},{64,56},{72,6... | collective-permute-start | bytes 147464 | tf_op jit(solution)/shard_map/ppermute | solution.py:635
  150.4 12.5 %collective-permute-start.16 = (f32[8,8,128]{2,1,0:T(8,128)S(1)}, f32[8,8,128]{2,1,0:T(8,128)S(1)}, u32[]{:S(2)}, u32[]{:S(2)}) collective-permute-start(f32[8,8,128]{2,1,0:T(8,128)S(1)} %get-tuple-element.56), channel_id=1, source_target_pairs={{0,1},{1,2},{2,3},{3,4},{4,5},{5,6},{6,7},{8,9},{9,10},{10,11},{11... | collective-permute-start | bytes 98312 | tf_op jit(solution)/shard_map/ppermute | solution.py:635
  154.1 8.9 %collective-permute-start.17 = (f32[8,8,128]{2,1,0:T(8,128)S(1)}, f32[8,8,128]{2,1,0:T(8,128)S(1)}, u32[]{:S(2)}, u32[]{:S(2)}) collective-permute-start(f32[8,8,128]{2,1,0:T(8,128)S(1)} %get-tuple-element.56), channel_id=1, source_target_pairs={{1,0},{2,1},{3,2},{4,3},{5,4},{6,5},{7,6},{9,8},{10,9},{11,10},{12... | collective-permute-start | bytes 98312 | tf_op jit(solution)/shard_map/ppermute | solution.py:635

commit v8 on v5

--- a/solution.py
+++ b/solution.py
@@ -85,19 +85,22 @@
     return total + (up + down)
 
 
-def sweep(old, new, weight, weight_at, source, source_at, low, high, count, step, scale):
+def sweep(old, new, weight, weight_at, source, source_at, low, high, count, step, scale, rows=(8, 32)):
+    top, bottom = rows
+    inner = slice(top - 8, bottom - 8)
+
     def body(x, _):
         for r in range(count):
             parts = []
             for c in range(2):
-                total = neighbour(old, x, c, r, count, step)
+                total = neighbour(old, x, c, r, count, step, top, bottom)
                 if scale != 1.0:
                     total = total * scale
-                parts.append(source[x + source_at, c, r] + total)
-            w = [weight[x + weight_at, c, r] for c in range(2)]
+                parts.append(source[x + source_at, c, r, inner, :] + total)
+            w = [weight[x + weight_at, c, r, inner, :] for c in range(2)]
             moved = product(w, parts)
             for c in range(2):
-                new[x, c, r, 8:32, :] = (1.0 - OMEGA) * old[x, c, r, 8:32, :] + moved[c]
+                new[x, c, r, top:bottom, :] = (1.0 - OMEGA) * old[x, c, r, top:bottom, :] + moved[c]
         return 0
 
     lax.fori_loop(low, high, body, 0)
@@ -111,7 +114,7 @@
     lax.fori_loop(0, count, body, 0)
 
 
-def clear_edges(ref, count):
+def clear_edges(ref, count, begin=0):
     zero = jnp.zeros((8, 128), F32)
 
     def body(x, _):
@@ -121,7 +124,7 @@
                 ref[x, c, r, 32:40, :] = zero
         return 0
 
-    lax.fori_loop(0, count, body, 0)
+    lax.fori_loop(begin, count, body, 0)
 
 
 def dense(parts):
@@ -232,14 +235,6 @@
 
 
 def down_body(v, source, weight, diag, weight_one, diag_one, first_copy):
-    def first(x, _):
-        for r in range(4):
-            e = product([weight[x, c, r] for c in range(2)], [source[x, c, r] for c in range(2)])
-            for c in range(2):
-                v.start[x, c, r, 8:32, :] = e[c]
-        return 0
-
-    lax.fori_loop(0, 16, first, 0)
     sweep(v.start, v.guess, weight, 0, source, 0, 1, 15, 4, 1, 1.0)
     copies = [keep(v, first_copy, v.guess.at[2:14, :, :, 8:32, :], v.out_guess)]
 
@@ -302,6 +297,12 @@
                 target[x, c, r, 8 * tile : 8 * tile + 8, :] = parts[r]
 
 
+def begin_from(v, x, r, source, weight):
+    e = product(weight, source)
+    for c in range(2):
+        v.start[x, c, r, 8:32, :] = e[c]
+
+
 def clear_down(v):
     clear_edges(v.start, 16)
     clear_edges(v.guess, 16)
@@ -319,6 +320,7 @@
             w = scaled_inverse(v.diag[x, 0, r], v.diag[x, 1, r], 1.0)
             for c in range(2):
                 v.weight[x, c, r] = w[c]
+            begin_from(v, x, r, [v.source[x, c, r] for c in range(2)], w)
         return 0
 
     lax.fori_loop(0, 16, filled, 0)
@@ -396,18 +398,22 @@
                 row = slice(c * 4 + r, c * 4 + r + 1)
                 v.first[x + 7, c, r, 7:8, :] = v.low[EDGE + x, row]
                 v.first[x + 7, c, r, 32:33, :] = v.high[EDGE + 4 + x, row]
-    for load in loads:
+    for load in loads[0:3]:
         load.wait()
 
     def residual(x, _):
         for r in range(4):
             moved = product([v.diag[x, c, r] for c in range(2)], [v.first[x + 1, c, r, 8:32, :] for c in range(2)])
-            for c in range(2):
-                v.source[x, c, r] = v.right[x, c, r] + neighbour(v.first, x + 1, c, r, 4, 1) - moved[c]
+            value = [v.right[x, c, r] + neighbour(v.first, x + 1, c, r, 4, 1) - moved[c] for c in range(2)]
+            for c in range(2):
+                v.source[x, c, r] = value[c]
+            begin_from(v, x, r, value, [v.weight[x, c, r] for c in range(2)])
         return 0
 
     lax.fori_loop(0, 16, residual, 0)
     copies = [keep(v, 8, v.source.at[4:12], v.out_source)]
+    for load in loads[3:5]:
+        load.wait()
     copies += down_body(v, v.source, v.weight, v.diag, v.weight_one, v.diag_one, 5)
     for copy in copies:
         copy.wait()
@@ -530,8 +536,8 @@
     answer = solve_two(v.where[0] - begin, v.source_two, v.weight_two, v.ping, v.pong, window, planes, groups)
     clear_edges(v.one, count)
     clear_edges(v.one_next, count)
-    clear_edges(v.ea, 16)
-    clear_edges(v.eb, 16)
+    clear_edges(v.ea, 12, 4)
+    clear_edges(v.eb, 11, 5)
     for load in loads:
         load.wait()
 
@@ -561,7 +567,7 @@
 
     lax.fori_loop(2, 6, correct, 0)
     sweep(v.ea, v.eb, v.weight, 0, v.source, 0, 5, 11, 4, 1, 1.0)
-    sweep(v.eb, v.ea, v.weight, 0, v.source, 0, 6, 10, 4, 1, 1.0)
+    sweep(v.eb, v.ea, v.weight, 0, v.source, 0, 6, 10, 4, 1, 1.0, (16, 24) if second else (8, 32))
     return copies
 
 

time: 168 us -> 167 us (level)
  no operation moved by 1% of the time
where the time goes in v8:
time: 167 us; the launch traced here: 166 us
  starting transfers between devices  86.2 us (52%)
  waiting for transfers between devices  48.2 us (29%)
  Pallas kernels  28.9 us (17%)
  local copies, waits for them, and re-layouts  2.42 us (1%)
    ppermute x20, starting transfers between devices, shifted(): return lax.ppermute(block, axis, pairs)  55.6 us
    all_to_all x2, starting transfers between devices, gather_two(): lax.all_to_all(sent, ('gx', 'gy'), 0, 0).reshape(count_x, count_y, width)  30.7 us
    pallas_call x5, Pallas kernels, run(): pl.pallas_call(lambda *refs: kernel(SimpleNamespace(**dict(zip(names, ref...  28.9 us
    ppermute x20, waiting for transfers between devices, shifted(): return lax.ppermute(block, axis, pairs)  26.2 us
    all_to_all x2, waiting for transfers between devices, gather_two(): lax.all_to_all(sent, ('gx', 'gy'), 0, 0).reshape(count_x, count_y, width)  22 us
  transfers between devices with their start and end apart: 22, of which 11 were waited for; matrix products, arithmetic and copies ran while one was open for 0% of the time, Pallas kernels for 0%

profile of v8, /device:TPU:1, one launch (start us, length us, event | category | flops | bytes accessed | tf_op | source)
XLA Modules:
  0.0 166.3 jit_solution(8750602535140581702)
XLA Ops:
  0.0 1.5 pack.1
  1.5 5.6 %collective-permute-start = (f32[2,4,3,8,128]{4,3,2,1,0:T(8,128)S(1)}, f32[2,4,3,8,128]{4,3,2,1,0:T(8,128)S(1)}, u32[]{:S(2)}, u32[]{:S(2)}) collective-permute-start(f32[2,4,3,8,128]{4,3,2,1,0:T(8,128)S(1)} %get-tuple-element.35), channel_id=1, source_target_pairs={{0,16},{8,24},{16,32},{24,40},{32,48},{40,56},{48,64},{56,72},{64,... | collective-permute-start | bytes 294920 | tf_op jit(solution)/shard_map/ppermute | solution.py:646
  7.2 2.3 %collective-permute-start.1 = (f32[4,4,3,8,128]{4,3,2,1,0:T(8,128)S(1)}, f32[4,4,3,8,128]{4,3,2,1,0:T(8,128)S(1)}, u32[]{:S(2)}, u32[]{:S(2)}) collective-permute-start(f32[4,4,3,8,128]{4,3,2,1,0:T(8,128)S(1)} %get-tuple-element.36), channel_id=1, source_target_pairs={{0,8},{8,16},{16,24},{24,32},{32,40},{40,48},{48,56},{56,64},{64,7... | collective-permute-start | bytes 589832 | tf_op jit(solution)/shard_map/ppermute | solution.py:646
  9.5 1.3 collective-permute-start.2
  10.8 1.3 collective-permute-start.3
  12.1 0.0 collective-permute-done
  12.1 0.6 collective-permute-done.1
  12.8 3.8 %collective-permute-done.2 = f32[4,4,3,8,128]{4,3,2,1,0:T(8,128)S(1)} collective-permute-done((f32[4,4,3,8,128]{4,3,2,1,0:T(8,128)S(1)}, f32[4,4,3,8,128]{4,3,2,1,0:T(8,128)S(1)}, u32[]{:S(2)}, u32[]{:S(2)}) %collective-permute-start.2) | collective-permute-done | bytes 196640 | tf_op jit(solution)/shard_map/ppermute | solution.py:646
  16.7 2.0 %collective-permute-done.3 = f32[2,4,3,8,128]{4,3,2,1,0:T(8,128)S(1)} collective-permute-done((f32[2,4,3,8,128]{4,3,2,1,0:T(8,128)S(1)}, f32[2,4,3,8,128]{4,3,2,1,0:T(8,128)S(1)}, u32[]{:S(2)}, u32[]{:S(2)}) %collective-permute-start.3) | collective-permute-done | bytes 98336 | tf_op jit(solution)/shard_map/ppermute | solution.py:646
  18.6 3.7 %collective-permute-start.5 = (f32[16,4,3,8,128]{4,3,2,1,0:T(8,128)S(1)}, f32[16,4,3,8,128]{4,3,2,1,0:T(8,128)S(1)}, u32[]{:S(2)}, u32[]{:S(2)}) collective-permute-start(f32[16,4,3,8,128]{4,3,2,1,0:T(8,128)S(1)} %constant_dynamic-update-slice_fusion.refs_0_), channel_id=1, source_target_pairs={{1,0},{2,1},{3,2},{4,3},{5,4},{6,5},{7,6},{9,8},{10,9},{11,10},{12... | collective-permute-start | bytes 2359304 | tf_op jit(solution)/shard_map/ppermute | solution.py:646
  22.3 3.0 %collective-permute-start.4 = (f32[16,4,3,8,128]{4,3,2,1,0:T(8,128)S(1)}, f32[16,4,3,8,128]{4,3,2,1,0:T(8,128)S(1)}, u32[]{:S(2)}, u32[]{:S(2)}) collective-permute-start(f32[16,4,3,8,128]{4,3,2,1,0:T(8,128)S(1)} %constant_dynamic-update-slice_fusion.refs_0_), channel_id=1, source_target_pairs={{0,1},{1,2},{2,3},{3,4},{4,5},{5,6},{6,7},{8,9},{9,10},{10,11},{11... | collective-permute-start | bytes 2359304 | tf_op jit(solution)/shard_map/ppermute | solution.py:646
  25.3 7.7 %collective-permute-done.5.refs_2_ = f32[16,4,3,8,128]{4,3,2,1,0:T(8,128)S(1)} collective-permute-done((f32[16,4,3,8,128]{4,3,2,1,0:T(8,128)S(1)}, f32[16,4,3,8,128]{4,3,2,1,0:T(8,128)S(1)}, u32[]{:S(2)}, u32[]{:S(2)}) %collective-permute-start.5) | collective-permute-done | bytes 786464 | tf_op jit(solution)/shard_map/ppermute | solution.py:646
  33.0 1.2 collective-permute-done.4.refs_1_
  34.2 6.0 %down_first.1 = (f32[16,2,4,24,128]{4,3,2,1,0:T(8,128)}, f32[16,2,4,24,128]{4,3,2,1,0:T(8,128)}, f32[16,2,4,24,128]{4,3,2,1,0:T(8,128)}, f32[6,2,2,24,128]{4,3,2...) custom-call(f32[16,4,3,8,128]{4,3,2,1,0:T(8,128)S(1)} %constant_dyna, ...), custom_call_target="tpu_custom_call" | custom-call | tf_op jit(solution)/shard_map/down_first/pallas_call | solution.py:29
  40.3 1.3 broadcast_in_dim.17
  41.5 19.0 %all-to-all-start = ((f32[256,1,768]{2,1,0:T(1,128)}), f32[256,1,768]{2,1,0:T(1,128)S(1)}, u32[]{:S(2)}, u32[]{:S(2)}) async-start(f32[256,1,768]{2,1,0:T(1,128)} %broadcast_in_dim.17), calls=%async_computation | async-start | bytes 1572864 | tf_op jit(solution)/shard_map/all_to_all | solution.py:653
  60.5 4.1 %collective-permute-start.7 = (f32[8,8,128]{2,1,0:T(8,128)S(1)}, f32[8,8,128]{2,1,0:T(8,128)S(1)}, u32[]{:S(2)}, u32[]{:S(2)}) collective-permute-start(f32[8,8,128]{2,1,0:T(8,128)S(1)} %get-tuple-element.40), channel_id=1, source_target_pairs={{1,0},{2,1},{3,2},{4,3},{5,4},{6,5},{7,6},{9,8},{10,9},{11,10},{12... | collective-permute-start | bytes 98312 | tf_op jit(solution)/shard_map/ppermute | solution.py:646
  64.6 1.9 %collective-permute-start.6 = (f32[8,8,128]{2,1,0:T(8,128)S(1)}, f32[8,8,128]{2,1,0:T(8,128)S(1)}, u32[]{:S(2)}, u32[]{:S(2)}) collective-permute-start(f32[8,8,128]{2,1,0:T(8,128)S(1)} %get-tuple-element.40), channel_id=1, source_target_pairs={{0,1},{1,2},{2,3},{3,4},{4,5},{5,6},{6,7},{8,9},{9,10},{10,11},{11... | collective-permute-start | bytes 98312 | tf_op jit(solution)/shard_map/ppermute | solution.py:646
  66.5 2.9 %collective-permute-start.8 = (f32[12,8,128]{2,1,0:T(8,128)S(1)}, f32[12,8,128]{2,1,0:T(8,128)S(1)}, u32[]{:S(2)}, u32[]{:S(2)}) collective-permute-start(f32[12,8,128]{2,1,0:T(8,128)S(1)} %get-tuple-element.41), channel_id=1, source_target_pairs={{0,8},{8,16},{16,24},{24,32},{32,40},{40,48},{48,56},{56,64},{64,7... | collective-permute-start | bytes 147464 | tf_op jit(solution)/shard_map/ppermute | solution.py:646
  69.4 1.3 collective-permute-start.9
  70.7 0.1 pad_add_fusion.refs_0_
  70.8 15.1 %all-to-all-done = f32[256,1,768]{2,1,0:T(1,128)S(1)} async-done(((f32[256,1,768]{2,1,0:T(1,128)}), f32[256,1,768]{2,1,0:T(1,128)S(1)}, u32[]{:S(2)}, u32[]{:S(2)}) %all-to-all-start) | async-done | bytes 786464 | tf_op jit(solution)/shard_map/all_to_all | solution.py:653
  85.9 0.1 copy.9
  85.9 0.0 collective-permute-done.8.refs_4_
  86.0 7.0 %up_first.1 = (f32[4,2,3,8,128]{4,3,2,1,0:T(8,128)S(1)}, f32[3,2,3,8,128]{4,3,2,1,0:T(8,128)S(1)}, f32[3,2,3,8,128]{4,3,2,1,0:T(8,128)S(1)}, f32[8,8,128]{2,1,0:...) custom-call(s32[2]{0:T(128)S(1)} %pad_add_fusion.refs_0_, f32[32,8,768]{2,1,0:T(8,128)S(1)} %bitcast.9, ...), custom_call_target="tpu_custom_call" | custom-call | tf_op jit(solution)/shard_map/up_first/pallas_call | solution.py:29
  92.9 4.0 %collective-permute-start.10 = (f32[3,2,3,8,128]{4,3,2,1,0:T(8,128)S(1)}, f32[3,2,3,8,128]{4,3,2,1,0:T(8,128)S(1)}, u32[]{:S(2)}, u32[]{:S(2)}) collective-permute-start(f32[3,2,3,8,128]{4,3,2,1,0:T(8,128)S(1)} %get-tuple-element.49), channel_id=1, source_target_pairs={{0,16},{8,24},{16,32},{24,40},{32,48},{40,56},{48,64},{56,72},{64,... | collective-permute-start | bytes 221192 | tf_op jit(solution)/shard_map/ppermute | solution.py:646
  97.0 1.3 collective-permute-start.12
  98.3 4.0 %collective-permute-start.11 = (f32[4,2,3,8,128]{4,3,2,1,0:T(8,128)S(1)}, f32[4,2,3,8,128]{4,3,2,1,0:T(8,128)S(1)}, u32[]{:S(2)}, u32[]{:S(2)}) collective-permute-start(f32[4,2,3,8,128]{4,3,2,1,0:T(8,128)S(1)} %get-tuple-element.50), channel_id=1, source_target_pairs={{0,8},{8,16},{16,24},{24,32},{32,40},{40,48},{48,56},{56,64},{64,7... | collective-permute-start | bytes 294920 | tf_op jit(solution)/shard_map/ppermute | solution.py:646
  102.3 1.3 collective-permute-start.13
  103.6 0.0 collective-permute-done.10
  103.6 0.3 collective-permute-done.11
  103.9 0.0 collective-permute-done.12
  103.9 4.9 %collective-permute-done.13 = f32[3,2,3,8,128]{4,3,2,1,0:T(8,128)S(1)} collective-permute-done((f32[3,2,3,8,128]{4,3,2,1,0:T(8,128)S(1)}, f32[3,2,3,8,128]{4,3,2,1,0:T(8,128)S(1)}, u32[]{:S(2)}, u32[]{:S(2)}) %collective-permute-start.13) | collective-permute-done | bytes 73760 | tf_op jit(solution)/shard_map/ppermute | solution.py:646
  108.9 5.3 %collective-permute-start.15 = (f32[116,8,128]{2,1,0:T(8,128)S(1)}, f32[116,8,128]{2,1,0:T(8,128)S(1)}, u32[]{:S(2)}, u32[]{:S(2)}) collective-permute-start(f32[116,8,128]{2,1,0:T(8,128)S(1)} %pad_maximum_fusion.refs_0_), channel_id=1, source_target_pairs={{1,0},{2,1},{3,2},{4,3},{5,4},{6,5},{7,6},{9,8},{10,9},{11,10},{12... | collective-permute-start | bytes 1425416 | tf_op jit(solution)/shard_map/ppermute | solution.py:646
  114.3 2.1 %collective-permute-start.14 = (f32[116,8,128]{2,1,0:T(8,128)S(1)}, f32[116,8,128]{2,1,0:T(8,128)S(1)}, u32[]{:S(2)}, u32[]{:S(2)}) collective-permute-start(f32[116,8,128]{2,1,0:T(8,128)S(1)} %pad_maximum_fusion.refs_0_), channel_id=1, source_target_pairs={{0,1},{1,2},{2,3},{3,4},{4,5},{5,6},{6,7},{8,9},{9,10},{10,11},{11... | collective-permute-start | bytes 1425416 | tf_op jit(solution)/shard_map/ppermute | solution.py:646
  116.4 4.4 %collective-permute-done.15.refs_2_ = f32[116,8,128]{2,1,0:T(8,128)S(1)} collective-permute-done((f32[116,8,128]{2,1,0:T(8,128)S(1)}, f32[116,8,128]{2,1,0:T(8,128)S(1)}, u32[]{:S(2)}, u32[]{:S(2)}) %collective-permute-start.15) | collective-permute-done | bytes 475168 | tf_op jit(solution)/shard_map/ppermute | solution.py:646
  120.8 1.2 collective-permute-done.14.refs_1_
  122.0 6.9 %down_second.1 = (f32[8,2,4,24,128]{4,3,2,1,0:T(8,128)}, f32[12,2,4,24,128]{4,3,2,1,0:T(8,128)}, f32[6,2,2,24,128]{4,3,2,1,0:T(8,128)}, f32[6,2,2,40,128]{4,3,2,...) custom-call(f32[116,8,128]{2,1,0:T(8,128)S(1)} %pad_maximum_fusion.r, ...), custom_call_target="tpu_custom_call" | custom-call | tf_op jit(solution)/shard_map/down_second/pallas_call | solution.py:29
  129.0 1.0 broadcast_in_dim.19
  129.9 11.7 %all-to-all-start.1 = ((f32[256,1,384]{2,1,0:T(1,128)}), f32[256,1,384]{2,1,0:T(1,128)S(1)}, u32[]{:S(2)}, u32[]{:S(2)}) async-start(f32[256,1,384]{2,1,0:T(1,128)} %broadcast_in_dim.19), calls=%async_computation.1 | async-start | bytes 786432 | tf_op jit(solution)/shard_map/all_to_all | solution.py:653
  141.6 3.3 %collective-permute-start.18 = (f32[12,8,128]{2,1,0:T(8,128)S(1)}, f32[12,8,128]{2,1,0:T(8,128)S(1)}, u32[]{:S(2)}, u32[]{:S(2)}) collective-permute-start(f32[12,8,128]{2,1,0:T(8,128)S(1)} %get-tuple-element.57), channel_id=1, source_target_pairs={{0,8},{8,16},{16,24},{24,32},{32,40},{40,48},{48,56},{56,64},{64,7... | collective-permute-start | bytes 147464 | tf_op jit(solution)/shard_map/ppermute | solution.py:646
  144.9 1.3 collective-permute-start.19
  146.2 2.6 %collective-permute-start.17 = (f32[8,8,128]{2,1,0:T(8,128)S(1)}, f32[8,8,128]{2,1,0:T(8,128)S(1)}, u32[]{:S(2)}, u32[]{:S(2)}) collective-permute-start(f32[8,8,128]{2,1,0:T(8,128)S(1)} %get-tuple-element.56), channel_id=1, source_target_pairs={{1,0},{2,1},{3,2},{4,3},{5,4},{6,5},{7,6},{9,8},{10,9},{11,10},{12... | collective-permute-start | bytes 98312 | tf_op jit(solution)/shard_map/ppermute | solution.py:646
  148.8 3.0 %collective-permute-start.16 = (f32[8,8,128]{2,1,0:T(8,128)S(1)}, f32[8,8,128]{2,1,0:T(8,128)S(1)}, u32[]{:S(2)}, u32[]{:S(2)}) collective-permute-start(f32[8,8,128]{2,1,0:T(8,128)S(1)} %get-tuple-element.56), channel_id=1, source_target_pairs={{0,1},{1,2},{2,3},{3,4},{4,5},{5,6},{6,7},{8,9},{9,10},{10,11},{11... | collective-permute-start | bytes 98312 | tf_op jit(solution)/shard_map/ppermute | solution.py:646
  151.8 6.9 %all-to-all-done.1 = f32[256,1,384]{2,1,0:T(1,128)S(1)} async-done(((f32[256,1,384]{2,1,0:T(1,128)}), f32[256,1,384]{2,1,0:T(1,128)S(1)}, u32[]{:S(2)}, u32[]{:S(2)}) %all-to-all-start.1) | async-done | bytes 393248 | tf_op jit(solution)/shard_map/all_to_all | solution.py:653
  158.7 0.0 collective-permute-done.18.refs_4_
  158.7 0.0 collective-permute-done.19.refs_5_
  158.7 7.5 %up_second.1 = f32[2,4,8,384]{3,2,1,0:T(8,128)} custom-call(s32[2]{0:T(128)S(1)} %pad_add_fusion.refs_0_, f32[32,8,384]{2,1,0:T(8,128)S(1)} %bitcast.10, f32[8,8,128]{2,1,0:T(8,128)S(1)} %collective-permute-done.16.refs_2_, f32[8,8,128]{2,1,0:T(8,128)S(1)} %collective-permute-done.17.refs_3_, f32[12,8,128]{2,1,0:T(8,128)S(1)} %collective-permute-done.18.refs_4_, ...), custom_call_target="tpu_custom_call" | custom-call | tf_op jit(solution)/shard_map/up_second/pallas_call | solution.py:29
  (19 shorter events, 0.2 us)
Async XLA Ops:
  1.5 10.6 %collective-permute-start = (f32[2,4,3,8,128]{4,3,2,1,0:T(8,128)S(1)}, f32[2,4,3,8,128]{4,3,2,1,0:T(8,128)S(1)}, u32[]{:S(2)}, u32[]{:S(2)}) collective-permute-start(f32[2,4,3,8,128]{4,3,2,1,0:T(8,128)S(1)} %get-tuple-element.35), channel_id=1, source_target_pairs={{0,16},{8,24},{16,32},{24,40},{32,48},{40,56},{48,64},{56,72},{64,... | collective-permute-start | bytes 294920 | tf_op jit(solution)/shard_map/ppermute | solution.py:646
  7.2 5.6 %collective-permute-start.1 = (f32[4,4,3,8,128]{4,3,2,1,0:T(8,128)S(1)}, f32[4,4,3,8,128]{4,3,2,1,0:T(8,128)S(1)}, u32[]{:S(2)}, u32[]{:S(2)}) collective-permute-start(f32[4,4,3,8,128]{4,3,2,1,0:T(8,128)S(1)} %get-tuple-element.36), channel_id=1, source_target_pairs={{0,8},{8,16},{16,24},{24,32},{32,40},{40,48},{48,56},{56,64},{64,7... | collective-permute-start | bytes 589832 | tf_op jit(solution)/shard_map/ppermute | solution.py:646
  9.5 7.1 %collective-permute-start.2 = (f32[4,4,3,8,128]{4,3,2,1,0:T(8,128)S(1)}, f32[4,4,3,8,128]{4,3,2,1,0:T(8,128)S(1)}, u32[]{:S(2)}, u32[]{:S(2)}) collective-permute-start(f32[4,4,3,8,128]{4,3,2,1,0:T(8,128)S(1)} %get-tuple-element.36), channel_id=1, source_target_pairs={{8,0},{16,8},{24,16},{32,24},{40,32},{48,40},{56,48},{64,56},{72,6... | collective-permute-start | bytes 589832 | tf_op jit(solution)/shard_map/ppermute | solution.py:646
  10.8 7.8 %collective-permute-start.3 = (f32[2,4,3,8,128]{4,3,2,1,0:T(8,128)S(1)}, f32[2,4,3,8,128]{4,3,2,1,0:T(8,128)S(1)}, u32[]{:S(2)}, u32[]{:S(2)}) collective-permute-start(f32[2,4,3,8,128]{4,3,2,1,0:T(8,128)S(1)} %get-tuple-element.37), channel_id=1, source_target_pairs={{16,0},{24,8},{32,16},{40,24},{48,32},{56,40},{64,48},{72,56},{80,... | collective-permute-start | bytes 294920 | tf_op jit(solution)/shard_map/ppermute | solution.py:646
  18.6 14.4 %collective-permute-start.5 = (f32[16,4,3,8,128]{4,3,2,1,0:T(8,128)S(1)}, f32[16,4,3,8,128]{4,3,2,1,0:T(8,128)S(1)}, u32[]{:S(2)}, u32[]{:S(2)}) collective-permute-start(f32[16,4,3,8,128]{4,3,2,1,0:T(8,128)S(1)} %constant_dynamic-update-slice_fusion.refs_0_), channel_id=1, source_target_pairs={{1,0},{2,1},{3,2},{4,3},{5,4},{6,5},{7,6},{9,8},{10,9},{11,10},{12... | collective-permute-start | bytes 2359304 | tf_op jit(solution)/shard_map/ppermute | solution.py:646
  22.3 11.9 %collective-permute-start.4 = (f32[16,4,3,8,128]{4,3,2,1,0:T(8,128)S(1)}, f32[16,4,3,8,128]{4,3,2,1,0:T(8,128)S(1)}, u32[]{:S(2)}, u32[]{:S(2)}) collective-permute-start(f32[16,4,3,8,128]{4,3,2,1,0:T(8,128)S(1)} %constant_dynamic-update-slice_fusion.refs_0_), channel_id=1, source_target_pairs={{0,1},{1,2},{2,3},{3,4},{4,5},{5,6},{6,7},{8,9},{9,10},{10,11},{11... | collective-permute-start | bytes 2359304 | tf_op jit(solution)/shard_map/ppermute | solution.py:646
  41.5 44.3 %all-to-all-start = ((f32[256,1,768]{2,1,0:T(1,128)}), f32[256,1,768]{2,1,0:T(1,128)S(1)}, u32[]{:S(2)}, u32[]{:S(2)}) async-start(f32[256,1,768]{2,1,0:T(1,128)} %broadcast_in_dim.17), calls=%async_computation | async-start | bytes 1572864 | tf_op jit(solution)/shard_map/all_to_all | solution.py:653
  60.5 25.4 %collective-permute-start.7 = (f32[8,8,128]{2,1,0:T(8,128)S(1)}, f32[8,8,128]{2,1,0:T(8,128)S(1)}, u32[]{:S(2)}, u32[]{:S(2)}) collective-permute-start(f32[8,8,128]{2,1,0:T(8,128)S(1)} %get-tuple-element.40), channel_id=1, source_target_pairs={{1,0},{2,1},{3,2},{4,3},{5,4},{6,5},{7,6},{9,8},{10,9},{11,10},{12... | collective-permute-start | bytes 98312 | tf_op jit(solution)/shard_map/ppermute | solution.py:646
  64.6 21.3 %collective-permute-start.6 = (f32[8,8,128]{2,1,0:T(8,128)S(1)}, f32[8,8,128]{2,1,0:T(8,128)S(1)}, u32[]{:S(2)}, u32[]{:S(2)}) collective-permute-start(f32[8,8,128]{2,1,0:T(8,128)S(1)} %get-tuple-element.40), channel_id=1, source_target_pairs={{0,1},{1,2},{2,3},{3,4},{4,5},{5,6},{6,7},{8,9},{9,10},{10,11},{11... | collective-permute-start | bytes 98312 | tf_op jit(solution)/shard_map/ppermute | solution.py:646
  66.5 19.4 %collective-permute-start.8 = (f32[12,8,128]{2,1,0:T(8,128)S(1)}, f32[12,8,128]{2,1,0:T(8,128)S(1)}, u32[]{:S(2)}, u32[]{:S(2)}) collective-permute-start(f32[12,8,128]{2,1,0:T(8,128)S(1)} %get-tuple-element.41), channel_id=1, source_target_pairs={{0,8},{8,16},{16,24},{24,32},{32,40},{40,48},{48,56},{56,64},{64,7... | collective-permute-start | bytes 147464 | tf_op jit(solution)/shard_map/ppermute | solution.py:646
  69.4 16.6 %collective-permute-start.9 = (f32[12,8,128]{2,1,0:T(8,128)S(1)}, f32[12,8,128]{2,1,0:T(8,128)S(1)}, u32[]{:S(2)}, u32[]{:S(2)}) collective-permute-start(f32[12,8,128]{2,1,0:T(8,128)S(1)} %get-tuple-element.42), channel_id=1, source_target_pairs={{8,0},{16,8},{24,16},{32,24},{40,32},{48,40},{56,48},{64,56},{72,6... | collective-permute-start | bytes 147464 | tf_op jit(solution)/shard_map/ppermute | solution.py:646
  92.9 10.7 %collective-permute-start.10 = (f32[3,2,3,8,128]{4,3,2,1,0:T(8,128)S(1)}, f32[3,2,3,8,128]{4,3,2,1,0:T(8,128)S(1)}, u32[]{:S(2)}, u32[]{:S(2)}) collective-permute-start(f32[3,2,3,8,128]{4,3,2,1,0:T(8,128)S(1)} %get-tuple-element.49), channel_id=1, source_target_pairs={{0,16},{8,24},{16,32},{24,40},{32,48},{40,56},{48,64},{56,72},{64,... | collective-permute-start | bytes 221192 | tf_op jit(solution)/shard_map/ppermute | solution.py:646
  97.0 6.9 %collective-permute-start.12 = (f32[4,2,3,8,128]{4,3,2,1,0:T(8,128)S(1)}, f32[4,2,3,8,128]{4,3,2,1,0:T(8,128)S(1)}, u32[]{:S(2)}, u32[]{:S(2)}) collective-permute-start(f32[4,2,3,8,128]{4,3,2,1,0:T(8,128)S(1)} %get-tuple-element.50), channel_id=1, source_target_pairs={{8,0},{16,8},{24,16},{32,24},{40,32},{48,40},{56,48},{64,56},{72,6... | collective-permute-start | bytes 294920 | tf_op jit(solution)/shard_map/ppermute | solution.py:646
  98.3 5.6 %collective-permute-start.11 = (f32[4,2,3,8,128]{4,3,2,1,0:T(8,128)S(1)}, f32[4,2,3,8,128]{4,3,2,1,0:T(8,128)S(1)}, u32[]{:S(2)}, u32[]{:S(2)}) collective-permute-start(f32[4,2,3,8,128]{4,3,2,1,0:T(8,128)S(1)} %get-tuple-element.50), channel_id=1, source_target_pairs={{0,8},{8,16},{16,24},{24,32},{32,40},{40,48},{48,56},{56,64},{64,7... | collective-permute-start | bytes 294920 | tf_op jit(solution)/shard_map/ppermute | solution.py:646
  102.3 6.6 %collective-permute-start.13 = (f32[3,2,3,8,128]{4,3,2,1,0:T(8,128)S(1)}, f32[3,2,3,8,128]{4,3,2,1,0:T(8,128)S(1)}, u32[]{:S(2)}, u32[]{:S(2)}) collective-permute-start(f32[3,2,3,8,128]{4,3,2,1,0:T(8,128)S(1)} %get-tuple-element.51), channel_id=1, source_target_pairs={{16,0},{24,8},{32,16},{40,24},{48,32},{56,40},{64,48},{72,56},{80,... | collective-permute-start | bytes 221192 | tf_op jit(solution)/shard_map/ppermute | solution.py:646
  108.9 11.9 %collective-permute-start.15 = (f32[116,8,128]{2,1,0:T(8,128)S(1)}, f32[116,8,128]{2,1,0:T(8,128)S(1)}, u32[]{:S(2)}, u32[]{:S(2)}) collective-permute-start(f32[116,8,128]{2,1,0:T(8,128)S(1)} %pad_maximum_fusion.refs_0_), channel_id=1, source_target_pairs={{1,0},{2,1},{3,2},{4,3},{5,4},{6,5},{7,6},{9,8},{10,9},{11,10},{12... | collective-permute-start | bytes 1425416 | tf_op jit(solution)/shard_map/ppermute | solution.py:646
  114.3 7.7 %collective-permute-start.14 = (f32[116,8,128]{2,1,0:T(8,128)S(1)}, f32[116,8,128]{2,1,0:T(8,128)S(1)}, u32[]{:S(2)}, u32[]{:S(2)}) collective-permute-start(f32[116,8,128]{2,1,0:T(8,128)S(1)} %pad_maximum_fusion.refs_0_), channel_id=1, source_target_pairs={{0,1},{1,2},{2,3},{3,4},{4,5},{5,6},{6,7},{8,9},{9,10},{10,11},{11... | collective-permute-start | bytes 1425416 | tf_op jit(solution)/shard_map/ppermute | solution.py:646
  129.9 28.7 %all-to-all-start.1 = ((f32[256,1,384]{2,1,0:T(1,128)}), f32[256,1,384]{2,1,0:T(1,128)S(1)}, u32[]{:S(2)}, u32[]{:S(2)}) async-start(f32[256,1,384]{2,1,0:T(1,128)} %broadcast_in_dim.19), calls=%async_computation.1 | async-start | bytes 786432 | tf_op jit(solution)/shard_map/all_to_all | solution.py:653
  141.6 17.1 %collective-permute-start.18 = (f32[12,8,128]{2,1,0:T(8,128)S(1)}, f32[12,8,128]{2,1,0:T(8,128)S(1)}, u32[]{:S(2)}, u32[]{:S(2)}) collective-permute-start(f32[12,8,128]{2,1,0:T(8,128)S(1)} %get-tuple-element.57), channel_id=1, source_target_pairs={{0,8},{8,16},{16,24},{24,32},{32,40},{40,48},{48,56},{56,64},{64,7... | collective-permute-start | bytes 147464 | tf_op jit(solution)/shard_map/ppermute | solution.py:646
  144.9 13.8 %collective-permute-start.19 = (f32[12,8,128]{2,1,0:T(8,128)S(1)}, f32[12,8,128]{2,1,0:T(8,128)S(1)}, u32[]{:S(2)}, u32[]{:S(2)}) collective-permute-start(f32[12,8,128]{2,1,0:T(8,128)S(1)} %get-tuple-element.58), channel_id=1, source_target_pairs={{8,0},{16,8},{24,16},{32,24},{40,32},{48,40},{56,48},{64,56},{72,6... | collective-permute-start | bytes 147464 | tf_op jit(solution)/shard_map/ppermute | solution.py:646
  146.2 12.5 %collective-permute-start.17 = (f32[8,8,128]{2,1,0:T(8,128)S(1)}, f32[8,8,128]{2,1,0:T(8,128)S(1)}, u32[]{:S(2)}, u32[]{:S(2)}) collective-permute-start(f32[8,8,128]{2,1,0:T(8,128)S(1)} %get-tuple-element.56), channel_id=1, source_target_pairs={{1,0},{2,1},{3,2},{4,3},{5,4},{6,5},{7,6},{9,8},{10,9},{11,10},{12... | collective-permute-start | bytes 98312 | tf_op jit(solution)/shard_map/ppermute | solution.py:646
  148.8 9.9 %collective-permute-start.16 = (f32[8,8,128]{2,1,0:T(8,128)S(1)}, f32[8,8,128]{2,1,0:T(8,128)S(1)}, u32[]{:S(2)}, u32[]{:S(2)}) collective-permute-start(f32[8,8,128]{2,1,0:T(8,128)S(1)} %get-tuple-element.56), channel_id=1, source_target_pairs={{0,1},{1,2},{2,3},{3,4},{4,5},{5,6},{6,7},{8,9},{9,10},{10,11},{11... | collective-permute-start | bytes 98312 | tf_op jit(solution)/shard_map/ppermute | solution.py:646
